TPU v7x, 32 devices: a whole 2x2x4 slice. The times are simulated.
32 devices in a mesh: row: 16 (over z, y, core), col: 2 (over x).
Axes of the slice: x: 2, y: 2, z: 4, core: 2. Of those that a mesh axis runs over, the one named last changes fastest.
Arguments:
- tokens: bfloat16 [8192, 512], P('row', 'col'), may hold values from -6 to 6
- prev_logits: bfloat16 [8, 8192, 1024], P('col', 'row'), may hold values from -5 to 5
- doc_lengths: int32 [1, 33], replicated, may hold values from 1 to 512, as said below
- qkv_weight: bfloat16 [3, 512, 512], P(None, 'row', 'col'), may hold values from -0.25 to 0.25
- qv_bias: float32 [2, 512], P(None, 'col'), may hold values from -3 to 3
- out_weight: bfloat16 [512, 512], P('col', 'row'), may hold values from -2 to 2
- out_bias: float32 [2, 512], P(None, 'col'), may hold values from -2 to 2
- up_weight: bfloat16 [512, 2048], P('row', 'col'), may hold values from -0.25 to 0.25
- up_bias: float32 [2048], P('col'), may hold values from -3 to 3
- down_weight: bfloat16 [2048, 512], P('col', 'row'), may hold values from -0.125 to 0.125
- norm_gain: float32 [2, 512], P(None, 'col'), may hold values from 0.25 to 1.75
- norm_shift: float32 [2, 512], P(None, 'col'), may hold values from -2 to 2
- out_grad: bfloat16 [8192, 512], P('row', 'col'), may hold values from -6 to 6
- logit_grad: bfloat16 [8, 8192, 1024], P('col', 'row'), may hold values from -5 to 5
Outputs:
- output: bfloat16 [8192, 512], P('row', 'col')
- new_logits: bfloat16 [8, 8192, 1024], P('col', 'row')
- tokens_grad: bfloat16 [8192, 512], P('row', 'col')
- prev_grad: bfloat16 [8, 8192, 1024], P('col', 'row')
- qkv_weight_grad: float32 [3, 512, 512], P(None, 'row', 'col')
- qv_bias_grad: float32 [2, 512], P(None, 'col')
- out_weight_grad: float32 [512, 512], P('col', 'row')
- out_bias_grad: float32 [2, 512], P(None, 'col')
- up_weight_grad: float32 [512, 2048], P('row', 'col')
- up_bias_grad: float32 [2048], P('col')
- down_weight_grad: float32 [2048, 512], P('col', 'row')
- norm_gain_grad: float32 [2, 512], P(None, 'col')
- norm_shift_grad: float32 [2, 512], P(None, 'col')
Inputs may be any that keep to these rules, and one draw needn't show every extreme that they name: Each row of doc_lengths sums to 8192, its longest document has exactly 512 tokens, and every nonzero multiple of 512 below 8192 lies inside a document with at least 128 of its tokens on each side of that position.
All inputs are finite; a program needn't handle non-finite values.
Results may differ from a plain program's by a relative error of at most 0.02.
Values may be sent and summed in bfloat16 or wider, within the bound.
No kernel may reach another device: no remote copies, remote signals or barrier semaphores. Data moves between devices by JAX's collectives and lax.ppermute only.
A program may use at most 128 MiB of HBM per device.

v0:
```python
import jax
import jax.numpy as jnp
from jax import lax
from jax.sharding import PartitionSpec as P

D = 512
HEAD_DIM = 64
MAXDOC = 512


EPSILON = 1e-05
MASKED_SCORE = -1e30
ERF_RATE = 0.7071067811865476
DENSITY_RATE = 0.3989422804014327


def with_halo(block, sides, width):
    for axis, dim in sides:
        count = lax.axis_size(axis)
        forward = [(i, i + 1) for i in range(count - 1)]
        backward = [(target, source) for source, target in forward]
        low = lax.ppermute(
            lax.slice_in_dim(block, block.shape[dim] - width, None, axis=dim), axis, forward
        )
        high = lax.ppermute(lax.slice_in_dim(block, 0, width, axis=dim), axis, backward)
        block = jnp.concatenate([low, block, high], axis=dim)
    return block


def to_band(dense_block, band_width):
    leading = dense_block.shape[:-2]
    rows_count = dense_block.shape[-2]
    key_span = dense_block.shape[-1]
    flattened = dense_block.reshape(leading + (rows_count * key_span,))
    flattened = jnp.concatenate(
        [flattened, jnp.zeros(leading + (rows_count,), dense_block.dtype)], -1
    )
    return flattened.reshape(leading + (rows_count, key_span + 1))[..., :band_width]


def to_dense(banded, key_span):
    leading = banded.shape[:-2]
    rows_count = banded.shape[-2]
    band_width = banded.shape[-1]
    padded = jnp.pad(banded, [(0, 0)] * (banded.ndim - 1) + [(0, key_span + 1 - band_width)])
    flattened = padded.reshape(leading + (rows_count * (key_span + 1),))[
        ..., : rows_count * key_span
    ]
    return flattened.reshape(leading + (rows_count, key_span))


def gelu_slope(hidden):
    return (
        0.5 * (1.0 + lax.erf(hidden * ERF_RATE))
        + hidden * jnp.exp(-0.5 * hidden * hidden) * DENSITY_RATE
    )


def features(local_part):
    return lax.all_gather(local_part, "col", axis=1, tiled=True)


def feature_sum(partial_term):
    return lax.psum_scatter(
        partial_term.astype(jnp.bfloat16), "col", scatter_dimension=1, tiled=True
    ).astype(jnp.float32)


def weight_sum(partial_term):
    return lax.psum_scatter(
        partial_term.astype(jnp.bfloat16), "row", scatter_dimension=1, tiled=True
    ).astype(jnp.float32)


def project_in(inputs_full, weight):
    return jnp.einsum(
        "td,sdo->sto",
        inputs_full,
        lax.all_gather(weight, "row", axis=1, tiled=True),
        preferred_element_type=jnp.float32,
    )


def project_out(activation, weight):
    return jnp.dot(
        activation,
        lax.all_gather(weight, "row", axis=1, tiled=True),
        preferred_element_type=jnp.float32,
    )


def back_out(grad_full, weight):
    return jnp.einsum(
        "td,id->ti",
        grad_full,
        lax.all_gather(weight, "row", axis=1, tiled=True),
        preferred_element_type=jnp.float32,
    )


def back_in(grad_stack, weight):
    return jnp.einsum(
        "sto,sdo->td",
        grad_stack,
        lax.all_gather(weight, "row", axis=1, tiled=True),
        preferred_element_type=jnp.float32,
    )


def finish_norm(hidden, mean_rows, squares):
    inverse_std = lax.rsqrt(squares - mean_rows * mean_rows + EPSILON)
    return ((hidden - mean_rows[:, None]) * inverse_std[:, None], inverse_std)


def normalize_split(hidden):
    row_sums, squares = lax.psum((jnp.sum(hidden, 1), jnp.sum(hidden * hidden, 1)), "col")
    return finish_norm(hidden, row_sums / D, squares / D)


def finish_back(upstream, normed, inverse_std, mean_grad, mean_cross):
    return inverse_std[:, None] * (upstream - mean_grad[:, None] - normed * mean_cross[:, None])


def norm_back_split(upstream, normed, inverse_std):
    grad_sums, cross_sums = lax.psum((jnp.sum(upstream, 1), jnp.sum(upstream * normed, 1)), "col")
    return finish_back(upstream, normed, inverse_std, grad_sums / D, cross_sums / D)


def block_inputs(queries, key_value, segment, anchor, block_rows):
    heads_here = key_value.shape[2] // HEAD_DIM
    key_span = block_rows + 2 * MAXDOC
    query_heads = queries.reshape(block_rows, heads_here, HEAD_DIM)
    key_heads = key_value[0, anchor : anchor + key_span].reshape(key_span, heads_here, HEAD_DIM)
    value_heads = key_value[1, anchor : anchor + key_span].reshape(key_span, heads_here, HEAD_DIM)
    query_segment = segment[anchor + MAXDOC : anchor + MAXDOC + block_rows]
    same = (query_segment[:, None] == segment[None, :]).astype(jnp.float32)
    allowed = to_band(same, 2 * MAXDOC) > 0.5
    return (query_heads, key_heads, value_heads, allowed)


def block_scores(query_heads, key_heads, previous, allowed):
    dense_block = jnp.einsum(
        "qhe,khe->hqk", query_heads, key_heads, preferred_element_type=jnp.float32
    )
    scores = to_band(dense_block, 2 * MAXDOC) * HEAD_DIM ** (-0.5) + previous.astype(jnp.float32)
    return (scores, jnp.where(allowed, scores, MASKED_SCORE))


def attend_forward(queries, key_value, previous, segment, block_rows):
    key_span = block_rows + 2 * MAXDOC
    outputs, logits, totals = ([], [], [])
    query_heads, key_heads, value_heads, allowed = block_inputs(
        queries, key_value, segment, 0, block_rows
    )
    scores, masked = block_scores(query_heads, key_heads, previous, allowed)
    row_peak = jnp.max(masked, -1, keepdims=True)
    log_total = row_peak + jnp.log(jnp.sum(jnp.exp(masked - row_peak), -1, keepdims=True))
    spread = to_dense(jnp.exp(masked - log_total).astype(jnp.bfloat16), key_span)
    attended = jnp.einsum("hqk,khe->qhe", spread, value_heads, preferred_element_type=jnp.float32)
    outputs.append(attended.reshape(block_rows, -1))
    logits.append(jnp.where(allowed, scores, 0.0).astype(jnp.bfloat16))
    totals.append(log_total)
    return (outputs[0], logits[0], totals[0])


def attend_backward(
    queries, key_value, previous, segment, block_rows, log_totals, attended_grad, logit_grad
):
    key_span = block_rows + 2 * MAXDOC
    heads_here = key_value.shape[2] // HEAD_DIM
    key_grads = jnp.zeros(key_value.shape, jnp.float32)
    query_grads, prev_grads = ([], [])
    query_heads, key_heads, value_heads, allowed = block_inputs(
        queries, key_value, segment, 0, block_rows
    )
    scores, masked = block_scores(query_heads, key_heads, previous, allowed)
    probabilities = jnp.exp(masked - log_totals)
    spread = to_dense(probabilities.astype(jnp.bfloat16), key_span)
    grad_heads = attended_grad.reshape(block_rows, heads_here, HEAD_DIM)
    prob_grad = to_band(
        jnp.einsum("qhe,khe->hqk", grad_heads, value_heads, preferred_element_type=jnp.float32),
        2 * MAXDOC,
    )
    inner_sum = jnp.sum(probabilities * prob_grad, -1, keepdims=True)
    score_grad = probabilities * (prob_grad - inner_sum) + logit_grad.astype(jnp.float32)
    score_grad = jnp.where(allowed, score_grad, 0.0).astype(jnp.bfloat16)
    prev_grads.append(score_grad)
    dense_grad = to_dense(score_grad, key_span)
    query_part = jnp.einsum(
        "hqk,khe->qhe", dense_grad, key_heads, preferred_element_type=jnp.float32
    )
    query_grads.append((query_part * HEAD_DIM ** (-0.5)).reshape(block_rows, -1))
    key_part = jnp.einsum(
        "hqk,qhe->khe", dense_grad, query_heads, preferred_element_type=jnp.float32
    )
    value_part = jnp.einsum("hqk,qhe->khe", spread, grad_heads, preferred_element_type=jnp.float32)
    update = jnp.stack(
        [(key_part * HEAD_DIM ** (-0.5)).reshape(key_span, -1), value_part.reshape(key_span, -1)]
    )
    key_grads = key_grads.at[:, 0:key_span].add(update)
    return (query_grads[0], key_grads, prev_grads[0])


def on_device(
    tokens,
    prev_logits,
    doc_lengths,
    qkv_weight,
    qv_bias,
    out_weight,
    out_bias,
    up_weight,
    up_bias,
    down_weight,
    norm_gain,
    norm_shift,
    out_grad,
    logit_grad,
):
    rows_here = tokens.shape[0]
    block_rows = min(512, rows_here)
    row_index = lax.axis_index("row")
    token_count = rows_here * lax.axis_size("row")
    seq_tokens = token_count // doc_lengths.shape[0]
    positions = jnp.arange(rows_here + 2 * MAXDOC, dtype=jnp.int32) + row_index * rows_here - MAXDOC
    doc_ends = (
        jnp.cumsum(doc_lengths, 1)
        + seq_tokens * jnp.arange(doc_lengths.shape[0], dtype=jnp.int32)[:, None]
    ).reshape(-1)
    segment = jnp.sum((doc_ends[None, :] <= positions[:, None]).astype(jnp.int32), 1)
    segment = jnp.where((positions >= 0) & (positions < token_count), segment, -1)
    tokens_full = features(tokens)
    qkv_sums = project_in(tokens_full, qkv_weight)
    queries = (qkv_sums[0] + qv_bias[0]).astype(jnp.bfloat16)
    key_value = jnp.stack([qkv_sums[1], qkv_sums[2] + qv_bias[1]]).astype(jnp.bfloat16)
    key_ext = with_halo(key_value, (("row", 1),), MAXDOC)
    attended, new_logits, log_totals = attend_forward(
        queries, key_ext, prev_logits, segment, block_rows
    )
    attended = attended.astype(jnp.bfloat16)
    attn_part = project_out(attended, out_weight)
    out_grad_wide = out_grad.astype(jnp.float32)
    normed_one, inverse_one = normalize_split(
        tokens.astype(jnp.float32) + feature_sum(attn_part) + out_bias[0]
    )
    upper = normed_one * norm_gain[0] + norm_shift[0]
    upper_low = features(upper.astype(jnp.bfloat16))
    hidden_pre = project_in(upper_low, up_weight[None])[0] + up_bias
    act_low = jax.nn.gelu(hidden_pre, approximate=False).astype(jnp.bfloat16)
    down_part = project_out(act_low, down_weight)
    normed_two, inverse_two = normalize_split(upper + feature_sum(down_part) + out_bias[1])
    output = normed_two * norm_gain[1] + norm_shift[1]
    res_two = norm_back_split(out_grad_wide * norm_gain[1], normed_two, inverse_two)
    ffn_low = res_two.astype(jnp.bfloat16)
    ffn_full = features(ffn_low)
    ffn_bias_grad = jnp.sum(ffn_low.astype(jnp.float32), 0)
    two_gain = jnp.sum(out_grad_wide * normed_two, 0)
    two_shift = jnp.sum(out_grad_wide, 0)
    act_grad = back_out(ffn_full, down_weight)
    hidden_grad = (act_grad * gelu_slope(hidden_pre)).astype(jnp.bfloat16)
    down_weight_grad = weight_sum(
        jnp.einsum("ti,td->id", act_low, ffn_full, preferred_element_type=jnp.float32)
    )
    up_weight_grad = weight_sum(
        jnp.einsum("td,to->do", upper_low, hidden_grad, preferred_element_type=jnp.float32)[None]
    )[0]
    lower_part = back_in(hidden_grad[None], up_weight[None])
    upper_grad = feature_sum(lower_part) + res_two
    res_one = norm_back_split(upper_grad * norm_gain[0], normed_one, inverse_one)
    branch_low = res_one.astype(jnp.bfloat16)
    branch_full = features(branch_low)
    one_gain = jnp.sum(upper_grad * normed_one, 0)
    one_shift = jnp.sum(upper_grad, 0)
    attn_bias_grad = jnp.sum(branch_low.astype(jnp.float32), 0)
    out_weight_grad = weight_sum(
        jnp.einsum("ti,td->id", attended, branch_full, preferred_element_type=jnp.float32)
    )
    attended_grad = back_out(branch_full, out_weight).astype(jnp.bfloat16)
    query_grad, key_grads, prev_grad = attend_backward(
        queries, key_ext, prev_logits, segment, block_rows, log_totals, attended_grad, logit_grad
    )
    rim_grads = jnp.concatenate([key_grads[:, :MAXDOC], key_grads[:, MAXDOC + rows_here :]], 1)
    arrived = with_halo(rim_grads.astype(jnp.bfloat16), (("row", 1),), MAXDOC).astype(
        rim_grads.dtype
    )
    own_rows = key_grads[:, MAXDOC : MAXDOC + rows_here]
    own_rows = own_rows + arrived[:, :MAXDOC]
    own_rows = own_rows + arrived[:, 3 * MAXDOC :]
    qkv_grads = jnp.concatenate([query_grad[None], own_rows], 0).astype(jnp.bfloat16)
    qkv_weight_grad = weight_sum(
        jnp.einsum("td,sto->sdo", tokens_full, qkv_grads, preferred_element_type=jnp.float32)
    )
    tokens_grad = (feature_sum(back_in(qkv_grads, qkv_weight)) + res_one).astype(jnp.bfloat16)
    qkv_wide = qkv_grads.astype(jnp.float32)
    qv_part = jnp.stack([jnp.sum(qkv_wide[0], 0), jnp.sum(qkv_wide[2], 0)])
    bias_part = jnp.stack([attn_bias_grad, ffn_bias_grad])
    hidden_part = jnp.sum(hidden_grad.astype(jnp.float32), 0)
    gain_part = jnp.stack([one_gain, two_gain])
    shift_part = jnp.stack([one_shift, two_shift])
    qv_bias_grad, out_bias_grad, up_bias_grad, norm_gain_grad, norm_shift_grad = lax.psum(
        (qv_part, bias_part, hidden_part, gain_part, shift_part), "row"
    )
    return (
        output.astype(jnp.bfloat16),
        new_logits,
        tokens_grad,
        prev_grad,
        qkv_weight_grad,
        qv_bias_grad,
        out_weight_grad,
        out_bias_grad,
        up_weight_grad,
        up_bias_grad,
        down_weight_grad,
        norm_gain_grad,
        norm_shift_grad,
    )


def solution(mesh):
    return jax.shard_map(
        on_device,
        mesh=mesh,
        in_specs=(
            P("row", "col"),
            P("col", "row", None),
            P(),
            P(None, "row", "col"),
            P(None, "col"),
            P("col", "row"),
            P(None, "col"),
            P("row", "col"),
            P("col"),
            P("col", "row"),
            P(None, "col"),
            P(None, "col"),
            P("row", "col"),
            P("col", "row", None),
        ),
        out_specs=(
            P("row", "col"),
            P("col", "row", None),
            P("row", "col"),
            P("col", "row", None),
            P(None, "row", "col"),
            P(None, "col"),
            P("col", "row"),
            P(None, "col"),
            P("row", "col"),
            P("col"),
            P("col", "row"),
            P(None, "col"),
            P(None, "col"),
        ),
        check_vma=False,
    )
```

profile of v0, /device:TPU:0, one launch (start us, length us, event | category | flops | bytes accessed | tf_op | source)
XLA Modules:
  0.0 643.8 jit_solution(229700125990471223)
XLA Ops:
  8.1 25.7 %all_gather.28 = bf16[3,512,256]{2,1,0:T(8,128)(2,1)S(1)} all-gather(bf16[3,32,256]{2,1,0:T(8,128)(2,1)} %param.21), channel_id=1, replica_groups=mesh['row'=16,'col'=2] {'row'}, dimensions={1}, use_global_device_ids=true | all-gather | bytes 835584 | tf_op jit(solution)/shard_map/all_gather | solution.py:79
  33.8 9.4 %all_gather.29 = bf16[512,512]{1,0:T(8,128)(2,1)S(1)} all-gather(bf16[512,256]{1,0:T(8,128)(2,1)} %param.18), channel_id=1, replica_groups=mesh['row'=16,'col'=2] {'col'}, dimensions={1}, use_global_device_ids=true | all-gather | bytes 786432 | tf_op jit(solution)/shard_map/all_gather | solution.py:60
  45.6 2.3 collective-permute-start
  50.2 1.8 convert_element_type.145
  52.1 2.8 reshape.181
  54.9 20.7 %all_gather.30 = bf16[256,512]{0,1:T(8,128)(2,1)} all-gather(bf16[256,32]{0,1:T(8,128)(2,1)S(1)} %copy-done.25), channel_id=1, replica_groups=mesh['row'=16,'col'=2] {'row'}, dimensions={1}, use_global_device_ids=true | all-gather | bytes 278528 | tf_op jit(solution)/shard_map/all_gather | solution.py:87
  78.4 1.9 convolution_bitcast_fusion.1
  80.3 20.0 %copy.54 = f32[1,4,512,1536]{3,1,2,0:T(4,128)S(1)} copy(f32[1,4,512,1536]{3,2,1,0:T(8,128)S(1)} %convolution_bitcast_fusion.1) | data formatting | bytes 25165824
  100.3 4.9 concatenate.28
  105.3 14.1 %reshape.206 = f32[3147776]{0:T(1024)} reshape(f32[4,786944]{1,0:T(4,128)} %concatenate.28) | data formatting | bytes 25182208
  119.3 20.8 %reshape.183 = f32[4,512,1537]{2,1,0:T(8,128)} reshape(f32[3147776]{0:T(1024)} %reshape.206) | data formatting | bytes 25182208 | tf_op jit(solution)/shard_map/reshape | solution.py:38
  140.2 7.4 %select_convert_fusion.1 = (bf16[4,512,1024]{2,1,0:T(8,128)(2,1)}, f32[4,512,1024]{2,1,0:T(8,128)S(1)}) fusion(pred[512,1024]{1,0:T(8,128)(4,1)S(1)} %convert_compare_fusion, bf16[4,512,1024]{2,1,0:T(8,128)(2,1)} %param.19, f32[4,512,1537]{2,1,0:T(8,128)} %reshape.183), kind=kLoop, calls=%fused_computation.6 | loop fusion | flops 8388608 | bytes 25690112 | tf_op jit(solution)/shard_map/convert_element_type | solution.py:161
  148.8 2.2 exponential_reduce_fusion
  151.0 1.5 fusion.16
  152.6 3.4 pad.15
  155.9 14.3 %reshape.208 = bf16[3147776]{0:T(1024)(128)(2,1)} reshape(bf16[4,512,1537]{2,1,0:T(8,128)(2,1)} %pad.15) | data formatting | bytes 12591104
  170.2 7.8 %reshape.184 = bf16[4,786944]{1,0:T(4,128)(2,1)} reshape(bf16[3147776]{0:T(1024)(128)(2,1)} %reshape.208) | data formatting | bytes 12591104 | tf_op jit(solution)/shard_map/reshape | solution.py:46
  178.0 5.7 slice.148
  183.8 2.1 fusion.46
  189.1 10.7 %reduce-scatter.8.cloned.1.call-done = bf16[512,256]{1,0:T(8,128)(2,1)} async-done(((bf16[512,512]{1,0:T(8,128)(2,1)}), bf16[512,256]{1,0:T(8,128)(2,1)}) %reduce-scatter.8.cloned.1.call-update) | async-done | bytes 262160 | tf_op jit(solution)/shard_map/reduce_scatter | solution.py:64
  201.0 4.9 all-reduce.10
  207.1 7.6 %all_gather.31 = bf16[512,512]{1,0:T(8,128)(2,1)S(1)} all-gather(bf16[512,256]{1,0:T(8,128)(2,1)S(1)} %fusion.63), channel_id=1, replica_groups=mesh['row'=16,'col'=2] {'col'}, dimensions={1}, use_global_device_ids=true | all-gather | bytes 786432 | tf_op jit(solution)/shard_map/all_gather | solution.py:60
  214.7 11.3 %all-gather.6.cloned.1.call-done = bf16[512,1024]{1,0:T(8,128)(2,1)} async-done(((bf16[32,1024]{1,0:T(8,128)(2,1)}), bf16[512,1024]{1,0:T(8,128)(2,1)}) %all-gather.6.cloned.1.call-update) | async-done | bytes 1048592 | tf_op jit(solution)/shard_map/all_gather | solution.py:79
  225.9 7.3 %fusion.23 = (bf16[512,1024]{1,0:T(8,128)(2,1)}, f32[512,1024]{1,0:T(8,128)}) fusion(f32[1024]{0:T(1024)S(1)} %copy-done.32, bf16[512,512]{1,0:T(8,128)(2,1)S(1)} %all_gather.31, bf16[512,1024]{1,0:T(8,128)(2,1)} %all-gather.6.cloned.1.call-done), kind=kOutput, calls=%fused_computation.35 | convolution fusion | flops 571473920 | bytes 4722688 | tf_op jit(solution)/shard_map/td,sdo->sto/dot_general | solution.py:76
  233.3 32.0 %all-gather.4.cloned.1.call-done = bf16[1024,512]{0,1:T(8,128)(2,1)} async-done(((bf16[1024,32]{0,1:T(8,128)(2,1)}), bf16[1024,512]{0,1:T(8,128)(2,1)}) %all-gather.4.cloned.1.call-update) | async-done | bytes 1048592 | tf_op jit(solution)/shard_map/all_gather | solution.py:87
  265.3 3.1 convolution_convert_fusion.5
  268.5 13.7 %reduce-scatter.10.cloned.1.call-done = bf16[512,256]{1,0:T(8,128)(2,1)} async-done(((bf16[512,512]{1,0:T(8,128)(2,1)}), bf16[512,256]{1,0:T(8,128)(2,1)}) %reduce-scatter.10.cloned.1.call-update) | async-done | bytes 262160 | tf_op jit(solution)/shard_map/reduce_scatter | solution.py:64
  283.5 4.9 all-reduce.9
  288.8 4.9 all-reduce.8
  293.8 2.1 convert_reduce_fusion.2
  295.9 7.0 %all_gather.34 = bf16[512,512]{1,0:T(8,128)(2,1)S(1)} all-gather(bf16[512,256]{1,0:T(8,128)(2,1)S(1)} %get-tuple-element.116), channel_id=1, replica_groups=mesh['row'=16,'col'=2] {'col'}, dimensions={1}, use_global_device_ids=true | all-gather | bytes 786432 | tf_op jit(solution)/shard_map/all_gather | solution.py:60
  302.9 3.0 convert_reduce_fusion
  306.9 1.5 convolution_convert_fusion.4
  308.5 14.7 %reduce-scatter.12.cloned.1.call-done = bf16[512,256]{1,0:T(8,128)(2,1)} async-done(((bf16[512,512]{1,0:T(8,128)(2,1)}), bf16[512,256]{1,0:T(8,128)(2,1)}) %reduce-scatter.12.cloned.1.call-update) | async-done | bytes 262160 | tf_op jit(solution)/shard_map/reduce_scatter | solution.py:64
  323.2 1.4 multiply_reduce_fusion.1
  324.6 4.9 all-reduce.7
  329.6 2.1 convert_reduce_fusion.3
  331.7 7.7 %all_gather.35 = bf16[512,512]{1,0:T(8,128)(2,1)S(1)} all-gather(bf16[512,256]{1,0:T(8,128)(2,1)S(1)} %get-tuple-element.113), channel_id=1, replica_groups=mesh['row'=16,'col'=2] {'col'}, dimensions={1}, use_global_device_ids=true | all-gather | bytes 786432 | tf_op jit(solution)/shard_map/all_gather | solution.py:60
  340.5 3.0 convolution_convert_fusion
  343.6 3.0 fusion.37
  347.2 1.8 convolution_bitcast_fusion
  349.0 19.9 %copy.56 = f32[1,4,512,1536]{3,1,2,0:T(4,128)S(1)} copy(f32[1,4,512,1536]{3,2,1,0:T(8,128)S(1)} %convolution_bitcast_fusion) | data formatting | bytes 25165824
  368.9 4.9 concatenate.29
  373.9 14.1 %reshape.210 = f32[3147776]{0:T(1024)} reshape(f32[4,786944]{1,0:T(4,128)} %concatenate.29) | data formatting | bytes 25182208
  388.0 20.8 %reshape.189 = f32[4,512,1537]{2,1,0:T(8,128)} reshape(f32[3147776]{0:T(1024)} %reshape.210) | data formatting | bytes 25182208 | tf_op jit(solution)/shard_map/reshape | solution.py:38
  408.8 26.5 %select_convert_fusion = bf16[4,512,1024]{2,1,0:T(8,128)(2,1)} fusion(bf16[4,512,1024]{2,1,0:T(8,128)(2,1)} %param.31, f32[4,512,1537]{2,1,0:T(8,128)} %reshape.189, pred[512,1024]{1,0:T(8,128)(4,1)S(1)} %convert_compare_fusion, f32[4,512]{1,0:T(4,128)S(1)} %log_add_fusion, f32[4,512,1024]{2,1,0:T(8,128)} %copy-done), kind=kOutput, calls=%fused_computation.3 | output fusion | flops 23071744 | bytes 43008000 | tf_op jit(solution)/shard_map/sub | solution.py:185
  435.3 5.5 pad.16
  440.8 14.2 %reshape.212 = bf16[3147776]{0:T(1024)(128)(2,1)} reshape(bf16[4,512,1537]{2,1,0:T(8,128)(2,1)} %pad.16) | data formatting | bytes 12591104
  454.9 7.9 %reshape.190 = bf16[4,786944]{1,0:T(4,128)(2,1)} reshape(bf16[3147776]{0:T(1024)(128)(2,1)} %reshape.212) | data formatting | bytes 12591104 | tf_op jit(solution)/shard_map/reshape | solution.py:46
  462.8 5.9 slice.150
  468.7 3.4 fusion.18
  472.1 3.3 fusion.8
  475.4 1.9 copy.48
  477.3 1.9 copy.47
  480.5 2.3 collective-permute-start.2
  484.1 3.9 fusion.43
  489.2 1.4 fusion.52
  492.1 1.4 copy.51
  497.7 1.6 convert_element_type.185
  499.4 69.2 %all-reduce.6 = (f32[2,256]{1,0:T(2,128)}, f32[2,256]{1,0:T(2,128)}, f32[1024]{0:T(1024)}, f32[2,256]{1,0:T(2,128)}, f32[2,256]{1,0:T(2,128)}) all-reduce(f32[2,256]{1,0:T(2,128)S(1)} %pad_maximum_fusion.9, f32[2,256]{1,0:T(2,128)S(1)} %pad_maximum_fusion.10, ...), channel_id=1, replica_groups=mesh['row'=16,'col'=2] {'row'}, use_global_device_ids=true, to_apply=%region_28.29 | all-reduce | flops 3072 | bytes 24576 | tf_op jit(solution)/shard_map/psum | solution.py:300
  568.7 1.5 bitcast_convert_fusion
  570.2 48.5 %all-reduce.13.cloned.1.call-done = bf16[3,512,256]{2,0,1:T(4,128)(2,1)} async-done(((bf16[3,512,256]{2,0,1:T(4,128)(2,1)}), bf16[3,512,256]{2,0,1:T(4,128)(2,1)}) %all-reduce.13.cloned.1.call-update) | async-done | bytes 786448
  620.1 14.4 %reduce-scatter.14.cloned.1.call-done = bf16[512,256]{1,0:T(8,128)(2,1)} async-done(((bf16[512,512]{1,0:T(8,128)(2,1)}), bf16[512,256]{1,0:T(8,128)(2,1)}) %reduce-scatter.14.cloned.1.call-update) | async-done | bytes 262160 | tf_op jit(solution)/shard_map/reduce_scatter | solution.py:64
  634.5 1.7 add_convert_fusion
  (154 shorter events, 29.2 us)
Async XLA Ops:
  8.0 191.8 %reduce-scatter.8.cloned.1.call-start = ((), (), s32[]{:S(2)}) async-start(), calls=%async_computation.7 | async-start | bytes 786432 | tf_op jit(solution)/shard_map/reduce_scatter | solution.py:64
  33.8 10.9 %copy-start.9 = (bf16[3,512,256]{2,1,0:T(8,128)(2,1)}, bf16[3,512,256]{2,1,0:T(8,128)(2,1)S(1)}, u32[]{:S(2)}) copy-start(bf16[3,512,256]{2,1,0:T(8,128)(2,1)S(1)} %all_gather.28) | copy-start | bytes 2359300
  43.2 1.6 copy-start.14
  44.6 4.6 copy-start.29
  45.6 30.4 %collective-permute-start = (bf16[2,512,256]{1,2,0:T(8,128)(2,1)}, bf16[2,512,256]{1,2,0:T(8,128)(2,1)}, u32[]{:S(2)}, u32[]{:S(2)}) collective-permute-start(bf16[2,512,256]{1,2,0:T(8,128)(2,1)} %pad_maximum_fusion.6), channel_id=1, source_target_pairs={{0,2},{2,4},{4,6},{6,8},{8,10},{10,12},{12,14},{14,16},{16,18},{18... | collective-permute-start | bytes 1572872 | tf_op jit(solution)/shard_map/ppermute | solution.py:22
  47.9 28.1 %collective-permute-start.1 = (bf16[2,512,256]{1,2,0:T(8,128)(2,1)}, bf16[2,512,256]{1,2,0:T(8,128)(2,1)}, u32[]{:S(2)}, u32[]{:S(2)}) collective-permute-start(bf16[2,512,256]{1,2,0:T(8,128)(2,1)} %pad_maximum_fusion.6), channel_id=1, source_target_pairs={{2,0},{4,2},{6,4},{8,6},{10,8},{12,10},{14,12},{16,14},{18,16},{20... | collective-permute-start | bytes 1572872 | tf_op jit(solution)/shard_map/ppermute | solution.py:25
  50.2 4.7 copy-start.25
  77.5 0.9 copy-start.6
  147.6 3.5 copy-start
  183.7 2.9 copy-start.3
  183.7 2.9 copy-start.11
  183.7 5.3 copy-start.26
  183.8 5.3 copy-start.27
  183.8 5.3 copy-start.28
  183.8 16.0 %copy-start.4 = (bf16[512,256]{1,0:T(8,128)(2,1)S(1)}, bf16[512,256]{1,0:T(8,128)(2,1)}, u32[]{:S(2)}) copy-start(bf16[512,256]{1,0:T(8,128)(2,1)} %param.18) | copy-start | bytes 786436
  186.6 46.7 %copy-start.19 = (bf16[4,64,512]{2,1,0:T(8,128)(2,1)}, bf16[4,64,512]{2,1,0:T(8,128)(2,1)S(1)}, u32[]{:S(2)}) copy-start(bf16[4,64,512]{2,1,0:T(8,128)(2,1)S(1)} %fusion.46) | copy-start | bytes 786436
  186.6 39.3 %copy-start.32 = (f32[1024]{0:T(1024)S(1)}, f32[1024]{0:T(1024)}, u32[]{:S(2)}) copy-start(f32[1024]{0:T(1024)} %param.26) | copy-start | bytes 12292
  187.8 38.2 %all-gather.6.cloned.1.call-start = ((), (), s32[]{:S(2)}) async-start(), calls=%async_computation.15 | async-start | bytes 1114112 | tf_op jit(solution)/shard_map/all_gather | solution.py:79
  188.4 76.9 %all-gather.4.cloned.1.call-start = ((), (), s32[]{:S(2)}) async-start(), calls=%async_computation.8 | async-start | bytes 1114112 | tf_op jit(solution)/shard_map/all_gather | solution.py:87
  188.9 93.2 %reduce-scatter.10.cloned.1.call-start = ((), (), s32[]{:S(2)}) async-start(), calls=%async_computation.9 | async-start | bytes 786432 | tf_op jit(solution)/shard_map/reduce_scatter | solution.py:64
  214.7 18.6 %copy-start.21 = (bf16[512,512]{1,0:T(8,128)(2,1)}, bf16[512,512]{1,0:T(8,128)(2,1)S(1)}, u32[]{:S(2)}) copy-start(bf16[512,512]{1,0:T(8,128)(2,1)S(1)} %all_gather.31) | copy-start | bytes 1572868
  233.3 48.8 %copy-start.5 = (bf16[512,256]{1,0:T(8,128)(2,1)S(1)}, bf16[512,256]{1,0:T(8,128)(2,1)}, u32[]{:S(2)}) copy-start(bf16[512,256]{1,0:T(8,128)(2,1)} %reduce-scatter.8.cloned.1.call-done) | copy-start | bytes 786436
  265.3 23.2 %copy-start.18 = (bf16[512,256]{1,0:T(8,128)(2,1)S(1)}, bf16[512,256]{1,0:T(8,128)(2,1)}, u32[]{:S(2)}) copy-start(bf16[512,256]{1,0:T(8,128)(2,1)} %param.30) | copy-start | bytes 786436
  268.4 54.8 %reduce-scatter.12.cloned.1.call-start = ((), (), s32[]{:S(2)}) async-start(), calls=%async_computation.10 | async-start | bytes 786432 | tf_op jit(solution)/shard_map/reduce_scatter | solution.py:64
  293.8 9.1 %copy-start.31 = (bf16[1024,512]{0,1:T(8,128)(2,1)S(1)}, bf16[1024,512]{0,1:T(8,128)(2,1)}, u32[]{:S(2)}) copy-start(bf16[1024,512]{0,1:T(8,128)(2,1)} %all-gather.4.cloned.1.call-done) | copy-start | bytes 3145732
  302.9 3.0 copy-start.23
  302.9 4.0 copy-start.30
  305.9 1.0 copy-start.34
  308.4 187.9 %reduce-scatter.16.cloned.1.call-start = ((), (), s32[]{:S(2)}) async-start(), calls=%async_computation.12 | async-start | bytes 278528 | tf_op jit(solution)/shard_map/reduce_scatter | solution.py:70
  323.2 16.2 %copy-start.20 = (bf16[4,64,512]{2,1,0:T(8,128)(2,1)S(1)}, bf16[4,64,512]{2,1,0:T(8,128)(2,1)}, u32[]{:S(2)}) copy-start(bf16[4,64,512]{2,1,0:T(8,128)(2,1)} %copy-done.19) | copy-start | bytes 786436
  331.7 8.8 %copy-start.24 = (bf16[512,512]{1,0:T(8,128)(2,1)S(1)}, bf16[512,512]{1,0:T(8,128)(2,1)}, u32[]{:S(2)}) copy-start(bf16[512,512]{1,0:T(8,128)(2,1)} %copy-done.23) | copy-start | bytes 1572868
  340.4 3.2 copy-start.22
  340.5 157.2 %reduce-scatter.20.cloned.1.call-start = ((), (), s32[]{:S(2)}) async-start(), calls=%async_computation.14 | async-start | bytes 1114112 | tf_op jit(solution)/shard_map/reduce_scatter | solution.py:70
  343.5 3.3 copy-start.12
  343.6 225.1 %reduce-scatter.18.cloned.1.call-start = ((), (), s32[]{:S(2)}) async-start(), calls=%async_computation.13 | async-start | bytes 1114112 | tf_op jit(solution)/shard_map/reduce_scatter | solution.py:70
  346.6 272.0 %all-reduce.13.cloned.1.call-start = ((), (), s32[]{:S(2)}) async-start(), calls=%async_computation.16 | async-start | bytes 2097152
  347.2 1.8 copy-start.7
  454.9 17.1 %slice-start = ((s8[6291456]{0:T(1024)(128)(4,1)}), s8[2097152]{0:T(1024)(128)(4,1)S(1)}, s32[]{:S(2)}) async-start(s8[6291456]{0:T(1024)(128)(4,1)} %bitcast.108), calls=%async_computation.17 | async-start | bytes 4194304
  462.8 9.3 %slice-start.1 = ((s8[6291456]{0:T(1024)(128)(4,1)}), s8[4194304]{0:T(1024)(128)(4,1)S(1)}, s32[]{:S(2)}) async-start(s8[6291456]{0:T(1024)(128)(4,1)} %bitcast.108), calls=%async_computation.18 | async-start | bytes 8388608
  468.7 3.4 copy-start.1
  468.7 3.4 copy-start.8
  479.2 5.0 copy-start.2
  480.5 8.7 %collective-permute-start.2 = (bf16[2,512,256]{2,1,0:T(8,128)(2,1)}, bf16[2,512,256]{2,1,0:T(8,128)(2,1)}, u32[]{:S(2)}, u32[]{:S(2)}) collective-permute-start(bf16[2,512,256]{2,1,0:T(8,128)(2,1)} %get-tuple-element.121), channel_id=1, source_target_pairs={{0,2},{2,4},{4,6},{6,8},{8,10},{10,12},{12,14},{14,16},{16,18},{18... | collective-permute-start | bytes 1572872 | tf_op jit(solution)/shard_map/ppermute | solution.py:22
  482.8 6.3 collective-permute-start.3
  489.1 2.3 copy-start.15
  490.6 0.8 copy-start.16
  492.0 1.5 copy-start.33
  492.0 2.8 copy-start.10
  492.0 2.8 copy-start.17
  493.5 141.0 %reduce-scatter.14.cloned.1.call-start = ((), (), s32[]{:S(2)}) async-start(), calls=%async_computation.11 | async-start | bytes 786432 | tf_op jit(solution)/shard_map/reduce_scatter | solution.py:64
  497.7 136.9 %copy-start.13 = (f32[512,256]{1,0:T(8,128)S(1)}, f32[512,256]{1,0:T(8,128)}, u32[]{:S(2)}) copy-start(f32[512,256]{1,0:T(8,128)} %get-tuple-element.114) | copy-start | bytes 1572868
Sparse Core Ops, SparseCore 0:
  187.9 11.8 reduce-scatter.7
  268.5 13.5 reduce-scatter.9
  308.6 14.5 reduce-scatter.11
Sparse Core Ops, SparseCore 1:
  190.6 35.2 all-gather.5
  228.2 37.0 all-gather.3
  340.5 55.3 reduce-scatter.15
  400.0 56.4 reduce-scatter.19
  460.1 62.4 reduce-scatter.17
  526.5 92.1 all-reduce.12
  620.8 13.6 reduce-scatter.13
where the time goes:
time: 652 us; the launch traced here: 644 us
  local copies, waits for them, and re-layouts  202 us (31%)
  blocking collectives  167 us (26%)
  waiting for transfers between devices  146 us (22%)
  other arithmetic  60.9 us (9%)
  matrix products  42.5 us (7%)
  between operations  17.1 us (3%)
  starting transfers between devices  7.76 us (1%)
    unnamed x82, local copies, waits for them, and re-layouts  101 us
    psum x1, blocking collectives, on_device(): lax.psum((qv_part, bias_part, hidden_part, gain_part, shift_part), 'row')  69.2 us
    reduce_scatter x4, waiting for transfers between devices, feature_sum(): lax.psum_scatter(partial_term.astype(jnp.bfloat16), 'col', scatter_dimens...  53.5 us
    unnamed x11, waiting for transfers between devices  49.6 us
    reshape x3, local copies, waits for them, and re-layouts, to_band(): flattened.reshape(leading + (rows_count, key_span + 1))[..., :band_width]  44.4 us
    all_gather x1, waiting for transfers between devices, project_out(): lax.all_gather(weight, 'row', axis=1, tiled=True)  32 us
    all_gather x4, blocking collectives, features(): return lax.all_gather(local_part, 'col', axis=1, tiled=True)  31.7 us
    sub x1, other arithmetic, attend_backward(): prob_grad - inner_sum  26.5 us
  transfers between devices with their start and end apart: 14, of which 7 were waited for; matrix products, arithmetic and copies ran while one was open for 27% of the time, Pallas kernels for 0%

commit v1 on v0

v1 whole, which is shorter than its diff:
```python
import functools

import jax
import jax.numpy as jnp
from jax import lax
from jax.experimental import pallas as pl
from jax.experimental.pallas import tpu as pltpu
from jax.sharding import PartitionSpec as P

D = 512
HEAD_DIM = 64
MAXDOC = 512
BAND = 2 * MAXDOC
BLOCK = 128
WINDOW = BAND + BLOCK
HALO = MAXDOC - 128
PAD = MAXDOC - HALO

EPSILON = 1e-05
MASKED_SCORE = -1e30
ERF_RATE = 0.7071067811865476
DENSITY_RATE = 0.3989422804014327

F32 = jnp.float32
BF16 = jnp.bfloat16
SMEM = pltpu.MemorySpace.SMEM
VMEM_LIMIT = 48 << 20


def dot_nn(a, b):
    return lax.dot_general(a, b, (((1,), (0,)), ((), ())), preferred_element_type=F32)


def dot_nt(a, b):
    return lax.dot_general(a, b, (((1,), (1,)), ((), ())), preferred_element_type=F32)


def dot_tn(a, b):
    return lax.dot_general(a, b, (((0,), (0,)), ((), ())), preferred_element_type=F32)


def params():
    return pltpu.CompilerParams(
        dimension_semantics=("arbitrary",), vmem_limit_bytes=VMEM_LIMIT
    )


def cost(flops, moved, special=0):
    return pl.CostEstimate(flops=flops, bytes_accessed=moved, transcendentals=special)


def whole(shape):
    return pl.BlockSpec(shape, lambda b: (0,) * len(shape))


def rows(width, height=BLOCK):
    return pl.BlockSpec((height, width), lambda b: (b, 0))


def heads_block(heads, width):
    return pl.BlockSpec((heads, BLOCK, width), lambda b: (0, b, 0))


def struct(shape, dtype):
    return jax.ShapeDtypeStruct(shape, dtype)


def segment_of(positions, lengths_ref, token_count):
    sequences, documents = lengths_ref.shape
    found = jnp.zeros(positions.shape, jnp.int32)
    end = jnp.int32(0)
    for sequence in range(sequences):
        for document in range(documents):
            end = end + lengths_ref[sequence, document]
            found = found + (positions >= end).astype(jnp.int32)
    return jnp.where((positions >= 0) & (positions < token_count), found, -1)


def dense_kernel(fill, token_count, lengths_ref, base_ref, band_ref, dense_ref):
    first = base_ref[0] + pl.program_id(0) * BLOCK
    query = first + lax.broadcasted_iota(jnp.int32, (BLOCK, 1), 0)
    key = first - MAXDOC + lax.broadcasted_iota(jnp.int32, (1, WINDOW), 1)
    same = segment_of(query, lengths_ref, token_count) == segment_of(
        key, lengths_ref, token_count
    )
    for head in range(band_ref.shape[0]):
        wide = jnp.concatenate(
            [band_ref[head].astype(F32), jnp.zeros((BLOCK, BLOCK), F32)], 1
        )
        turned = pltpu.roll(wide, 0, 1, stride=1, stride_axis=0)
        dense_ref[head] = jnp.where(same, turned, fill).astype(BF16)


def to_dense(banded, lengths, base, fill, token_count):
    heads, count, _ = banded.shape
    return pl.pallas_call(
        functools.partial(dense_kernel, fill, token_count),
        grid=(count // BLOCK,),
        in_specs=[
            pl.BlockSpec(memory_space=SMEM),
            pl.BlockSpec(memory_space=SMEM),
            heads_block(heads, BAND),
        ],
        out_specs=heads_block(heads, WINDOW),
        out_shape=struct((heads, count, WINDOW), BF16),
        compiler_params=params(),
        cost_estimate=cost(heads * count * WINDOW * 8, heads * count * (BAND + WINDOW) * 2),
        name="to_dense",
    )(lengths, base, banded)


def band_kernel(masked, dense_ref, band_ref):
    lane = lax.broadcasted_iota(jnp.int32, (BLOCK, BLOCK), 1)
    row = lax.broadcasted_iota(jnp.int32, (BLOCK, BLOCK), 0)
    source = (lane + row) & (BLOCK - 1)
    near = lane + row < BLOCK
    for head in range(band_ref.shape[0]):
        pieces = []
        for place in range(WINDOW // BLOCK):
            piece = dense_ref[head, :, place * BLOCK : (place + 1) * BLOCK].astype(F32)
            if masked:
                piece = jnp.where(piece < 0.5 * MASKED_SCORE, 0.0, piece)
            pieces.append(jnp.take_along_axis(piece, source, axis=1))
        for place in range(BAND // BLOCK):
            band_ref[head, :, place * BLOCK : (place + 1) * BLOCK] = jnp.where(
                near, pieces[place], pieces[place + 1]
            ).astype(BF16)


def to_band(dense, masked):
    heads, count, _ = dense.shape
    return pl.pallas_call(
        functools.partial(band_kernel, masked),
        grid=(count // BLOCK,),
        in_specs=[heads_block(heads, WINDOW)],
        out_specs=heads_block(heads, BAND),
        out_shape=struct((heads, count, BAND), BF16),
        compiler_params=params(),
        cost_estimate=cost(heads * count * WINDOW * 8, heads * count * (BAND + WINDOW) * 2),
        name="to_band",
    )(dense)


def head_split(block, size):
    if size == 1:
        return block
    lane = lax.broadcasted_iota(jnp.int32, block.shape, 1)
    return jnp.concatenate(
        [
            jnp.where((lane >= h * HEAD_DIM) & (lane < (h + 1) * HEAD_DIM), block, 0)
            for h in range(size)
        ],
        0,
    )


def head_join(stacked, size):
    if size == 1:
        return stacked
    height = stacked.shape[0] // size
    joined = stacked[:height]
    lane = lax.broadcasted_iota(jnp.int32, joined.shape, 1)
    for h in range(1, size):
        joined = jnp.where(lane >= h * HEAD_DIM, stacked[h * height : (h + 1) * height], joined)
    return joined


def forward_kernel(
    slot_ref, token_ref, low_ref, high_ref, near_ref, far_ref, bias_ref, prev_ref,
    score_ref, prob_ref, attended_ref, query_ref, key_ref, value_ref, weight_ref,
):
    step = pl.program_id(0)
    half, _, depth, width = near_ref.shape
    count = token_ref.shape[0]
    heads = prev_ref.shape[0]
    size = min(2, heads)
    span = size * HEAD_DIM

    @pl.when(step == 0)
    def _():
        for place in range(2 * half):
            slot = slot_ref[place]

            @pl.when(slot < half)
            def _():
                weight_ref[:, place * depth : (place + 1) * depth, :] = near_ref[slot]

            @pl.when(slot >= half)
            def _():
                weight_ref[:, place * depth : (place + 1) * depth, :] = far_ref[slot - half]

        low_rows, high_rows = low_ref[...], high_ref[...]
        own = token_ref[...]
        empty = jnp.zeros((PAD, width), BF16)
        query = (dot_nn(own, weight_ref[0]) + bias_ref[0:1, :]).astype(BF16)
        query_ref[...] = query * jnp.asarray(HEAD_DIM ** (-0.5), BF16)
        for out_ref, which in ((key_ref, 1), (value_ref, 2)):
            shift = bias_ref[1:2, :] if which == 2 else 0.0
            weight = weight_ref[which]
            out_ref[0:PAD, :] = empty
            out_ref[PAD:MAXDOC, :] = (dot_nn(low_rows, weight) + shift).astype(BF16)
            out_ref[MAXDOC : MAXDOC + count, :] = (dot_nn(own, weight) + shift).astype(BF16)
            out_ref[MAXDOC + count : MAXDOC + count + HALO, :] = (
                dot_nn(high_rows, weight) + shift
            ).astype(BF16)
            out_ref[MAXDOC + count + HALO :, :] = empty

    start = pl.multiple_of(step * BLOCK, BLOCK)
    for group in range(heads // size):
        lanes = slice(group * span, (group + 1) * span)
        query = head_split(query_ref[pl.ds(start, BLOCK), lanes], size)
        dense = dot_nt(query, key_ref[pl.ds(start, WINDOW), lanes])
        weights = []
        for h in range(size):
            head = group * size + h
            score = dense[h * BLOCK : (h + 1) * BLOCK] + prev_ref[head].astype(F32)
            score_ref[head] = score.astype(BF16)
            peak = jnp.max(score, -1, keepdims=True)
            grown = jnp.exp(score - peak)
            total = jnp.sum(grown, -1, keepdims=True)
            prob = (grown * (1.0 / total)).astype(BF16)
            prob_ref[head] = prob
            weights.append(prob)
        mixed = dot_nn(jnp.concatenate(weights, 0), value_ref[pl.ds(start, WINDOW), lanes])
        attended_ref[:, lanes] = head_join(mixed, size).astype(BF16)


def attend_forward(slots, tokens, low, high, near, far, bias, prev):
    heads, count, _ = prev.shape
    half, _, depth, width = near.shape
    features = tokens.shape[1]
    extended = count + BAND
    flops = 2 * features * width * (3 * count + 4 * HALO) + 4 * heads * count * WINDOW * 128
    return pl.pallas_call(
        forward_kernel,
        grid=(count // BLOCK,),
        in_specs=[
            pl.BlockSpec(memory_space=SMEM),
            whole(tokens.shape),
            whole(low.shape),
            whole(high.shape),
            whole(near.shape),
            whole(far.shape),
            whole(bias.shape),
            heads_block(heads, WINDOW),
        ],
        out_specs=[
            heads_block(heads, WINDOW),
            heads_block(heads, WINDOW),
            rows(width),
            whole((count, width)),
            whole((extended, width)),
            whole((extended, width)),
            whole((3, features, width)),
        ],
        out_shape=[
            struct((heads, count, WINDOW), BF16),
            struct((heads, count, WINDOW), BF16),
            struct((count, width), BF16),
            struct((count, width), BF16),
            struct((extended, width), BF16),
            struct((extended, width), BF16),
            struct((3, features, width), BF16),
        ],
        compiler_params=params(),
        cost_estimate=cost(flops, heads * count * WINDOW * 6, heads * count * WINDOW),
        name="attend_forward",
    )(slots, tokens, low, high, near, far, bias, prev)


def backward_kernel(
    grad_ref, query_ref, key_ref, value_ref, prob_ref, logit_ref,
    prev_ref, query_grad_ref, key_grad_ref, value_grad_ref, key_sum, value_sum,
):
    step = pl.program_id(0)
    heads = prob_ref.shape[0]
    size = min(2, heads)
    span = size * HEAD_DIM

    @pl.when(step == 0)
    def _():
        key_sum[...] = jnp.zeros_like(key_sum)
        value_sum[...] = jnp.zeros_like(value_sum)

    start = pl.multiple_of(step * BLOCK, BLOCK)
    window = pl.ds(start, WINDOW)
    for group in range(heads // size):
        lanes = slice(group * span, (group + 1) * span)
        query = head_split(query_ref[:, lanes], size)
        grad = head_split(grad_ref[:, lanes], size)
        key = key_ref[window, lanes]
        prob_grad = dot_nt(grad, value_ref[window, lanes])
        probs, scores = [], []
        for h in range(size):
            head = group * size + h
            low = prob_ref[head]
            prob = low.astype(F32)
            slope = prob_grad[h * BLOCK : (h + 1) * BLOCK]
            inner = jnp.sum(prob * slope, -1, keepdims=True)
            score = (prob * (slope - inner) + logit_ref[head].astype(F32)).astype(BF16)
            prev_ref[head] = score
            probs.append(low)
            scores.append(score)
        stacked = jnp.concatenate(scores, 0)
        mixed = head_join(dot_nn(stacked, key), size) * HEAD_DIM ** (-0.5)
        query_grad_ref[:, lanes] = mixed.astype(BF16)
        key_sum[lanes, window] += dot_tn(query, stacked)
        value_sum[lanes, window] += dot_tn(grad, jnp.concatenate(probs, 0))

    @pl.when(step == pl.num_programs(0) - 1)
    def _():
        key_grad_ref[...] = key_sum[...].astype(BF16).T
        value_grad_ref[...] = value_sum[...].astype(BF16).T


def attend_backward(grad, query, key, value, prob, logit):
    heads, count, _ = prob.shape
    width = query.shape[1]
    extended = count + BAND
    return pl.pallas_call(
        backward_kernel,
        grid=(count // BLOCK,),
        in_specs=[
            rows(width),
            rows(width),
            whole((extended, width)),
            whole((extended, width)),
            heads_block(heads, WINDOW),
            heads_block(heads, WINDOW),
        ],
        out_specs=[
            heads_block(heads, WINDOW),
            rows(width),
            whole((extended, width)),
            whole((extended, width)),
        ],
        out_shape=[
            struct((heads, count, WINDOW), BF16),
            struct((count, width), BF16),
            struct((extended, width), BF16),
            struct((extended, width), BF16),
        ],
        scratch_shapes=[pltpu.VMEM((width, extended), F32), pltpu.VMEM((width, extended), F32)],
        compiler_params=params(),
        cost_estimate=cost(8 * heads * count * WINDOW * 128, heads * count * WINDOW * 6),
        name="attend_backward",
    )(grad, query, key, value, prob, logit)


def order_kernel(slot_ref, near_ref, far_ref, out_ref):
    half, depth, _ = near_ref.shape
    for place in range(2 * half):
        slot = slot_ref[place]

        @pl.when(slot < half)
        def _():
            out_ref[place * depth : (place + 1) * depth, :] = near_ref[slot]

        @pl.when(slot >= half)
        def _():
            out_ref[place * depth : (place + 1) * depth, :] = far_ref[slot - half]


def in_order(slots, near, far):
    half, depth, width = near.shape
    return pl.pallas_call(
        order_kernel,
        grid=(1,),
        in_specs=[pl.BlockSpec(memory_space=SMEM), whole(near.shape), whole(far.shape)],
        out_specs=whole((2 * half * depth, width)),
        out_shape=struct((2 * half * depth, width), BF16),
        compiler_params=params(),
        cost_estimate=cost(0, 4 * half * depth * width * 2),
        name="in_order",
    )(slots, near, far)


def mean_of(x):
    return jnp.sum(x, -1, keepdims=True) * (1.0 / D)


def normalized(hidden):
    mean = mean_of(hidden)
    inverse = lax.rsqrt(mean_of(hidden * hidden) - mean * mean + EPSILON)
    return (hidden - mean) * inverse, inverse


def norm_back(upstream, normed, inverse):
    return inverse * (upstream - mean_of(upstream) - normed * mean_of(upstream * normed))


def added(own_ref, other_ref, swap):
    other = other_ref[...]
    if swap:
        middle = other.shape[1] // 2
        other = jnp.concatenate([other[:, middle:], other[:, :middle]], 1)
    return own_ref[...].astype(F32) + other.astype(F32)


def first_kernel(
    hidden_units, own_ref, other_ref, token_ref, weight_ref, norm_ref, up_bias_ref,
    normed_ref, inverse_ref, upper_ref, act_ref, slope_ref, part_ref,
):
    width = own_ref.shape[1]
    features = token_ref.shape[1]
    branch = dot_nt(own_ref[...], weight_ref[:, :width]) + dot_nt(
        other_ref[...], weight_ref[:, width:features]
    )
    hidden = token_ref[...].astype(F32) + branch + norm_ref[4:5, :]
    normed, inverse = normalized(hidden)
    normed_ref[...] = normed
    inverse_ref[...] = inverse
    upper = (normed * norm_ref[0:1, :] + norm_ref[2:3, :]).astype(BF16)
    upper_ref[...] = upper
    pre = dot_nn(upper, weight_ref[:, features : features + hidden_units]) + up_bias_ref[...]
    share = 0.5 * (1.0 + lax.erf(pre * ERF_RATE))
    act = (pre * share).astype(BF16)
    act_ref[...] = act
    slope_ref[...] = (share + pre * jnp.exp(-0.5 * pre * pre) * DENSITY_RATE).astype(BF16)
    part_ref[...] = dot_nt(act, weight_ref[:, features + hidden_units :]).astype(BF16)


def feed_first(own, other, tokens, weight, norms, up_bias):
    count, features = tokens.shape
    width = own.shape[1]
    hidden_units = up_bias.shape[1]
    return pl.pallas_call(
        functools.partial(first_kernel, hidden_units),
        grid=(count // BLOCK,),
        in_specs=[
            rows(width),
            rows(other.shape[1]),
            rows(features),
            whole(weight.shape),
            whole(norms.shape),
            whole(up_bias.shape),
        ],
        out_specs=[
            rows(features),
            rows(1),
            rows(features),
            rows(hidden_units),
            rows(hidden_units),
            rows(features),
        ],
        out_shape=[
            struct((count, features), F32),
            struct((count, 1), F32),
            struct((count, features), BF16),
            struct((count, hidden_units), BF16),
            struct((count, hidden_units), BF16),
            struct((count, features), BF16),
        ],
        compiler_params=params(),
        cost_estimate=cost(
            2 * count * weight.size, 2 * weight.size + count * features * 12, count * hidden_units
        ),
        name="feed_first",
    )(own, other, tokens, weight, norms, up_bias)


def column_sum(ref, value):
    partial = jnp.sum(value, 0, keepdims=True)

    @pl.when(pl.program_id(0) == 0)
    def _():
        ref[...] = partial

    @pl.when(pl.program_id(0) > 0)
    def _():
        ref[...] += partial


def second_kernel(
    swap, hidden_units, part_ref, recv_ref, normed_ref, grad_ref, slope_ref, weight_ref, norm_ref,
    output_ref, res_ref, low_ref, hidden_ref, lower_ref,
    bias_sum, gain_sum, shift_sum, hidden_sum,
):
    own = output_ref.shape[1]
    features = part_ref.shape[1]
    upper = normed_ref[...] * norm_ref[0:1, :] + norm_ref[2:3, :]
    hidden = upper + added(part_ref, recv_ref, swap) + norm_ref[5:6, :]
    normed, inverse = normalized(hidden)
    output_ref[...] = (
        normed[:, :own] * norm_ref[1:2, :own] + norm_ref[3:4, :own]
    ).astype(BF16)
    grad = grad_ref[...].astype(F32)
    res = norm_back(grad * norm_ref[1:2, :], normed, inverse)
    res_ref[...] = res
    low = res.astype(BF16)
    low_ref[...] = low
    act_grad = dot_nn(low, weight_ref[:, features + hidden_units :])
    hidden_grad = (act_grad * slope_ref[...].astype(F32)).astype(BF16)
    hidden_ref[...] = hidden_grad
    lower_ref[...] = dot_nt(
        hidden_grad, weight_ref[:, features : features + hidden_units]
    ).astype(BF16)
    column_sum(bias_sum, low[:, :own].astype(F32))
    column_sum(gain_sum, grad[:, :own] * normed[:, :own])
    column_sum(shift_sum, grad[:, :own])
    column_sum(hidden_sum, hidden_grad.astype(F32))


def feed_second(swap, own, part, recv, normed, grad, slope, weight, norms):
    count, features = part.shape
    hidden_units = slope.shape[1]
    return pl.pallas_call(
        functools.partial(second_kernel, swap, hidden_units),
        grid=(count // BLOCK,),
        in_specs=[
            rows(features),
            rows(features),
            rows(features),
            rows(features),
            rows(hidden_units),
            whole(weight.shape),
            whole(norms.shape),
        ],
        out_specs=[
            rows(own),
            rows(features),
            rows(features),
            rows(hidden_units),
            rows(features),
            whole((1, own)),
            whole((1, own)),
            whole((1, own)),
            whole((1, hidden_units)),
        ],
        out_shape=[
            struct((count, own), BF16),
            struct((count, features), F32),
            struct((count, features), BF16),
            struct((count, hidden_units), BF16),
            struct((count, features), BF16),
            struct((1, own), F32),
            struct((1, own), F32),
            struct((1, own), F32),
            struct((1, hidden_units), F32),
        ],
        compiler_params=params(),
        cost_estimate=cost(
            4 * count * features * hidden_units, 2 * weight.size + count * features * 20
        ),
        name="feed_second",
    )(part, recv, normed, grad, slope, weight, norms)


def third_kernel(
    swap, part_ref, recv_ref, res_ref, normed_ref, inverse_ref, weight_ref, norm_ref,
    low_ref, attended_ref, own_ref, gain_sum, shift_sum, bias_sum,
):
    own = own_ref.shape[1]
    grad = added(part_ref, recv_ref, swap) + res_ref[...]
    normed = normed_ref[...]
    res = norm_back(grad * norm_ref[0:1, :], normed, inverse_ref[...])
    own_ref[...] = res[:, :own]
    low = res.astype(BF16)
    low_ref[...] = low
    attended_ref[...] = dot_nn(low, weight_ref[:, : attended_ref.shape[1]]).astype(BF16)
    column_sum(gain_sum, grad[:, :own] * normed[:, :own])
    column_sum(shift_sum, grad[:, :own])
    column_sum(bias_sum, low[:, :own].astype(F32))


def feed_third(swap, own, width, part, recv, res, normed, inverse, weight, norms):
    count, features = part.shape
    return pl.pallas_call(
        functools.partial(third_kernel, swap),
        grid=(count // BLOCK,),
        in_specs=[
            rows(features),
            rows(features),
            rows(features),
            rows(features),
            rows(1),
            whole((features, features)),
            whole(norms.shape),
        ],
        out_specs=[
            rows(features),
            rows(width),
            rows(own),
            whole((1, own)),
            whole((1, own)),
            whole((1, own)),
        ],
        out_shape=[
            struct((count, features), BF16),
            struct((count, width), BF16),
            struct((count, own), F32),
            struct((1, own), F32),
            struct((1, own), F32),
            struct((1, own), F32),
        ],
        compiler_params=params(),
        cost_estimate=cost(2 * count * features * width, count * features * 16),
        name="feed_third",
    )(part, recv, res, normed, inverse, weight, norms)


def spread_rows(block_ref, scratch, keep_ref, send_ref, which):
    half, _, depth, _ = keep_ref.shape
    for slot in range(2 * half):
        start = pl.multiple_of(block_ref[slot] * depth, depth)
        piece = scratch[pl.ds(start, depth), :]
        if slot < half:
            keep_ref[slot, which] = piece
        else:
            send_ref[slot - half, which] = piece.astype(BF16)


def feed_grad_kernel(
    block_ref, low_ref, act_ref, upper_ref, hidden_ref, keep_ref, send_ref, scratch
):
    scratch[...] = dot_tn(upper_ref[...], hidden_ref[...])
    spread_rows(block_ref, scratch, keep_ref, send_ref, 0)
    scratch[...] = dot_tn(low_ref[...], act_ref[...])
    spread_rows(block_ref, scratch, keep_ref, send_ref, 1)


def feed_grads(blocks, low, act, upper, hidden):
    count, features = low.shape
    units = act.shape[1]
    half = blocks.shape[0] // 2
    depth = features // (2 * half)
    chunk = min(256, units)
    column = pl.BlockSpec((count, chunk), lambda b: (0, b))
    result = pl.BlockSpec((half, 2, depth, chunk), lambda b: (0, 0, 0, b))
    return pl.pallas_call(
        feed_grad_kernel,
        grid=(units // chunk,),
        in_specs=[
            pl.BlockSpec(memory_space=SMEM),
            whole(low.shape),
            column,
            whole(upper.shape),
            column,
        ],
        out_specs=[result, result],
        out_shape=[
            struct((half, 2, depth, units), F32),
            struct((half, 2, depth, units), BF16),
        ],
        scratch_shapes=[pltpu.VMEM((features, chunk), F32)],
        compiler_params=params(),
        cost_estimate=cost(4 * count * features * units, 8 * features * units),
        name="feed_grads",
    )(blocks, low, act, upper, hidden)


def project_grad_kernel(
    block_ref, token_ref, low_ref, high_ref, query_ref, key_ref, value_ref, branch_ref,
    attended_ref, keep_ref, send_ref, query_sum, value_sum, scratch,
):
    count = token_ref.shape[0]
    scratch[...] = dot_tn(token_ref[...], query_ref[...])
    spread_rows(block_ref, scratch, keep_ref, send_ref, 0)
    for which, ref in ((1, key_ref), (2, value_ref)):
        scratch[...] = (
            dot_tn(token_ref[...], ref[MAXDOC : MAXDOC + count, :])
            + dot_tn(low_ref[...], ref[PAD:MAXDOC, :])
            + dot_tn(high_ref[...], ref[MAXDOC + count : MAXDOC + count + HALO, :])
        )
        spread_rows(block_ref, scratch, keep_ref, send_ref, which)
    scratch[...] = dot_tn(branch_ref[...], attended_ref[...])
    spread_rows(block_ref, scratch, keep_ref, send_ref, 3)
    query_sum[...] = jnp.sum(query_ref[...].astype(F32), 0, keepdims=True)
    value_sum[...] = jnp.sum(value_ref[...].astype(F32), 0, keepdims=True)


def project_grads(blocks, tokens, low, high, query, key, value, branch, attended):
    count, features = tokens.shape
    width = query.shape[1]
    half = blocks.shape[0] // 2
    depth = features // (2 * half)
    operands = (tokens, low, high, query, key, value, branch, attended)
    return pl.pallas_call(
        project_grad_kernel,
        grid=(1,),
        in_specs=[pl.BlockSpec(memory_space=SMEM)] + [whole(x.shape) for x in operands],
        out_specs=[
            whole((half, 4, depth, width)),
            whole((half, 4, depth, width)),
            whole((1, width)),
            whole((1, width)),
        ],
        out_shape=[
            struct((half, 4, depth, width), F32),
            struct((half, 4, depth, width), BF16),
            struct((1, width), F32),
            struct((1, width), F32),
        ],
        scratch_shapes=[pltpu.VMEM((features, width), F32)],
        compiler_params=params(),
        cost_estimate=cost(2 * features * width * (4 * count + 4 * HALO), 4 << 20),
        name="project_grads",
    )(blocks, *operands)


def token_grad_kernel(query_ref, key_ref, value_ref, weight_ref, low_ref, own_ref, high_ref):
    count = query_ref.shape[0]

    def piece(start, size):
        return dot_nt(key_ref[start : start + size, :], weight_ref[1]) + dot_nt(
            value_ref[start : start + size, :], weight_ref[2]
        )

    for start in range(0, HALO, BLOCK):
        low_ref[start : start + BLOCK, :] = piece(PAD + start, BLOCK).astype(BF16)
        high_ref[start : start + BLOCK, :] = piece(MAXDOC + count + start, BLOCK).astype(BF16)
    for start in range(0, count, BLOCK):
        own_ref[start : start + BLOCK, :] = piece(MAXDOC + start, BLOCK) + dot_nt(
            query_ref[start : start + BLOCK, :], weight_ref[0]
        )


def token_grads(query, key, value, weight):
    count = query.shape[0]
    features = weight.shape[1]
    operands = (query, key, value, weight)
    return pl.pallas_call(
        token_grad_kernel,
        grid=(1,),
        in_specs=[whole(x.shape) for x in operands],
        out_specs=[
            whole((HALO, features)),
            whole((count, features)),
            whole((HALO, features)),
        ],
        out_shape=[
            struct((HALO, features), BF16),
            struct((count, features), F32),
            struct((HALO, features), BF16),
        ],
        compiler_params=params(),
        cost_estimate=cost(2 * features * query.shape[1] * (3 * count + 4 * HALO), 4 << 20),
        name="token_grads",
    )(*operands)


def from_next(x, axis, step):
    count = lax.axis_size(axis)
    return lax.ppermute(x, axis, [((i + step) % count, i) for i in range(count)])


def with_partner(x, bit):
    count = lax.axis_size("row")
    return lax.ppermute(x, "row", [(i, i ^ bit) for i in range(count)])


def others(x):
    return [from_next(x, "col", step) for step in range(1, lax.axis_size("col"))]


def bits_of(count):
    return [1 << place for place in range(count.bit_length() - 1)]


def gather_rows(shard):
    order = bits_of(lax.axis_size("row"))[::-1]
    held = shard[None]
    for bit in order[:-1]:
        held = jnp.concatenate([held, with_partner(held, bit)], 0)
    return held, with_partner(held, order[-1])


def reduce_rows(keep, send):
    for bit in bits_of(lax.axis_size("row")):
        total = keep + with_partner(send, bit).astype(F32)
        half = total.shape[0] // 2
        if half:
            keep, send = total[:half], total[half:].astype(BF16)
    return total[0]


def sum_rows(value):
    for bit in bits_of(lax.axis_size("row")):
        value = value + with_partner(value, bit)
    return value


def exchanged(part):
    arrived = others(part)
    if len(arrived) == 1:
        return arrived[0]
    shift = part.shape[1] // (len(arrived) + 1)
    total = sum(
        jnp.roll(x.astype(F32), step * shift, 1) for step, x in enumerate(arrived, 1)
    )
    return total.astype(BF16)


def on_device(
    tokens,
    prev_logits,
    doc_lengths,
    qkv_weight,
    qv_bias,
    out_weight,
    out_bias,
    up_weight,
    up_bias,
    down_weight,
    norm_gain,
    norm_shift,
    out_grad,
    logit_grad,
):
    count, own = tokens.shape
    width = qkv_weight.shape[2]
    row_count, col_count = lax.axis_size("row"), lax.axis_size("col")
    row_index, col_index = lax.axis_index("row"), lax.axis_index("col")
    token_count = count * row_count
    swap = col_count == 2

    order = bits_of(row_count)
    top = len(order) - 1

    def reversed_bits(x):
        return sum(((x >> place) & 1) << (top - place) for place in range(top + 1))

    places = jnp.arange(row_count, dtype=jnp.int32)
    offset = col_index * (row_count // col_count)
    slots = reversed_bits(((places + offset) % row_count) ^ row_index)
    blocks = ((reversed_bits(places) ^ row_index) - offset) % row_count
    base = (row_index * count)[None]

    tokens_full = jnp.concatenate([tokens] + others(tokens), 1)
    near, far = gather_rows(qkv_weight)
    forward = [(i, i + 1) for i in range(row_count - 1)]
    backward = [(b, a) for a, b in forward]
    low_tokens = lax.ppermute(tokens_full[count - HALO :], "row", forward)
    high_tokens = lax.ppermute(tokens_full[:HALO], "row", backward)
    out_turned = out_weight.T
    out_turned = jnp.concatenate([out_turned] + others(out_turned), 1)
    norms = jnp.concatenate([norm_gain, norm_shift, out_bias], 0)
    norms = jnp.concatenate([norms] + others(norms), 1)
    grad_full = jnp.concatenate([out_grad] + others(out_grad), 1)
    feed_near, feed_far = gather_rows(
        jnp.concatenate([out_turned, up_weight, down_weight.T], 1)
    )

    prev_dense = to_dense(prev_logits, doc_lengths, base, MASKED_SCORE, token_count)
    scores, probs, attended, query, key, value, weight = attend_forward(
        slots, tokens_full, low_tokens, high_tokens, near, far, qv_bias, prev_dense
    )
    attended_other = jnp.concatenate(others(attended), 1)
    logit_dense = to_dense(logit_grad, doc_lengths, base, 0.0, token_count)
    feed = in_order(slots, feed_near, feed_far)

    normed, inverse, upper, act, slope, down_part = feed_first(
        attended, attended_other, tokens_full, feed, norms, up_bias[None]
    )
    down_other = exchanged(down_part)
    new_logits = to_band(scores, True)
    output, res_two, ffn_low, hidden_grad, lower_part, ffn_bias, two_gain, two_shift, hidden_sum = (
        feed_second(swap, own, down_part, down_other, normed, grad_full, slope, feed, norms)
    )
    lower_other = exchanged(lower_part)
    feed_keep, feed_send = feed_grads(blocks, ffn_low, act, upper, hidden_grad)
    branch_low, attended_grad, res_one, one_gain, one_shift, attn_bias = feed_third(
        swap, own, width, lower_part, lower_other, res_two, normed, inverse, feed, norms
    )
    prev_dense_grad, query_grad, key_grad, value_grad = attend_backward(
        attended_grad, query, key, value, probs, logit_dense
    )
    keep, send, query_sum, value_sum = project_grads(
        blocks, tokens_full, low_tokens, high_tokens, query_grad, key_grad, value_grad,
        branch_low, attended,
    )
    feed_grad = reduce_rows(feed_keep, feed_send)
    project_grad = reduce_rows(keep, send)
    low_part, center, high_part = token_grads(query_grad, key_grad, value_grad, weight)
    arrived_low = lax.ppermute(high_part, "row", forward).astype(F32)
    arrived_high = lax.ppermute(low_part, "row", backward).astype(F32)
    rest = ((0, count - HALO), (0, 0))
    center = center + jnp.pad(arrived_low, rest) + jnp.pad(arrived_high, ((count - HALO, 0), (0, 0)))
    tokens_grad = center[:, :own] + res_one
    for step in range(1, col_count):
        part = center[:, step * own : (step + 1) * own].astype(BF16)
        tokens_grad = tokens_grad + from_next(part, "col", -step).astype(F32)
    prev_grad = to_band(prev_dense_grad, False)

    sums = sum_rows(
        jnp.concatenate(
            [
                query_sum, value_sum, attn_bias, ffn_bias, one_gain, two_gain, one_shift,
                two_shift, hidden_sum.reshape(-1, own),
            ],
            0,
        )
    )
    return (
        output,
        new_logits,
        tokens_grad.astype(BF16),
        prev_grad,
        project_grad[:3],
        sums[0:2],
        project_grad[3].T,
        sums[2:4],
        feed_grad[0],
        sums[8:].reshape(-1),
        feed_grad[1].T,
        sums[4:6],
        sums[6:8],
    )


def solution(mesh):
    return jax.shard_map(
        on_device,
        mesh=mesh,
        in_specs=(
            P("row", "col"),
            P("col", "row", None),
            P(),
            P(None, "row", "col"),
            P(None, "col"),
            P("col", "row"),
            P(None, "col"),
            P("row", "col"),
            P("col"),
            P("col", "row"),
            P(None, "col"),
            P(None, "col"),
            P("row", "col"),
            P("col", "row", None),
        ),
        out_specs=(
            P("row", "col"),
            P("col", "row", None),
            P("row", "col"),
            P("col", "row", None),
            P(None, "row", "col"),
            P(None, "col"),
            P("col", "row"),
            P(None, "col"),
            P("row", "col"),
            P("col"),
            P("col", "row"),
            P(None, "col"),
            P(None, "col"),
        ),
        check_vma=False,
    )
```

time: 652 us -> 225 us (0.35); the launches traced: 644 us -> 224 us
  local copies, waits for them, and re-layouts: 202 us -> 18.8 us
  blocking collectives: 167 us -> 0 us
  Pallas kernels: 0 us -> 68.8 us
  waiting for transfers between devices: 146 us -> 79.6 us
  other arithmetic: 60.9 us -> 4.55 us
  starting transfers between devices: 7.76 us -> 51 us
  matrix products: 42.5 us -> 0 us
  between operations: 17.1 us -> 1.3 us
    psum x5 -> x0, blocking collectives: 89 us -> none  [the longest x1 69.2 us: on_device(): lax.psum((qv_part, bias_part, hidden_part, gain_part, shift_part), 'row')]
    unnamed x82 -> x93, local copies, waits for them, and re-layouts: 101 us -> 14.5 us
    ppermute x4 -> x32, waiting for transfers between devices: 0.01 us -> 79.6 us  [the longest x20 50.6 us: with_partner(): return lax.ppermute(x, 'row', [(i, i ^ bit) for i in range(count)])]
    all_gather x6 -> x0, blocking collectives: 78.1 us -> none  [the longest x4 31.7 us: features(): return lax.all_gather(local_part, 'col', axis=1, tiled=True)]
    pallas_call x0 -> x13, Pallas kernels: none -> 68.8 us  [the longest x1 11.8 us: attend_forward(): pl.pallas_call(forward_kernel, grid=(count // BLOCK,), in_specs=[pl.Block...]
    reshape x5 -> x1, local copies, waits for them, and re-layouts: 60.1 us -> 0.01 us  [on_device(): hidden_sum.reshape(-1, own)]
    reduce_scatter x7 -> x0, waiting for transfers between devices: 53.5 us -> none  [the longest x4 53.5 us: feature_sum(): lax.psum_scatter(partial_term.astype(jnp.bfloat16), 'col', scatter_dimens...]
    unnamed x11 -> x0, waiting for transfers between devices: 49.6 us -> none
  transfers between devices with their start and end apart: 14 -> 32, of which waited for: 7 -> 15; matrix products, arithmetic and copies ran while one was open for 27% -> 3% of each run, Pallas kernels for 0% -> 18%
where the time goes in v1:
time: 225 us; the launch traced here: 224 us
  waiting for transfers between devices  79.6 us (35%)
  Pallas kernels  68.8 us (31%)
  starting transfers between devices  51 us (23%)
  local copies, waits for them, and re-layouts  18.8 us (8%)
  other arithmetic  4.55 us (2%)
    ppermute x20, waiting for transfers between devices, with_partner(): return lax.ppermute(x, 'row', [(i, i ^ bit) for i in range(count)])  50.6 us
    ppermute x20, starting transfers between devices, with_partner(): return lax.ppermute(x, 'row', [(i, i ^ bit) for i in range(count)])  32.4 us
    ppermute x8, waiting for transfers between devices, from_next(): lax.ppermute(x, axis, [((i + step) % count, i) for i in range(count)])  28.9 us
    unnamed x93, local copies, waits for them, and re-layouts  14.5 us
    pallas_call x1, Pallas kernels, attend_forward(): pl.pallas_call(forward_kernel, grid=(count // BLOCK,), in_specs=[pl.Block...  11.8 us
    ppermute x8, starting transfers between devices, from_next(): lax.ppermute(x, axis, [((i + step) % count, i) for i in range(count)])  11.7 us
    pallas_call x1, Pallas kernels, attend_backward(): pl.pallas_call(backward_kernel, grid=(count // BLOCK,), in_specs=[rows(wi...  10.7 us
    pallas_call x2, Pallas kernels, to_dense(): pl.pallas_call(functools.partial(dense_kernel, fill, token_count), grid=(...  10.5 us
  transfers between devices with their start and end apart: 32, of which 15 were waited for; matrix products, arithmetic and copies ran while one was open for 3% of the time, Pallas kernels for 18%

profile of v1, /device:TPU:0, one launch (start us, length us, event | category | flops | bytes accessed | tf_op | source)
XLA Modules:
  0.0 224.0 jit_solution(12021083092281958183)
XLA Ops:
  0.7 3.0 %collective-permute-start.8 = (bf16[32,256]{1,0:T(8,128)(2,1)}, bf16[32,256]{1,0:T(8,128)(2,1)S(1)}, u32[]{:S(2)}, u32[]{:S(2)}) collective-permute-start(bf16[32,256]{1,0:T(8,128)(2,1)} %bitcast.30), channel_id=1, source_target_pairs={{1,0},{0,1},{3,2},{2,3},{5,4},{4,5},{7,6},{6,7},{9,8},{8,9},{11,10... | collective-permute-start | bytes 49160 | tf_op jit(solution)/shard_map/ppermute | solution.py:744
  3.7 1.9 collective-permute-done.8
  5.6 0.9 maximum_bitcast_fusion
  6.5 3.2 %collective-permute-start.9 = (bf16[1,32,2560]{2,1,0:T(8,128)(2,1)S(1)}, bf16[1,32,2560]{2,1,0:T(8,128)(2,1)S(1)}, u32[]{:S(2)}, u32[]{:S(2)}) collective-permute-start(bf16[1,32,2560]{2,1,0:T(8,128)(2,1)S(1)} %maximum_bitcast_fusion), channel_id=1, source_target_pairs={{0,16},{2,18},{4,20},{6,22},{8,24},{10,26},{12,28},{14,30},{16,0},... | collective-permute-start | bytes 491528 | tf_op jit(solution)/shard_map/ppermute | solution.py:749
  9.7 6.6 %collective-permute-done.9 = bf16[1,32,2560]{2,1,0:T(8,128)(2,1)S(1)} collective-permute-done((bf16[1,32,2560]{2,1,0:T(8,128)(2,1)S(1)}, bf16[1,32,2560]{2,1,0:T(8,128)(2,1)S(1)}, u32[]{:S(2)}, u32[]{:S(2)}) %collective-permute-start.9) | collective-permute-done | bytes 163872 | tf_op jit(solution)/shard_map/ppermute | solution.py:749
  17.1 7.8 %collective-permute-done.10 = bf16[2,32,2560]{2,1,0:T(8,128)(2,1)S(1)} collective-permute-done((bf16[2,32,2560]{2,1,0:T(8,128)(2,1)S(1)}, bf16[2,32,2560]{2,1,0:T(8,128)(2,1)S(1)}, u32[]{:S(2)}, u32[]{:S(2)}) %collective-permute-start.10) | collective-permute-done | bytes 327712 | tf_op jit(solution)/shard_map/ppermute | solution.py:749
  24.9 1.7 collective-permute-start.11
  26.6 2.9 %collective-permute-start.3 = (bf16[1,3,32,256]{3,2,1,0:T(8,128)(2,1)S(1)}, bf16[1,3,32,256]{3,2,1,0:T(8,128)(2,1)S(1)}, u32[]{:S(2)}, u32[]{:S(2)}) collective-permute-start(bf16[1,3,32,256]{3,2,1,0:T(8,128)(2,1)S(1)} %bitcast.25), channel_id=1, source_target_pairs={{0,16},{2,18},{4,20},{6,22},{8,24},{10,26},{12,28},{14,30},{16,0},... | collective-permute-start | bytes 147464 | tf_op jit(solution)/shard_map/ppermute | solution.py:749
  29.5 1.5 collective-permute-start
  31.6 1.8 collective-permute-start.4
  33.4 2.9 %collective-permute-done.4 = bf16[2,3,32,256]{3,2,1,0:T(8,128)(2,1)S(1)} collective-permute-done((bf16[2,3,32,256]{3,2,1,0:T(8,128)(2,1)S(1)}, bf16[2,3,32,256]{3,2,1,0:T(8,128)(2,1)S(1)}, u32[]{:S(2)}, u32[]{:S(2)}) %collective-permute-start.4) | collective-permute-done | bytes 98336 | tf_op jit(solution)/shard_map/ppermute | solution.py:749
  36.8 4.8 %collective-permute-done.11 = bf16[4,32,2560]{2,1,0:T(8,128)(2,1)S(1)} collective-permute-done((bf16[4,32,2560]{2,1,0:T(8,128)(2,1)S(1)}, bf16[4,32,2560]{2,1,0:T(8,128)(2,1)S(1)}, u32[]{:S(2)}, u32[]{:S(2)}) %collective-permute-start.11) | collective-permute-done | bytes 655392 | tf_op jit(solution)/shard_map/ppermute | solution.py:749
  41.9 0.9 fusion.18
  42.9 2.4 %collective-permute-start.1 = (bf16[384,512]{1,0:T(8,128)(2,1)}, bf16[384,512]{1,0:T(8,128)(2,1)S(1)}, u32[]{:S(2)}, u32[]{:S(2)}) collective-permute-start(bf16[384,512]{1,0:T(8,128)(2,1)} %get-tuple-element.96), channel_id=1, source_target_pairs={{0,2},{2,4},{4,6},{6,8},{8,10},{10,12},{12,14},{14,16},{16,18},{18... | collective-permute-start | bytes 1179656 | tf_op jit(solution)/shard_map/ppermute | solution.py:833
  45.3 1.3 collective-permute-start.2
  46.6 0.8 pad_maximum_fusion.3.near_ref
  47.4 1.9 collective-permute-start.6
  49.3 2.2 copy-done.2
  51.5 5.3 %to_dense.2.prev_ref = bf16[4,512,1152]{2,1,0:T(8,128)(2,1)} custom-call(s32[1,33]{1,0:T(1,128)S(1)} %copy-done.21, s32[1]{0:T(128)} %bitcast.1.base_ref, bf16[4,512,1024]{2,1,0:T(8,128)(2,1)S(1)} %copy-done.2), custom_call_target="tpu_custom_call" | custom-call | flops 18874368 | bytes 8912896 | tf_op jit(solution)/shard_map/to_dense/pallas_call | solution.py:96
  56.9 11.8 %attend_forward.1 = (bf16[4,512,1152]{2,1,0:T(8,128)(2,1)}, bf16[4,512,1152]{2,1,0:T(8,128)(2,1)}, bf16[512,256]{1,0:T(8,128)(2,1)S(1)}, bf16[512,256]{1,0:T(8,1...) custom-call(s32[16]{0:T(128)S(1)} %shift-left_add_fusion.slot_ref, ...), custom_call_target="tpu_custom_call" | custom-call | flops 2013265920 | bytes 14155776 | tf_op jit(solution)/shard_map/attend_forward/pallas_call | solution.py:234
  68.7 0.9 copy-done.5
  69.6 0.9 copy-done.7
  70.5 0.9 copy-done.30
  71.3 1.5 collective-permute-start.7
  73.5 6.3 %collective-permute-done.13 = f32[6,256]{1,0:T(8,128)S(1)} collective-permute-done((f32[6,256]{1,0:T(8,128)S(1)}, f32[6,256]{1,0:T(8,128)S(1)}, u32[]{:S(2)}, u32[]{:S(2)}) %collective-permute-start.13) | collective-permute-done | bytes 6176 | tf_op jit(solution)/shard_map/ppermute | solution.py:744
  79.8 1.1 in_order.1.weight_ref
  80.9 1.5 copy-done
  82.4 5.9 %feed_first.1 = (f32[512,512]{1,0:T(8,128)S(1)}, f32[512,1]{1,0:T(8,128)S(1)}, bf16[512,512]{1,0:T(8,128)(2,1)S(1)}, bf16[512,1024]{1,0:T(8,128)(2,1)S(1)}, bf16...) custom-call(bf16[512,256]{1,0:T(8,128)(2,1)S(1)} %get-tuple-element.54.own_ref.attended_ref, ...), custom_call_target="tpu_custom_call" | custom-call | flops 1342177280 | bytes 5767168 | tf_op jit(solution)/shard_map/feed_first/pallas_call | solution.py:427
  88.3 1.0 copy-done.4
  89.3 1.5 collective-permute-start.14
  91.3 16.5 %collective-permute-done.15 = bf16[512,256]{1,0:T(8,128)(2,1)S(1)} collective-permute-done((bf16[512,256]{1,0:T(8,128)(2,1)S(1)}, bf16[512,256]{1,0:T(8,128)(2,1)S(1)}, u32[]{:S(2)}, u32[]{:S(2)}) %collective-permute-start.15) | collective-permute-done | bytes 262176 | tf_op jit(solution)/shard_map/ppermute | solution.py:744
  108.0 6.5 %feed_second.1 = (bf16[512,256]{1,0:T(8,128)(2,1)}, f32[512,512]{1,0:T(8,128)S(1)}, bf16[512,512]{1,0:T(8,128)(2,1)S(1)}, bf16[512,1024]{1,0:T(8,128)(2,1)S(1)},...) custom-call(bf16[512,512]{1,0:T(8,128)(2,1)S(1)} %get-tuple-element., ...), custom_call_target="tpu_custom_call" | custom-call | flops 1073741824 | bytes 7864320 | tf_op jit(solution)/shard_map/feed_second/pallas_call | solution.py:507
  114.5 1.6 collective-permute-start.16
  116.1 5.2 %to_dense.3.logit_ref = bf16[4,512,1152]{2,1,0:T(8,128)(2,1)} custom-call(s32[1,33]{1,0:T(1,128)S(1)} %copy-done.21, s32[1]{0:T(128)} %bitcast.1.base_ref, bf16[4,512,1024]{2,1,0:T(8,128)(2,1)S(1)} %copy-done.3), custom_call_target="tpu_custom_call" | custom-call | flops 18874368 | bytes 8912896 | tf_op jit(solution)/shard_map/to_dense/pallas_call | solution.py:96
  122.5 4.2 %collective-permute-done.16.recv_ref = bf16[512,512]{1,0:T(8,128)(2,1)} collective-permute-done((bf16[512,512]{1,0:T(8,128)(2,1)S(1)}, bf16[512,512]{1,0:T(8,128)(2,1)}, u32[]{:S(2)}, u32[]{:S(2)}) %collective-permute-start.16) | collective-permute-done | bytes 524320 | tf_op jit(solution)/shard_map/ppermute | solution.py:744
  126.7 1.0 copy-done.12
  127.8 3.4 %feed_third.1 = (bf16[512,512]{1,0:T(8,128)(2,1)S(1)}, bf16[512,256]{1,0:T(8,128)(2,1)S(1)}, f32[512,256]{1,0:T(8,128)S(1)}, f32[1,256]{1,0:T(1,128)S(1)}, f32[1,256]{1,0:T(1,128)S(1)}, /*index=5*/f32[1,256]{1,0:T(1,128)S(1)}) custom-call(bf16[512,512]{1,0:T(8,128)(2,1)S(1)} %copy-done.12, bf16[512,512]{1,0:T(8,128)(2,1)} %collective-permute-done.16.recv_ref, ...), custom_call_target="tpu_custom_call" | custom-call | flops 134217728 | bytes 4194304 | tf_op jit(solution)/shard_map/feed_third/pallas_call | solution.py:568
  131.2 10.7 %attend_backward.1 = (bf16[4,512,1152]{2,1,0:T(8,128)(2,1)}, bf16[512,256]{1,0:T(8,128)(2,1)S(1)}, bf16[1536,256]{1,0:T(8,128)(2,1)S(1)}, bf16[1536,256]{1,0:T(8,128)(2,1)S(1)}) custom-call(bf16[512,256]{1,0:T(8,128)(2,1)S(1)} %get-tuple-element.63.grad_ref, bf16[512,256]{1,0:T(8,128)(2,1)S(1)} %copy-done.18, bf16[1536,256]{1,0:T(8,128)(2,1)S(1)} %copy-done.6, ...), custom_call_target="tpu_custom_call" | custom-call | flops 2415919104 | bytes 14155776 | tf_op jit(solution)/shard_map/attend_backward/pallas_call | solution.py:320
  141.9 2.8 %project_grads.1 = (f32[8,4,32,256]{3,2,1,0:T(8,128)S(1)}, bf16[8,4,32,256]{3,2,1,0:T(8,128)(2,1)S(1)}, f32[1,256]{1,0:T(1,128)S(1)}, f32[1,256]{1,0:T(1,128)S(1)}) custom-call(s32[16]{0:T(128)S(1)} %and_select_fusion.block_ref, bf16[512,512]{1,0:T(8,128)(2,1)S(1)} %constant_dynamic-update-slice_fusion.token_ref, bf16[384,512]{1,0:T(8,128)(2,1)S(1)} %copy-done.14, ...), custom_call_target="tpu_custom_call" | custom-call | flops 939524096 | bytes 4194304 | tf_op jit(solution)/shard_map/project_grads/pallas_call | solution.py:678
  144.7 0.8 copy-done.24
  145.7 1.2 collective-permute-done.24
  146.8 2.9 %collective-permute-start.25 = (f32[12,256]{1,0:T(8,128)S(1)}, f32[12,256]{1,0:T(8,128)S(1)}, u32[]{:S(2)}, u32[]{:S(2)}) collective-permute-start(f32[12,256]{1,0:T(8,128)S(1)} %add.104), channel_id=1, source_target_pairs={{0,4},{2,6},{4,0},{6,2},{8,12},{10,14},{12,8},{14,10},{16,20},{18,... | collective-permute-start | bytes 36872 | tf_op jit(solution)/shard_map/ppermute | solution.py:749
  149.8 2.3 %copy-done.1 = bf16[4,512,1152]{2,1,0:T(8,128)(2,1)S(1)} copy-done((bf16[4,512,1152]{2,1,0:T(8,128)(2,1)S(1)}, bf16[4,512,1152]{2,1,0:T(8,128)(2,1)}, u32[]{:S(2)}) %copy-start.1) | copy-done | bytes 4718616
  152.1 4.9 %to_band.2 = bf16[4,512,1024]{2,1,0:T(8,128)(2,1)} custom-call(bf16[4,512,1152]{2,1,0:T(8,128)(2,1)S(1)} %copy-done.1), custom_call_target="tpu_custom_call" | custom-call | flops 18874368 | bytes 8912896 | tf_op jit(solution)/shard_map/to_band/pallas_call | solution.py:132
  157.1 1.7 collective-permute-start.26
  158.8 1.2 copy-done.33
  160.0 1.0 copy-done.35
  161.0 4.1 %feed_grads.1 = (f32[8,2,32,1024]{3,2,1,0:T(8,128)}, bf16[8,2,32,1024]{3,2,1,0:T(8,128)(2,1)S(1)}) custom-call(s32[16]{0:T(128)S(1)} %and_select_fusion.block_ref, bf16[512,512]{1,0:T(8,128)(2,1)S(1)} %copy-done.27, bf16[512,1024]{1,0:T(8,128)(2,1)S(1)} %copy-done.33, bf16[512,512]{1,0:T(8,128)(2,1)S(1)} %copy-done.35, bf16[512,1024]{1,0:T(8,128)(2,1)S(1)} %copy-done.23), custom_call_target="tpu_custom_call" | custom-call | flops 1073741824 | bytes 4194304 | tf_op jit(solution)/shard_map/feed_grads/pallas_call | solution.py:630
  165.7 4.1 %collective-permute-start.27 = (f32[12,256]{1,0:T(8,128)S(1)}, f32[12,256]{1,0:T(8,128)S(1)}, u32[]{:S(2)}, u32[]{:S(2)}) collective-permute-start(f32[12,256]{1,0:T(8,128)S(1)} %add.106), channel_id=1, source_target_pairs={{0,16},{2,18},{4,20},{6,22},{8,24},{10,26},{12,28},{14,30},{16,0},... | collective-permute-start | bytes 36872 | tf_op jit(solution)/shard_map/ppermute | solution.py:749
  169.8 2.1 token_grads.1
  171.9 1.7 collective-permute-start.17
  173.6 1.5 collective-permute-start.18
  175.1 4.9 %to_band.3 = bf16[4,512,1024]{2,1,0:T(8,128)(2,1)} custom-call(bf16[4,512,1152]{2,1,0:T(8,128)(2,1)S(1)} %bitcast.23), custom_call_target="tpu_custom_call" | custom-call | flops 18874368 | bytes 8912896 | tf_op jit(solution)/shard_map/to_band/pallas_call | solution.py:132
  181.5 1.5 collective-permute-start.19
  183.2 5.4 %collective-permute-start.21 = (bf16[4,4,32,256]{3,2,1,0:T(8,128)(2,1)S(1)}, bf16[4,4,32,256]{3,2,1,0:T(8,128)(2,1)S(1)}, u32[]{:S(2)}, u32[]{:S(2)}) collective-permute-start(bf16[4,4,32,256]{3,2,1,0:T(8,128)(2,1)S(1)} %slice.164), channel_id=1, source_target_pairs={{0,4},{2,6},{4,0},{6,2},{8,12},{10,14},{12,8},{14,10},{16,20},{18,... | collective-permute-start | bytes 786440 | tf_op jit(solution)/shard_map/ppermute | solution.py:749
  189.1 6.7 %collective-permute-done.21 = bf16[4,4,32,256]{3,2,1,0:T(8,128)(2,1)S(1)} collective-permute-done((bf16[4,4,32,256]{3,2,1,0:T(8,128)(2,1)S(1)}, bf16[4,4,32,256]{3,2,1,0:T(8,128)(2,1)S(1)}, u32[]{:S(2)}, u32[]{:S(2)}) %collective-permute-start.21) | collective-permute-done | bytes 262176 | tf_op jit(solution)/shard_map/ppermute | solution.py:749
  196.0 0.8 collective-permute-start.22
  196.8 0.8 fusion.1
  197.6 3.4 %collective-permute-done.22 = bf16[2,4,32,256]{3,2,1,0:T(8,128)(2,1)S(1)} collective-permute-done((bf16[2,4,32,256]{3,2,1,0:T(8,128)(2,1)S(1)}, bf16[2,4,32,256]{3,2,1,0:T(8,128)(2,1)S(1)}, u32[]{:S(2)}, u32[]{:S(2)}) %collective-permute-start.22) | collective-permute-done | bytes 131104 | tf_op jit(solution)/shard_map/ppermute | solution.py:749
  201.6 4.0 %collective-permute-done.29 = bf16[4,2,32,1024]{3,2,1,0:T(8,128)(2,1)S(1)} collective-permute-done((bf16[4,2,32,1024]{3,2,1,0:T(8,128)(2,1)S(1)}, bf16[4,2,32,1024]{3,2,1,0:T(8,128)(2,1)S(1)}, u32[]{:S(2)}, u32[]{:S(2)}) %collective-permute-start.29) | collective-permute-done | bytes 524320 | tf_op jit(solution)/shard_map/ppermute | solution.py:749
  205.8 2.2 collective-permute-start.30
  208.7 5.8 %collective-permute-done.30 = bf16[2,2,32,1024]{3,2,1,0:T(8,128)(2,1)S(1)} collective-permute-done((bf16[2,2,32,1024]{3,2,1,0:T(8,128)(2,1)S(1)}, bf16[2,2,32,1024]{3,2,1,0:T(8,128)(2,1)S(1)}, u32[]{:S(2)}, u32[]{:S(2)}) %collective-permute-start.30) | collective-permute-done | bytes 262176 | tf_op jit(solution)/shard_map/ppermute | solution.py:749
  214.6 1.2 collective-permute-start.31
  216.5 6.8 %collective-permute-done.31 = bf16[1,2,32,1024]{3,2,1,0:T(8,128)(2,1)S(1)} collective-permute-done((bf16[1,2,32,1024]{3,2,1,0:T(8,128)(2,1)S(1)}, bf16[1,2,32,1024]{3,2,1,0:T(8,128)(2,1)S(1)}, u32[]{:S(2)}, u32[]{:S(2)}) %collective-permute-start.31) | collective-permute-done | bytes 131104 | tf_op jit(solution)/shard_map/ppermute | solution.py:749
  (150 shorter events, 10.6 us)
Async XLA Ops:
  0.6 25.9 %copy-start.37 = (bf16[3,32,256]{2,1,0:T(8,128)(2,1)S(1)}, bf16[3,32,256]{2,1,0:T(8,128)(2,1)}, u32[]{:S(2)}) copy-start(bf16[3,32,256]{2,1,0:T(8,128)(2,1)} %param.17) | copy-start | bytes 147460
  0.7 28.8 %copy-start.38 = (bf16[512,256]{1,0:T(8,128)(2,1)S(1)}, bf16[512,256]{1,0:T(8,128)(2,1)}, u32[]{:S(2)}) copy-start(bf16[512,256]{1,0:T(8,128)(2,1)} %param.14) | copy-start | bytes 786436
  0.7 4.9 %collective-permute-start.8 = (bf16[32,256]{1,0:T(8,128)(2,1)}, bf16[32,256]{1,0:T(8,128)(2,1)S(1)}, u32[]{:S(2)}, u32[]{:S(2)}) collective-permute-start(bf16[32,256]{1,0:T(8,128)(2,1)} %bitcast.30), channel_id=1, source_target_pairs={{1,0},{0,1},{3,2},{2,3},{5,4},{4,5},{7,6},{6,7},{9,8},{8,9},{11,10... | collective-permute-start | bytes 49160 | tf_op jit(solution)/shard_map/ppermute | solution.py:744
  6.5 9.7 %collective-permute-start.9 = (bf16[1,32,2560]{2,1,0:T(8,128)(2,1)S(1)}, bf16[1,32,2560]{2,1,0:T(8,128)(2,1)S(1)}, u32[]{:S(2)}, u32[]{:S(2)}) collective-permute-start(bf16[1,32,2560]{2,1,0:T(8,128)(2,1)S(1)} %maximum_bitcast_fusion), channel_id=1, source_target_pairs={{0,16},{2,18},{4,20},{6,22},{8,24},{10,26},{12,28},{14,30},{16,0},... | collective-permute-start | bytes 491528 | tf_op jit(solution)/shard_map/ppermute | solution.py:749
  16.3 8.6 %collective-permute-start.10 = (bf16[2,32,2560]{2,1,0:T(8,128)(2,1)S(1)}, bf16[2,32,2560]{2,1,0:T(8,128)(2,1)S(1)}, u32[]{:S(2)}, u32[]{:S(2)}) collective-permute-start(bf16[2,32,2560]{2,1,0:T(8,128)(2,1)S(1)} %pad_maximum_fusion.4), channel_id=1, source_target_pairs={{0,8},{2,10},{4,12},{6,14},{8,0},{10,2},{12,4},{14,6},{16,24},{18,... | collective-permute-start | bytes 983048 | tf_op jit(solution)/shard_map/ppermute | solution.py:749
  24.9 16.8 %collective-permute-start.11 = (bf16[4,32,2560]{2,1,0:T(8,128)(2,1)S(1)}, bf16[4,32,2560]{2,1,0:T(8,128)(2,1)S(1)}, u32[]{:S(2)}, u32[]{:S(2)}) collective-permute-start(bf16[4,32,2560]{2,1,0:T(8,128)(2,1)S(1)} %pad_maximum_fusion.1), channel_id=1, source_target_pairs={{0,4},{2,6},{4,0},{6,2},{8,12},{10,14},{12,8},{14,10},{16,20},{18,... | collective-permute-start | bytes 1966088 | tf_op jit(solution)/shard_map/ppermute | solution.py:749
  26.6 5.0 %collective-permute-start.3 = (bf16[1,3,32,256]{3,2,1,0:T(8,128)(2,1)S(1)}, bf16[1,3,32,256]{3,2,1,0:T(8,128)(2,1)S(1)}, u32[]{:S(2)}, u32[]{:S(2)}) collective-permute-start(bf16[1,3,32,256]{3,2,1,0:T(8,128)(2,1)S(1)} %bitcast.25), channel_id=1, source_target_pairs={{0,16},{2,18},{4,20},{6,22},{8,24},{10,26},{12,28},{14,30},{16,0},... | collective-permute-start | bytes 147464 | tf_op jit(solution)/shard_map/ppermute | solution.py:749
  29.5 12.4 %collective-permute-start = (bf16[512,256]{1,0:T(8,128)(2,1)S(1)}, bf16[512,256]{1,0:T(8,128)(2,1)S(1)}, u32[]{:S(2)}, u32[]{:S(2)}) collective-permute-start(bf16[512,256]{1,0:T(8,128)(2,1)S(1)} %copy-done.38), channel_id=1, source_target_pairs={{1,0},{0,1},{3,2},{2,3},{5,4},{4,5},{7,6},{6,7},{9,8},{8,9},{11,10... | collective-permute-start | bytes 786440 | tf_op jit(solution)/shard_map/ppermute | solution.py:744
  31.6 4.7 %collective-permute-start.4 = (bf16[2,3,32,256]{3,2,1,0:T(8,128)(2,1)S(1)}, bf16[2,3,32,256]{3,2,1,0:T(8,128)(2,1)S(1)}, u32[]{:S(2)}, u32[]{:S(2)}) collective-permute-start(bf16[2,3,32,256]{3,2,1,0:T(8,128)(2,1)S(1)} %pad_maximum_fusion.6), channel_id=1, source_target_pairs={{0,8},{2,10},{4,12},{6,14},{8,0},{10,2},{12,4},{14,6},{16,24},{18,... | collective-permute-start | bytes 294920 | tf_op jit(solution)/shard_map/ppermute | solution.py:749
  36.3 10.3 %collective-permute-start.5 = (bf16[4,3,32,256]{3,2,1,0:T(8,128)(2,1)S(1)}, bf16[4,3,32,256]{3,2,1,0:T(8,128)(2,1)S(1)}, u32[]{:S(2)}, u32[]{:S(2)}) collective-permute-start(bf16[4,3,32,256]{3,2,1,0:T(8,128)(2,1)S(1)} %pad_maximum_fusion.5), channel_id=1, source_target_pairs={{0,4},{2,6},{4,0},{6,2},{8,12},{10,14},{12,8},{14,10},{16,20},{18,... | collective-permute-start | bytes 589832 | tf_op jit(solution)/shard_map/ppermute | solution.py:749
  41.8 7.5 %copy-start.21 = (s32[1,33]{1,0:T(1,128)S(1)}, s32[1,33]{1,0:T(1,128)}, u32[]{:S(2)}) copy-start(s32[1,33]{1,0:T(1,128)} %lengths_ref.3) | copy-start | bytes 400
  41.8 37.9 %collective-permute-start.12 = (bf16[8,32,2560]{2,1,0:T(8,128)(2,1)S(1)}, bf16[8,32,2560]{2,1,0:T(8,128)(2,1)S(1)}, u32[]{:S(2)}, u32[]{:S(2)}) collective-permute-start(bf16[8,32,2560]{2,1,0:T(8,128)(2,1)S(1)} %pad_maximum_fusion.near_ref), channel_id=1, source_target_pairs={{0,2},{2,0},{4,6},{6,4},{8,10},{10,8},{12,14},{14,12},{16,18},{18,... | collective-permute-start | bytes 3932168 | tf_op jit(solution)/shard_map/ppermute | solution.py:749
  42.9 14.0 %collective-permute-start.1 = (bf16[384,512]{1,0:T(8,128)(2,1)}, bf16[384,512]{1,0:T(8,128)(2,1)S(1)}, u32[]{:S(2)}, u32[]{:S(2)}) collective-permute-start(bf16[384,512]{1,0:T(8,128)(2,1)} %get-tuple-element.96), channel_id=1, source_target_pairs={{0,2},{2,4},{4,6},{6,8},{8,10},{10,12},{12,14},{14,16},{16,18},{18... | collective-permute-start | bytes 1179656 | tf_op jit(solution)/shard_map/ppermute | solution.py:833
  45.3 11.6 %collective-permute-start.2 = (bf16[384,512]{1,0:T(8,128)(2,1)}, bf16[384,512]{1,0:T(8,128)(2,1)}, u32[]{:S(2)}, u32[]{:S(2)}) collective-permute-start(bf16[384,512]{1,0:T(8,128)(2,1)} %get-tuple-element.95), channel_id=1, source_target_pairs={{2,0},{4,2},{6,4},{8,6},{10,8},{12,10},{14,12},{16,14},{18,16},{20... | collective-permute-start | bytes 1179656 | tf_op jit(solution)/shard_map/ppermute | solution.py:834
  47.4 9.5 %collective-permute-start.6 = (bf16[8,3,32,256]{3,2,1,0:T(8,128)(2,1)}, bf16[8,3,32,256]{3,2,1,0:T(8,128)(2,1)}, u32[]{:S(2)}, u32[]{:S(2)}) collective-permute-start(bf16[8,3,32,256]{3,2,1,0:T(8,128)(2,1)} %pad_maximum_fusion.3.near_ref), channel_id=1, source_target_pairs={{0,2},{2,0},{4,6},{6,4},{8,10},{10,8},{12,14},{14,12},{16,18},{18,... | collective-permute-start | bytes 1179656 | tf_op jit(solution)/shard_map/ppermute | solution.py:749
  51.5 5.4 %copy-start.29 = (f32[2,256]{1,0:T(2,128)S(1)}, f32[2,256]{1,0:T(2,128)}, u32[]{:S(2)}) copy-start(f32[2,256]{1,0:T(2,128)} %bias_ref.1) | copy-start | bytes 6148
  56.8 16.0 %copy-start.40 = (f32[2,256]{1,0:T(2,128)S(1)}, f32[2,256]{1,0:T(2,128)}, u32[]{:S(2)}) copy-start(f32[2,256]{1,0:T(2,128)} %param.20) | copy-start | bytes 6148
  56.8 16.0 %copy-start.41 = (f32[2,256]{1,0:T(2,128)S(1)}, f32[2,256]{1,0:T(2,128)}, u32[]{:S(2)}) copy-start(f32[2,256]{1,0:T(2,128)} %param.25) | copy-start | bytes 6148
  56.8 16.0 %copy-start.42 = (f32[2,256]{1,0:T(2,128)S(1)}, f32[2,256]{1,0:T(2,128)}, u32[]{:S(2)}) copy-start(f32[2,256]{1,0:T(2,128)} %param.24) | copy-start | bytes 6148
  56.9 11.8 %copy-start.13 = (bf16[384,512]{1,0:T(8,128)(2,1)}, bf16[384,512]{1,0:T(8,128)(2,1)S(1)}, u32[]{:S(2)}) copy-start(bf16[384,512]{1,0:T(8,128)(2,1)S(1)} %collective-permute-done.1.low_ref) | copy-start | bytes 1179652
  71.3 9.5 %copy-start.17 = (bf16[512,256]{1,0:T(8,128)(2,1)}, bf16[512,256]{1,0:T(8,128)(2,1)S(1)}, u32[]{:S(2)}) copy-start(bf16[512,256]{1,0:T(8,128)(2,1)S(1)} %get-tuple-element.64.query_ref) | copy-start | bytes 786436
  71.3 11.0 %copy-start.15 = (bf16[512,256]{1,0:T(8,128)(2,1)}, bf16[512,256]{1,0:T(8,128)(2,1)S(1)}, u32[]{:S(2)}) copy-start(bf16[512,256]{1,0:T(8,128)(2,1)S(1)} %get-tuple-element.54.own_ref.attended_ref) | copy-start | bytes 786436
  71.3 11.0 %collective-permute-start.7 = (bf16[512,256]{1,0:T(8,128)(2,1)S(1)}, bf16[512,256]{1,0:T(8,128)(2,1)S(1)}, u32[]{:S(2)}, u32[]{:S(2)}) collective-permute-start(bf16[512,256]{1,0:T(8,128)(2,1)S(1)} %get-tuple-element.54.own_ref.attended_ref), channel_id=1, source_target_pairs={{1,0},{0,1},{3,2},{2,3},{5,4},{4,5},{7,6},{6,7},{9,8},{8,9},{11,10... | collective-permute-start | bytes 786440 | tf_op jit(solution)/shard_map/ppermute | solution.py:744
  72.9 6.9 %collective-permute-start.13 = (f32[6,256]{1,0:T(8,128)S(1)}, f32[6,256]{1,0:T(8,128)S(1)}, u32[]{:S(2)}, u32[]{:S(2)}) collective-permute-start(f32[6,256]{1,0:T(8,128)S(1)} %pad_maximum_fusion.8), channel_id=1, source_target_pairs={{1,0},{0,1},{3,2},{2,3},{5,4},{4,5},{7,6},{6,7},{9,8},{8,9},{11,10... | collective-permute-start | bytes 18440 | tf_op jit(solution)/shard_map/ppermute | solution.py:744
  82.4 8.4 %copy-start.39 = (bf16[512,256]{1,0:T(8,128)(2,1)S(1)}, bf16[512,256]{1,0:T(8,128)(2,1)}, u32[]{:S(2)}) copy-start(bf16[512,256]{1,0:T(8,128)(2,1)} %param.26) | copy-start | bytes 786436
  89.3 18.7 %copy-start.32 = (bf16[512,1024]{1,0:T(8,128)(2,1)}, bf16[512,1024]{1,0:T(8,128)(2,1)S(1)}, u32[]{:S(2)}) copy-start(bf16[512,1024]{1,0:T(8,128)(2,1)S(1)} %get-tuple-element.90.act_ref) | copy-start | bytes 3145732
  89.3 25.2 %copy-start.34 = (bf16[512,512]{1,0:T(8,128)(2,1)}, bf16[512,512]{1,0:T(8,128)(2,1)S(1)}, u32[]{:S(2)}) copy-start(bf16[512,512]{1,0:T(8,128)(2,1)S(1)} %get-tuple-element.91.upper_ref) | copy-start | bytes 1572868
  89.3 18.6 %collective-permute-start.14 = (bf16[512,512]{1,0:T(8,128)(2,1)S(1)}, bf16[512,512]{1,0:T(8,128)(2,1)S(1)}, u32[]{:S(2)}, u32[]{:S(2)}) collective-permute-start(bf16[512,512]{1,0:T(8,128)(2,1)S(1)} %get-tuple-element.55.part_ref), channel_id=1, source_target_pairs={{1,0},{0,1},{3,2},{2,3},{5,4},{4,5},{7,6},{6,7},{9,8},{8,9},{11,10... | collective-permute-start | bytes 1572872 | tf_op jit(solution)/shard_map/ppermute | solution.py:744
  90.8 17.1 %collective-permute-start.15 = (bf16[512,256]{1,0:T(8,128)(2,1)S(1)}, bf16[512,256]{1,0:T(8,128)(2,1)S(1)}, u32[]{:S(2)}, u32[]{:S(2)}) collective-permute-start(bf16[512,256]{1,0:T(8,128)(2,1)S(1)} %copy-done.39), channel_id=1, source_target_pairs={{1,0},{0,1},{3,2},{2,3},{5,4},{4,5},{7,6},{6,7},{9,8},{8,9},{11,10... | collective-permute-start | bytes 786440 | tf_op jit(solution)/shard_map/ppermute | solution.py:744
  107.9 8.1 %copy-start.3 = (bf16[4,512,1024]{2,1,0:T(8,128)(2,1)S(1)}, bf16[4,512,1024]{2,1,0:T(8,128)(2,1)}, u32[]{:S(2)}) copy-start(bf16[4,512,1024]{2,1,0:T(8,128)(2,1)} %band_ref.3) | copy-start | bytes 12582916
  114.5 6.8 %copy-start.11 = (bf16[512,512]{1,0:T(8,128)(2,1)}, bf16[512,512]{1,0:T(8,128)(2,1)S(1)}, u32[]{:S(2)}) copy-start(bf16[512,512]{1,0:T(8,128)(2,1)S(1)} %get-tuple-element.60.part_ref) | copy-start | bytes 1572868
  114.5 6.8 %copy-start.22 = (bf16[512,1024]{1,0:T(8,128)(2,1)}, bf16[512,1024]{1,0:T(8,128)(2,1)S(1)}, u32[]{:S(2)}) copy-start(bf16[512,1024]{1,0:T(8,128)(2,1)S(1)} %get-tuple-element.92.hidden_ref) | copy-start | bytes 3145732
  114.5 6.8 %copy-start.26 = (bf16[512,512]{1,0:T(8,128)(2,1)}, bf16[512,512]{1,0:T(8,128)(2,1)S(1)}, u32[]{:S(2)}) copy-start(bf16[512,512]{1,0:T(8,128)(2,1)S(1)} %get-tuple-element.89.low_ref) | copy-start | bytes 1572868
  114.5 12.2 %collective-permute-start.16 = (bf16[512,512]{1,0:T(8,128)(2,1)S(1)}, bf16[512,512]{1,0:T(8,128)(2,1)}, u32[]{:S(2)}, u32[]{:S(2)}) collective-permute-start(bf16[512,512]{1,0:T(8,128)(2,1)S(1)} %get-tuple-element.60.part_ref), channel_id=1, source_target_pairs={{1,0},{0,1},{3,2},{2,3},{5,4},{4,5},{7,6},{6,7},{9,8},{8,9},{11,10... | collective-permute-start | bytes 1572872 | tf_op jit(solution)/shard_map/ppermute | solution.py:744
  127.7 3.4 %copy-start.6 = (bf16[1536,256]{1,0:T(8,128)(2,1)S(1)}, bf16[1536,256]{1,0:T(8,128)(2,1)}, u32[]{:S(2)}) copy-start(bf16[1536,256]{1,0:T(8,128)(2,1)} %copy-done.5) | copy-start | bytes 2359300
  127.7 3.4 %copy-start.8 = (bf16[1536,256]{1,0:T(8,128)(2,1)S(1)}, bf16[1536,256]{1,0:T(8,128)(2,1)}, u32[]{:S(2)}) copy-start(bf16[1536,256]{1,0:T(8,128)(2,1)} %copy-done.7) | copy-start | bytes 2359300
  127.8 3.4 %copy-start.18 = (bf16[512,256]{1,0:T(8,128)(2,1)S(1)}, bf16[512,256]{1,0:T(8,128)(2,1)}, u32[]{:S(2)}) copy-start(bf16[512,256]{1,0:T(8,128)(2,1)} %copy-done.17) | copy-start | bytes 786436
  131.2 10.7 %copy-start.14 = (bf16[384,512]{1,0:T(8,128)(2,1)S(1)}, bf16[384,512]{1,0:T(8,128)(2,1)}, u32[]{:S(2)}) copy-start(bf16[384,512]{1,0:T(8,128)(2,1)} %copy-done.13) | copy-start | bytes 1179652
  131.2 10.7 %copy-start.16 = (bf16[512,256]{1,0:T(8,128)(2,1)S(1)}, bf16[512,256]{1,0:T(8,128)(2,1)}, u32[]{:S(2)}) copy-start(bf16[512,256]{1,0:T(8,128)(2,1)} %copy-done.15) | copy-start | bytes 786436
  141.9 3.7 %copy-start.19 = (bf16[512,256]{1,0:T(8,128)(2,1)}, bf16[512,256]{1,0:T(8,128)(2,1)S(1)}, u32[]{:S(2)}) copy-start(bf16[512,256]{1,0:T(8,128)(2,1)S(1)} %get-tuple-element.68.query_ref) | copy-start | bytes 786436
  141.9 33.2 %slice-start = ((s8[4718592]{0:T(1024)(128)(4,1)}), s8[524288]{0:T(1024)(128)(4,1)S(1)}, s32[]{:S(2)}) async-start(s8[4718592]{0:T(1024)(128)(4,1)} %bitcast.22), calls=%async_computation | async-start | bytes 1048576
  145.6 1.2 collective-permute-start.24
  146.8 10.2 %collective-permute-start.25 = (f32[12,256]{1,0:T(8,128)S(1)}, f32[12,256]{1,0:T(8,128)S(1)}, u32[]{:S(2)}, u32[]{:S(2)}) collective-permute-start(f32[12,256]{1,0:T(8,128)S(1)} %add.104), channel_id=1, source_target_pairs={{0,4},{2,6},{4,0},{6,2},{8,12},{10,14},{12,8},{14,10},{16,20},{18,... | collective-permute-start | bytes 36872 | tf_op jit(solution)/shard_map/ppermute | solution.py:749
  152.1 6.7 %copy-start.23 = (bf16[512,1024]{1,0:T(8,128)(2,1)S(1)}, bf16[512,1024]{1,0:T(8,128)(2,1)}, u32[]{:S(2)}) copy-start(bf16[512,1024]{1,0:T(8,128)(2,1)} %copy-done.22) | copy-start | bytes 3145732
  152.1 6.7 %copy-start.27 = (bf16[512,512]{1,0:T(8,128)(2,1)S(1)}, bf16[512,512]{1,0:T(8,128)(2,1)}, u32[]{:S(2)}) copy-start(bf16[512,512]{1,0:T(8,128)(2,1)} %copy-done.26) | copy-start | bytes 1572868
  152.1 23.0 %slice-start.1 = ((s8[4718592]{0:T(1024)(128)(4,1)}), s8[4194304]{0:T(1024)(128)(4,1)S(1)}, s32[]{:S(2)}) async-start(s8[4718592]{0:T(1024)(128)(4,1)} %bitcast.22), calls=%async_computation.1 | async-start | bytes 8388608
  157.0 8.2 %copy-start.25 = (bf16[8,4,32,256]{3,2,1,0:T(8,128)(2,1)S(1)}, bf16[8,4,32,256]{3,2,1,0:T(8,128)(2,1)}, u32[]{:S(2)}) copy-start(bf16[8,4,32,256]{3,2,1,0:T(8,128)(2,1)} %copy-done.24) | copy-start | bytes 1572868
  157.0 12.7 %copy-start.10 = (bf16[1536,256]{1,0:T(8,128)(2,1)S(1)}, bf16[1536,256]{1,0:T(8,128)(2,1)}, u32[]{:S(2)}) copy-start(bf16[1536,256]{1,0:T(8,128)(2,1)} %copy-done.9) | copy-start | bytes 2359300
  157.0 12.7 %copy-start.20 = (bf16[512,256]{1,0:T(8,128)(2,1)S(1)}, bf16[512,256]{1,0:T(8,128)(2,1)}, u32[]{:S(2)}) copy-start(bf16[512,256]{1,0:T(8,128)(2,1)} %copy-done.19) | copy-start | bytes 786436
  157.0 12.7 %copy-start.31 = (bf16[3,512,256]{2,1,0:T(8,128)(2,1)S(1)}, bf16[3,512,256]{2,1,0:T(8,128)(2,1)}, u32[]{:S(2)}) copy-start(bf16[3,512,256]{2,1,0:T(8,128)(2,1)} %copy-done.30) | copy-start | bytes 2359300
  157.1 8.6 %collective-permute-start.26 = (f32[12,256]{1,0:T(8,128)S(1)}, f32[12,256]{1,0:T(8,128)S(1)}, u32[]{:S(2)}, u32[]{:S(2)}) collective-permute-start(f32[12,256]{1,0:T(8,128)S(1)} %add.105), channel_id=1, source_target_pairs={{0,8},{2,10},{4,12},{6,14},{8,0},{10,2},{12,4},{14,6},{16,24},{18,... | collective-permute-start | bytes 36872 | tf_op jit(solution)/shard_map/ppermute | solution.py:749
  165.2 23.5 %collective-permute-start.28 = (bf16[8,2,32,1024]{3,2,1,0:T(8,128)(2,1)S(1)}, bf16[8,2,32,1024]{3,2,1,0:T(8,128)(2,1)S(1)}, u32[]{:S(2)}, u32[]{:S(2)}) collective-permute-start(bf16[8,2,32,1024]{3,2,1,0:T(8,128)(2,1)S(1)} %get-tuple-element.94), channel_id=1, source_target_pairs={{0,2},{2,0},{4,6},{6,4},{8,10},{10,8},{12,14},{14,12},{16,18},{18,... | collective-permute-start | bytes 3145736 | tf_op jit(solution)/shard_map/ppermute | solution.py:749
  165.2 17.9 %collective-permute-start.20 = (bf16[8,4,32,256]{3,2,1,0:T(8,128)(2,1)S(1)}, bf16[8,4,32,256]{3,2,1,0:T(8,128)(2,1)S(1)}, u32[]{:S(2)}, u32[]{:S(2)}) collective-permute-start(bf16[8,4,32,256]{3,2,1,0:T(8,128)(2,1)S(1)} %copy-done.25), channel_id=1, source_target_pairs={{0,2},{2,0},{4,6},{6,4},{8,10},{10,8},{12,14},{14,12},{16,18},{18,... | collective-permute-start | bytes 1572872 | tf_op jit(solution)/shard_map/ppermute | solution.py:749
  165.7 14.3 %collective-permute-start.27 = (f32[12,256]{1,0:T(8,128)S(1)}, f32[12,256]{1,0:T(8,128)S(1)}, u32[]{:S(2)}, u32[]{:S(2)}) collective-permute-start(f32[12,256]{1,0:T(8,128)S(1)} %add.106), channel_id=1, source_target_pairs={{0,16},{2,18},{4,20},{6,22},{8,24},{10,26},{12,28},{14,30},{16,0},... | collective-permute-start | bytes 36872 | tf_op jit(solution)/shard_map/ppermute | solution.py:749
  171.9 9.3 %collective-permute-start.17 = (bf16[384,512]{1,0:T(8,128)(2,1)S(1)}, bf16[384,512]{1,0:T(8,128)(2,1)S(1)}, u32[]{:S(2)}, u32[]{:S(2)}) collective-permute-start(bf16[384,512]{1,0:T(8,128)(2,1)S(1)} %get-tuple-element.73), channel_id=1, source_target_pairs={{0,2},{2,4},{4,6},{6,8},{8,10},{10,12},{12,14},{14,16},{16,18},{18... | collective-permute-start | bytes 1179656 | tf_op jit(solution)/shard_map/ppermute | solution.py:875
  173.6 7.7 %collective-permute-start.18 = (bf16[384,512]{1,0:T(8,128)(2,1)S(1)}, bf16[384,512]{1,0:T(8,128)(2,1)S(1)}, u32[]{:S(2)}, u32[]{:S(2)}) collective-permute-start(bf16[384,512]{1,0:T(8,128)(2,1)S(1)} %get-tuple-element.74), channel_id=1, source_target_pairs={{2,0},{4,2},{6,4},{8,6},{10,8},{12,10},{14,12},{16,14},{18,16},{20... | collective-permute-start | bytes 1179656 | tf_op jit(solution)/shard_map/ppermute | solution.py:876
  181.4 7.2 %copy-start.36 = (f32[8,2,32,1024]{3,2,1,0:T(8,128)S(1)}, f32[8,2,32,1024]{3,2,1,0:T(8,128)}, u32[]{:S(2)}) copy-start(f32[8,2,32,1024]{3,2,1,0:T(8,128)} %get-tuple-element.93) | copy-start | bytes 6291460
  181.5 15.3 %collective-permute-start.19 = (bf16[512,256]{1,0:T(8,128)(2,1)S(1)}, bf16[512,256]{1,0:T(8,128)(2,1)S(1)}, u32[]{:S(2)}, u32[]{:S(2)}) collective-permute-start(bf16[512,256]{1,0:T(8,128)(2,1)S(1)} %slice.165), channel_id=1, source_target_pairs={{1,0},{0,1},{3,2},{2,3},{5,4},{4,5},{7,6},{6,7},{9,8},{8,9},{11,10... | collective-permute-start | bytes 786440 | tf_op jit(solution)/shard_map/ppermute | solution.py:744
  183.2 12.6 %collective-permute-start.21 = (bf16[4,4,32,256]{3,2,1,0:T(8,128)(2,1)S(1)}, bf16[4,4,32,256]{3,2,1,0:T(8,128)(2,1)S(1)}, u32[]{:S(2)}, u32[]{:S(2)}) collective-permute-start(bf16[4,4,32,256]{3,2,1,0:T(8,128)(2,1)S(1)} %slice.164), channel_id=1, source_target_pairs={{0,4},{2,6},{4,0},{6,2},{8,12},{10,14},{12,8},{14,10},{16,20},{18,... | collective-permute-start | bytes 786440 | tf_op jit(solution)/shard_map/ppermute | solution.py:749
  189.1 16.6 %collective-permute-start.29 = (bf16[4,2,32,1024]{3,2,1,0:T(8,128)(2,1)S(1)}, bf16[4,2,32,1024]{3,2,1,0:T(8,128)(2,1)S(1)}, u32[]{:S(2)}, u32[]{:S(2)}) collective-permute-start(bf16[4,2,32,1024]{3,2,1,0:T(8,128)(2,1)S(1)} %slice.162), channel_id=1, source_target_pairs={{0,4},{2,6},{4,0},{6,2},{8,12},{10,14},{12,8},{14,10},{16,20},{18,... | collective-permute-start | bytes 1572872 | tf_op jit(solution)/shard_map/ppermute | solution.py:749
  196.0 5.0 %collective-permute-start.22 = (bf16[2,4,32,256]{3,2,1,0:T(8,128)(2,1)S(1)}, bf16[2,4,32,256]{3,2,1,0:T(8,128)(2,1)S(1)}, u32[]{:S(2)}, u32[]{:S(2)}) collective-permute-start(bf16[2,4,32,256]{3,2,1,0:T(8,128)(2,1)S(1)} %slice.167), channel_id=1, source_target_pairs={{0,8},{2,10},{4,12},{6,14},{8,0},{10,2},{12,4},{14,6},{16,24},{18,... | collective-permute-start | bytes 393224 | tf_op jit(solution)/shard_map/ppermute | solution.py:749
  201.1 7.0 %collective-permute-start.23 = (bf16[1,4,32,256]{3,2,1,0:T(8,128)(2,1)S(1)}, bf16[1,4,32,256]{3,2,1,0:T(8,128)(2,1)S(1)}, u32[]{:S(2)}, u32[]{:S(2)}) collective-permute-start(bf16[1,4,32,256]{3,2,1,0:T(8,128)(2,1)S(1)} %slice.168), channel_id=1, source_target_pairs={{0,16},{2,18},{4,20},{6,22},{8,24},{10,26},{12,28},{14,30},{16,0},... | collective-permute-start | bytes 196616 | tf_op jit(solution)/shard_map/ppermute | solution.py:749
  205.8 8.7 %collective-permute-start.30 = (bf16[2,2,32,1024]{3,2,1,0:T(8,128)(2,1)S(1)}, bf16[2,2,32,1024]{3,2,1,0:T(8,128)(2,1)S(1)}, u32[]{:S(2)}, u32[]{:S(2)}) collective-permute-start(bf16[2,2,32,1024]{3,2,1,0:T(8,128)(2,1)S(1)} %slice.163), channel_id=1, source_target_pairs={{0,8},{2,10},{4,12},{6,14},{8,0},{10,2},{12,4},{14,6},{16,24},{18,... | collective-permute-start | bytes 786440 | tf_op jit(solution)/shard_map/ppermute | solution.py:749
  214.6 8.7 %collective-permute-start.31 = (bf16[1,2,32,1024]{3,2,1,0:T(8,128)(2,1)S(1)}, bf16[1,2,32,1024]{3,2,1,0:T(8,128)(2,1)S(1)}, u32[]{:S(2)}, u32[]{:S(2)}) collective-permute-start(bf16[1,2,32,1024]{3,2,1,0:T(8,128)(2,1)S(1)} %slice.166), channel_id=1, source_target_pairs={{0,16},{2,18},{4,20},{6,22},{8,24},{10,26},{12,28},{14,30},{16,0},... | collective-permute-start | bytes 393224 | tf_op jit(solution)/shard_map/ppermute | solution.py:749
  (13 other events, 19.2 us)

commit v2 on v1

v2 whole, which is shorter than its diff:
```python
import functools

import jax
import jax.numpy as jnp
from jax import lax
from jax.experimental import pallas as pl
from jax.experimental.pallas import tpu as pltpu
from jax.sharding import PartitionSpec as P

D = 512
HEAD_DIM = 64
MAXDOC = 512
BAND = 2 * MAXDOC
BLOCK = 128
WINDOW = BAND + BLOCK
HALO = MAXDOC - 128
PAD = MAXDOC - HALO

EPSILON = 1e-05
MASKED_SCORE = -1e30
ERF_RATE = 0.7071067811865476
DENSITY_RATE = 0.3989422804014327

F32 = jnp.float32
BF16 = jnp.bfloat16
SMEM = pltpu.MemorySpace.SMEM
VMEM_LIMIT = 24 << 20
CHUNKS = 2
SUM_ROWS = 16
FLOPS_PER_MICROSECOND = 1.0e9


def dot_nn(a, b):
    return lax.dot_general(a, b, (((1,), (0,)), ((), ())), preferred_element_type=F32)


def dot_nt(a, b):
    return lax.dot_general(a, b, (((1,), (1,)), ((), ())), preferred_element_type=F32)


def dot_tn(a, b):
    return lax.dot_general(a, b, (((0,), (0,)), ((), ())), preferred_element_type=F32)


def params():
    return pltpu.CompilerParams(
        dimension_semantics=("arbitrary",), vmem_limit_bytes=VMEM_LIMIT
    )


def lasting(microseconds):
    return pl.CostEstimate(
        flops=int(microseconds * FLOPS_PER_MICROSECOND), bytes_accessed=0, transcendentals=0
    )


def whole(shape):
    return pl.BlockSpec(shape, lambda b: (0,) * len(shape))


def rows(width, first=0):
    return pl.BlockSpec((BLOCK, width), lambda b: (b + first, 0))


def heads_block(heads, width, first=0):
    return pl.BlockSpec((heads, BLOCK, width), lambda b: (0, b + first, 0))


def struct(shape, dtype):
    return jax.ShapeDtypeStruct(shape, dtype)


def segment_of(positions, lengths_ref, token_count):
    sequences, documents = lengths_ref.shape
    found = jnp.zeros(positions.shape, jnp.int32)
    end = jnp.int32(0)
    for sequence in range(sequences):
        for document in range(documents):
            end = end + lengths_ref[sequence, document]
            found = found + (positions >= end).astype(jnp.int32)
    return jnp.where((positions >= 0) & (positions < token_count), found, -1)


def dense_kernel(fill, token_count, offset, lengths_ref, base_ref, band_ref, dense_ref):
    first = base_ref[0] + (pl.program_id(0) + offset) * BLOCK
    query = first + lax.broadcasted_iota(jnp.int32, (BLOCK, 1), 0)
    key = first - MAXDOC + lax.broadcasted_iota(jnp.int32, (1, WINDOW), 1)
    same = segment_of(query, lengths_ref, token_count) == segment_of(
        key, lengths_ref, token_count
    )
    for head in range(band_ref.shape[0]):
        wide = jnp.concatenate(
            [band_ref[head].astype(F32), jnp.zeros((BLOCK, BLOCK), F32)], 1
        )
        turned = pltpu.roll(wide, 0, 1, stride=1, stride_axis=0)
        dense_ref[head] = jnp.where(same, turned, fill).astype(BF16)


def to_dense(banded, lengths, base, fill, token_count, chunk):
    heads, count, _ = banded.shape
    count //= CHUNKS
    offset = chunk * (count // BLOCK)
    return pl.pallas_call(
        functools.partial(dense_kernel, fill, token_count, offset),
        grid=(count // BLOCK,),
        in_specs=[
            pl.BlockSpec(memory_space=SMEM),
            pl.BlockSpec(memory_space=SMEM),
            heads_block(heads, BAND, offset),
        ],
        out_specs=heads_block(heads, WINDOW),
        out_shape=struct((heads, count, WINDOW), BF16),
        compiler_params=params(),
        cost_estimate=lasting(1.0),
        name="to_dense",
    )(lengths, base, banded)


def band_kernel(masked, *refs):
    dense_refs, band_ref = refs[:-1], refs[-1]
    lane = lax.broadcasted_iota(jnp.int32, (BLOCK, BLOCK), 1)
    row = lax.broadcasted_iota(jnp.int32, (BLOCK, BLOCK), 0)
    source = (lane + row) & (BLOCK - 1)
    near = lane + row < BLOCK
    steps = pl.num_programs(0) // CHUNKS

    def turn(dense_ref):
        for head in range(band_ref.shape[0]):
            pieces = []
            for place in range(WINDOW // BLOCK):
                piece = dense_ref[head, :, place * BLOCK : (place + 1) * BLOCK].astype(F32)
                if masked:
                    piece = jnp.where(piece < 0.5 * MASKED_SCORE, 0.0, piece)
                pieces.append(jnp.take_along_axis(piece, source, axis=1))
            for place in range(BAND // BLOCK):
                band_ref[head, :, place * BLOCK : (place + 1) * BLOCK] = jnp.where(
                    near, pieces[place], pieces[place + 1]
                ).astype(BF16)

    for chunk, dense_ref in enumerate(dense_refs):

        @pl.when(pl.program_id(0) // steps == chunk)
        def _():
            turn(dense_ref)


def to_band(chunks, masked):
    heads, count, _ = chunks[0].shape
    steps = count // BLOCK

    def block_of(chunk):
        return pl.BlockSpec(
            (heads, BLOCK, WINDOW), lambda b: (0, jnp.clip(b - chunk * steps, 0, steps - 1), 0)
        )

    return pl.pallas_call(
        functools.partial(band_kernel, masked),
        grid=(CHUNKS * steps,),
        in_specs=[block_of(chunk) for chunk in range(CHUNKS)],
        out_specs=heads_block(heads, BAND),
        out_shape=struct((heads, CHUNKS * count, BAND), BF16),
        compiler_params=params(),
        cost_estimate=lasting(5.0),
        name="to_band",
    )(*chunks)


def head_split(block, size):
    if size == 1:
        return block
    lane = lax.broadcasted_iota(jnp.int32, block.shape, 1)
    return jnp.concatenate(
        [
            jnp.where((lane >= h * HEAD_DIM) & (lane < (h + 1) * HEAD_DIM), block, 0)
            for h in range(size)
        ],
        0,
    )


def head_join(stacked, size):
    if size == 1:
        return stacked
    height = stacked.shape[0] // size
    joined = stacked[:height]
    lane = lax.broadcasted_iota(jnp.int32, joined.shape, 1)
    for h in range(1, size):
        joined = jnp.where(lane >= h * HEAD_DIM, stacked[h * height : (h + 1) * height], joined)
    return joined


def project_kernel(
    slot_ref, token_ref, low_ref, high_ref, near_ref, far_ref, bias_ref,
    query_ref, key_ref, value_ref, weight_ref,
):
    half, _, depth, width = near_ref.shape
    count = token_ref.shape[0]
    for place in range(2 * half):
        slot = slot_ref[place]

        @pl.when(slot < half)
        def _():
            weight_ref[:, place * depth : (place + 1) * depth, :] = near_ref[slot]

        @pl.when(slot >= half)
        def _():
            weight_ref[:, place * depth : (place + 1) * depth, :] = far_ref[slot - half]

    low_rows, high_rows = low_ref[...], high_ref[...]
    own = token_ref[...]
    empty = jnp.zeros((PAD, width), BF16)
    query = (dot_nn(own, weight_ref[0]) + bias_ref[0:1, :]).astype(BF16)
    query_ref[...] = query * jnp.asarray(HEAD_DIM ** (-0.5), BF16)
    for out_ref, which in ((key_ref, 1), (value_ref, 2)):
        shift = bias_ref[1:2, :] if which == 2 else 0.0
        weight = weight_ref[which]
        out_ref[0:PAD, :] = empty
        out_ref[PAD:MAXDOC, :] = (dot_nn(low_rows, weight) + shift).astype(BF16)
        out_ref[MAXDOC : MAXDOC + count, :] = (dot_nn(own, weight) + shift).astype(BF16)
        out_ref[MAXDOC + count : MAXDOC + count + HALO, :] = (
            dot_nn(high_rows, weight) + shift
        ).astype(BF16)
        out_ref[MAXDOC + count + HALO :, :] = empty


def project(slots, tokens, low, high, near, far, bias):
    count, features = tokens.shape
    width = near.shape[3]
    operands = (tokens, low, high, near, far, bias)
    shapes = ((count, width), (count + BAND, width), (count + BAND, width), (3, features, width))
    return pl.pallas_call(
        project_kernel,
        grid=(1,),
        in_specs=[pl.BlockSpec(memory_space=SMEM)] + [whole(x.shape) for x in operands],
        out_specs=[whole(shape) for shape in shapes],
        out_shape=[struct(shape, BF16) for shape in shapes],
        compiler_params=params(),
        cost_estimate=lasting(2.0),
        name="project",
    )(slots, *operands)


def forward_kernel(
    offset, query_ref, key_ref, value_ref, prev_ref, score_ref, prob_ref, attended_ref
):
    heads = prev_ref.shape[0]
    size = min(2, heads)
    span = size * HEAD_DIM
    window = pl.ds(pl.multiple_of((pl.program_id(0) + offset) * BLOCK, BLOCK), WINDOW)
    for group in range(heads // size):
        lanes = slice(group * span, (group + 1) * span)
        query = head_split(query_ref[:, lanes], size)
        dense = dot_nt(query, key_ref[window, lanes])
        weights = []
        for h in range(size):
            head = group * size + h
            score = dense[h * BLOCK : (h + 1) * BLOCK] + prev_ref[head].astype(F32)
            score_ref[head] = score.astype(BF16)
            peak = jnp.max(score, -1, keepdims=True)
            grown = jnp.exp(score - peak)
            total = jnp.sum(grown, -1, keepdims=True)
            prob = (grown * (1.0 / total)).astype(BF16)
            prob_ref[head] = prob
            weights.append(prob)
        mixed = dot_nn(jnp.concatenate(weights, 0), value_ref[window, lanes])
        attended_ref[:, lanes] = head_join(mixed, size).astype(BF16)


def attend_forward(query, key, value, prev, chunk):
    heads, count, _ = prev.shape
    width = query.shape[1]
    offset = chunk * (count // BLOCK)
    return pl.pallas_call(
        functools.partial(forward_kernel, offset),
        grid=(count // BLOCK,),
        in_specs=[
            rows(width, offset),
            whole(key.shape),
            whole(value.shape),
            heads_block(heads, WINDOW),
        ],
        out_specs=[heads_block(heads, WINDOW), heads_block(heads, WINDOW), rows(width)],
        out_shape=[
            struct((heads, count, WINDOW), BF16),
            struct((heads, count, WINDOW), BF16),
            struct((count, width), BF16),
        ],
        compiler_params=params(),
        cost_estimate=lasting(3.8),
        name="attend_forward",
    )(query, key, value, prev)


def backward_kernel(
    offset, last, grad_ref, query_ref, key_ref, value_ref, prob_ref, logit_ref, *refs
):
    if last:
        key_start, value_start = refs[:2]
        prev_ref, query_grad_ref, key_grad_ref, value_grad_ref, key_sum, value_sum = refs[2:]
    else:
        prev_ref, query_grad_ref, key_sum, value_sum = refs
    step = pl.program_id(0)
    heads = prob_ref.shape[0]
    size = min(2, heads)
    span = size * HEAD_DIM

    @pl.when(step == 0)
    def _():
        if last:
            key_sum[...] = key_start[...]
            value_sum[...] = value_start[...]
        else:
            key_sum[...] = jnp.zeros_like(key_sum)
            value_sum[...] = jnp.zeros_like(value_sum)

    window = pl.ds(pl.multiple_of((step + offset) * BLOCK, BLOCK), WINDOW)
    for group in range(heads // size):
        lanes = slice(group * span, (group + 1) * span)
        query = head_split(query_ref[:, lanes], size)
        grad = head_split(grad_ref[:, lanes], size)
        key = key_ref[window, lanes]
        prob_grad = dot_nt(grad, value_ref[window, lanes])
        probs, scores = [], []
        for h in range(size):
            head = group * size + h
            low = prob_ref[head]
            prob = low.astype(F32)
            slope = prob_grad[h * BLOCK : (h + 1) * BLOCK]
            inner = jnp.sum(prob * slope, -1, keepdims=True)
            score = (prob * (slope - inner) + logit_ref[head].astype(F32)).astype(BF16)
            prev_ref[head] = score
            probs.append(low)
            scores.append(score)
        stacked = jnp.concatenate(scores, 0)
        mixed = head_join(dot_nn(stacked, key), size) * HEAD_DIM ** (-0.5)
        query_grad_ref[:, lanes] = mixed.astype(BF16)
        key_sum[lanes, window] += dot_tn(query, stacked)
        value_sum[lanes, window] += dot_tn(grad, jnp.concatenate(probs, 0))

    if last:

        @pl.when(step == pl.num_programs(0) - 1)
        def _():
            key_grad_ref[...] = key_sum[...].astype(BF16).T
            value_grad_ref[...] = value_sum[...].astype(BF16).T


def attend_backward(grad, query, key, value, prob, logit, chunk, sums):
    heads, count, _ = prob.shape
    extended, width = key.shape
    offset = chunk * (count // BLOCK)
    last = sums is not None
    turned = (width, extended)
    scratch = [pltpu.VMEM(turned, F32), pltpu.VMEM(turned, F32)] if last else []
    ends = [whole((extended, width))] * 2 if last else [whole(turned)] * 2
    end_shapes = [struct((extended, width), BF16)] * 2 if last else [struct(turned, F32)] * 2
    return pl.pallas_call(
        functools.partial(backward_kernel, offset, last),
        grid=(count // BLOCK,),
        in_specs=[
            rows(width),
            rows(width, offset),
            whole((extended, width)),
            whole((extended, width)),
            heads_block(heads, WINDOW),
            heads_block(heads, WINDOW),
        ]
        + ([whole(turned)] * 2 if last else []),
        out_specs=[heads_block(heads, WINDOW), rows(width)] + ends,
        out_shape=[struct((heads, count, WINDOW), BF16), struct((count, width), BF16)]
        + end_shapes,
        scratch_shapes=scratch,
        compiler_params=params(),
        cost_estimate=lasting(1.4),
        name="attend_backward",
    )(grad, query, key, value, prob, logit, *(sums or ()))


def order_kernel(slot_ref, near_ref, far_ref, *out_refs):
    half, depth, _ = near_ref.shape

    def put(place, source_ref, slot):
        first = 0
        for out_ref in out_refs:
            last = first + out_ref.shape[1]
            out_ref[place * depth : (place + 1) * depth, :] = source_ref[slot, :, first:last]
            first = last

    for place in range(2 * half):
        slot = slot_ref[place]

        @pl.when(slot < half)
        def _():
            put(place, near_ref, slot)

        @pl.when(slot >= half)
        def _():
            put(place, far_ref, slot - half)


def in_order(slots, near, far, widths):
    half, depth, _ = near.shape
    shapes = [(2 * half * depth, width) for width in widths]
    return pl.pallas_call(
        order_kernel,
        grid=(1,),
        in_specs=[pl.BlockSpec(memory_space=SMEM), whole(near.shape), whole(far.shape)],
        out_specs=[whole(shape) for shape in shapes],
        out_shape=[struct(shape, BF16) for shape in shapes],
        compiler_params=params(),
        cost_estimate=lasting(0.9),
        name="in_order",
    )(slots, near, far)


def mean_of(x):
    return jnp.sum(x, -1, keepdims=True) * (1.0 / D)


def normalized(hidden):
    mean = mean_of(hidden)
    inverse = lax.rsqrt(mean_of(hidden * hidden) - mean * mean + EPSILON)
    return (hidden - mean) * inverse, inverse


def norm_back(upstream, normed, inverse):
    return inverse * (upstream - mean_of(upstream) - normed * mean_of(upstream * normed))


def added(own_ref, other_ref, swap):
    other = other_ref[...]
    if swap:
        middle = other.shape[1] // 2
        other = jnp.concatenate([other[:, middle:], other[:, :middle]], 1)
    return own_ref[...].astype(F32) + other.astype(F32)


def first_kernel(
    own_ref, other_ref, token_ref, out_ref, up_ref, down_ref, norm_ref, up_bias_ref,
    normed_ref, inverse_ref, upper_ref, act_ref, slope_ref, part_ref,
):
    width = own_ref.shape[1]
    branch = dot_nt(own_ref[...], out_ref[:, :width]) + dot_nt(other_ref[...], out_ref[:, width:])
    hidden = token_ref[...].astype(F32) + branch + norm_ref[4:5, :]
    normed, inverse = normalized(hidden)
    normed_ref[...] = normed
    inverse_ref[...] = inverse
    upper = (normed * norm_ref[0:1, :] + norm_ref[2:3, :]).astype(BF16)
    upper_ref[...] = upper
    pre = dot_nn(upper, up_ref[...]) + up_bias_ref[...]
    share = 0.5 * (1.0 + lax.erf(pre * ERF_RATE))
    act = (pre * share).astype(BF16)
    act_ref[...] = act
    slope_ref[...] = (share + pre * jnp.exp(-0.5 * pre * pre) * DENSITY_RATE).astype(BF16)
    part_ref[...] = dot_nt(act, down_ref[...]).astype(BF16)


def feed_first(own, other, tokens, weights, norms, up_bias, chunk):
    count, width = own.shape
    features = tokens.shape[1]
    units = up_bias.shape[1]
    return pl.pallas_call(
        first_kernel,
        grid=(count // BLOCK,),
        in_specs=[
            rows(width),
            rows(other.shape[1]),
            rows(features, chunk * (count // BLOCK)),
            *weight_blocks(features, units),
            whole(norms.shape),
            whole(up_bias.shape),
        ],
        out_specs=[
            rows(features),
            rows(1),
            rows(features),
            rows(units),
            rows(units),
            rows(features),
        ],
        out_shape=[
            struct((count, features), F32),
            struct((count, 1), F32),
            struct((count, features), BF16),
            struct((count, units), BF16),
            struct((count, units), BF16),
            struct((count, features), BF16),
        ],
        compiler_params=params(),
        cost_estimate=lasting(1.0),
        name="feed_first",
    )(own, other, tokens, *weights, norms, up_bias)


def weight_blocks(features, units):
    return [
        pl.BlockSpec((features, features), lambda b: (0, 0)),
        pl.BlockSpec((features, units), lambda b: (0, 0)),
        pl.BlockSpec((features, units), lambda b: (0, 0)),
    ]


def add_sums(start_ref, sum_ref, first, values):
    @pl.when(pl.program_id(0) == 0)
    def _():
        sum_ref[...] = start_ref[...]

    for place, value in enumerate(values):
        sum_ref[first + place : first + place + 1, :] += jnp.sum(value, 0, keepdims=True)


def second_kernel(
    swap, start_ref, part_ref, recv_ref, normed_ref, grad_ref, slope_ref, up_ref, down_ref,
    norm_ref, *refs,
):
    sum_ref, output_ref, res_ref, low_ref, hidden_ref, lower_ref = refs[-6:]
    own = output_ref.shape[1]
    upper = normed_ref[...] * norm_ref[0:1, :] + norm_ref[2:3, :]
    hidden = upper + added(part_ref, recv_ref, swap) + norm_ref[5:6, :]
    normed, inverse = normalized(hidden)
    output_ref[...] = (
        normed[:, :own] * norm_ref[1:2, :own] + norm_ref[3:4, :own]
    ).astype(BF16)
    grad = grad_ref[...].astype(F32)
    res = norm_back(grad * norm_ref[1:2, :], normed, inverse)
    res_ref[...] = res
    low = res.astype(BF16)
    low_ref[...] = low
    act_grad = dot_nn(low, down_ref[...])
    hidden_grad = (act_grad * slope_ref[...].astype(F32)).astype(BF16)
    hidden_ref[...] = hidden_grad
    lower_ref[...] = dot_nt(hidden_grad, up_ref[...]).astype(BF16)
    wide = hidden_grad.astype(F32)
    add_sums(start_ref, sum_ref, 3, [low[:, :own].astype(F32)])
    for place, value in (
        (5, grad[:, :own] * normed[:, :own]),
        (7, grad[:, :own]),
        *((8 + k, wide[:, k * own : (k + 1) * own]) for k in range(wide.shape[1] // own)),
    ):
        sum_ref[place : place + 1, :] += jnp.sum(value, 0, keepdims=True)


def feed_second(swap, sums, held, part, recv, normed, grad, slope, weights, norms, chunk):
    count, features = part.shape
    own = sums.shape[1]
    units = slope.shape[1]
    offset = chunk * (count // BLOCK)
    return pl.pallas_call(
        functools.partial(second_kernel, swap),
        grid=(count // BLOCK,),
        in_specs=[
            whole(sums.shape),
            rows(features),
            rows(features),
            rows(features),
            rows(features, offset),
            rows(units),
            *weight_blocks(features, units)[1:],
            whole(norms.shape),
            *([] if held is None else [pl.BlockSpec(memory_space=pl.ANY)]),
        ],
        out_specs=[
            whole(sums.shape),
            rows(own, offset),
            rows(features),
            rows(features),
            rows(units),
            rows(features),
        ],
        out_shape=[
            struct(sums.shape, F32),
            struct((CHUNKS * count, own), BF16),
            struct((count, features), F32),
            struct((count, features), BF16),
            struct((count, units), BF16),
            struct((count, features), BF16),
        ],
        input_output_aliases={} if held is None else {9: 1},
        compiler_params=params(),
        cost_estimate=lasting(0.7),
        name="feed_second",
    )(sums, part, recv, normed, grad, slope, *weights[1:], norms, *(() if held is None else (held,)))


def third_kernel(
    swap, start_ref, part_ref, recv_ref, res_ref, normed_ref, inverse_ref, out_ref, norm_ref,
    sum_ref, low_ref, attended_ref, own_ref,
):
    own = own_ref.shape[1]
    grad = added(part_ref, recv_ref, swap) + res_ref[...]
    normed = normed_ref[...]
    res = norm_back(grad * norm_ref[0:1, :], normed, inverse_ref[...])
    own_ref[...] = res[:, :own]
    low = res.astype(BF16)
    low_ref[...] = low
    attended_ref[...] = dot_nn(low, out_ref[:, : attended_ref.shape[1]]).astype(BF16)
    add_sums(start_ref, sum_ref, 2, [low[:, :own].astype(F32)])
    for place, value in ((4, grad[:, :own] * normed[:, :own]), (6, grad[:, :own])):
        sum_ref[place : place + 1, :] += jnp.sum(value, 0, keepdims=True)


def feed_third(swap, sums, width, part, recv, res, normed, inverse, weights, norms):
    count, features = part.shape
    own = sums.shape[1]
    return pl.pallas_call(
        functools.partial(third_kernel, swap),
        grid=(count // BLOCK,),
        in_specs=[
            whole(sums.shape),
            rows(features),
            rows(features),
            rows(features),
            rows(features),
            rows(1),
            whole((features, features)),
            whole(norms.shape),
        ],
        out_specs=[whole(sums.shape), rows(features), rows(width), rows(own)],
        out_shape=[
            struct(sums.shape, F32),
            struct((count, features), BF16),
            struct((count, width), BF16),
            struct((count, own), F32),
        ],
        compiler_params=params(),
        cost_estimate=lasting(0.2),
        name="feed_third",
    )(sums, part, recv, res, normed, inverse, weights[0], norms)


def spread_rows(block_ref, scratch, keep_ref, send_ref, which, kinds):
    features = scratch.shape[0]
    count = block_ref.shape[0]
    depth = features // count
    half = count // 2
    for slot in range(count):
        start = pl.multiple_of(block_ref[slot] * depth, depth)
        piece = scratch[pl.ds(start, depth), :]
        first = ((slot % half) * kinds + which) * depth
        if slot < half:
            keep_ref[first : first + depth, :] = piece
        else:
            send_ref[first : first + depth, :] = piece.astype(BF16)


def split_sums(total):
    high = total.astype(BF16)
    low = (total - high.astype(F32)).astype(BF16)
    return high, low, high.astype(F32) + low.astype(F32)


def feed_grad_kernel(up_block_ref, down_block_ref, *refs):
    low_refs, upper_refs, act_refs, hidden_refs = (
        refs[k * CHUNKS : (k + 1) * CHUNKS] for k in range(4)
    )
    up_keep, up_send, down_keep, down_send, scratch = refs[4 * CHUNKS :]
    scratch[...] = sum(dot_tn(a[...], b[...]) for a, b in zip(upper_refs, hidden_refs))
    spread_rows(up_block_ref, scratch, up_keep, up_send, 0, 1)
    scratch[...] = sum(dot_tn(a[...], b[...]) for a, b in zip(low_refs, act_refs))
    spread_rows(down_block_ref, scratch, down_keep, down_send, 0, 1)


def feed_grads(up_blocks, down_blocks, low, act, upper, hidden):
    count, features = low[0].shape
    units = act[0].shape[1]
    chunk = min(256, units)
    column = pl.BlockSpec((count, chunk), lambda b: (0, b))
    height = features // 2
    result = pl.BlockSpec((height, chunk), lambda b: (0, b))
    return pl.pallas_call(
        feed_grad_kernel,
        grid=(units // chunk,),
        in_specs=[pl.BlockSpec(memory_space=SMEM)] * 2
        + [whole((count, features))] * (2 * CHUNKS)
        + [column] * (2 * CHUNKS),
        out_specs=[result] * 4,
        out_shape=[struct((height, units), F32), struct((height, units), BF16)] * 2,
        scratch_shapes=[pltpu.VMEM((features, chunk), F32)],
        compiler_params=params(),
        cost_estimate=lasting(1.0),
        name="feed_grads",
    )(up_blocks, down_blocks, *low, *upper, *act, *hidden)


def project_grad_kernel(block_ref, start_ref, *refs):
    query_refs, branch_refs, attended_refs = (
        refs[k * CHUNKS : (k + 1) * CHUNKS] for k in range(3)
    )
    token_ref, low_ref, high_ref, key_ref, value_ref = refs[3 * CHUNKS : 3 * CHUNKS + 5]
    keep_ref, send_ref, sum_ref, scratch = refs[3 * CHUNKS + 5 :]
    count = token_ref.shape[0]
    part = count // CHUNKS
    scratch[...] = sum(
        dot_tn(token_ref[k * part : (k + 1) * part, :], ref[...])
        for k, ref in enumerate(query_refs)
    )
    spread_rows(block_ref, scratch, keep_ref, send_ref, 0, 4)
    for which, ref in ((1, key_ref), (2, value_ref)):
        scratch[...] = (
            dot_tn(token_ref[...], ref[MAXDOC : MAXDOC + count, :])
            + dot_tn(low_ref[...], ref[PAD:MAXDOC, :])
            + dot_tn(high_ref[...], ref[MAXDOC + count : MAXDOC + count + HALO, :])
        )
        spread_rows(block_ref, scratch, keep_ref, send_ref, which, 4)
    scratch[...] = sum(dot_tn(a[...], b[...]) for a, b in zip(branch_refs, attended_refs))
    spread_rows(block_ref, scratch, keep_ref, send_ref, 3, 4)
    total = start_ref[...]
    place = lax.broadcasted_iota(jnp.int32, total.shape, 0)
    query_sum = sum(
        jnp.sum(ref[...].astype(F32), 0, keepdims=True) for ref in query_refs
    )
    value_sum = jnp.sum(value_ref[...].astype(F32), 0, keepdims=True)
    total = total + jnp.where(place == 0, query_sum, 0.0) + jnp.where(place == 1, value_sum, 0.0)
    height = keep_ref.shape[0]
    high, low, sum_ref[...] = split_sums(total)
    send_ref[height : height + SUM_ROWS, :] = high
    send_ref[height + SUM_ROWS :, :] = low


def project_grads(blocks, sums, tokens, low, high, query, key, value, branch, attended):
    features = tokens.shape[1]
    width = key.shape[1]
    half = blocks.shape[0] // 2
    depth = features // (2 * half)
    height = half * 4 * depth
    operands = (sums, *query, *branch, *attended, tokens, low, high, key, value)
    return pl.pallas_call(
        project_grad_kernel,
        grid=(1,),
        in_specs=[pl.BlockSpec(memory_space=SMEM)] + [whole(x.shape) for x in operands],
        out_specs=[
            whole((height, width)),
            whole((height + 2 * SUM_ROWS, width)),
            whole(sums.shape),
        ],
        out_shape=[
            struct((height, width), F32),
            struct((height + 2 * SUM_ROWS, width), BF16),
            struct(sums.shape, F32),
        ],
        scratch_shapes=[pltpu.VMEM((features, width), F32)],
        compiler_params=params(),
        cost_estimate=lasting(0.6),
        name="project_grads",
    )(blocks, *operands)


def fold_kernel(arrivals, sends, kinds, *refs):
    keep_ref, *refs = refs
    arrived_refs, refs = refs[:arrivals], refs[arrivals:]
    height = keep_ref.shape[0]
    with_sums = arrived_refs[0].shape[0] > height
    if with_sums:
        start_ref, *refs = refs
    size = height // (sends + 1)

    def total(first):
        parts = [ref[first : first + size, :].astype(F32) for ref in arrived_refs]
        if arrivals == 1:
            return keep_ref[first : first + size, :] + parts[0]
        return (keep_ref[first : first + size, :] + parts[0]) + (parts[1] + parts[2])

    stays = total(0)
    depth = size // kinds
    for kind in range(kinds):
        refs[kind][...] = stays[kind * depth : (kind + 1) * depth, :]
    send_outs = refs[kinds : kinds + sends]
    for place, send_out in enumerate(send_outs):
        send_out[:size, :] = total((place + 1) * size).astype(BF16)
    if with_sums:
        parts = [
            ref[height : height + SUM_ROWS, :].astype(F32)
            + ref[height + SUM_ROWS :, :].astype(F32)
            for ref in arrived_refs
        ]
        summed = start_ref[...] + parts[0]
        if arrivals > 1:
            summed = summed + (parts[1] + parts[2])
        sum_out = refs[kinds + sends]
        if sends:
            high, low, sum_out[...] = split_sums(summed)
            for send_out in send_outs:
                send_out[size : size + SUM_ROWS, :] = high
                send_out[size + SUM_ROWS :, :] = low
        else:
            sum_out[...] = summed


def fold(keep, arrived, sums, sends, kinds):
    height, width = keep.shape
    extra = arrived[0].shape[0] - height
    size = height // (sends + 1)
    operands = (keep, *arrived) + (() if sums is None else (sums,))
    shapes = [struct((size // kinds, width), F32)] * kinds
    shapes += [struct((size + extra, width), BF16)] * sends
    shapes += [] if sums is None else [struct(sums.shape, F32)]
    result = pl.pallas_call(
        functools.partial(fold_kernel, len(arrived), sends, kinds),
        grid=(1,),
        in_specs=[whole(x.shape) for x in operands],
        out_specs=[whole(x.shape) for x in shapes],
        out_shape=shapes,
        compiler_params=params(),
        cost_estimate=lasting(0.2),
        name="fold",
    )(*operands)
    if not sends:
        return result
    return result[0], result[1 : 1 + sends], (None if sums is None else result[-1])


def token_grad_kernel(*refs):
    query_refs, res_refs = refs[:CHUNKS], refs[CHUNKS : 2 * CHUNKS]
    key_ref, value_ref, weight_ref, low_ref, own_ref, high_ref = refs[2 * CHUNKS :]
    count = own_ref.shape[0]
    own = res_refs[0].shape[1]

    def piece(start):
        return dot_nt(key_ref[start : start + BLOCK, :], weight_ref[1]) + dot_nt(
            value_ref[start : start + BLOCK, :], weight_ref[2]
        )

    for start in range(0, HALO, BLOCK):
        low_ref[start : start + BLOCK, :] = piece(PAD + start).astype(BF16)
        high_ref[start : start + BLOCK, :] = piece(MAXDOC + count + start).astype(BF16)
    for start in range(0, count, BLOCK):
        chunk, inside = divmod(start, count // CHUNKS)
        total = piece(MAXDOC + start) + dot_nt(
            query_refs[chunk][inside : inside + BLOCK, :], weight_ref[0]
        )
        own_ref[start : start + BLOCK, :] = total
        own_ref[start : start + BLOCK, :own] += res_refs[chunk][inside : inside + BLOCK, :]


def token_grads(query, res, key, value, weight):
    count = CHUNKS * query[0].shape[0]
    features = weight.shape[1]
    operands = (*query, *res, key, value, weight)
    return pl.pallas_call(
        token_grad_kernel,
        grid=(1,),
        in_specs=[whole(x.shape) for x in operands],
        out_specs=[
            whole((HALO, features)),
            whole((count, features)),
            whole((HALO, features)),
        ],
        out_shape=[
            struct((HALO, features), BF16),
            struct((count, features), F32),
            struct((HALO, features), BF16),
        ],
        compiler_params=params(),
        cost_estimate=lasting(0.6),
        name="token_grads",
    )(*operands)


def from_next(x, axis, step):
    count = lax.axis_size(axis)
    return lax.ppermute(x, axis, [((i + step) % count, i) for i in range(count)])


def with_partner(x, bit):
    count = lax.axis_size("row")
    return lax.ppermute(x, "row", [(i, i ^ bit) for i in range(count)])


def others(x):
    return [from_next(x, "col", step) for step in range(1, lax.axis_size("col"))]


def bits_of(count):
    return [1 << place for place in range(count.bit_length() - 1)]


def after(value, *needed):
    return lax.optimization_barrier((value, *needed))[0]


def high_first(count):
    bits = bits_of(count)[::-1]
    return [bits[:2], *([bit] for bit in bits[2:])]


def high_late(count):
    bits = bits_of(count)[::-1]
    return [*([bit] for bit in bits[2:-1]), bits[:2], bits[-1:]]


def slots_of(steps, distance):
    bits = [bit for step in steps for bit in step]
    return sum(((distance & bit) // bit) << place for place, bit in enumerate(bits))


def distances_of(steps, slots):
    bits = [bit for step in steps for bit in step]
    return sum(((slots >> place) & 1) * bit for place, bit in enumerate(bits))


def partners_of(step):
    return step if len(step) == 1 else (step[0], step[1], step[0] + step[1])


def gather_rows(shard, steps, waits=(), fillers=()):
    waits, fillers, done = list(waits), list(fillers), []
    held = shard[None]
    stages = [held]
    for place, step in enumerate(steps):
        arrived = [with_partner(held, bit) for bit in partners_of(step)]
        if fillers:
            done.append(fillers.pop(0)(held))
            *arrived, done[-1] = lax.optimization_barrier((*arrived, done[-1]))
        if waits:
            needed = waits.pop(0)
            if needed is not None:
                arrived[0] = after(arrived[0], needed)
        if place < len(steps) - 1:
            held = jnp.concatenate([held, *arrived], 0)
            stages.append(held)
    return stages, arrived[0], done


class Gather:
    def __init__(self, shard, steps):
        self.held, self.steps = shard[None], list(steps)
        self.move()

    def move(self):
        self.arrived = [with_partner(self.held, bit) for bit in partners_of(self.steps.pop(0))]

    def put(self, *needed):
        while True:
            arrived = self.arrived
            self.held = jnp.concatenate([after(self.held, *needed), *arrived], 0)
            self.move()
            if len(self.steps) < 2:
                return

    def last(self):
        return self.arrived[0]


class Reduction:
    def __init__(self, steps, keep, send, sums, kinds):
        self.steps = steps[::-1]
        self.keep, self.send, self.sums, self.kinds = keep, send, sums, kinds
        self.arrived = None

    def move(self):
        self.step = self.steps.pop(0)
        self.arrived = [
            with_partner(x, bit) for x, bit in zip(self.send, partners_of(self.step))
        ]

    def add(self, *needed):
        keep = after(self.keep, *needed)
        if not self.steps:
            self.result = fold(keep, self.arrived, self.sums, 0, self.kinds)
            return
        sends = len(partners_of(self.steps[0]))
        self.keep, self.send, self.sums = fold(keep, self.arrived, self.sums, sends, 1)
        self.move()


def exchanged(part):
    arrived = others(part)
    if len(arrived) == 1:
        return arrived[0]
    shift = part.shape[1] // (len(arrived) + 1)
    total = sum(
        jnp.roll(x.astype(F32), step * shift, 1) for step, x in enumerate(arrived, 1)
    )
    return total.astype(BF16)


def on_device(
    tokens,
    prev_logits,
    doc_lengths,
    qkv_weight,
    qv_bias,
    out_weight,
    out_bias,
    up_weight,
    up_bias,
    down_weight,
    norm_gain,
    norm_shift,
    out_grad,
    logit_grad,
):
    count, own = tokens.shape
    width = qkv_weight.shape[2]
    row_count, col_count = lax.axis_size("row"), lax.axis_size("col")
    row_index, col_index = lax.axis_index("row"), lax.axis_index("col")
    token_count = count * row_count
    swap = col_count == 2
    hidden_rows = up_bias.shape[0] // own

    early, late = high_first(row_count), high_late(row_count)
    places = jnp.arange(row_count, dtype=jnp.int32)
    offset = col_index * (row_count // col_count)
    distance = ((places + offset) % row_count) ^ row_index
    slots, late_slots = slots_of(early, distance), slots_of(late, distance)
    blocks = ((distances_of(early, places) ^ row_index) - offset) % row_count
    late_blocks = ((distances_of(late, places) ^ row_index) - offset) % row_count
    base = (row_index * count)[None]

    out_turned = out_weight.T
    norms = jnp.concatenate([norm_gain, norm_shift, out_bias], 0)
    first = norms.astype(BF16)
    rest = norms - first.astype(F32)
    second = rest.astype(BF16)
    third = (rest - second.astype(F32)).astype(BF16)
    mixed = jnp.concatenate([tokens, out_turned, first, second, third], 0)
    arrived = others(mixed)
    depth = out_turned.shape[0]
    tokens_full = jnp.concatenate([tokens] + [x[:count] for x in arrived], 1)
    out_rows = jnp.concatenate([out_turned] + [x[count : count + depth] for x in arrived], 1)
    pieces = [x[count + depth :].astype(F32).reshape(3, -1, own) for x in arrived]
    norms = jnp.concatenate([norms] + [(x[0] + x[1]) + x[2] for x in pieces], 1)

    def dense_of(banded, fill, chunk):
        return lambda held: to_dense(
            after(banded, held), doc_lengths, base, fill, token_count, chunk
        )

    prev_logits = pltpu.with_memory_space_constraint(prev_logits, pltpu.HBM)
    logit_grad = pltpu.with_memory_space_constraint(logit_grad, pltpu.HBM)
    stages, far, prev_dense = gather_rows(
        qkv_weight,
        early,
        (),
        [dense_of(prev_logits, MASKED_SCORE, 0), dense_of(prev_logits, MASKED_SCORE, 1)],
    )
    near = stages[-1]
    forward = [(i, i + 1) for i in range(row_count - 1)]
    backward = [(b, a) for a, b in forward]
    low_tokens = lax.ppermute(tokens_full[count - HALO :], "row", forward)
    high_tokens = lax.ppermute(tokens_full[:HALO], "row", backward)
    grad_full = jnp.concatenate([out_grad] + others(after(out_grad, tokens_full)), 1)

    scores, probs, attended, attended_other, logit_dense = [], [], [], [], []
    up_shard = after(jnp.concatenate([out_rows, up_weight], 1), stages[1])
    down_shard = after(down_weight.T, stages[0])

    up_gather = Gather(up_shard, early)
    down_gather = Gather(down_shard, late)
    up_gather.put()
    down_gather.put()
    query, key, value, weight = project(
        slots, after(tokens_full, up_gather.held, down_gather.held, grad_full), low_tokens,
        high_tokens, near, far, qv_bias,
    )
    for chunk in range(CHUNKS):
        score, prob, mix = attend_forward(query, key, value, prev_dense[chunk], chunk)
        query = after(query, mix)
        scores.append(score)
        probs.append(prob)
        attended.append(mix)
        attended_other.append(jnp.concatenate(others(mix), 1))
    up_gather.put(mix)
    down_gather.put(mix)
    scores_low = after(scores[0], attended_other[0], up_gather.held)
    new_logits = to_band([scores_low, *scores[1:]], True)

    up_near = after(up_gather.held, new_logits)
    weights = in_order(
        slots, up_near, up_gather.last(), (tokens_full.shape[1], up_weight.shape[1])
    )
    down_near = after(down_gather.held, weights[0])
    weights = (
        *weights,
        *in_order(late_slots, down_near, down_gather.last(), (up_weight.shape[1],)),
    )
    ups = up_bias[None]
    firsts = []
    for chunk in range(CHUNKS):
        result = feed_first(
            attended[chunk], attended_other[chunk], tokens_full, weights, norms, ups, chunk
        )
        ups = after(ups, result[-1])
        firsts.append((*result, exchanged(result[-1])))
    normed, inverse, upper, act, slope, down_part, down_other = zip(*firsts)

    logit_dense.append(dense_of(logit_grad, 0.0, 0)(down_part[-1]))
    sums = after(jnp.zeros((SUM_ROWS, own), F32), logit_dense[-1])
    output = None
    seconds = []
    for chunk in range(CHUNKS):
        sums, output, *result = feed_second(
            swap, sums, output, down_part[chunk], down_other[chunk],
            normed[chunk], grad_full, slope[chunk], weights, norms, chunk,
        )
        seconds.append((*result, exchanged(result[-1])))
    res_two, ffn_low, hidden_grad, lower_part, lower_other = zip(*seconds)
    logit_dense.append(dense_of(logit_grad, 0.0, 1)(lower_part[-1]))
    sums = after(sums, logit_dense[-1])

    branch_low, res_one, query_grad, prev_dense_grad = [], [], [], []
    partial = None
    for chunk in range(CHUNKS):
        sums, low, attended_grad, res = feed_third(
            swap, sums, width, lower_part[chunk], lower_other[chunk], res_two[chunk],
            normed[chunk], inverse[chunk], weights, norms,
        )
        branch_low.append(low)
        res_one.append(res)
        if chunk == 0:
            up_keep, up_send, down_keep, down_send = feed_grads(
                late_blocks, blocks, (after(ffn_low[0], low), *ffn_low[1:]), act, upper,
                hidden_grad,
            )
            up_sum = Reduction(late, up_keep, [up_send], None, 1)
            down_sum = Reduction(early, down_keep, [down_send], None, 1)
            up_sum.move()
            down_sum.move()
            attended_grad = after(attended_grad, up_keep)
        prev, query_part, *partial = attend_backward(
            attended_grad, query, key, value, probs[chunk], logit_dense[chunk], chunk, partial
        )
        sums = after(sums, query_part)
        if chunk == 0:
            down_sum.add(query_part)
            up_sum.add(down_sum.keep)
            sums = after(sums, up_sum.keep)
        prev_dense_grad.append(prev)
        query_grad.append(query_part)
    key_grad, value_grad = partial
    low_part, center, high_part = token_grads(query_grad, res_one, key_grad, value_grad, weight)
    arrived_low = lax.ppermute(high_part, "row", forward).astype(F32)
    arrived_high = lax.ppermute(low_part, "row", backward).astype(F32)
    down_sum.add(low_part)
    keep, send, sums = project_grads(
        blocks, after(sums, down_sum.keep), tokens_full, low_tokens, high_tokens, query_grad,
        key_grad, value_grad, branch_low, attended,
    )
    last = Reduction(early, keep, [send], sums, 4)
    last.move()
    up_sum.add(keep)
    last.add(up_sum.keep)
    center = center + jnp.pad(after(arrived_low, last.keep), ((0, count - HALO), (0, 0)))
    center = center + jnp.pad(arrived_high, ((count - HALO, 0), (0, 0)))
    tokens_grad = center[:, :own]
    for step in range(1, col_count):
        part = center[:, step * own : (step + 1) * own].astype(BF16)
        tokens_grad = tokens_grad + from_next(part, "col", -step).astype(F32)
    prev_dense_grad[0] = after(prev_dense_grad[0], center)
    prev_grad = to_band(prev_dense_grad, False)
    for sums_of in (last, down_sum, up_sum):
        while not hasattr(sums_of, "result"):
            sums_of.add(prev_grad)
    *project_grad, out_grad_rows, sums = last.result
    feed_grad = (up_sum.result[0], down_sum.result[0])
    return (
        output,
        new_logits,
        tokens_grad.astype(BF16),
        prev_grad,
        jnp.stack(project_grad),
        sums[0:2],
        out_grad_rows.T,
        sums[2:4],
        feed_grad[0],
        sums[8 : 8 + hidden_rows].reshape(-1),
        feed_grad[1].T,
        sums[4:6],
        sums[6:8],
    )


def solution(mesh):
    return jax.shard_map(
        on_device,
        mesh=mesh,
        in_specs=(
            P("row", "col"),
            P("col", "row", None),
            P(),
            P(None, "row", "col"),
            P(None, "col"),
            P("col", "row"),
            P(None, "col"),
            P("row", "col"),
            P("col"),
            P("col", "row"),
            P(None, "col"),
            P(None, "col"),
            P("row", "col"),
            P("col", "row", None),
        ),
        out_specs=(
            P("row", "col"),
            P("col", "row", None),
            P("row", "col"),
            P("col", "row", None),
            P(None, "row", "col"),
            P(None, "col"),
            P("col", "row"),
            P(None, "col"),
            P("row", "col"),
            P("col"),
            P("col", "row"),
            P(None, "col"),
            P(None, "col"),
        ),
        check_vma=False,
    )
```

time: 225 us -> 167 us (0.74)
  waiting for transfers between devices: 79.6 us -> 28.3 us
  starting transfers between devices: 51 us -> 64.1 us
  local copies, waits for them, and re-layouts: 18.8 us -> 5.76 us
  Pallas kernels: 68.8 us -> 63.3 us
    ppermute x20 -> x30, waiting for transfers between devices: 50.6 us -> 23.4 us  [with_partner(): return lax.ppermute(x, 'row', [(i, i ^ bit) for i in range(count)])]
    ppermute x8 -> x9, waiting for transfers between devices: 28.9 us -> 4.82 us  [from_next(): lax.ppermute(x, axis, [((i + step) % count, i) for i in range(count)])]
    ppermute x20 -> x30, starting transfers between devices: 32.4 us -> 49.2 us  [with_partner(): return lax.ppermute(x, 'row', [(i, i ^ bit) for i in range(count)])]
    unnamed x93 -> x37, local copies, waits for them, and re-layouts: 14.5 us -> 3.16 us
    ppermute x8 -> x9, starting transfers between devices: 11.7 us -> 6.94 us  [from_next(): lax.ppermute(x, axis, [((i + step) % count, i) for i in range(count)])]
    pallas_call x8 -> x24, Pallas kernels: 55.3 us -> 52.5 us  [the longest x4 12.5 us: to_dense(): pl.pallas_call(functools.partial(dense_kernel, fill, token_count, offset)...]
  transfers between devices with their start and end apart: 32 -> 43, of which waited for: 15 -> 11; matrix products, arithmetic and copies ran while one was open for 3% -> 4% of each run, Pallas kernels for 18% -> 34%
where the time goes in v2:
time: 167 us; the launch traced here: 166 us
  starting transfers between devices  64.1 us (38%)
  Pallas kernels  63.3 us (38%)
  waiting for transfers between devices  28.3 us (17%)
  local copies, waits for them, and re-layouts  5.76 us (3%)
  other arithmetic  3.51 us (2%)
    ppermute x30, starting transfers between devices, with_partner(): return lax.ppermute(x, 'row', [(i, i ^ bit) for i in range(count)])  49.2 us
    ppermute x30, waiting for transfers between devices, with_partner(): return lax.ppermute(x, 'row', [(i, i ^ bit) for i in range(count)])  23.4 us
    pallas_call x4, Pallas kernels, to_dense(): pl.pallas_call(functools.partial(dense_kernel, fill, token_count, offset)...  12.5 us
    pallas_call x2, Pallas kernels, to_band(): pl.pallas_call(functools.partial(band_kernel, masked), grid=(CHUNKS * ste...  10.1 us
    pallas_call x2, Pallas kernels, attend_backward(): pl.pallas_call(functools.partial(backward_kernel, offset, last), grid=(co...  9.07 us
    pallas_call x2, Pallas kernels, attend_forward(): pl.pallas_call(functools.partial(forward_kernel, offset), grid=(count //...  7.56 us
    ppermute x9, starting transfers between devices, from_next(): lax.ppermute(x, axis, [((i + step) % count, i) for i in range(count)])  6.94 us
    pallas_call x2, Pallas kernels, feed_second(): pl.pallas_call(functools.partial(second_kernel, swap), grid=(count // BLO...  4.85 us
  transfers between devices with their start and end apart: 43, of which 11 were waited for; matrix products, arithmetic and copies ran while one was open for 4% of the time, Pallas kernels for 34%

profile of v2, /device:TPU:0, one launch (start us, length us, event | category | flops | bytes accessed | tf_op | source)
XLA Modules:
  0.0 166.4 jit_solution(11706834969850239557)
XLA Ops:
  0.6 4.1 %collective-permute-start.1 = (bf16[1,3,32,256]{3,2,1,0:T(8,128)(2,1)}, bf16[1,3,32,256]{3,2,1,0:T(8,128)(2,1)S(1)}, u32[]{:S(2)}, u32[]{:S(2)}) collective-permute-start(bf16[1,3,32,256]{3,2,1,0:T(8,128)(2,1)} %bitcast.25), channel_id=1, source_target_pairs={{0,16},{2,18},{4,20},{6,22},{8,24},{10,26},{12,28},{14,30},{16,0},... | collective-permute-start | bytes 147464 | tf_op jit(solution)/shard_map/ppermute | solution.py:866
  4.7 1.6 collective-permute-start.2
  6.3 0.7 subtract_convert_fusion
  7.1 0.7 fusion.3
  7.8 1.9 %concatenate.38 = bf16[562,256]{1,0:T(8,128)(2,1)S(1)} concatenate(bf16[512,256]{1,0:T(8,128)(2,1)} %param.14, bf16[32,256]{1,0:T(8,128)(2,1)} %bitcast.29, bf16[6,256]{1,0:T(8,128)(2,1)S(1)} %fusion.3, bf16[6,256]{1,0:T(8,128)(2,1)S(1)} %get-tuple-element.281, bf16[6,256]{1,0:T(8,128)(2,1)S(1)} %get-tuple-element.280), dimensions={0} | concatenate | bytes 575488 | tf_op jit(solution)/shard_map/concatenate | solution.py:1016
  9.7 1.8 %collective-permute-start = (bf16[562,256]{1,0:T(8,128)(2,1)S(1)}, bf16[562,256]{1,0:T(8,128)(2,1)S(1)}, u32[]{:S(2)}, u32[]{:S(2)}) collective-permute-start(bf16[562,256]{1,0:T(8,128)(2,1)S(1)} %concatenate.38), channel_id=1, source_target_pairs={{1,0},{0,1},{3,2},{2,3},{5,4},{4,5},{7,6},{6,7},{9,8},{8,9},{11,10... | collective-permute-start | bytes 863240 | tf_op jit(solution)/shard_map/ppermute | solution.py:861
  11.4 1.5 collective-permute-start.7
  13.0 0.8 constant_dynamic-update-slice_fusion.6
  13.8 1.0 constant_dynamic-update-slice_fusion.1
  15.4 3.1 %to_dense.4.prev_ref = bf16[4,256,1152]{2,1,0:T(8,128)(2,1)S(1)} custom-call(s32[1,33]{1,0:T(1,128)S(1)} %copy-done, s32[1]{0:T(128)} %bitcast.base_ref, bf16[4,512,1024]{2,1,0:T(8,128)(2,1)} %band_ref.1), custom_call_target="tpu_custom_call" | custom-call | flops 1000000000 | tf_op jit(solution)/shard_map/to_dense/pallas_call | solution.py:103
  19.3 3.2 %to_dense.5.prev_ref = bf16[4,256,1152]{2,1,0:T(8,128)(2,1)S(1)} custom-call(s32[1,33]{1,0:T(1,128)S(1)} %copy-done, s32[1]{0:T(128)} %bitcast.base_ref, bf16[4,512,1024]{2,1,0:T(8,128)(2,1)} %band_ref.1), custom_call_target="tpu_custom_call" | custom-call | flops 1000000000 | tf_op jit(solution)/shard_map/to_dense/pallas_call | solution.py:103
  22.6 1.8 %collective-permute-done.11 = bf16[4,3,32,256]{3,2,1,0:T(8,128)(2,1)S(1)} collective-permute-done((bf16[4,3,32,256]{3,2,1,0:T(8,128)(2,1)S(1)}, bf16[4,3,32,256]{3,2,1,0:T(8,128)(2,1)S(1)}, u32[]{:S(2)}, u32[]{:S(2)}) %collective-permute-start.11) | collective-permute-done | bytes 196640 | tf_op jit(solution)/shard_map/ppermute | solution.py:866
  24.5 1.8 %collective-permute-start.4 = (bf16[1,32,1536]{2,1,0:T(8,128)(2,1)S(1)}, bf16[1,32,1536]{2,1,0:T(8,128)(2,1)S(1)}, u32[]{:S(2)}, u32[]{:S(2)}) collective-permute-start(bf16[1,32,1536]{2,1,0:T(8,128)(2,1)S(1)} %bitcast.21), channel_id=1, source_target_pairs={{0,16},{2,18},{4,20},{6,22},{8,24},{10,26},{12,28},{14,30},{16,0},... | collective-permute-start | bytes 294920 | tf_op jit(solution)/shard_map/ppermute | solution.py:866
  26.3 2.5 %collective-permute-start.5 = (bf16[1,32,1536]{2,1,0:T(8,128)(2,1)S(1)}, bf16[1,32,1536]{2,1,0:T(8,128)(2,1)S(1)}, u32[]{:S(2)}, u32[]{:S(2)}) collective-permute-start(bf16[1,32,1536]{2,1,0:T(8,128)(2,1)S(1)} %bitcast.22), channel_id=1, source_target_pairs={{0,8},{2,10},{4,12},{6,14},{8,0},{10,2},{12,4},{14,6},{16,24},{18,... | collective-permute-start | bytes 294920 | tf_op jit(solution)/shard_map/ppermute | solution.py:866
  29.7 3.4 %collective-permute-done.4 = bf16[1,32,1536]{2,1,0:T(8,128)(2,1)S(1)} collective-permute-done((bf16[1,32,1536]{2,1,0:T(8,128)(2,1)S(1)}, bf16[1,32,1536]{2,1,0:T(8,128)(2,1)S(1)}, u32[]{:S(2)}, u32[]{:S(2)}) %collective-permute-start.4) | collective-permute-done | bytes 98336 | tf_op jit(solution)/shard_map/ppermute | solution.py:866
  33.2 1.3 collective-permute-start.10
  34.5 3.1 %collective-permute-start.9 = (bf16[384,512]{1,0:T(8,128)(2,1)S(1)}, bf16[384,512]{1,0:T(8,128)(2,1)S(1)}, u32[]{:S(2)}, u32[]{:S(2)}) collective-permute-start(bf16[384,512]{1,0:T(8,128)(2,1)S(1)} %get-tuple-element.275), channel_id=1, source_target_pairs={{0,2},{2,4},{4,6},{6,8},{8,10},{10,12},{12,14},{14,16},{16,18},{18... | collective-permute-start | bytes 1179656 | tf_op jit(solution)/shard_map/ppermute | solution.py:1040
  37.6 1.1 collective-permute-start.17
  38.8 2.6 %collective-permute-start.18 = (bf16[2,32,1024]{2,1,0:T(8,128)(2,1)S(1)}, bf16[2,32,1024]{2,1,0:T(8,128)(2,1)S(1)}, u32[]{:S(2)}, u32[]{:S(2)}) collective-permute-start(bf16[2,32,1024]{2,1,0:T(8,128)(2,1)S(1)} %pad_maximum_fusion.3), channel_id=1, source_target_pairs={{0,8},{2,10},{4,12},{6,14},{8,0},{10,2},{12,4},{14,6},{16,24},{18,... | collective-permute-start | bytes 393224 | tf_op jit(solution)/shard_map/ppermute | solution.py:866
  41.4 0.9 collective-permute-start.19
  42.8 1.8 %project.1 = (bf16[512,256]{1,0:T(8,128)(2,1)S(1)}, bf16[1536,256]{1,0:T(8,128)(2,1)S(1)}, bf16[1536,256]{1,0:T(8,128)(2,1)S(1)}, bf16[3,512,256]{2,1,0:T(8,128)(2,1)S(1)}) custom-call(s32[16]{0:T(128)S(1)} %add_add_fusion.1.slot_ref, bf16[512,512]{1,0:T(8,128)(2,1)S(1)} %pad_maximum_fusion.token_ref.refs_6_, ...), custom_call_target="tpu_custom_call" | custom-call | flops 2000000000 | tf_op jit(solution)/shard_map/project/pallas_call | solution.py:231
  44.5 3.8 %attend_forward.2 = (bf16[4,256,1152]{2,1,0:T(8,128)(2,1)S(1)}, bf16[4,256,1152]{2,1,0:T(8,128)(2,1)S(1)}, bf16[256,256]{1,0:T(8,128)(2,1)S(1)}) custom-call(bf16[512,256]{1,0:T(8,128)(2,1)S(1)} %get-tuple-element.200.query_ref, bf16[1536,256]{1,0:T(8,128)(2,1)S(1)} %get-tuple-element.152.key_ref, bf16[1536,256]{1,0:T(8,128)(2,1)S(1)} %get-tuple-element.153.value_ref, ...), custom_call_target="tpu_custom_call" | custom-call | flops 3800000000 | tf_op jit(solution)/shard_map/attend_forward/pallas_call | solution.py:273
  48.8 3.8 %attend_forward.3 = (bf16[4,256,1152]{2,1,0:T(8,128)(2,1)S(1)}, bf16[4,256,1152]{2,1,0:T(8,128)(2,1)S(1)}, bf16[256,256]{1,0:T(8,128)(2,1)S(1)}) custom-call(bf16[512,256]{1,0:T(8,128)(2,1)S(1)} %get-tuple-element.200.query_ref, bf16[1536,256]{1,0:T(8,128)(2,1)S(1)} %get-tuple-element.152.key_ref, bf16[1536,256]{1,0:T(8,128)(2,1)S(1)} %get-tuple-element.153.value_ref, ...), custom_call_target="tpu_custom_call" | custom-call | flops 3800000000 | tf_op jit(solution)/shard_map/attend_forward/pallas_call | solution.py:273
  53.2 1.2 collective-permute-start.13
  54.4 2.6 %collective-permute-start.16 = (bf16[8,32,1536]{2,1,0:T(8,128)(2,1)S(1)}, bf16[8,32,1536]{2,1,0:T(8,128)(2,1)S(1)}, u32[]{:S(2)}, u32[]{:S(2)}) collective-permute-start(bf16[8,32,1536]{2,1,0:T(8,128)(2,1)S(1)} %constant_dynamic-update-slice_fusion.7.near_ref), channel_id=1, source_target_pairs={{0,2},{2,0},{4,6},{6,4},{8,10},{10,8},{12,14},{14,12},{16,18},{18,... | collective-permute-start | bytes 2359304 | tf_op jit(solution)/shard_map/ppermute | solution.py:866
  57.2 5.1 %to_band.2 = bf16[4,512,1024]{2,1,0:T(8,128)(2,1)} custom-call(bf16[4,256,1152]{2,1,0:T(8,128)(2,1)S(1)} %get-tuple-element.161.refs_0_, bf16[4,256,1152]{2,1,0:T(8,128)(2,1)S(1)} %get-tuple-element.162.refs_1_), custom_call_target="tpu_custom_call" | custom-call | flops 5000000000 | tf_op jit(solution)/shard_map/to_band/pallas_call | solution.py:156
  62.2 0.8 in_order.2
  63.1 1.0 in_order.3.down_ref
  64.1 2.2 %feed_first.2 = (f32[256,512]{1,0:T(8,128)S(1)}, f32[256,1]{1,0:T(8,128)S(1)}, bf16[256,512]{1,0:T(8,128)(2,1)S(1)}, bf16[256,1024]{1,0:T(8,128)(2,1)S(1)}, bf16...) custom-call(bf16[256,256]{1,0:T(8,128)(2,1)S(1)} %get-tuple-element.155.own_ref.refs_4_, ...), custom_call_target="tpu_custom_call" | custom-call | flops 1000000000 | tf_op jit(solution)/shard_map/feed_first/pallas_call | solution.py:462
  66.7 2.2 %feed_first.3 = (f32[256,512]{1,0:T(8,128)S(1)}, f32[256,1]{1,0:T(8,128)S(1)}, bf16[256,512]{1,0:T(8,128)(2,1)S(1)}, bf16[256,1024]{1,0:T(8,128)(2,1)S(1)}, bf16...) custom-call(bf16[256,256]{1,0:T(8,128)(2,1)S(1)} %get-tuple-element.158.own_ref.refs_5_, ...), custom_call_target="tpu_custom_call" | custom-call | flops 1000000000 | tf_op jit(solution)/shard_map/feed_first/pallas_call | solution.py:462
  68.9 1.8 %collective-permute-start.22 = (bf16[256,512]{1,0:T(8,128)(2,1)S(1)}, bf16[256,512]{1,0:T(8,128)(2,1)S(1)}, u32[]{:S(2)}, u32[]{:S(2)}) collective-permute-start(bf16[256,512]{1,0:T(8,128)(2,1)S(1)} %get-tuple-element.170.part_ref), channel_id=1, source_target_pairs={{1,0},{0,1},{3,2},{2,3},{5,4},{4,5},{7,6},{6,7},{9,8},{8,9},{11,10... | collective-permute-start | bytes 786440 | tf_op jit(solution)/shard_map/ppermute | solution.py:861
  70.6 3.1 %to_dense.6.logit_ref = bf16[4,256,1152]{2,1,0:T(8,128)(2,1)S(1)} custom-call(s32[1,33]{1,0:T(1,128)S(1)} %copy-done.1, s32[1]{0:T(128)} %bitcast.base_ref, bf16[4,512,1024]{2,1,0:T(8,128)(2,1)} %band_ref.3), custom_call_target="tpu_custom_call" | custom-call | flops 1000000000 | tf_op jit(solution)/shard_map/to_dense/pallas_call | solution.py:103
  73.7 1.7 %collective-permute-done.21.recv_ref = bf16[256,512]{1,0:T(8,128)(2,1)S(1)} collective-permute-done((bf16[256,512]{1,0:T(8,128)(2,1)S(1)}, bf16[256,512]{1,0:T(8,128)(2,1)S(1)}, u32[]{:S(2)}, u32[]{:S(2)}) %collective-permute-start.21) | collective-permute-done | bytes 262176 | tf_op jit(solution)/shard_map/ppermute | solution.py:861
  75.5 2.4 %feed_second.2 = (f32[16,256]{1,0:T(8,128)S(1)}, bf16[512,256]{1,0:T(8,128)(2,1)}, f32[256,512]{1,0:T(8,128)S(1)}, bf16[256,512]{1,0:T(8,128)(2,1)S(1)}, bf16[25...) custom-call(f32[16,256]{1,0:T(8,128)S(1)} %broadcast_in_dim.18.start_ref, ...), custom_call_target="tpu_custom_call" | custom-call | flops 700000000 | tf_op jit(solution)/shard_map/feed_second/pallas_call | solution.py:548
  78.2 2.9 %collective-permute-done.22.recv_ref = bf16[256,512]{1,0:T(8,128)(2,1)S(1)} collective-permute-done((bf16[256,512]{1,0:T(8,128)(2,1)S(1)}, bf16[256,512]{1,0:T(8,128)(2,1)S(1)}, u32[]{:S(2)}, u32[]{:S(2)}) %collective-permute-start.22) | collective-permute-done | bytes 262176 | tf_op jit(solution)/shard_map/ppermute | solution.py:861
  81.1 2.4 %feed_second.3 = (f32[16,256]{1,0:T(8,128)S(1)}, bf16[512,256]{1,0:T(8,128)(2,1)}, f32[256,512]{1,0:T(8,128)S(1)}, bf16[256,512]{1,0:T(8,128)(2,1)S(1)}, bf16[25...) custom-call(f32[16,256]{1,0:T(8,128)S(1)} %get-tuple-element.175.start_ref, ...), custom_call_target="tpu_custom_call", output_to_operand_aliasing={{1}: (9, {})} | custom-call | flops 700000000 | tf_op jit(solution)/shard_map/feed_second/pallas_call | solution.py:548
  83.5 3.1 %to_dense.7.logit_ref = bf16[4,256,1152]{2,1,0:T(8,128)(2,1)S(1)} custom-call(s32[1,33]{1,0:T(1,128)S(1)} %copy-done.1, s32[1]{0:T(128)} %bitcast.base_ref, bf16[4,512,1024]{2,1,0:T(8,128)(2,1)} %band_ref.3), custom_call_target="tpu_custom_call" | custom-call | flops 1000000000 | tf_op jit(solution)/shard_map/to_dense/pallas_call | solution.py:103
  86.6 0.8 feed_third.2
  87.4 3.4 %feed_grads.1 = (f32[256,1024]{1,0:T(8,128)S(1)}, bf16[256,1024]{1,0:T(8,128)(2,1)S(1)}, f32[256,1024]{1,0:T(8,128)S(1)}, bf16[256,1024]{1,0:T(8,128)(2,1)S(1)}) custom-call(s32[16]{0:T(128)S(1)} %and_select_fusion.1.up_block_ref, s32[16]{0:T(128)S(1)} %and_select_fusion.down_block_ref.block_ref, bf16[256,512]{1,0:T(8,128)(2,1)S(1)} %get-tuple-element.190.refs_0_, ...), custom_call_target="tpu_custom_call" | custom-call | flops 1000000000 | tf_op jit(solution)/shard_map/feed_grads/pallas_call | solution.py:670
  91.7 4.1 %attend_backward.2 = (bf16[4,256,1152]{2,1,0:T(8,128)(2,1)S(1)}, bf16[256,256]{1,0:T(8,128)(2,1)S(1)}, f32[256,1536]{1,0:T(8,128)S(1)}, f32[256,1536]{1,0:T(8,128)S(1)}) custom-call(bf16[256,256]{1,0:T(8,128)(2,1)S(1)} %get-tuple-element.199.grad_ref, bf16[512,256]{1,0:T(8,128)(2,1)S(1)} %get-tuple-element.200.query_ref, ...), custom_call_target="tpu_custom_call" | custom-call | flops 1400000000 | tf_op jit(solution)/shard_map/attend_backward/pallas_call | solution.py:357
  95.9 3.4 %collective-permute-start.28 = (bf16[128,1024]{1,0:T(8,128)(2,1)S(1)}, bf16[128,1024]{1,0:T(8,128)(2,1)S(1)}, u32[]{:S(2)}, u32[]{:S(2)}) collective-permute-start(bf16[128,1024]{1,0:T(8,128)(2,1)S(1)} %get-tuple-element.231), channel_id=1, source_target_pairs={{0,4},{2,6},{4,0},{6,2},{8,12},{10,14},{12,8},{14,10},{16,20},{18,... | collective-permute-start | bytes 786440 | tf_op jit(solution)/shard_map/ppermute | solution.py:866
  99.6 0.7 feed_third.3
  100.4 4.9 %attend_backward.3 = (bf16[4,256,1152]{2,1,0:T(8,128)(2,1)S(1)}, bf16[256,256]{1,0:T(8,128)(2,1)S(1)}, bf16[1536,256]{1,0:T(8,128)(2,1)S(1)}, bf16[1536,256]{1,0:T(8,128)(2,1)S(1)}) custom-call(bf16[256,256]{1,0:T(8,128)(2,1)S(1)} %get-tuple-element.215.grad_ref, bf16[512,256]{1,0:T(8,128)(2,1)S(1)} %get-tuple-element.200.query_ref, ...), custom_call_target="tpu_custom_call" | custom-call | flops 1400000000 | tf_op jit(solution)/shard_map/attend_backward/pallas_call | solution.py:357
  105.3 2.1 %token_grads.1 = (bf16[384,512]{1,0:T(8,128)(2,1)S(1)}, f32[512,512]{1,0:T(8,128)S(1)}, bf16[384,512]{1,0:T(8,128)(2,1)S(1)}) custom-call(bf16[256,256]{1,0:T(8,128)(2,1)S(1)} %get-tuple-element.202.refs_0_, bf16[256,256]{1,0:T(8,128)(2,1)S(1)} %get-tuple-element.219.refs_1_, f32[256,256]{1,0:T(8,128)S(1)} %get-tuple-element.220.refs_2_, ...), custom_call_target="tpu_custom_call" | custom-call | flops 600000000 | tf_op jit(solution)/shard_map/token_grads/pallas_call | solution.py:839
  107.5 1.9 %project_grads.1 = (f32[1024,256]{1,0:T(8,128)S(1)}, bf16[1056,256]{1,0:T(8,128)(2,1)S(1)}, f32[16,256]{1,0:T(8,128)S(1)}) custom-call(s32[16]{0:T(128)S(1)} %and_select_fusion.down_block_ref.block_ref, f32[16,256]{1,0:T(8,128)S(1)} %get-tuple-element.233.start_ref, bf16[256,256]{1,0:T(8,128)(2,1)S(1)} %get-tuple-element.202.refs_0_, ...), custom_call_target="tpu_custom_call" | custom-call | flops 600000000 | tf_op jit(solution)/shard_map/project_grads/pallas_call | solution.py:727
  109.5 2.4 %collective-permute-start.27 = (bf16[384,512]{1,0:T(8,128)(2,1)S(1)}, bf16[384,512]{1,0:T(8,128)(2,1)S(1)}, u32[]{:S(2)}, u32[]{:S(2)}) collective-permute-start(bf16[384,512]{1,0:T(8,128)(2,1)S(1)} %get-tuple-element.226), channel_id=1, source_target_pairs={{0,2},{2,4},{4,6},{6,8},{8,10},{10,12},{12,14},{14,16},{16,18},{18... | collective-permute-start | bytes 1179656 | tf_op jit(solution)/shard_map/ppermute | solution.py:1132
  112.0 1.3 collective-permute-start.33
  113.3 6.9 %collective-permute-start.29 = (bf16[64,1024]{1,0:T(8,128)(2,1)S(1)}, bf16[64,1024]{1,0:T(8,128)(2,1)S(1)}, u32[]{:S(2)}, u32[]{:S(2)}) collective-permute-start(bf16[64,1024]{1,0:T(8,128)(2,1)S(1)} %get-tuple-element.237), channel_id=1, source_target_pairs={{0,16},{2,18},{4,20},{6,22},{8,24},{10,26},{12,28},{14,30},{16,0},... | collective-permute-start | bytes 393224 | tf_op jit(solution)/shard_map/ppermute | solution.py:866
  120.2 4.2 %collective-permute-start.30 = (bf16[64,1024]{1,0:T(8,128)(2,1)S(1)}, bf16[64,1024]{1,0:T(8,128)(2,1)S(1)}, u32[]{:S(2)}, u32[]{:S(2)}) collective-permute-start(bf16[64,1024]{1,0:T(8,128)(2,1)S(1)} %get-tuple-element.238), channel_id=1, source_target_pairs={{0,8},{2,10},{4,12},{6,14},{8,0},{10,2},{12,4},{14,6},{16,24},{18,... | collective-permute-start | bytes 393224 | tf_op jit(solution)/shard_map/ppermute | solution.py:866
  124.4 6.5 %collective-permute-done.29.refs_1_ = bf16[64,1024]{1,0:T(8,128)(2,1)S(1)} collective-permute-done((bf16[64,1024]{1,0:T(8,128)(2,1)S(1)}, bf16[64,1024]{1,0:T(8,128)(2,1)S(1)}, u32[]{:S(2)}, u32[]{:S(2)}) %collective-permute-start.29) | collective-permute-done | bytes 131104 | tf_op jit(solution)/shard_map/ppermute | solution.py:866
  130.9 1.6 collective-permute-start.31
  132.5 6.2 %collective-permute-done.31.refs_3_ = bf16[64,1024]{1,0:T(8,128)(2,1)S(1)} collective-permute-done((bf16[64,1024]{1,0:T(8,128)(2,1)S(1)}, bf16[64,1024]{1,0:T(8,128)(2,1)S(1)}, u32[]{:S(2)}, u32[]{:S(2)}) %collective-permute-start.31) | collective-permute-done | bytes 131104 | tf_op jit(solution)/shard_map/ppermute | solution.py:866
  138.8 2.9 %collective-permute-start.40 = (bf16[32,1024]{1,0:T(8,128)(2,1)S(1)}, bf16[32,1024]{1,0:T(8,128)(2,1)S(1)}, u32[]{:S(2)}, u32[]{:S(2)}) collective-permute-start(bf16[32,1024]{1,0:T(8,128)(2,1)S(1)} %get-tuple-element.266), channel_id=1, source_target_pairs={{0,16},{2,18},{4,20},{6,22},{8,24},{10,26},{12,28},{14,30},{16,0},... | collective-permute-start | bytes 196616 | tf_op jit(solution)/shard_map/ppermute | solution.py:866
  142.2 2.3 %collective-permute-start.42 = (bf16[32,1024]{1,0:T(8,128)(2,1)S(1)}, bf16[32,1024]{1,0:T(8,128)(2,1)S(1)}, u32[]{:S(2)}, u32[]{:S(2)}) collective-permute-start(bf16[32,1024]{1,0:T(8,128)(2,1)S(1)} %get-tuple-element.268), channel_id=1, source_target_pairs={{0,24},{2,26},{4,28},{6,30},{8,16},{10,18},{12,20},{14,22},{16,8},... | collective-permute-start | bytes 196616 | tf_op jit(solution)/shard_map/ppermute | solution.py:866
  145.0 2.1 %collective-permute-start.35 = (bf16[544,256]{1,0:T(8,128)(2,1)S(1)}, bf16[544,256]{1,0:T(8,128)(2,1)S(1)}, u32[]{:S(2)}, u32[]{:S(2)}) collective-permute-start(bf16[544,256]{1,0:T(8,128)(2,1)S(1)} %get-tuple-element.250), channel_id=1, source_target_pairs={{0,4},{2,6},{4,0},{6,2},{8,12},{10,14},{12,8},{14,10},{16,20},{18,... | collective-permute-start | bytes 835592 | tf_op jit(solution)/shard_map/ppermute | solution.py:866
  147.1 1.8 %collective-permute-done.39.refs_1_ = bf16[32,1024]{1,0:T(8,128)(2,1)S(1)} collective-permute-done((bf16[32,1024]{1,0:T(8,128)(2,1)S(1)}, bf16[32,1024]{1,0:T(8,128)(2,1)S(1)}, u32[]{:S(2)}, u32[]{:S(2)}) %collective-permute-start.39) | collective-permute-done | bytes 65568 | tf_op jit(solution)/shard_map/ppermute | solution.py:866
  149.0 5.0 %to_band.3 = bf16[4,512,1024]{2,1,0:T(8,128)(2,1)} custom-call(bf16[4,256,1152]{2,1,0:T(8,128)(2,1)S(1)} %get-tuple-element.247.refs_0_, bf16[4,256,1152]{2,1,0:T(8,128)(2,1)S(1)} %get-tuple-element.248.refs_1_), custom_call_target="tpu_custom_call" | custom-call | flops 5000000000 | tf_op jit(solution)/shard_map/to_band/pallas_call | solution.py:156
  154.7 0.7 fold.17
  155.4 1.3 collective-permute-start.36
  156.8 0.9 collective-permute-start.37
  157.7 2.2 %collective-permute-start.38 = (bf16[160,256]{1,0:T(8,128)(2,1)S(1)}, bf16[160,256]{1,0:T(8,128)(2,1)S(1)}, u32[]{:S(2)}, u32[]{:S(2)}) collective-permute-start(bf16[160,256]{1,0:T(8,128)(2,1)S(1)} %get-tuple-element.256), channel_id=1, source_target_pairs={{0,24},{2,26},{4,28},{6,30},{8,16},{10,18},{12,20},{14,22},{16,8},... | collective-permute-start | bytes 245768 | tf_op jit(solution)/shard_map/ppermute | solution.py:866
  159.9 0.8 fusion
  160.7 1.0 collective-permute-done.36.refs_1_
  161.7 2.2 %collective-permute-done.38.refs_3_ = bf16[160,256]{1,0:T(8,128)(2,1)S(1)} collective-permute-done((bf16[160,256]{1,0:T(8,128)(2,1)S(1)}, bf16[160,256]{1,0:T(8,128)(2,1)S(1)}, u32[]{:S(2)}, u32[]{:S(2)}) %collective-permute-start.38) | collective-permute-done | bytes 81952 | tf_op jit(solution)/shard_map/ppermute | solution.py:866
  (119 shorter events, 10.7 us)
Async XLA Ops:
  0.6 17.9 %collective-permute-start.1 = (bf16[1,3,32,256]{3,2,1,0:T(8,128)(2,1)}, bf16[1,3,32,256]{3,2,1,0:T(8,128)(2,1)S(1)}, u32[]{:S(2)}, u32[]{:S(2)}) collective-permute-start(bf16[1,3,32,256]{3,2,1,0:T(8,128)(2,1)} %bitcast.25), channel_id=1, source_target_pairs={{0,16},{2,18},{4,20},{6,22},{8,24},{10,26},{12,28},{14,30},{16,0},... | collective-permute-start | bytes 147464 | tf_op jit(solution)/shard_map/ppermute | solution.py:866
  4.7 13.8 %collective-permute-start.2 = (bf16[1,3,32,256]{3,2,1,0:T(8,128)(2,1)}, bf16[1,3,32,256]{3,2,1,0:T(8,128)(2,1)S(1)}, u32[]{:S(2)}, u32[]{:S(2)}) collective-permute-start(bf16[1,3,32,256]{3,2,1,0:T(8,128)(2,1)} %bitcast.26), channel_id=1, source_target_pairs={{0,8},{2,10},{4,12},{6,14},{8,0},{10,2},{12,4},{14,6},{16,24},{18,... | collective-permute-start | bytes 147464 | tf_op jit(solution)/shard_map/ppermute | solution.py:866
  6.3 12.2 %collective-permute-start.3 = (bf16[1,3,32,256]{3,2,1,0:T(8,128)(2,1)}, bf16[1,3,32,256]{3,2,1,0:T(8,128)(2,1)S(1)}, u32[]{:S(2)}, u32[]{:S(2)}) collective-permute-start(bf16[1,3,32,256]{3,2,1,0:T(8,128)(2,1)} %bitcast.27), channel_id=1, source_target_pairs={{0,24},{2,26},{4,28},{6,30},{8,16},{10,18},{12,20},{14,22},{16,8},... | collective-permute-start | bytes 147464 | tf_op jit(solution)/shard_map/ppermute | solution.py:866
  9.7 14.8 %collective-permute-start = (bf16[562,256]{1,0:T(8,128)(2,1)S(1)}, bf16[562,256]{1,0:T(8,128)(2,1)S(1)}, u32[]{:S(2)}, u32[]{:S(2)}) collective-permute-start(bf16[562,256]{1,0:T(8,128)(2,1)S(1)} %concatenate.38), channel_id=1, source_target_pairs={{1,0},{0,1},{3,2},{2,3},{5,4},{4,5},{7,6},{6,7},{9,8},{8,9},{11,10... | collective-permute-start | bytes 863240 | tf_op jit(solution)/shard_map/ppermute | solution.py:861
  11.4 11.1 %collective-permute-start.7 = (bf16[1,32,1024]{2,1,0:T(8,128)(2,1)}, bf16[1,32,1024]{2,1,0:T(8,128)(2,1)S(1)}, u32[]{:S(2)}, u32[]{:S(2)}) collective-permute-start(bf16[1,32,1024]{2,1,0:T(8,128)(2,1)} %bitcast.31), channel_id=1, source_target_pairs={{0,4},{2,6},{4,0},{6,2},{8,12},{10,14},{12,8},{14,10},{16,20},{18,... | collective-permute-start | bytes 196616 | tf_op jit(solution)/shard_map/ppermute | solution.py:866
  14.8 0.7 copy-start
  15.4 3.1 %copy-start.6 = (bf16[3,32,256]{2,1,0:T(8,128)(2,1)S(1)}, bf16[3,32,256]{2,1,0:T(8,128)(2,1)}, u32[]{:S(2)}) copy-start(bf16[3,32,256]{2,1,0:T(8,128)(2,1)} %param.17) | copy-start | bytes 147460
  18.6 5.7 %collective-permute-start.11 = (bf16[4,3,32,256]{3,2,1,0:T(8,128)(2,1)S(1)}, bf16[4,3,32,256]{3,2,1,0:T(8,128)(2,1)S(1)}, u32[]{:S(2)}, u32[]{:S(2)}) collective-permute-start(bf16[4,3,32,256]{3,2,1,0:T(8,128)(2,1)S(1)} %pad_maximum_fusion.2), channel_id=1, source_target_pairs={{0,4},{2,6},{4,0},{6,2},{8,12},{10,14},{12,8},{14,10},{16,20},{18,... | collective-permute-start | bytes 589832 | tf_op jit(solution)/shard_map/ppermute | solution.py:866
  19.2 3.3 %copy-start.9 = (bf16[1024,32]{0,1:T(8,128)(2,1)S(1)}, bf16[1024,32]{0,1:T(8,128)(2,1)}, u32[]{:S(2)}) copy-start(bf16[1024,32]{0,1:T(8,128)(2,1)} %param.23) | copy-start | bytes 196612
  19.2 5.3 %copy-start.7 = (bf16[32,1024]{1,0:T(8,128)(2,1)S(1)}, bf16[32,1024]{1,0:T(8,128)(2,1)}, u32[]{:S(2)}) copy-start(bf16[32,1024]{1,0:T(8,128)(2,1)} %param.21) | copy-start | bytes 196612
  19.2 5.3 %copy-start.8 = (bf16[256,32]{0,1:T(8,128)(2,1)S(1)}, bf16[256,32]{0,1:T(8,128)(2,1)}, u32[]{:S(2)}) copy-start(bf16[256,32]{0,1:T(8,128)(2,1)} %param.19) | copy-start | bytes 49156
  19.2 9.7 %copy-start.4 = (bf16[512,256]{1,0:T(8,128)(2,1)S(1)}, bf16[512,256]{1,0:T(8,128)(2,1)}, u32[]{:S(2)}) copy-start(bf16[512,256]{1,0:T(8,128)(2,1)} %param.14) | copy-start | bytes 786436
  22.5 6.6 %copy-start.5 = (bf16[512,256]{1,0:T(8,128)(2,1)S(1)}, bf16[512,256]{1,0:T(8,128)(2,1)}, u32[]{:S(2)}) copy-start(bf16[512,256]{1,0:T(8,128)(2,1)} %param.26) | copy-start | bytes 786436
  22.5 15.1 %copy-start.10 = (f32[2,256]{1,0:T(2,128)S(1)}, f32[2,256]{1,0:T(2,128)}, u32[]{:S(2)}) copy-start(f32[2,256]{1,0:T(2,128)} %param.20) | copy-start | bytes 6148
  22.5 15.1 %copy-start.11 = (f32[2,256]{1,0:T(2,128)S(1)}, f32[2,256]{1,0:T(2,128)}, u32[]{:S(2)}) copy-start(f32[2,256]{1,0:T(2,128)} %param.25) | copy-start | bytes 6148
  22.5 15.1 %copy-start.12 = (f32[2,256]{1,0:T(2,128)S(1)}, f32[2,256]{1,0:T(2,128)}, u32[]{:S(2)}) copy-start(f32[2,256]{1,0:T(2,128)} %param.24) | copy-start | bytes 6148
  24.4 18.4 %copy-start.3 = (f32[2,256]{1,0:T(2,128)S(1)}, f32[2,256]{1,0:T(2,128)}, u32[]{:S(2)}) copy-start(f32[2,256]{1,0:T(2,128)} %bias_ref.1) | copy-start | bytes 6148
  24.4 17.0 %collective-permute-start.12 = (bf16[8,3,32,256]{3,2,1,0:T(8,128)(2,1)S(1)}, bf16[8,3,32,256]{3,2,1,0:T(8,128)(2,1)S(1)}, u32[]{:S(2)}, u32[]{:S(2)}) collective-permute-start(bf16[8,3,32,256]{3,2,1,0:T(8,128)(2,1)S(1)} %constant_dynamic-update-slice_fusion.2.near_ref), channel_id=1, source_target_pairs={{0,2},{2,0},{4,6},{6,4},{8,10},{10,8},{12,14},{14,12},{16,18},{18,... | collective-permute-start | bytes 1179656 | tf_op jit(solution)/shard_map/ppermute | solution.py:866
  24.5 8.7 %collective-permute-start.4 = (bf16[1,32,1536]{2,1,0:T(8,128)(2,1)S(1)}, bf16[1,32,1536]{2,1,0:T(8,128)(2,1)S(1)}, u32[]{:S(2)}, u32[]{:S(2)}) collective-permute-start(bf16[1,32,1536]{2,1,0:T(8,128)(2,1)S(1)} %bitcast.21), channel_id=1, source_target_pairs={{0,16},{2,18},{4,20},{6,22},{8,24},{10,26},{12,28},{14,30},{16,0},... | collective-permute-start | bytes 294920 | tf_op jit(solution)/shard_map/ppermute | solution.py:866
  26.3 8.2 %collective-permute-start.5 = (bf16[1,32,1536]{2,1,0:T(8,128)(2,1)S(1)}, bf16[1,32,1536]{2,1,0:T(8,128)(2,1)S(1)}, u32[]{:S(2)}, u32[]{:S(2)}) collective-permute-start(bf16[1,32,1536]{2,1,0:T(8,128)(2,1)S(1)} %bitcast.22), channel_id=1, source_target_pairs={{0,8},{2,10},{4,12},{6,14},{8,0},{10,2},{12,4},{14,6},{16,24},{18,... | collective-permute-start | bytes 294920 | tf_op jit(solution)/shard_map/ppermute | solution.py:866
  28.7 8.8 %collective-permute-start.6 = (bf16[1,32,1536]{2,1,0:T(8,128)(2,1)S(1)}, bf16[1,32,1536]{2,1,0:T(8,128)(2,1)S(1)}, u32[]{:S(2)}, u32[]{:S(2)}) collective-permute-start(bf16[1,32,1536]{2,1,0:T(8,128)(2,1)S(1)} %bitcast.23), channel_id=1, source_target_pairs={{0,24},{2,26},{4,28},{6,30},{8,16},{10,18},{12,20},{14,22},{16,8},... | collective-permute-start | bytes 294920 | tf_op jit(solution)/shard_map/ppermute | solution.py:866
  29.1 9.7 %collective-permute-start.8 = (bf16[512,256]{1,0:T(8,128)(2,1)S(1)}, bf16[512,256]{1,0:T(8,128)(2,1)S(1)}, u32[]{:S(2)}, u32[]{:S(2)}) collective-permute-start(bf16[512,256]{1,0:T(8,128)(2,1)S(1)} %copy-done.5), channel_id=1, source_target_pairs={{1,0},{0,1},{3,2},{2,3},{5,4},{4,5},{7,6},{6,7},{9,8},{8,9},{11,10... | collective-permute-start | bytes 786440 | tf_op jit(solution)/shard_map/ppermute | solution.py:861
  33.2 9.1 %collective-permute-start.10 = (bf16[384,512]{1,0:T(8,128)(2,1)S(1)}, bf16[384,512]{1,0:T(8,128)(2,1)S(1)}, u32[]{:S(2)}, u32[]{:S(2)}) collective-permute-start(bf16[384,512]{1,0:T(8,128)(2,1)S(1)} %get-tuple-element.274), channel_id=1, source_target_pairs={{2,0},{4,2},{6,4},{8,6},{10,8},{12,10},{14,12},{16,14},{18,16},{20... | collective-permute-start | bytes 1179656 | tf_op jit(solution)/shard_map/ppermute | solution.py:1041
  34.5 8.3 %collective-permute-start.9 = (bf16[384,512]{1,0:T(8,128)(2,1)S(1)}, bf16[384,512]{1,0:T(8,128)(2,1)S(1)}, u32[]{:S(2)}, u32[]{:S(2)}) collective-permute-start(bf16[384,512]{1,0:T(8,128)(2,1)S(1)} %get-tuple-element.275), channel_id=1, source_target_pairs={{0,2},{2,4},{4,6},{6,8},{8,10},{10,12},{12,14},{14,16},{16,18},{18... | collective-permute-start | bytes 1179656 | tf_op jit(solution)/shard_map/ppermute | solution.py:1040
  37.6 16.8 %collective-permute-start.17 = (bf16[2,32,1024]{2,1,0:T(8,128)(2,1)S(1)}, bf16[2,32,1024]{2,1,0:T(8,128)(2,1)S(1)}, u32[]{:S(2)}, u32[]{:S(2)}) collective-permute-start(bf16[2,32,1024]{2,1,0:T(8,128)(2,1)S(1)} %pad_maximum_fusion.3), channel_id=1, source_target_pairs={{0,16},{2,18},{4,20},{6,22},{8,24},{10,26},{12,28},{14,30},{16,0},... | collective-permute-start | bytes 393224 | tf_op jit(solution)/shard_map/ppermute | solution.py:866
  38.8 18.3 %collective-permute-start.18 = (bf16[2,32,1024]{2,1,0:T(8,128)(2,1)S(1)}, bf16[2,32,1024]{2,1,0:T(8,128)(2,1)S(1)}, u32[]{:S(2)}, u32[]{:S(2)}) collective-permute-start(bf16[2,32,1024]{2,1,0:T(8,128)(2,1)S(1)} %pad_maximum_fusion.3), channel_id=1, source_target_pairs={{0,8},{2,10},{4,12},{6,14},{8,0},{10,2},{12,4},{14,6},{16,24},{18,... | collective-permute-start | bytes 393224 | tf_op jit(solution)/shard_map/ppermute | solution.py:866
  41.4 15.7 %collective-permute-start.19 = (bf16[2,32,1024]{2,1,0:T(8,128)(2,1)S(1)}, bf16[2,32,1024]{2,1,0:T(8,128)(2,1)S(1)}, u32[]{:S(2)}, u32[]{:S(2)}) collective-permute-start(bf16[2,32,1024]{2,1,0:T(8,128)(2,1)S(1)} %pad_maximum_fusion.3), channel_id=1, source_target_pairs={{0,24},{2,26},{4,28},{6,30},{8,16},{10,18},{12,20},{14,22},{16,8},... | collective-permute-start | bytes 393224 | tf_op jit(solution)/shard_map/ppermute | solution.py:866
  42.3 10.9 %collective-permute-start.14 = (bf16[4,32,1536]{2,1,0:T(8,128)(2,1)S(1)}, bf16[4,32,1536]{2,1,0:T(8,128)(2,1)S(1)}, u32[]{:S(2)}, u32[]{:S(2)}) collective-permute-start(bf16[4,32,1536]{2,1,0:T(8,128)(2,1)S(1)} %pad_maximum_fusion.1), channel_id=1, source_target_pairs={{0,4},{2,6},{4,0},{6,2},{8,12},{10,14},{12,8},{14,10},{16,20},{18,... | collective-permute-start | bytes 1179656 | tf_op jit(solution)/shard_map/ppermute | solution.py:866
  48.3 8.8 %collective-permute-start.15 = (bf16[256,256]{1,0:T(8,128)(2,1)S(1)}, bf16[256,256]{1,0:T(8,128)(2,1)S(1)}, u32[]{:S(2)}, u32[]{:S(2)}) collective-permute-start(bf16[256,256]{1,0:T(8,128)(2,1)S(1)} %get-tuple-element.155.own_ref.refs_4_), channel_id=1, source_target_pairs={{1,0},{0,1},{3,2},{2,3},{5,4},{4,5},{7,6},{6,7},{9,8},{8,9},{11,10... | collective-permute-start | bytes 393224 | tf_op jit(solution)/shard_map/ppermute | solution.py:861
  53.2 13.5 %collective-permute-start.13 = (bf16[256,256]{1,0:T(8,128)(2,1)S(1)}, bf16[256,256]{1,0:T(8,128)(2,1)S(1)}, u32[]{:S(2)}, u32[]{:S(2)}) collective-permute-start(bf16[256,256]{1,0:T(8,128)(2,1)S(1)} %get-tuple-element.158.own_ref.refs_5_), channel_id=1, source_target_pairs={{1,0},{0,1},{3,2},{2,3},{5,4},{4,5},{7,6},{6,7},{9,8},{8,9},{11,10... | collective-permute-start | bytes 393224 | tf_op jit(solution)/shard_map/ppermute | solution.py:861
  54.4 7.9 %collective-permute-start.16 = (bf16[8,32,1536]{2,1,0:T(8,128)(2,1)S(1)}, bf16[8,32,1536]{2,1,0:T(8,128)(2,1)S(1)}, u32[]{:S(2)}, u32[]{:S(2)}) collective-permute-start(bf16[8,32,1536]{2,1,0:T(8,128)(2,1)S(1)} %constant_dynamic-update-slice_fusion.7.near_ref), channel_id=1, source_target_pairs={{0,2},{2,0},{4,6},{6,4},{8,10},{10,8},{12,14},{14,12},{16,18},{18,... | collective-permute-start | bytes 2359304 | tf_op jit(solution)/shard_map/ppermute | solution.py:866
  57.1 6.0 %collective-permute-start.20 = (bf16[8,32,1024]{2,1,0:T(8,128)(2,1)S(1)}, bf16[8,32,1024]{2,1,0:T(8,128)(2,1)S(1)}, u32[]{:S(2)}, u32[]{:S(2)}) collective-permute-start(bf16[8,32,1024]{2,1,0:T(8,128)(2,1)S(1)} %constant_dynamic-update-slice_fusion.9.near_ref), channel_id=1, source_target_pairs={{0,2},{2,0},{4,6},{6,4},{8,10},{10,8},{12,14},{14,12},{16,18},{18,... | collective-permute-start | bytes 1572872 | tf_op jit(solution)/shard_map/ppermute | solution.py:866
  63.1 1.0 copy-start.2
  66.3 4.4 %copy-start.1 = (s32[1,33]{1,0:T(1,128)S(1)}, s32[1,33]{1,0:T(1,128)}, u32[]{:S(2)}) copy-start(s32[1,33]{1,0:T(1,128)} %lengths_ref.7) | copy-start | bytes 400
  66.3 9.2 %collective-permute-start.21 = (bf16[256,512]{1,0:T(8,128)(2,1)S(1)}, bf16[256,512]{1,0:T(8,128)(2,1)S(1)}, u32[]{:S(2)}, u32[]{:S(2)}) collective-permute-start(bf16[256,512]{1,0:T(8,128)(2,1)S(1)} %get-tuple-element.168.part_ref), channel_id=1, source_target_pairs={{1,0},{0,1},{3,2},{2,3},{5,4},{4,5},{7,6},{6,7},{9,8},{8,9},{11,10... | collective-permute-start | bytes 786440 | tf_op jit(solution)/shard_map/ppermute | solution.py:861
  68.9 12.2 %collective-permute-start.22 = (bf16[256,512]{1,0:T(8,128)(2,1)S(1)}, bf16[256,512]{1,0:T(8,128)(2,1)S(1)}, u32[]{:S(2)}, u32[]{:S(2)}) collective-permute-start(bf16[256,512]{1,0:T(8,128)(2,1)S(1)} %get-tuple-element.170.part_ref), channel_id=1, source_target_pairs={{1,0},{0,1},{3,2},{2,3},{5,4},{4,5},{7,6},{6,7},{9,8},{8,9},{11,10... | collective-permute-start | bytes 786440 | tf_op jit(solution)/shard_map/ppermute | solution.py:861
  77.9 8.7 %collective-permute-start.23 = (bf16[256,512]{1,0:T(8,128)(2,1)S(1)}, bf16[256,512]{1,0:T(8,128)(2,1)S(1)}, u32[]{:S(2)}, u32[]{:S(2)}) collective-permute-start(bf16[256,512]{1,0:T(8,128)(2,1)S(1)} %get-tuple-element.184.part_ref), channel_id=1, source_target_pairs={{1,0},{0,1},{3,2},{2,3},{5,4},{4,5},{7,6},{6,7},{9,8},{8,9},{11,10... | collective-permute-start | bytes 786440 | tf_op jit(solution)/shard_map/ppermute | solution.py:861
  90.8 5.0 %collective-permute-start.24 = (bf16[256,1024]{1,0:T(8,128)(2,1)S(1)}, bf16[256,1024]{1,0:T(8,128)(2,1)S(1)}, u32[]{:S(2)}, u32[]{:S(2)}) collective-permute-start(bf16[256,1024]{1,0:T(8,128)(2,1)S(1)} %get-tuple-element.207), channel_id=1, source_target_pairs={{0,2},{2,0},{4,6},{6,4},{8,10},{10,8},{12,14},{14,12},{16,18},{18,... | collective-permute-start | bytes 1572872 | tf_op jit(solution)/shard_map/ppermute | solution.py:866
  90.9 8.5 %collective-permute-start.25 = (bf16[256,1024]{1,0:T(8,128)(2,1)S(1)}, bf16[256,1024]{1,0:T(8,128)(2,1)S(1)}, u32[]{:S(2)}, u32[]{:S(2)}) collective-permute-start(bf16[256,1024]{1,0:T(8,128)(2,1)S(1)} %get-tuple-element.210), channel_id=1, source_target_pairs={{0,2},{2,0},{4,6},{6,4},{8,10},{10,8},{12,14},{14,12},{16,18},{18,... | collective-permute-start | bytes 1572872 | tf_op jit(solution)/shard_map/ppermute | solution.py:866
  91.3 8.3 %collective-permute-start.26 = (bf16[256,512]{1,0:T(8,128)(2,1)S(1)}, bf16[256,512]{1,0:T(8,128)(2,1)S(1)}, u32[]{:S(2)}, u32[]{:S(2)}) collective-permute-start(bf16[256,512]{1,0:T(8,128)(2,1)S(1)} %get-tuple-element.181.part_ref), channel_id=1, source_target_pairs={{1,0},{0,1},{3,2},{2,3},{5,4},{4,5},{7,6},{6,7},{9,8},{8,9},{11,10... | collective-permute-start | bytes 786440 | tf_op jit(solution)/shard_map/ppermute | solution.py:861
  95.9 11.6 %collective-permute-start.28 = (bf16[128,1024]{1,0:T(8,128)(2,1)S(1)}, bf16[128,1024]{1,0:T(8,128)(2,1)S(1)}, u32[]{:S(2)}, u32[]{:S(2)}) collective-permute-start(bf16[128,1024]{1,0:T(8,128)(2,1)S(1)} %get-tuple-element.231), channel_id=1, source_target_pairs={{0,4},{2,6},{4,0},{6,2},{8,12},{10,14},{12,8},{14,10},{16,20},{18,... | collective-permute-start | bytes 786440 | tf_op jit(solution)/shard_map/ppermute | solution.py:866
  109.5 35.1 %collective-permute-start.32 = (bf16[1056,256]{1,0:T(8,128)(2,1)S(1)}, bf16[1056,256]{1,0:T(8,128)(2,1)S(1)}, u32[]{:S(2)}, u32[]{:S(2)}) collective-permute-start(bf16[1056,256]{1,0:T(8,128)(2,1)S(1)} %get-tuple-element.242), channel_id=1, source_target_pairs={{0,2},{2,0},{4,6},{6,4},{8,10},{10,8},{12,14},{14,12},{16,18},{18,... | collective-permute-start | bytes 1622024 | tf_op jit(solution)/shard_map/ppermute | solution.py:866
  109.5 32.6 %collective-permute-start.27 = (bf16[384,512]{1,0:T(8,128)(2,1)S(1)}, bf16[384,512]{1,0:T(8,128)(2,1)S(1)}, u32[]{:S(2)}, u32[]{:S(2)}) collective-permute-start(bf16[384,512]{1,0:T(8,128)(2,1)S(1)} %get-tuple-element.226), channel_id=1, source_target_pairs={{0,2},{2,4},{4,6},{6,8},{8,10},{10,12},{12,14},{14,16},{16,18},{18... | collective-permute-start | bytes 1179656 | tf_op jit(solution)/shard_map/ppermute | solution.py:1132
  112.0 32.8 %collective-permute-start.33 = (bf16[384,512]{1,0:T(8,128)(2,1)S(1)}, bf16[384,512]{1,0:T(8,128)(2,1)S(1)}, u32[]{:S(2)}, u32[]{:S(2)}) collective-permute-start(bf16[384,512]{1,0:T(8,128)(2,1)S(1)} %get-tuple-element.229), channel_id=1, source_target_pairs={{2,0},{4,2},{6,4},{8,6},{10,8},{12,10},{14,12},{16,14},{18,16},{20... | collective-permute-start | bytes 1179656 | tf_op jit(solution)/shard_map/ppermute | solution.py:1133
  113.3 17.6 %collective-permute-start.29 = (bf16[64,1024]{1,0:T(8,128)(2,1)S(1)}, bf16[64,1024]{1,0:T(8,128)(2,1)S(1)}, u32[]{:S(2)}, u32[]{:S(2)}) collective-permute-start(bf16[64,1024]{1,0:T(8,128)(2,1)S(1)} %get-tuple-element.237), channel_id=1, source_target_pairs={{0,16},{2,18},{4,20},{6,22},{8,24},{10,26},{12,28},{14,30},{16,0},... | collective-permute-start | bytes 393224 | tf_op jit(solution)/shard_map/ppermute | solution.py:866
  120.2 12.3 %collective-permute-start.30 = (bf16[64,1024]{1,0:T(8,128)(2,1)S(1)}, bf16[64,1024]{1,0:T(8,128)(2,1)S(1)}, u32[]{:S(2)}, u32[]{:S(2)}) collective-permute-start(bf16[64,1024]{1,0:T(8,128)(2,1)S(1)} %get-tuple-element.238), channel_id=1, source_target_pairs={{0,8},{2,10},{4,12},{6,14},{8,0},{10,2},{12,4},{14,6},{16,24},{18,... | collective-permute-start | bytes 393224 | tf_op jit(solution)/shard_map/ppermute | solution.py:866
  130.9 7.9 %collective-permute-start.31 = (bf16[64,1024]{1,0:T(8,128)(2,1)S(1)}, bf16[64,1024]{1,0:T(8,128)(2,1)S(1)}, u32[]{:S(2)}, u32[]{:S(2)}) collective-permute-start(bf16[64,1024]{1,0:T(8,128)(2,1)S(1)} %get-tuple-element.239), channel_id=1, source_target_pairs={{0,24},{2,26},{4,28},{6,30},{8,16},{10,18},{12,20},{14,22},{16,8},... | collective-permute-start | bytes 393224 | tf_op jit(solution)/shard_map/ppermute | solution.py:866
  138.8 15.9 %collective-permute-start.40 = (bf16[32,1024]{1,0:T(8,128)(2,1)S(1)}, bf16[32,1024]{1,0:T(8,128)(2,1)S(1)}, u32[]{:S(2)}, u32[]{:S(2)}) collective-permute-start(bf16[32,1024]{1,0:T(8,128)(2,1)S(1)} %get-tuple-element.266), channel_id=1, source_target_pairs={{0,16},{2,18},{4,20},{6,22},{8,24},{10,26},{12,28},{14,30},{16,0},... | collective-permute-start | bytes 196616 | tf_op jit(solution)/shard_map/ppermute | solution.py:866
  141.7 13.0 %collective-permute-start.41 = (bf16[32,1024]{1,0:T(8,128)(2,1)S(1)}, bf16[32,1024]{1,0:T(8,128)(2,1)S(1)}, u32[]{:S(2)}, u32[]{:S(2)}) collective-permute-start(bf16[32,1024]{1,0:T(8,128)(2,1)S(1)} %get-tuple-element.267), channel_id=1, source_target_pairs={{0,8},{2,10},{4,12},{6,14},{8,0},{10,2},{12,4},{14,6},{16,24},{18,... | collective-permute-start | bytes 196616 | tf_op jit(solution)/shard_map/ppermute | solution.py:866
  142.2 12.5 %collective-permute-start.42 = (bf16[32,1024]{1,0:T(8,128)(2,1)S(1)}, bf16[32,1024]{1,0:T(8,128)(2,1)S(1)}, u32[]{:S(2)}, u32[]{:S(2)}) collective-permute-start(bf16[32,1024]{1,0:T(8,128)(2,1)S(1)} %get-tuple-element.268), channel_id=1, source_target_pairs={{0,24},{2,26},{4,28},{6,30},{8,16},{10,18},{12,20},{14,22},{16,8},... | collective-permute-start | bytes 196616 | tf_op jit(solution)/shard_map/ppermute | solution.py:866
  144.6 4.3 %collective-permute-start.39 = (bf16[32,1024]{1,0:T(8,128)(2,1)S(1)}, bf16[32,1024]{1,0:T(8,128)(2,1)S(1)}, u32[]{:S(2)}, u32[]{:S(2)}) collective-permute-start(bf16[32,1024]{1,0:T(8,128)(2,1)S(1)} %get-tuple-element.264), channel_id=1, source_target_pairs={{0,4},{2,6},{4,0},{6,2},{8,12},{10,14},{12,8},{14,10},{16,20},{18,... | collective-permute-start | bytes 196616 | tf_op jit(solution)/shard_map/ppermute | solution.py:866
  145.0 10.3 %collective-permute-start.35 = (bf16[544,256]{1,0:T(8,128)(2,1)S(1)}, bf16[544,256]{1,0:T(8,128)(2,1)S(1)}, u32[]{:S(2)}, u32[]{:S(2)}) collective-permute-start(bf16[544,256]{1,0:T(8,128)(2,1)S(1)} %get-tuple-element.250), channel_id=1, source_target_pairs={{0,4},{2,6},{4,0},{6,2},{8,12},{10,14},{12,8},{14,10},{16,20},{18,... | collective-permute-start | bytes 835592 | tf_op jit(solution)/shard_map/ppermute | solution.py:866
  148.9 11.0 %collective-permute-start.34 = (bf16[512,256]{1,0:T(8,128)(2,1)S(1)}, bf16[512,256]{1,0:T(8,128)(2,1)S(1)}, u32[]{:S(2)}, u32[]{:S(2)}) collective-permute-start(bf16[512,256]{1,0:T(8,128)(2,1)S(1)} %slice.99), channel_id=1, source_target_pairs={{1,0},{0,1},{3,2},{2,3},{5,4},{4,5},{7,6},{6,7},{9,8},{8,9},{11,10... | collective-permute-start | bytes 786440 | tf_op jit(solution)/shard_map/ppermute | solution.py:861
  155.4 6.3 %collective-permute-start.36 = (bf16[160,256]{1,0:T(8,128)(2,1)S(1)}, bf16[160,256]{1,0:T(8,128)(2,1)S(1)}, u32[]{:S(2)}, u32[]{:S(2)}) collective-permute-start(bf16[160,256]{1,0:T(8,128)(2,1)S(1)} %get-tuple-element.254), channel_id=1, source_target_pairs={{0,16},{2,18},{4,20},{6,22},{8,24},{10,26},{12,28},{14,30},{16,0},... | collective-permute-start | bytes 245768 | tf_op jit(solution)/shard_map/ppermute | solution.py:866
  156.8 5.0 %collective-permute-start.37 = (bf16[160,256]{1,0:T(8,128)(2,1)S(1)}, bf16[160,256]{1,0:T(8,128)(2,1)S(1)}, u32[]{:S(2)}, u32[]{:S(2)}) collective-permute-start(bf16[160,256]{1,0:T(8,128)(2,1)S(1)} %get-tuple-element.255), channel_id=1, source_target_pairs={{0,8},{2,10},{4,12},{6,14},{8,0},{10,2},{12,4},{14,6},{16,24},{18,... | collective-permute-start | bytes 245768 | tf_op jit(solution)/shard_map/ppermute | solution.py:866
  157.7 6.2 %collective-permute-start.38 = (bf16[160,256]{1,0:T(8,128)(2,1)S(1)}, bf16[160,256]{1,0:T(8,128)(2,1)S(1)}, u32[]{:S(2)}, u32[]{:S(2)}) collective-permute-start(bf16[160,256]{1,0:T(8,128)(2,1)S(1)} %get-tuple-element.256), channel_id=1, source_target_pairs={{0,24},{2,26},{4,28},{6,30},{8,16},{10,18},{12,20},{14,22},{16,8},... | collective-permute-start | bytes 245768 | tf_op jit(solution)/shard_map/ppermute | solution.py:866

commit v3 on v2

--- a/solution.py
+++ b/solution.py
@@ -111,7 +111,7 @@
         out_specs=heads_block(heads, WINDOW),
         out_shape=struct((heads, count, WINDOW), BF16),
         compiler_params=params(),
-        cost_estimate=lasting(1.0),
+        cost_estimate=lasting(8.0 if fill else 1.0),
         name="to_dense",
     )(lengths, base, banded)
 
@@ -189,31 +189,69 @@
     return joined
 
 
+def join_kernel(even_ref, *refs):
+    *part_refs, all_ref, inside_ref, across_ref = refs
+    count = all_ref.shape[0]
+    width = part_refs[0].shape[1]
+    even = even_ref[0] == 1
+    for place, ref in enumerate(part_refs):
+        lanes = slice(place * width, (place + 1) * width)
+        all_ref[:, lanes] = ref[...]
+        tail, head = ref[count - HALO :, :], ref[:HALO, :]
+        inside_ref[:, lanes] = jnp.where(even, tail, head)
+        across_ref[:, lanes] = jnp.where(even, head, tail)
+
+
+def join(even, parts):
+    count, width = parts[0].shape
+    features = len(parts) * width
+    shapes = ((count, features), (HALO, features), (HALO, features))
+    return pl.pallas_call(
+        join_kernel,
+        grid=(1,),
+        in_specs=[pl.BlockSpec(memory_space=SMEM)] + [whole(x.shape) for x in parts],
+        out_specs=[whole(shape) for shape in shapes],
+        out_shape=[struct(shape, BF16) for shape in shapes],
+        compiler_params=params(),
+        cost_estimate=lasting(0.5),
+        name="join",
+    )(even, *parts)
+
+
 def project_kernel(
-    slot_ref, token_ref, low_ref, high_ref, near_ref, far_ref, bias_ref,
-    query_ref, key_ref, value_ref, weight_ref,
+    slot_ref, even_ref, token_ref, inside_ref, across_ref, near_ref, far_ref, bias_ref,
+    query_ref, key_ref, value_ref, low_ref, high_ref, *weight_refs,
 ):
-    half, _, depth, width = near_ref.shape
+    half, _, depth, _ = near_ref.shape
     count = token_ref.shape[0]
+
+    def put(place, source_ref, slot):
+        for which, ref in enumerate(weight_refs):
+            ref[place * depth : (place + 1) * depth, :] = source_ref[slot, which]
+
     for place in range(2 * half):
         slot = slot_ref[place]
 
         @pl.when(slot < half)
         def _():
-            weight_ref[:, place * depth : (place + 1) * depth, :] = near_ref[slot]
+            put(place, near_ref, slot)
 
         @pl.when(slot >= half)
         def _():
-            weight_ref[:, place * depth : (place + 1) * depth, :] = far_ref[slot - half]
-
-    low_rows, high_rows = low_ref[...], high_ref[...]
+            put(place, far_ref, slot - half)
+
+    even = even_ref[0] == 1
+    inside, across = inside_ref[...], across_ref[...]
+    low_rows, high_rows = jnp.where(even, across, inside), jnp.where(even, inside, across)
+    low_ref[...] = low_rows
+    high_ref[...] = high_rows
     own = token_ref[...]
-    empty = jnp.zeros((PAD, width), BF16)
-    query = (dot_nn(own, weight_ref[0]) + bias_ref[0:1, :]).astype(BF16)
+    query = (dot_nn(own, weight_refs[0][...]) + bias_ref[0:1, :]).astype(BF16)
+    empty = jnp.zeros((PAD, query.shape[1]), BF16)
     query_ref[...] = query * jnp.asarray(HEAD_DIM ** (-0.5), BF16)
     for out_ref, which in ((key_ref, 1), (value_ref, 2)):
         shift = bias_ref[1:2, :] if which == 2 else 0.0
-        weight = weight_ref[which]
+        weight = weight_refs[which][...]
         out_ref[0:PAD, :] = empty
         out_ref[PAD:MAXDOC, :] = (dot_nn(low_rows, weight) + shift).astype(BF16)
         out_ref[MAXDOC : MAXDOC + count, :] = (dot_nn(own, weight) + shift).astype(BF16)
@@ -223,21 +261,23 @@
         out_ref[MAXDOC + count + HALO :, :] = empty
 
 
-def project(slots, tokens, low, high, near, far, bias):
+def project(slots, even, tokens, inside, across, near, far, bias):
     count, features = tokens.shape
     width = near.shape[3]
-    operands = (tokens, low, high, near, far, bias)
-    shapes = ((count, width), (count + BAND, width), (count + BAND, width), (3, features, width))
+    operands = (tokens, inside, across, near, far, bias)
+    extended = (count + BAND, width)
+    shapes = [(count, width), extended, extended, inside.shape, across.shape]
+    shapes += [(features, width)] * 3
     return pl.pallas_call(
         project_kernel,
         grid=(1,),
-        in_specs=[pl.BlockSpec(memory_space=SMEM)] + [whole(x.shape) for x in operands],
+        in_specs=[pl.BlockSpec(memory_space=SMEM)] * 2 + [whole(x.shape) for x in operands],
         out_specs=[whole(shape) for shape in shapes],
         out_shape=[struct(shape, BF16) for shape in shapes],
         compiler_params=params(),
         cost_estimate=lasting(2.0),
         name="project",
-    )(slots, *operands)
+    )(slots, even, *operands)
 
 
 def forward_kernel(
@@ -371,7 +411,7 @@
         + end_shapes,
         scratch_shapes=scratch,
         compiler_params=params(),
-        cost_estimate=lasting(1.4),
+        cost_estimate=lasting(3.0 if last else 20.0),
         name="attend_backward",
     )(grad, query, key, value, prob, logit, *(sums or ()))
 
@@ -436,11 +476,10 @@
 
 
 def first_kernel(
-    own_ref, other_ref, token_ref, out_ref, up_ref, down_ref, norm_ref, up_bias_ref,
-    normed_ref, inverse_ref, upper_ref, act_ref, slope_ref, part_ref,
+    own_ref, other_ref, token_ref, other_out_ref, out_ref, up_ref, down_ref, norm_ref,
+    up_bias_ref, normed_ref, inverse_ref, upper_ref, act_ref, slope_ref, part_ref,
 ):
-    width = own_ref.shape[1]
-    branch = dot_nt(own_ref[...], out_ref[:, :width]) + dot_nt(other_ref[...], out_ref[:, width:])
+    branch = dot_nt(own_ref[...], out_ref[...]) + dot_nt(other_ref[...], other_out_ref[...])
     hidden = token_ref[...].astype(F32) + branch + norm_ref[4:5, :]
     normed, inverse = normalized(hidden)
     normed_ref[...] = normed
@@ -455,7 +494,7 @@
     part_ref[...] = dot_nt(act, down_ref[...]).astype(BF16)
 
 
-def feed_first(own, other, tokens, weights, norms, up_bias, chunk):
+def feed_first(own, other, tokens, other_out, weights, norms, up_bias, chunk):
     count, width = own.shape
     features = tokens.shape[1]
     units = up_bias.shape[1]
@@ -466,7 +505,8 @@
             rows(width),
             rows(other.shape[1]),
             rows(features, chunk * (count // BLOCK)),
-            *weight_blocks(features, units),
+            whole(other_out.shape),
+            *(whole(x.shape) for x in weights),
             whole(norms.shape),
             whole(up_bias.shape),
         ],
@@ -489,15 +529,7 @@
         compiler_params=params(),
         cost_estimate=lasting(1.0),
         name="feed_first",
-    )(own, other, tokens, *weights, norms, up_bias)
-
-
-def weight_blocks(features, units):
-    return [
-        pl.BlockSpec((features, features), lambda b: (0, 0)),
-        pl.BlockSpec((features, units), lambda b: (0, 0)),
-        pl.BlockSpec((features, units), lambda b: (0, 0)),
-    ]
+    )(own, other, tokens, other_out, *weights, norms, up_bias)
 
 
 def add_sums(start_ref, sum_ref, first, values):
@@ -555,7 +587,7 @@
             rows(features),
             rows(features, offset),
             rows(units),
-            *weight_blocks(features, units)[1:],
+            *(whole(x.shape) for x in weights[1:]),
             whole(norms.shape),
             *([] if held is None else [pl.BlockSpec(memory_space=pl.ANY)]),
         ],
@@ -593,7 +625,7 @@
     own_ref[...] = res[:, :own]
     low = res.astype(BF16)
     low_ref[...] = low
-    attended_ref[...] = dot_nn(low, out_ref[:, : attended_ref.shape[1]]).astype(BF16)
+    attended_ref[...] = dot_nn(low, out_ref[...]).astype(BF16)
     add_sums(start_ref, sum_ref, 2, [low[:, :own].astype(F32)])
     for place, value in ((4, grad[:, :own] * normed[:, :own]), (6, grad[:, :own])):
         sum_ref[place : place + 1, :] += jnp.sum(value, 0, keepdims=True)
@@ -612,7 +644,7 @@
             rows(features),
             rows(features),
             rows(1),
-            whole((features, features)),
+            whole(weights[0].shape),
             whole(norms.shape),
         ],
         out_specs=[whole(sums.shape), rows(features), rows(width), rows(own)],
@@ -649,37 +681,36 @@
     return high, low, high.astype(F32) + low.astype(F32)
 
 
-def feed_grad_kernel(up_block_ref, down_block_ref, *refs):
+def feed_grad_kernel(block_ref, *refs):
     low_refs, upper_refs, act_refs, hidden_refs = (
         refs[k * CHUNKS : (k + 1) * CHUNKS] for k in range(4)
     )
-    up_keep, up_send, down_keep, down_send, scratch = refs[4 * CHUNKS :]
+    keep_ref, send_ref, scratch = refs[4 * CHUNKS :]
     scratch[...] = sum(dot_tn(a[...], b[...]) for a, b in zip(upper_refs, hidden_refs))
-    spread_rows(up_block_ref, scratch, up_keep, up_send, 0, 1)
+    spread_rows(block_ref, scratch, keep_ref, send_ref, 0, 2)
     scratch[...] = sum(dot_tn(a[...], b[...]) for a, b in zip(low_refs, act_refs))
-    spread_rows(down_block_ref, scratch, down_keep, down_send, 0, 1)
-
-
-def feed_grads(up_blocks, down_blocks, low, act, upper, hidden):
+    spread_rows(block_ref, scratch, keep_ref, send_ref, 1, 2)
+
+
+def feed_grads(blocks, low, act, upper, hidden):
     count, features = low[0].shape
     units = act[0].shape[1]
     chunk = min(256, units)
     column = pl.BlockSpec((count, chunk), lambda b: (0, b))
-    height = features // 2
-    result = pl.BlockSpec((height, chunk), lambda b: (0, b))
+    result = pl.BlockSpec((features, chunk), lambda b: (0, b))
     return pl.pallas_call(
         feed_grad_kernel,
         grid=(units // chunk,),
-        in_specs=[pl.BlockSpec(memory_space=SMEM)] * 2
+        in_specs=[pl.BlockSpec(memory_space=SMEM)]
         + [whole((count, features))] * (2 * CHUNKS)
         + [column] * (2 * CHUNKS),
-        out_specs=[result] * 4,
-        out_shape=[struct((height, units), F32), struct((height, units), BF16)] * 2,
+        out_specs=[result] * 2,
+        out_shape=[struct((features, units), F32), struct((features, units), BF16)],
         scratch_shapes=[pltpu.VMEM((features, chunk), F32)],
         compiler_params=params(),
         cost_estimate=lasting(1.0),
         name="feed_grads",
-    )(up_blocks, down_blocks, *low, *upper, *act, *hidden)
+    )(blocks, *low, *upper, *act, *hidden)
 
 
 def project_grad_kernel(block_ref, start_ref, *refs):
@@ -745,57 +776,33 @@
     )(blocks, *operands)
 
 
-def fold_kernel(arrivals, sends, kinds, *refs):
-    keep_ref, *refs = refs
-    arrived_refs, refs = refs[:arrivals], refs[arrivals:]
+def fold_kernel(with_sums, keep_ref, arrived_ref, *refs):
     height = keep_ref.shape[0]
-    with_sums = arrived_refs[0].shape[0] > height
+    size = height // 2
     if with_sums:
-        start_ref, *refs = refs
-    size = height // (sends + 1)
-
-    def total(first):
-        parts = [ref[first : first + size, :].astype(F32) for ref in arrived_refs]
-        if arrivals == 1:
-            return keep_ref[first : first + size, :] + parts[0]
-        return (keep_ref[first : first + size, :] + parts[0]) + (parts[1] + parts[2])
-
-    stays = total(0)
-    depth = size // kinds
-    for kind in range(kinds):
-        refs[kind][...] = stays[kind * depth : (kind + 1) * depth, :]
-    send_outs = refs[kinds : kinds + sends]
-    for place, send_out in enumerate(send_outs):
-        send_out[:size, :] = total((place + 1) * size).astype(BF16)
+        start_ref, keep_out, send_out, sum_out = refs
+    else:
+        keep_out, send_out = refs
+    keep_out[...] = keep_ref[:size, :] + arrived_ref[:size, :].astype(F32)
+    send_out[:size, :] = (keep_ref[size:, :] + arrived_ref[size:height, :].astype(F32)).astype(BF16)
     if with_sums:
-        parts = [
-            ref[height : height + SUM_ROWS, :].astype(F32)
-            + ref[height + SUM_ROWS :, :].astype(F32)
-            for ref in arrived_refs
-        ]
-        summed = start_ref[...] + parts[0]
-        if arrivals > 1:
-            summed = summed + (parts[1] + parts[2])
-        sum_out = refs[kinds + sends]
-        if sends:
-            high, low, sum_out[...] = split_sums(summed)
-            for send_out in send_outs:
-                send_out[size : size + SUM_ROWS, :] = high
-                send_out[size + SUM_ROWS :, :] = low
-        else:
-            sum_out[...] = summed
-
-
-def fold(keep, arrived, sums, sends, kinds):
+        high, low, sum_out[...] = split_sums(start_ref[...] + arrived_sums(arrived_ref, height))
+        send_out[size : size + SUM_ROWS, :] = high
+        send_out[size + SUM_ROWS :, :] = low
+
+
+def arrived_sums(ref, height):
+    return ref[height : height + SUM_ROWS, :].astype(F32) + ref[height + SUM_ROWS :, :].astype(F32)
+
+
+def fold(keep, arrived, sums):
     height, width = keep.shape
-    extra = arrived[0].shape[0] - height
-    size = height // (sends + 1)
-    operands = (keep, *arrived) + (() if sums is None else (sums,))
-    shapes = [struct((size // kinds, width), F32)] * kinds
-    shapes += [struct((size + extra, width), BF16)] * sends
+    extra = arrived.shape[0] - height
+    operands = (keep, arrived) + (() if sums is None else (sums,))
+    shapes = [struct((height // 2, width), F32), struct((height // 2 + extra, width), BF16)]
     shapes += [] if sums is None else [struct(sums.shape, F32)]
     result = pl.pallas_call(
-        functools.partial(fold_kernel, len(arrived), sends, kinds),
+        functools.partial(fold_kernel, sums is not None),
         grid=(1,),
         in_specs=[whole(x.shape) for x in operands],
         out_specs=[whole(x.shape) for x in shapes],
@@ -804,56 +811,132 @@
         cost_estimate=lasting(0.2),
         name="fold",
     )(*operands)
-    if not sends:
-        return result
-    return result[0], result[1 : 1 + sends], (None if sums is None else result[-1])
-
-
-def token_grad_kernel(*refs):
+    return result[0], result[1], (None if sums is None else result[2])
+
+
+def finish_kernel(kinds, sum_kinds, keep_ref, arrived_ref, *refs):
+    height = keep_ref.shape[0]
+    if sum_kinds:
+        start_ref, *refs = refs
+    first = 0
+    for kind, ref in zip(kinds, refs):
+        depth = ref.shape[-2]
+        for place in range(kind or 1):
+            rows_here = slice(first, first + depth)
+            total = keep_ref[rows_here, :] + arrived_ref[rows_here, :].astype(F32)
+            if kind:
+                ref[place] = total
+            else:
+                ref[...] = total
+            first += depth
+    if sum_kinds:
+        total = start_ref[...] + arrived_sums(arrived_ref, height)
+        first = 0
+        for kind, ref in zip(sum_kinds, refs[len(kinds) :]):
+            if ref.shape[0] == kind:
+                ref[...] = total[first : first + kind, :]
+            else:
+                ref[...] = jnp.concatenate([total[first + k : first + k + 1] for k in range(kind)], 1)
+            first += kind
+
+
+def finish(keep, arrived, sums, kinds, sum_kinds):
+    height, width = keep.shape
+    depth = height // sum(kind or 1 for kind in kinds)
+    operands = (keep, arrived) + (() if sums is None else (sums,))
+    shapes = [struct((kind, depth, width) if kind else (depth, width), F32) for kind in kinds]
+    shapes += [
+        struct((kind, width) if kind == 2 else (1, kind * width), F32) for kind in sum_kinds
+    ]
+    return pl.pallas_call(
+        functools.partial(finish_kernel, kinds, sum_kinds),
+        grid=(1,),
+        in_specs=[whole(x.shape) for x in operands],
+        out_specs=[whole(x.shape) for x in shapes],
+        out_shape=shapes,
+        compiler_params=params(),
+        cost_estimate=lasting(0.2),
+        name="finish",
+    )(*operands)
+
+
+def token_grad_kernel(even_ref, *refs):
     query_refs, res_refs = refs[:CHUNKS], refs[CHUNKS : 2 * CHUNKS]
-    key_ref, value_ref, weight_ref, low_ref, own_ref, high_ref = refs[2 * CHUNKS :]
+    key_ref, value_ref, *weight_refs, own_ref, inside_ref, across_ref = refs[2 * CHUNKS :]
     count = own_ref.shape[0]
     own = res_refs[0].shape[1]
+    even = even_ref[0] == 1
 
     def piece(start):
-        return dot_nt(key_ref[start : start + BLOCK, :], weight_ref[1]) + dot_nt(
-            value_ref[start : start + BLOCK, :], weight_ref[2]
+        return dot_nt(key_ref[start : start + BLOCK, :], weight_refs[1][...]) + dot_nt(
+            value_ref[start : start + BLOCK, :], weight_refs[2][...]
         )
 
     for start in range(0, HALO, BLOCK):
-        low_ref[start : start + BLOCK, :] = piece(PAD + start).astype(BF16)
-        high_ref[start : start + BLOCK, :] = piece(MAXDOC + count + start).astype(BF16)
+        low = piece(PAD + start).astype(BF16)
+        high = piece(MAXDOC + count + start).astype(BF16)
+        inside_ref[start : start + BLOCK, :] = jnp.where(even, high, low)
+        across_ref[start : start + BLOCK, :] = jnp.where(even, low, high)
     for start in range(0, count, BLOCK):
         chunk, inside = divmod(start, count // CHUNKS)
         total = piece(MAXDOC + start) + dot_nt(
-            query_refs[chunk][inside : inside + BLOCK, :], weight_ref[0]
+            query_refs[chunk][inside : inside + BLOCK, :], weight_refs[0][...]
         )
         own_ref[start : start + BLOCK, :] = total
         own_ref[start : start + BLOCK, :own] += res_refs[chunk][inside : inside + BLOCK, :]
 
 
-def token_grads(query, res, key, value, weight):
+def token_grads(even, query, res, key, value, weights):
     count = CHUNKS * query[0].shape[0]
-    features = weight.shape[1]
-    operands = (*query, *res, key, value, weight)
+    features = weights[0].shape[0]
+    operands = (*query, *res, key, value, *weights)
+    shapes = [struct((count, features), F32)] + [struct((HALO, features), BF16)] * 2
     return pl.pallas_call(
         token_grad_kernel,
         grid=(1,),
-        in_specs=[whole(x.shape) for x in operands],
-        out_specs=[
-            whole((HALO, features)),
-            whole((count, features)),
-            whole((HALO, features)),
-        ],
-        out_shape=[
-            struct((HALO, features), BF16),
-            struct((count, features), F32),
-            struct((HALO, features), BF16),
-        ],
+        in_specs=[pl.BlockSpec(memory_space=SMEM)] + [whole(x.shape) for x in operands],
+        out_specs=[whole(x.shape) for x in shapes],
+        out_shape=shapes,
         compiler_params=params(),
         cost_estimate=lasting(0.6),
         name="token_grads",
-    )(*operands)
+    )(even, *operands)
+
+
+def token_sum_kernel(even_ref, own_ref, inside_ref, across_ref, stays_ref, *leave_refs):
+    even = even_ref[0] == 1
+    width = stays_ref.shape[1]
+    inside, across = inside_ref[...].astype(F32), across_ref[...].astype(F32)
+    low, high = jnp.where(even, across, inside), jnp.where(even, inside, across)
+    rest = own_ref.shape[0] - HALO
+    for start in range(0, own_ref.shape[0], BLOCK):
+        piece = own_ref[start : start + BLOCK, :]
+        if start < HALO:
+            piece = piece + low[start : start + BLOCK, :]
+        if start >= rest:
+            piece = piece + high[start - rest : start - rest + BLOCK, :]
+        stays_ref[start : start + BLOCK, :] = piece[:, :width]
+        for place, ref in enumerate(leave_refs, 1):
+            ref[start : start + BLOCK, :] = piece[:, place * width : (place + 1) * width].astype(
+                BF16
+            )
+
+
+def token_sum(even, own, inside, across, width):
+    count, features = own.shape
+    shapes = [struct((count, width), F32)]
+    shapes += [struct((count, width), BF16)] * (features // width - 1)
+    return pl.pallas_call(
+        token_sum_kernel,
+        grid=(1,),
+        in_specs=[pl.BlockSpec(memory_space=SMEM)]
+        + [whole(x.shape) for x in (own, inside, across)],
+        out_specs=[whole(x.shape) for x in shapes],
+        out_shape=shapes,
+        compiler_params=params(),
+        cost_estimate=lasting(0.3),
+        name="token_sum",
+    )(even, own, inside, across)
 
 
 def from_next(x, axis, step):
@@ -861,11 +944,6 @@
     return lax.ppermute(x, axis, [((i + step) % count, i) for i in range(count)])
 
 
-def with_partner(x, bit):
-    count = lax.axis_size("row")
-    return lax.ppermute(x, "row", [(i, i ^ bit) for i in range(count)])
-
-
 def others(x):
     return [from_next(x, "col", step) for step in range(1, lax.axis_size("col"))]
 
@@ -874,93 +952,72 @@
     return [1 << place for place in range(count.bit_length() - 1)]
 
 
+def orders_of(count):
+    high = bits_of(count)[:0:-1]
+    return high + [1], high[2:] + high[:2] + [1]
+
+
+def slots_of(order, distance):
+    return sum(((distance & bit) // bit) << place for place, bit in enumerate(order))
+
+
+def distances_of(order, slots):
+    return sum(((slots >> place) & 1) * bit for place, bit in enumerate(order))
+
+
+def with_partner(x, step):
+    count = lax.axis_size("row")
+    orders = orders_of(count)
+    return lax.ppermute(x, "row", [(i, i ^ orders[i % 2][step]) for i in range(count)])
+
+
+def with_next(inside, across):
+    count = lax.axis_size("row")
+    pairs = [(i, i + 1 if i % 2 else i - 1) for i in range(1, count - 1)]
+    return (
+        lax.ppermute(inside, "row", [(i, i ^ 1) for i in range(count)]),
+        lax.ppermute(across, "row", pairs),
+    )
+
+
 def after(value, *needed):
     return lax.optimization_barrier((value, *needed))[0]
 
 
-def high_first(count):
-    bits = bits_of(count)[::-1]
-    return [bits[:2], *([bit] for bit in bits[2:])]
-
-
-def high_late(count):
-    bits = bits_of(count)[::-1]
-    return [*([bit] for bit in bits[2:-1]), bits[:2], bits[-1:]]
-
-
-def slots_of(steps, distance):
-    bits = [bit for step in steps for bit in step]
-    return sum(((distance & bit) // bit) << place for place, bit in enumerate(bits))
-
-
-def distances_of(steps, slots):
-    bits = [bit for step in steps for bit in step]
-    return sum(((slots >> place) & 1) * bit for place, bit in enumerate(bits))
-
-
-def partners_of(step):
-    return step if len(step) == 1 else (step[0], step[1], step[0] + step[1])
-
-
-def gather_rows(shard, steps, waits=(), fillers=()):
-    waits, fillers, done = list(waits), list(fillers), []
-    held = shard[None]
-    stages = [held]
-    for place, step in enumerate(steps):
-        arrived = [with_partner(held, bit) for bit in partners_of(step)]
-        if fillers:
-            done.append(fillers.pop(0)(held))
-            *arrived, done[-1] = lax.optimization_barrier((*arrived, done[-1]))
-        if waits:
-            needed = waits.pop(0)
-            if needed is not None:
-                arrived[0] = after(arrived[0], needed)
-        if place < len(steps) - 1:
-            held = jnp.concatenate([held, *arrived], 0)
-            stages.append(held)
-    return stages, arrived[0], done
-
-
 class Gather:
-    def __init__(self, shard, steps):
-        self.held, self.steps = shard[None], list(steps)
+    def __init__(self, shard):
+        self.held, self.step = shard[None], 0
+        self.count = len(bits_of(lax.axis_size("row")))
         self.move()
 
     def move(self):
-        self.arrived = [with_partner(self.held, bit) for bit in partners_of(self.steps.pop(0))]
+        self.arrived = with_partner(self.held, self.step)
+        self.step += 1
 
     def put(self, *needed):
-        while True:
-            arrived = self.arrived
-            self.held = jnp.concatenate([after(self.held, *needed), *arrived], 0)
-            self.move()
-            if len(self.steps) < 2:
-                return
-
-    def last(self):
-        return self.arrived[0]
+        self.held = jnp.concatenate([after(self.held, *needed), self.arrived], 0)
+        self.move()
 
 
 class Reduction:
-    def __init__(self, steps, keep, send, sums, kinds):
-        self.steps = steps[::-1]
-        self.keep, self.send, self.sums, self.kinds = keep, send, sums, kinds
-        self.arrived = None
+    def __init__(self, keep, send, sums, kinds, sum_kinds=()):
+        self.step = len(bits_of(lax.axis_size("row")))
+        self.keep, self.send, self.sums = keep, send, sums
+        self.kinds, self.sum_kinds = kinds, sum_kinds
+        self.result = None
+        self.move()
 
     def move(self):
-        self.step = self.steps.pop(0)
-        self.arrived = [
-            with_partner(x, bit) for x, bit in zip(self.send, partners_of(self.step))
-        ]
+        self.step -= 1
+        self.arrived = with_partner(self.send, self.step)
 
     def add(self, *needed):
         keep = after(self.keep, *needed)
-        if not self.steps:
-            self.result = fold(keep, self.arrived, self.sums, 0, self.kinds)
-            return
-        sends = len(partners_of(self.steps[0]))
-        self.keep, self.send, self.sums = fold(keep, self.arrived, self.sums, sends, 1)
-        self.move()
+        if self.step == 0:
+            self.result = finish(keep, self.arrived, self.sums, self.kinds, self.sum_kinds)
+        else:
+            self.keep, self.send, self.sums = fold(keep, self.arrived, self.sums)
+            self.move()
 
 
 def exchanged(part):
@@ -998,61 +1055,53 @@
     swap = col_count == 2
     hidden_rows = up_bias.shape[0] // own
 
-    early, late = high_first(row_count), high_late(row_count)
+    odd = row_index % 2 == 1
     places = jnp.arange(row_count, dtype=jnp.int32)
     offset = col_index * (row_count // col_count)
     distance = ((places + offset) % row_count) ^ row_index
-    slots, late_slots = slots_of(early, distance), slots_of(late, distance)
-    blocks = ((distances_of(early, places) ^ row_index) - offset) % row_count
-    late_blocks = ((distances_of(late, places) ^ row_index) - offset) % row_count
+    half = row_count // 2
+    even_order, odd_order = (order[:-1] for order in orders_of(row_count))
+    turned = odd ^ (distance % 2 == 1)
+    slots = jnp.where(turned, slots_of(odd_order, distance), slots_of(even_order, distance))
+    slots = slots + half * (distance % 2)
+    turned = odd ^ (places >= half)
+    met = jnp.where(turned, distances_of(odd_order, places), distances_of(even_order, places))
+    blocks = (((met + (places >= half)) ^ row_index) - offset) % row_count
     base = (row_index * count)[None]
 
-    out_turned = out_weight.T
-    norms = jnp.concatenate([norm_gain, norm_shift, out_bias], 0)
-    first = norms.astype(BF16)
-    rest = norms - first.astype(F32)
-    second = rest.astype(BF16)
-    third = (rest - second.astype(F32)).astype(BF16)
-    mixed = jnp.concatenate([tokens, out_turned, first, second, third], 0)
-    arrived = others(mixed)
-    depth = out_turned.shape[0]
-    tokens_full = jnp.concatenate([tokens] + [x[:count] for x in arrived], 1)
-    out_rows = jnp.concatenate([out_turned] + [x[count : count + depth] for x in arrived], 1)
-    pieces = [x[count + depth :].astype(F32).reshape(3, -1, own) for x in arrived]
-    norms = jnp.concatenate([norms] + [(x[0] + x[1]) + x[2] for x in pieces], 1)
-
-    def dense_of(banded, fill, chunk):
-        return lambda held: to_dense(
-            after(banded, held), doc_lengths, base, fill, token_count, chunk
-        )
+    even = 1 - row_index % 2
+    even = even.astype(jnp.int32)[None]
+
+    def dense_of(banded, fill, chunk, *needed):
+        dense = to_dense(after(banded, *needed), doc_lengths, base, fill, token_count, chunk)
+        return dense
 
     prev_logits = pltpu.with_memory_space_constraint(prev_logits, pltpu.HBM)
     logit_grad = pltpu.with_memory_space_constraint(logit_grad, pltpu.HBM)
-    stages, far, prev_dense = gather_rows(
-        qkv_weight,
-        early,
-        (),
-        [dense_of(prev_logits, MASKED_SCORE, 0), dense_of(prev_logits, MASKED_SCORE, 1)],
-    )
-    near = stages[-1]
-    forward = [(i, i + 1) for i in range(row_count - 1)]
-    backward = [(b, a) for a, b in forward]
-    low_tokens = lax.ppermute(tokens_full[count - HALO :], "row", forward)
-    high_tokens = lax.ppermute(tokens_full[:HALO], "row", backward)
-    grad_full = jnp.concatenate([out_grad] + others(after(out_grad, tokens_full)), 1)
-
-    scores, probs, attended, attended_other, logit_dense = [], [], [], [], []
-    up_shard = after(jnp.concatenate([out_rows, up_weight], 1), stages[1])
-    down_shard = after(down_weight.T, stages[0])
-
-    up_gather = Gather(up_shard, early)
-    down_gather = Gather(down_shard, late)
-    up_gather.put()
-    down_gather.put()
-    query, key, value, weight = project(
-        slots, after(tokens_full, up_gather.held, down_gather.held, grad_full), low_tokens,
-        high_tokens, near, far, qv_bias,
-    )
+
+    out_turned = out_weight.T
+    out_other = others(out_turned)
+    qkv_rows = Gather(qkv_weight)
+    tokens_full, inside, across = join(even, [tokens] + others(after(tokens, out_turned)))
+    feed_rows = Gather(jnp.concatenate([out_turned, *out_other, up_weight, down_weight.T], 1))
+    qkv_rows.put()
+    norms = jnp.concatenate([norm_gain, norm_shift, out_bias], 0)
+    grad_full = jnp.concatenate([out_grad] + others(out_grad), 1)
+    prev_dense = [dense_of(prev_logits, MASKED_SCORE, 0, qkv_rows.held, grad_full)]
+    inside, across = with_next(inside, across)
+    qkv_rows.put(prev_dense[0])
+    feed_rows.put(prev_dense[0])
+    prev_dense.append(
+        dense_of(prev_logits, MASKED_SCORE, 1, qkv_rows.held, feed_rows.held, tokens_full)
+    )
+    while qkv_rows.step < qkv_rows.count:
+        qkv_rows.put(prev_dense[1], inside, across)
+    feed_rows.put(qkv_rows.held)
+    query, key, value, low_tokens, high_tokens, *projections = project(
+        slots, even, after(tokens_full, feed_rows.held), inside, across, qkv_rows.held,
+        qkv_rows.arrived, qv_bias,
+    )
+    scores, probs, attended, attended_other = [], [], [], []
     for chunk in range(CHUNKS):
         score, prob, mix = attend_forward(query, key, value, prev_dense[chunk], chunk)
         query = after(query, mix)
@@ -1060,32 +1109,29 @@
         probs.append(prob)
         attended.append(mix)
         attended_other.append(jnp.concatenate(others(mix), 1))
-    up_gather.put(mix)
-    down_gather.put(mix)
-    scores_low = after(scores[0], attended_other[0], up_gather.held)
-    new_logits = to_band([scores_low, *scores[1:]], True)
-
-    up_near = after(up_gather.held, new_logits)
-    weights = in_order(
-        slots, up_near, up_gather.last(), (tokens_full.shape[1], up_weight.shape[1])
-    )
-    down_near = after(down_gather.held, weights[0])
-    weights = (
-        *weights,
-        *in_order(late_slots, down_near, down_gather.last(), (up_weight.shape[1],)),
-    )
+    norms = jnp.concatenate([norms] + others(after(norms, mix)), 1)
+    feed_rows.put(mix, attended_other[0])
+    while feed_rows.step < feed_rows.count:
+        feed_rows.put()
+    new_logits = to_band([after(scores[0], feed_rows.held), *scores[1:]], True)
+    other_out, *weights = in_order(
+        slots, after(feed_rows.held, new_logits), feed_rows.arrived,
+        (width, (col_count - 1) * width, up_weight.shape[1], up_weight.shape[1]),
+    )
+    weights[0], other_out = other_out, weights[0]
     ups = up_bias[None]
     firsts = []
     for chunk in range(CHUNKS):
         result = feed_first(
-            attended[chunk], attended_other[chunk], tokens_full, weights, norms, ups, chunk
+            attended[chunk], attended_other[chunk], tokens_full, other_out, weights, norms, ups,
+            chunk,
         )
         ups = after(ups, result[-1])
         firsts.append((*result, exchanged(result[-1])))
     normed, inverse, upper, act, slope, down_part, down_other = zip(*firsts)
 
-    logit_dense.append(dense_of(logit_grad, 0.0, 0)(down_part[-1]))
-    sums = after(jnp.zeros((SUM_ROWS, own), F32), logit_dense[-1])
+    logit_dense = [dense_of(logit_grad, 0.0, 0, down_part[-1])]
+    sums = after(jnp.zeros((SUM_ROWS, own), F32), logit_dense[0])
     output = None
     seconds = []
     for chunk in range(CHUNKS):
@@ -1095,8 +1141,9 @@
         )
         seconds.append((*result, exchanged(result[-1])))
     res_two, ffn_low, hidden_grad, lower_part, lower_other = zip(*seconds)
-    logit_dense.append(dense_of(logit_grad, 0.0, 1)(lower_part[-1]))
-    sums = after(sums, logit_dense[-1])
+    keep, send = feed_grads(blocks, ffn_low, act, upper, hidden_grad)
+    feed_sum = Reduction(keep, send, None, (0, 0))
+    sums = after(sums, keep)
 
     branch_low, res_one, query_grad, prev_dense_grad = [], [], [], []
     partial = None
@@ -1107,66 +1154,55 @@
         )
         branch_low.append(low)
         res_one.append(res)
-        if chunk == 0:
-            up_keep, up_send, down_keep, down_send = feed_grads(
-                late_blocks, blocks, (after(ffn_low[0], low), *ffn_low[1:]), act, upper,
-                hidden_grad,
-            )
-            up_sum = Reduction(late, up_keep, [up_send], None, 1)
-            down_sum = Reduction(early, down_keep, [down_send], None, 1)
-            up_sum.move()
-            down_sum.move()
-            attended_grad = after(attended_grad, up_keep)
         prev, query_part, *partial = attend_backward(
             attended_grad, query, key, value, probs[chunk], logit_dense[chunk], chunk, partial
         )
-        sums = after(sums, query_part)
         if chunk == 0:
-            down_sum.add(query_part)
-            up_sum.add(down_sum.keep)
-            sums = after(sums, up_sum.keep)
+            feed_sum.add(query_part)
+            logit_dense.append(dense_of(logit_grad, 0.0, 1, feed_sum.keep))
+            sums = after(sums, logit_dense[1])
         prev_dense_grad.append(prev)
         query_grad.append(query_part)
     key_grad, value_grad = partial
-    low_part, center, high_part = token_grads(query_grad, res_one, key_grad, value_grad, weight)
-    arrived_low = lax.ppermute(high_part, "row", forward).astype(F32)
-    arrived_high = lax.ppermute(low_part, "row", backward).astype(F32)
-    down_sum.add(low_part)
+    feed_sum.add(query_grad[-1])
     keep, send, sums = project_grads(
-        blocks, after(sums, down_sum.keep), tokens_full, low_tokens, high_tokens, query_grad,
+        blocks, after(sums, feed_sum.keep), tokens_full, low_tokens, high_tokens, query_grad,
         key_grad, value_grad, branch_low, attended,
     )
-    last = Reduction(early, keep, [send], sums, 4)
-    last.move()
-    up_sum.add(keep)
-    last.add(up_sum.keep)
-    center = center + jnp.pad(after(arrived_low, last.keep), ((0, count - HALO), (0, 0)))
-    center = center + jnp.pad(arrived_high, ((count - HALO, 0), (0, 0)))
-    tokens_grad = center[:, :own]
-    for step in range(1, col_count):
-        part = center[:, step * own : (step + 1) * own].astype(BF16)
+    last_sum = Reduction(keep, send, sums, (3, 0), (2, 2, 2, 2, hidden_rows))
+    center, inside, across = token_grads(
+        even, query_grad, res_one, after(key_grad, keep), value_grad, projections
+    )
+    last_sum.add(center)
+    inside, across = with_next(after(inside, last_sum.keep), across)
+    prev_dense_grad[0] = after(prev_dense_grad[0], last_sum.keep)
+    prev_grad = to_band(prev_dense_grad, False)
+    last_sum.add(prev_grad)
+    feed_sum.add(last_sum.keep)
+    tokens_grad, *parts = token_sum(even, after(center, feed_sum.keep), inside, across, own)
+    for step, part in enumerate(parts, 1):
         tokens_grad = tokens_grad + from_next(part, "col", -step).astype(F32)
-    prev_dense_grad[0] = after(prev_dense_grad[0], center)
-    prev_grad = to_band(prev_dense_grad, False)
-    for sums_of in (last, down_sum, up_sum):
-        while not hasattr(sums_of, "result"):
-            sums_of.add(prev_grad)
-    *project_grad, out_grad_rows, sums = last.result
-    feed_grad = (up_sum.result[0], down_sum.result[0])
+    last_sum.add(parts[0])
+    while feed_sum.result is None:
+        feed_sum.add(last_sum.keep)
+    while last_sum.result is None:
+        last_sum.add(feed_sum.result[0])
+    qkv_grad, out_grad_rows, qv_sum, bias_sum, gain_sum, shift_sum, hidden_sum = last_sum.result
+    up_grad, down_grad = feed_sum.result
     return (
         output,
         new_logits,
         tokens_grad.astype(BF16),
         prev_grad,
-        jnp.stack(project_grad),
-        sums[0:2],
+        qkv_grad,
+        qv_sum,
         out_grad_rows.T,
-        sums[2:4],
-        feed_grad[0],
-        sums[8 : 8 + hidden_rows].reshape(-1),
-        feed_grad[1].T,
-        sums[4:6],
-        sums[6:8],
+        bias_sum,
+        up_grad,
+        hidden_sum.reshape(-1),
+        down_grad.T,
+        gain_sum,
+        shift_sum,
     )
 
 

time: 167 us -> 137 us (0.82)
  starting transfers between devices: 64.1 us -> 46.6 us
  waiting for transfers between devices: 28.3 us -> 21.6 us
  local copies, waits for them, and re-layouts: 5.76 us -> 1.92 us
    ppermute x34 -> x20, starting transfers between devices: 57.2 us -> 34.1 us  [the longest x16 29.2 us: with_partner(): lax.ppermute(x, 'row', [(i, i ^ orders[i % 2][step]) for i in range(count)])]
    ppermute x34 -> x20, waiting for transfers between devices: 23.4 us -> 10.2 us  [the longest x16 10.2 us: with_partner(): lax.ppermute(x, 'row', [(i, i ^ orders[i % 2][step]) for i in range(count)])]
    ppermute x9 -> x11, waiting for transfers between devices: 4.82 us -> 11.4 us  [from_next(): lax.ppermute(x, axis, [((i + step) % count, i) for i in range(count)])]
    ppermute x9 -> x11, starting transfers between devices: 6.94 us -> 12.5 us  [from_next(): lax.ppermute(x, axis, [((i + step) % count, i) for i in range(count)])]
    concatenate x5 -> x6, local copies, waits for them, and re-layouts: 1.94 us -> 0.12 us  [the longest x5 0.1 us: put(): self.held = jnp.concatenate([after(self.held, *needed), self.arrived], 0)]
    pallas_call x10 -> x11, Pallas kernels: 4.58 us -> 4.38 us  [the longest x1 2.14 us: token_grads(): pl.pallas_call(token_grad_kernel, grid=(1,), in_specs=[pl.BlockSpec(memor...]
  transfers between devices with their start and end apart: 43 -> 31, of which waited for: 11 -> 9; matrix products, arithmetic and copies ran while one was open for 4% -> 2% of each run, Pallas kernels for 34% -> 44%
where the time goes in v3:
time: 137 us; the launch traced here: 136 us
  Pallas kernels  62.6 us (46%)
  starting transfers between devices  46.6 us (34%)
  waiting for transfers between devices  21.6 us (16%)
  other arithmetic  2.53 us (2%)
  local copies, waits for them, and re-layouts  1.92 us (1%)
    ppermute x16, starting transfers between devices, with_partner(): lax.ppermute(x, 'row', [(i, i ^ orders[i % 2][step]) for i in range(count)])  29.2 us
    ppermute x11, starting transfers between devices, from_next(): lax.ppermute(x, axis, [((i + step) % count, i) for i in range(count)])  12.5 us
    pallas_call x4, Pallas kernels, to_dense(): pl.pallas_call(functools.partial(dense_kernel, fill, token_count, offset)...  12.4 us
    ppermute x11, waiting for transfers between devices, from_next(): lax.ppermute(x, axis, [((i + step) % count, i) for i in range(count)])  11.4 us
    ppermute x16, waiting for transfers between devices, with_partner(): lax.ppermute(x, 'row', [(i, i ^ orders[i % 2][step]) for i in range(count)])  10.2 us
    pallas_call x2, Pallas kernels, to_band(): pl.pallas_call(functools.partial(band_kernel, masked), grid=(CHUNKS * ste...  10.1 us
    pallas_call x2, Pallas kernels, attend_backward(): pl.pallas_call(functools.partial(backward_kernel, offset, last), grid=(co...  9.21 us
    pallas_call x2, Pallas kernels, attend_forward(): pl.pallas_call(functools.partial(forward_kernel, offset), grid=(count //...  7.75 us
  transfers between devices with their start and end apart: 31, of which 9 were waited for; matrix products, arithmetic and copies ran while one was open for 2% of the time, Pallas kernels for 44%

profile of v3, /device:TPU:0, one launch (start us, length us, event | category | flops | bytes accessed | tf_op | source)
XLA Modules:
  0.0 136.4 jit_solution(7582552046368349173)
XLA Ops:
  0.6 3.0 %collective-permute-start.1 = (bf16[32,256]{1,0:T(8,128)(2,1)}, bf16[32,256]{1,0:T(8,128)(2,1)S(1)}, u32[]{:S(2)}, u32[]{:S(2)}) collective-permute-start(bf16[32,256]{1,0:T(8,128)(2,1)} %bitcast.16), channel_id=1, source_target_pairs={{1,0},{0,1},{3,2},{2,3},{5,4},{4,5},{7,6},{6,7},{9,8},{8,9},{11,10... | collective-permute-start | bytes 49160 | tf_op jit(solution)/shard_map/ppermute | solution.py:944
  3.7 3.0 %collective-permute-start.2 = (bf16[1,3,32,256]{3,2,1,0:T(8,128)(2,1)}, bf16[1,3,32,256]{3,2,1,0:T(8,128)(2,1)S(1)}, u32[]{:S(2)}, u32[]{:S(2)}) collective-permute-start(bf16[1,3,32,256]{3,2,1,0:T(8,128)(2,1)} %bitcast.14), channel_id=1, source_target_pairs={{0,16},{2,6},{4,20},{6,2},{8,24},{10,14},{12,28},{14,10},{16,0},{1... | collective-permute-start | bytes 147464 | tf_op jit(solution)/shard_map/ppermute | solution.py:971
  6.8 1.5 %collective-permute-start.3 = (bf16[512,256]{1,0:T(8,128)(2,1)}, bf16[512,256]{1,0:T(8,128)(2,1)S(1)}, u32[]{:S(2)}, u32[]{:S(2)}) collective-permute-start(bf16[512,256]{1,0:T(8,128)(2,1)} %param.26), channel_id=1, source_target_pairs={{1,0},{0,1},{3,2},{2,3},{5,4},{4,5},{7,6},{6,7},{9,8},{8,9},{11,10... | collective-permute-start | bytes 786440 | tf_op jit(solution)/shard_map/ppermute | solution.py:944
  8.3 1.0 constant_dynamic-update-slice_fusion.1
  9.3 0.9 maximum_bitcast_fusion
  10.2 0.4 collective-permute-start.4
  10.6 0.8 pad_maximum_fusion
  11.4 1.6 %collective-permute-start.5 = (bf16[2,3,32,256]{3,2,1,0:T(8,128)(2,1)S(1)}, bf16[2,3,32,256]{3,2,1,0:T(8,128)(2,1)S(1)}, u32[]{:S(2)}, u32[]{:S(2)}) collective-permute-start(bf16[2,3,32,256]{3,2,1,0:T(8,128)(2,1)S(1)} %pad_maximum_fusion), channel_id=1, source_target_pairs={{0,8},{2,18},{4,12},{6,22},{8,0},{10,26},{12,4},{14,30},{16,24},{1... | collective-permute-start | bytes 294920 | tf_op jit(solution)/shard_map/ppermute | solution.py:971
  13.1 4.2 %collective-permute-done.3 = bf16[512,256]{1,0:T(8,128)(2,1)S(1)} collective-permute-done((bf16[512,256]{1,0:T(8,128)(2,1)}, bf16[512,256]{1,0:T(8,128)(2,1)S(1)}, u32[]{:S(2)}, u32[]{:S(2)}) %collective-permute-start.3) | collective-permute-done | bytes 262176 | tf_op jit(solution)/shard_map/ppermute | solution.py:944
  17.3 0.6 copy-done
  17.9 3.1 %to_dense.4.prev_ref = bf16[4,256,1152]{2,1,0:T(8,128)(2,1)S(1)} custom-call(s32[1,33]{1,0:T(1,128)S(1)} %copy-done, s32[1]{0:T(128)} %bitcast.base_ref, bf16[4,512,1024]{2,1,0:T(8,128)(2,1)} %band_ref.1), custom_call_target="tpu_custom_call" | custom-call | flops 8000000000 | tf_op jit(solution)/shard_map/to_dense/pallas_call | solution.py:103
  21.1 1.7 %collective-permute-start.8 = (bf16[4,3,32,256]{3,2,1,0:T(8,128)(2,1)S(1)}, bf16[4,3,32,256]{3,2,1,0:T(8,128)(2,1)S(1)}, u32[]{:S(2)}, u32[]{:S(2)}) collective-permute-start(bf16[4,3,32,256]{3,2,1,0:T(8,128)(2,1)S(1)} %constant_dynamic-update-slice_fusion.4), channel_id=1, source_target_pairs={{0,4},{2,10},{4,0},{6,14},{8,12},{10,2},{12,8},{14,6},{16,20},{18,... | collective-permute-start | bytes 589832 | tf_op jit(solution)/shard_map/ppermute | solution.py:971
  22.8 1.6 %collective-permute-start.9 = (bf16[2,32,2560]{2,1,0:T(8,128)(2,1)S(1)}, bf16[2,32,2560]{2,1,0:T(8,128)(2,1)S(1)}, u32[]{:S(2)}, u32[]{:S(2)}) collective-permute-start(bf16[2,32,2560]{2,1,0:T(8,128)(2,1)S(1)} %constant_dynamic-update-slice_fusion.2), channel_id=1, source_target_pairs={{0,8},{2,18},{4,12},{6,22},{8,0},{10,26},{12,4},{14,30},{16,24},{1... | collective-permute-start | bytes 983048 | tf_op jit(solution)/shard_map/ppermute | solution.py:971
  24.7 0.7 collective-permute-start.7
  25.4 3.1 %to_dense.5.prev_ref = bf16[4,256,1152]{2,1,0:T(8,128)(2,1)S(1)} custom-call(s32[1,33]{1,0:T(1,128)S(1)} %copy-done.1, s32[1]{0:T(128)} %bitcast.base_ref, bf16[4,512,1024]{2,1,0:T(8,128)(2,1)} %band_ref.1), custom_call_target="tpu_custom_call" | custom-call | flops 8000000000 | tf_op jit(solution)/shard_map/to_dense/pallas_call | solution.py:103
  28.6 8.0 %collective-permute-start.10 = (bf16[8,3,32,256]{3,2,1,0:T(8,128)(2,1)S(1)}, bf16[8,3,32,256]{3,2,1,0:T(8,128)(2,1)S(1)}, u32[]{:S(2)}, u32[]{:S(2)}) collective-permute-start(bf16[8,3,32,256]{3,2,1,0:T(8,128)(2,1)S(1)} %constant_dynamic-update-slice_fusion.6.near_ref), channel_id=1, source_target_pairs={{0,2},{2,0},{4,6},{6,4},{8,10},{10,8},{12,14},{14,12},{16,18},{18,... | collective-permute-start | bytes 1179656 | tf_op jit(solution)/shard_map/ppermute | solution.py:971
  36.7 2.4 %collective-permute-start.13 = (bf16[4,32,2560]{2,1,0:T(8,128)(2,1)S(1)}, bf16[4,32,2560]{2,1,0:T(8,128)(2,1)S(1)}, u32[]{:S(2)}, u32[]{:S(2)}) collective-permute-start(bf16[4,32,2560]{2,1,0:T(8,128)(2,1)S(1)} %constant_dynamic-update-slice_fusion.8), channel_id=1, source_target_pairs={{0,4},{2,10},{4,0},{6,14},{8,12},{10,2},{12,8},{14,6},{16,20},{18,... | collective-permute-start | bytes 1966088 | tf_op jit(solution)/shard_map/ppermute | solution.py:971
  39.1 1.8 %project.1 = (bf16[512,256]{1,0:T(8,128)(2,1)S(1)}, bf16[1536,256]{1,0:T(8,128)(2,1)S(1)}, bf16[1536,256]{1,0:T(8,128)(2,1)S(1)}, bf16[384,512]{1,0:T(8,128)(2,1...) custom-call(s32[16]{0:T(128)S(1)} %fusion.7.slot_ref, ...), custom_call_target="tpu_custom_call" | custom-call | flops 2000000000 | tf_op jit(solution)/shard_map/project/pallas_call | solution.py:271
  40.9 3.9 %attend_forward.2 = (bf16[4,256,1152]{2,1,0:T(8,128)(2,1)S(1)}, bf16[4,256,1152]{2,1,0:T(8,128)(2,1)S(1)}, bf16[256,256]{1,0:T(8,128)(2,1)S(1)}) custom-call(bf16[512,256]{1,0:T(8,128)(2,1)S(1)} %get-tuple-element.195.query_ref, bf16[1536,256]{1,0:T(8,128)(2,1)S(1)} %get-tuple-element.153.key_ref, bf16[1536,256]{1,0:T(8,128)(2,1)S(1)} %get-tuple-element.154.value_ref, ...), custom_call_target="tpu_custom_call" | custom-call | flops 3800000000 | tf_op jit(solution)/shard_map/attend_forward/pallas_call | solution.py:313
  44.8 0.8 collective-permute-start.12
  45.6 3.9 %attend_forward.3 = (bf16[4,256,1152]{2,1,0:T(8,128)(2,1)S(1)}, bf16[4,256,1152]{2,1,0:T(8,128)(2,1)S(1)}, bf16[256,256]{1,0:T(8,128)(2,1)S(1)}) custom-call(bf16[512,256]{1,0:T(8,128)(2,1)S(1)} %get-tuple-element.195.query_ref, bf16[1536,256]{1,0:T(8,128)(2,1)S(1)} %get-tuple-element.153.key_ref, bf16[1536,256]{1,0:T(8,128)(2,1)S(1)} %get-tuple-element.154.value_ref, ...), custom_call_target="tpu_custom_call" | custom-call | flops 3800000000 | tf_op jit(solution)/shard_map/attend_forward/pallas_call | solution.py:313
  49.5 1.1 collective-permute-done.12.other_ref
  50.8 0.8 collective-permute-start.15
  51.6 1.3 collective-permute-start.11
  52.9 1.7 %collective-permute-done.15 = f32[6,256]{1,0:T(8,128)S(1)} collective-permute-done((f32[6,256]{1,0:T(8,128)S(1)}, f32[6,256]{1,0:T(8,128)S(1)}, u32[]{:S(2)}, u32[]{:S(2)}) %collective-permute-start.15) | collective-permute-done | bytes 6176 | tf_op jit(solution)/shard_map/ppermute | solution.py:944
  54.6 5.1 %to_band.2 = bf16[4,512,1024]{2,1,0:T(8,128)(2,1)} custom-call(bf16[4,256,1152]{2,1,0:T(8,128)(2,1)S(1)} %get-tuple-element.160.refs_0_, bf16[4,256,1152]{2,1,0:T(8,128)(2,1)S(1)} %get-tuple-element.161.refs_1_), custom_call_target="tpu_custom_call" | custom-call | flops 5000000000 | tf_op jit(solution)/shard_map/to_band/pallas_call | solution.py:156
  59.6 1.1 in_order.1
  60.7 2.2 %feed_first.2 = (f32[256,512]{1,0:T(8,128)S(1)}, f32[256,1]{1,0:T(8,128)S(1)}, bf16[256,512]{1,0:T(8,128)(2,1)S(1)}, bf16[256,1024]{1,0:T(8,128)(2,1)S(1)}, bf16...) custom-call(bf16[256,256]{1,0:T(8,128)(2,1)S(1)} %get-tuple-element.155.own_ref.refs_4_, ...), custom_call_target="tpu_custom_call" | custom-call | flops 1000000000 | tf_op jit(solution)/shard_map/feed_first/pallas_call | solution.py:501
  62.9 0.7 collective-permute-start.16
  63.6 2.1 %feed_first.3 = (f32[256,512]{1,0:T(8,128)S(1)}, f32[256,1]{1,0:T(8,128)S(1)}, bf16[256,512]{1,0:T(8,128)(2,1)S(1)}, bf16[256,1024]{1,0:T(8,128)(2,1)S(1)}, bf16...) custom-call(bf16[256,256]{1,0:T(8,128)(2,1)S(1)} %get-tuple-element.157.own_ref.refs_5_, ...), custom_call_target="tpu_custom_call" | custom-call | flops 1000000000 | tf_op jit(solution)/shard_map/feed_first/pallas_call | solution.py:501
  65.8 1.5 %collective-permute-start.17 = (bf16[256,512]{1,0:T(8,128)(2,1)S(1)}, bf16[256,512]{1,0:T(8,128)(2,1)S(1)}, u32[]{:S(2)}, u32[]{:S(2)}) collective-permute-start(bf16[256,512]{1,0:T(8,128)(2,1)S(1)} %get-tuple-element.170.part_ref), channel_id=1, source_target_pairs={{1,0},{0,1},{3,2},{2,3},{5,4},{4,5},{7,6},{6,7},{9,8},{8,9},{11,10... | collective-permute-start | bytes 786440 | tf_op jit(solution)/shard_map/ppermute | solution.py:944
  67.2 3.1 %to_dense.6.logit_ref = bf16[4,256,1152]{2,1,0:T(8,128)(2,1)S(1)} custom-call(s32[1,33]{1,0:T(1,128)S(1)} %copy-done.1, s32[1]{0:T(128)} %bitcast.base_ref, bf16[4,512,1024]{2,1,0:T(8,128)(2,1)} %band_ref.3), custom_call_target="tpu_custom_call" | custom-call | flops 1000000000 | tf_op jit(solution)/shard_map/to_dense/pallas_call | solution.py:103
  70.3 1.9 %collective-permute-done.16.recv_ref = bf16[256,512]{1,0:T(8,128)(2,1)S(1)} collective-permute-done((bf16[256,512]{1,0:T(8,128)(2,1)S(1)}, bf16[256,512]{1,0:T(8,128)(2,1)S(1)}, u32[]{:S(2)}, u32[]{:S(2)}) %collective-permute-start.16) | collective-permute-done | bytes 262176 | tf_op jit(solution)/shard_map/ppermute | solution.py:944
  72.2 2.4 %feed_second.2 = (f32[16,256]{1,0:T(8,128)S(1)}, bf16[512,256]{1,0:T(8,128)(2,1)}, f32[256,512]{1,0:T(8,128)S(1)}, bf16[256,512]{1,0:T(8,128)(2,1)S(1)}, bf16[25...) custom-call(f32[16,256]{1,0:T(8,128)S(1)} %broadcast_in_dim.18.start_ref, ...), custom_call_target="tpu_custom_call" | custom-call | flops 700000000 | tf_op jit(solution)/shard_map/feed_second/pallas_call | solution.py:580
  74.6 0.7 collective-permute-start.18
  75.3 2.5 %collective-permute-done.17.recv_ref = bf16[256,512]{1,0:T(8,128)(2,1)S(1)} collective-permute-done((bf16[256,512]{1,0:T(8,128)(2,1)S(1)}, bf16[256,512]{1,0:T(8,128)(2,1)S(1)}, u32[]{:S(2)}, u32[]{:S(2)}) %collective-permute-start.17) | collective-permute-done | bytes 262176 | tf_op jit(solution)/shard_map/ppermute | solution.py:944
  77.8 2.4 %feed_second.3 = (f32[16,256]{1,0:T(8,128)S(1)}, bf16[512,256]{1,0:T(8,128)(2,1)}, f32[256,512]{1,0:T(8,128)S(1)}, bf16[256,512]{1,0:T(8,128)(2,1)S(1)}, bf16[25...) custom-call(f32[16,256]{1,0:T(8,128)S(1)} %get-tuple-element.175.start_ref, ...), custom_call_target="tpu_custom_call", output_to_operand_aliasing={{1}: (9, {})} | custom-call | flops 700000000 | tf_op jit(solution)/shard_map/feed_second/pallas_call | solution.py:580
  80.3 3.3 %feed_grads.1 = (f32[512,1024]{1,0:T(8,128)S(1)}, bf16[512,1024]{1,0:T(8,128)(2,1)S(1)}) custom-call(s32[16]{0:T(128)S(1)} %and_select_fusion.block_ref, bf16[256,512]{1,0:T(8,128)(2,1)S(1)} %get-tuple-element.181.refs_0_, bf16[256,512]{1,0:T(8,128)(2,1)S(1)} %get-tuple-element.182.refs_1_, bf16[256,512]{1,0:T(8,128)(2,1)S(1)} %get-tuple-element.183.refs_2_, ...), custom_call_target="tpu_custom_call" | custom-call | flops 1000000000 | tf_op jit(solution)/shard_map/feed_grads/pallas_call | solution.py:701
  83.7 0.7 collective-permute-start.20
  84.4 0.7 feed_third.2
  85.1 4.2 %attend_backward.2 = (bf16[4,256,1152]{2,1,0:T(8,128)(2,1)S(1)}, bf16[256,256]{1,0:T(8,128)(2,1)S(1)}, f32[256,1536]{1,0:T(8,128)S(1)}, f32[256,1536]{1,0:T(8,128)S(1)}) custom-call(bf16[256,256]{1,0:T(8,128)(2,1)S(1)} %get-tuple-element.194.grad_ref, bf16[512,256]{1,0:T(8,128)(2,1)S(1)} %get-tuple-element.195.query_ref, ...), custom_call_target="tpu_custom_call" | custom-call | flops 20000000000 | tf_op jit(solution)/shard_map/attend_backward/pallas_call | solution.py:397
  89.6 1.6 %collective-permute-start.21 = (bf16[256,1024]{1,0:T(8,128)(2,1)S(1)}, bf16[256,1024]{1,0:T(8,128)(2,1)S(1)}, u32[]{:S(2)}, u32[]{:S(2)}) collective-permute-start(bf16[256,1024]{1,0:T(8,128)(2,1)S(1)} %get-tuple-element.217), channel_id=1, source_target_pairs={{0,4},{2,10},{4,0},{6,14},{8,12},{10,2},{12,8},{14,6},{16,20},{18,... | collective-permute-start | bytes 1572872 | tf_op jit(solution)/shard_map/ppermute | solution.py:971
  91.2 3.1 %to_dense.7.logit_ref = bf16[4,256,1152]{2,1,0:T(8,128)(2,1)S(1)} custom-call(s32[1,33]{1,0:T(1,128)S(1)} %copy-done.1, s32[1]{0:T(128)} %bitcast.base_ref, bf16[4,512,1024]{2,1,0:T(8,128)(2,1)} %band_ref.3), custom_call_target="tpu_custom_call" | custom-call | flops 1000000000 | tf_op jit(solution)/shard_map/to_dense/pallas_call | solution.py:103
  94.3 0.8 feed_third.3
  95.1 5.0 %attend_backward.3 = (bf16[4,256,1152]{2,1,0:T(8,128)(2,1)S(1)}, bf16[256,256]{1,0:T(8,128)(2,1)S(1)}, bf16[1536,256]{1,0:T(8,128)(2,1)S(1)}, bf16[1536,256]{1,0:T(8,128)(2,1)S(1)}) custom-call(bf16[256,256]{1,0:T(8,128)(2,1)S(1)} %get-tuple-element.207.grad_ref, bf16[512,256]{1,0:T(8,128)(2,1)S(1)} %get-tuple-element.195.query_ref, ...), custom_call_target="tpu_custom_call" | custom-call | flops 3000000000 | tf_op jit(solution)/shard_map/attend_backward/pallas_call | solution.py:397
  100.2 1.9 %project_grads.1 = (f32[1024,256]{1,0:T(8,128)S(1)}, bf16[1056,256]{1,0:T(8,128)(2,1)S(1)}, f32[16,256]{1,0:T(8,128)S(1)}) custom-call(s32[16]{0:T(128)S(1)} %and_select_fusion.block_ref, f32[16,256]{1,0:T(8,128)S(1)} %get-tuple-element.219.start_ref, bf16[256,256]{1,0:T(8,128)(2,1)S(1)} %get-tuple-element.197.refs_0_, ...), custom_call_target="tpu_custom_call" | custom-call | flops 600000000 | tf_op jit(solution)/shard_map/project_grads/pallas_call | solution.py:758
  102.2 2.1 %token_grads.1 = (f32[512,512]{1,0:T(8,128)S(1)}, bf16[384,512]{1,0:T(8,128)(2,1)S(1)}, bf16[384,512]{1,0:T(8,128)(2,1)S(1)}) custom-call(s32[1]{0:T(128)} %bitcast.1.even_ref, bf16[256,256]{1,0:T(8,128)(2,1)S(1)} %get-tuple-element.197.refs_0_, bf16[256,256]{1,0:T(8,128)(2,1)S(1)} %get-tuple-element.211.refs_1_, f32[256,256]{1,0:T(8,128)S(1)} %get-tuple-element.212.refs_2_, ...), custom_call_target="tpu_custom_call" | custom-call | flops 600000000 | tf_op jit(solution)/shard_map/token_grads/pallas_call | solution.py:894
  104.3 0.6 collective-permute-start.24
  105.0 0.7 collective-permute-start.26
  105.8 3.5 %collective-permute-start.25 = (bf16[384,512]{1,0:T(8,128)(2,1)S(1)}, bf16[384,512]{1,0:T(8,128)(2,1)S(1)}, u32[]{:S(2)}, u32[]{:S(2)}) collective-permute-start(bf16[384,512]{1,0:T(8,128)(2,1)S(1)} %get-tuple-element.247), channel_id=1, source_target_pairs={{0,2},{2,0},{4,6},{6,4},{8,10},{10,8},{12,14},{14,12},{16,18},{18,... | collective-permute-start | bytes 1179656 | tf_op jit(solution)/shard_map/ppermute | solution.py:978
  109.2 1.7 %collective-permute-start.23 = (bf16[544,256]{1,0:T(8,128)(2,1)S(1)}, bf16[544,256]{1,0:T(8,128)(2,1)S(1)}, u32[]{:S(2)}, u32[]{:S(2)}) collective-permute-start(bf16[544,256]{1,0:T(8,128)(2,1)S(1)} %get-tuple-element.239), channel_id=1, source_target_pairs={{0,4},{2,10},{4,0},{6,14},{8,12},{10,2},{12,8},{14,6},{16,20},{18,... | collective-permute-start | bytes 835592 | tf_op jit(solution)/shard_map/ppermute | solution.py:971
  110.9 5.0 %to_band.3 = bf16[4,512,1024]{2,1,0:T(8,128)(2,1)} custom-call(bf16[4,256,1152]{2,1,0:T(8,128)(2,1)S(1)} %get-tuple-element.236.refs_0_, bf16[4,256,1152]{2,1,0:T(8,128)(2,1)S(1)} %get-tuple-element.237.refs_1_), custom_call_target="tpu_custom_call" | custom-call | flops 5000000000 | tf_op jit(solution)/shard_map/to_band/pallas_call | solution.py:156
  116.0 4.9 %collective-permute-done.23.arrived_ref = bf16[544,256]{1,0:T(8,128)(2,1)S(1)} collective-permute-done((bf16[544,256]{1,0:T(8,128)(2,1)S(1)}, bf16[544,256]{1,0:T(8,128)(2,1)S(1)}, u32[]{:S(2)}, u32[]{:S(2)}) %collective-permute-start.23) | collective-permute-done | bytes 278560 | tf_op jit(solution)/shard_map/ppermute | solution.py:971
  121.0 3.6 %collective-permute-start.28 = (bf16[288,256]{1,0:T(8,128)(2,1)S(1)}, bf16[288,256]{1,0:T(8,128)(2,1)S(1)}, u32[]{:S(2)}, u32[]{:S(2)}) collective-permute-start(bf16[288,256]{1,0:T(8,128)(2,1)S(1)} %get-tuple-element.252), channel_id=1, source_target_pairs={{0,8},{2,18},{4,12},{6,22},{8,0},{10,26},{12,4},{14,30},{16,24},{1... | collective-permute-start | bytes 442376 | tf_op jit(solution)/shard_map/ppermute | solution.py:971
  124.6 0.2 token_sum.1
  124.9 1.6 %collective-permute-start.27 = (bf16[512,256]{1,0:T(8,128)(2,1)S(1)}, bf16[512,256]{1,0:T(8,128)(2,1)S(1)}, u32[]{:S(2)}, u32[]{:S(2)}) collective-permute-start(bf16[512,256]{1,0:T(8,128)(2,1)S(1)} %get-tuple-element.250), channel_id=1, source_target_pairs={{1,0},{0,1},{3,2},{2,3},{5,4},{4,5},{7,6},{6,7},{9,8},{8,9},{11,10... | collective-permute-start | bytes 786440 | tf_op jit(solution)/shard_map/ppermute | solution.py:944
  126.4 0.8 collective-permute-start.29
  127.2 0.5 collective-permute-done.28.arrived_ref
  127.8 1.7 %collective-permute-start.30 = (bf16[160,256]{1,0:T(8,128)(2,1)S(1)}, bf16[160,256]{1,0:T(8,128)(2,1)S(1)}, u32[]{:S(2)}, u32[]{:S(2)}) collective-permute-start(bf16[160,256]{1,0:T(8,128)(2,1)S(1)} %get-tuple-element.259), channel_id=1, source_target_pairs={{0,16},{2,6},{4,20},{6,2},{8,24},{10,14},{12,28},{14,10},{16,0},{1... | collective-permute-start | bytes 245768 | tf_op jit(solution)/shard_map/ppermute | solution.py:971
  129.5 3.7 %collective-permute-done.29.arrived_ref = bf16[64,1024]{1,0:T(8,128)(2,1)S(1)} collective-permute-done((bf16[64,1024]{1,0:T(8,128)(2,1)S(1)}, bf16[64,1024]{1,0:T(8,128)(2,1)S(1)}, u32[]{:S(2)}, u32[]{:S(2)}) %collective-permute-start.29) | collective-permute-done | bytes 131104 | tf_op jit(solution)/shard_map/ppermute | solution.py:971
  133.2 0.7 finish.2
  133.9 1.0 collective-permute-done.30.arrived_ref
  134.9 0.7 finish.3
  135.6 0.8 add_convert_fusion
  (65 shorter events, 1.4 us)
Async XLA Ops:
  0.6 8.7 %collective-permute-start.1 = (bf16[32,256]{1,0:T(8,128)(2,1)}, bf16[32,256]{1,0:T(8,128)(2,1)S(1)}, u32[]{:S(2)}, u32[]{:S(2)}) collective-permute-start(bf16[32,256]{1,0:T(8,128)(2,1)} %bitcast.16), channel_id=1, source_target_pairs={{1,0},{0,1},{3,2},{2,3},{5,4},{4,5},{7,6},{6,7},{9,8},{8,9},{11,10... | collective-permute-start | bytes 49160 | tf_op jit(solution)/shard_map/ppermute | solution.py:944
  3.6 20.8 %collective-permute-start = (bf16[512,256]{1,0:T(8,128)(2,1)}, bf16[512,256]{1,0:T(8,128)(2,1)S(1)}, u32[]{:S(2)}, u32[]{:S(2)}) collective-permute-start(bf16[512,256]{1,0:T(8,128)(2,1)} %refs_0_.1), channel_id=1, source_target_pairs={{1,0},{0,1},{3,2},{2,3},{5,4},{4,5},{7,6},{6,7},{9,8},{8,9},{11,10... | collective-permute-start | bytes 786440 | tf_op jit(solution)/shard_map/ppermute | solution.py:944
  3.7 6.9 %collective-permute-start.2 = (bf16[1,3,32,256]{3,2,1,0:T(8,128)(2,1)}, bf16[1,3,32,256]{3,2,1,0:T(8,128)(2,1)S(1)}, u32[]{:S(2)}, u32[]{:S(2)}) collective-permute-start(bf16[1,3,32,256]{3,2,1,0:T(8,128)(2,1)} %bitcast.14), channel_id=1, source_target_pairs={{0,16},{2,6},{4,20},{6,2},{8,24},{10,14},{12,28},{14,10},{16,0},{1... | collective-permute-start | bytes 147464 | tf_op jit(solution)/shard_map/ppermute | solution.py:971
  6.8 10.5 %collective-permute-start.3 = (bf16[512,256]{1,0:T(8,128)(2,1)}, bf16[512,256]{1,0:T(8,128)(2,1)S(1)}, u32[]{:S(2)}, u32[]{:S(2)}) collective-permute-start(bf16[512,256]{1,0:T(8,128)(2,1)} %param.26), channel_id=1, source_target_pairs={{1,0},{0,1},{3,2},{2,3},{5,4},{4,5},{7,6},{6,7},{9,8},{8,9},{11,10... | collective-permute-start | bytes 786440 | tf_op jit(solution)/shard_map/ppermute | solution.py:944
  10.2 12.6 %collective-permute-start.4 = (bf16[1,32,2560]{2,1,0:T(8,128)(2,1)S(1)}, bf16[1,32,2560]{2,1,0:T(8,128)(2,1)S(1)}, u32[]{:S(2)}, u32[]{:S(2)}) collective-permute-start(bf16[1,32,2560]{2,1,0:T(8,128)(2,1)S(1)} %maximum_bitcast_fusion), channel_id=1, source_target_pairs={{0,16},{2,6},{4,20},{6,2},{8,24},{10,14},{12,28},{14,10},{16,0},{1... | collective-permute-start | bytes 491528 | tf_op jit(solution)/shard_map/ppermute | solution.py:971
  11.4 9.7 %collective-permute-start.5 = (bf16[2,3,32,256]{3,2,1,0:T(8,128)(2,1)S(1)}, bf16[2,3,32,256]{3,2,1,0:T(8,128)(2,1)S(1)}, u32[]{:S(2)}, u32[]{:S(2)}) collective-permute-start(bf16[2,3,32,256]{3,2,1,0:T(8,128)(2,1)S(1)} %pad_maximum_fusion), channel_id=1, source_target_pairs={{0,8},{2,18},{4,12},{6,22},{8,0},{10,26},{12,4},{14,30},{16,24},{1... | collective-permute-start | bytes 294920 | tf_op jit(solution)/shard_map/ppermute | solution.py:971
  17.3 0.7 copy-start
  17.9 6.6 %copy-start.2 = (bf16[512,256]{1,0:T(8,128)(2,1)S(1)}, bf16[512,256]{1,0:T(8,128)(2,1)}, u32[]{:S(2)}) copy-start(bf16[512,256]{1,0:T(8,128)(2,1)} %refs_0_.1) | copy-start | bytes 786436
  21.1 4.3 %copy-start.1 = (s32[1,33]{1,0:T(1,128)S(1)}, s32[1,33]{1,0:T(1,128)}, u32[]{:S(2)}) copy-start(s32[1,33]{1,0:T(1,128)} %lengths_ref.7) | copy-start | bytes 400
  21.1 7.4 %collective-permute-start.8 = (bf16[4,3,32,256]{3,2,1,0:T(8,128)(2,1)S(1)}, bf16[4,3,32,256]{3,2,1,0:T(8,128)(2,1)S(1)}, u32[]{:S(2)}, u32[]{:S(2)}) collective-permute-start(bf16[4,3,32,256]{3,2,1,0:T(8,128)(2,1)S(1)} %constant_dynamic-update-slice_fusion.4), channel_id=1, source_target_pairs={{0,4},{2,10},{4,0},{6,14},{8,12},{10,2},{12,8},{14,6},{16,20},{18,... | collective-permute-start | bytes 589832 | tf_op jit(solution)/shard_map/ppermute | solution.py:971
  22.8 13.8 %collective-permute-start.9 = (bf16[2,32,2560]{2,1,0:T(8,128)(2,1)S(1)}, bf16[2,32,2560]{2,1,0:T(8,128)(2,1)S(1)}, u32[]{:S(2)}, u32[]{:S(2)}) collective-permute-start(bf16[2,32,2560]{2,1,0:T(8,128)(2,1)S(1)} %constant_dynamic-update-slice_fusion.2), channel_id=1, source_target_pairs={{0,8},{2,18},{4,12},{6,22},{8,0},{10,26},{12,4},{14,30},{16,24},{1... | collective-permute-start | bytes 983048 | tf_op jit(solution)/shard_map/ppermute | solution.py:971
  24.6 3.9 %collective-permute-start.6 = (bf16[384,512]{1,0:T(8,128)(2,1)S(1)}, bf16[384,512]{1,0:T(8,128)(2,1)S(1)}, u32[]{:S(2)}, u32[]{:S(2)}) collective-permute-start(bf16[384,512]{1,0:T(8,128)(2,1)S(1)} %get-tuple-element.147), channel_id=1, source_target_pairs={{0,2},{2,0},{4,6},{6,4},{8,10},{10,8},{12,14},{14,12},{16,18},{18,... | collective-permute-start | bytes 1179656 | tf_op jit(solution)/shard_map/ppermute | solution.py:978
  24.7 14.5 %copy-start.4 = (f32[2,256]{1,0:T(2,128)S(1)}, f32[2,256]{1,0:T(2,128)}, u32[]{:S(2)}) copy-start(f32[2,256]{1,0:T(2,128)} %bias_ref.1) | copy-start | bytes 6148
  24.7 3.8 %collective-permute-start.7 = (bf16[384,512]{1,0:T(8,128)(2,1)S(1)}, bf16[384,512]{1,0:T(8,128)(2,1)S(1)}, u32[]{:S(2)}, u32[]{:S(2)}) collective-permute-start(bf16[384,512]{1,0:T(8,128)(2,1)S(1)} %get-tuple-element.148), channel_id=1, source_target_pairs={{2,4},{4,2},{6,8},{8,6},{10,12},{12,10},{14,16},{16,14},{18,20},{2... | collective-permute-start | bytes 1179656 | tf_op jit(solution)/shard_map/ppermute | solution.py:979
  28.6 10.5 %collective-permute-start.10 = (bf16[8,3,32,256]{3,2,1,0:T(8,128)(2,1)S(1)}, bf16[8,3,32,256]{3,2,1,0:T(8,128)(2,1)S(1)}, u32[]{:S(2)}, u32[]{:S(2)}) collective-permute-start(bf16[8,3,32,256]{3,2,1,0:T(8,128)(2,1)S(1)} %constant_dynamic-update-slice_fusion.6.near_ref), channel_id=1, source_target_pairs={{0,2},{2,0},{4,6},{6,4},{8,10},{10,8},{12,14},{14,12},{16,18},{18,... | collective-permute-start | bytes 1179656 | tf_op jit(solution)/shard_map/ppermute | solution.py:971
  36.7 13.9 %collective-permute-start.13 = (bf16[4,32,2560]{2,1,0:T(8,128)(2,1)S(1)}, bf16[4,32,2560]{2,1,0:T(8,128)(2,1)S(1)}, u32[]{:S(2)}, u32[]{:S(2)}) collective-permute-start(bf16[4,32,2560]{2,1,0:T(8,128)(2,1)S(1)} %constant_dynamic-update-slice_fusion.8), channel_id=1, source_target_pairs={{0,4},{2,10},{4,0},{6,14},{8,12},{10,2},{12,8},{14,6},{16,20},{18,... | collective-permute-start | bytes 1966088 | tf_op jit(solution)/shard_map/ppermute | solution.py:971
  44.8 5.7 %collective-permute-start.12 = (bf16[256,256]{1,0:T(8,128)(2,1)S(1)}, bf16[256,256]{1,0:T(8,128)(2,1)S(1)}, u32[]{:S(2)}, u32[]{:S(2)}) collective-permute-start(bf16[256,256]{1,0:T(8,128)(2,1)S(1)} %get-tuple-element.155.own_ref.refs_4_), channel_id=1, source_target_pairs={{1,0},{0,1},{3,2},{2,3},{5,4},{4,5},{7,6},{6,7},{9,8},{8,9},{11,10... | collective-permute-start | bytes 393224 | tf_op jit(solution)/shard_map/ppermute | solution.py:944
  49.4 1.3 copy-start.5
  49.4 1.3 copy-start.6
  49.5 1.3 copy-start.7
  50.6 9.0 %collective-permute-start.14 = (bf16[8,32,2560]{2,1,0:T(8,128)(2,1)S(1)}, bf16[8,32,2560]{2,1,0:T(8,128)(2,1)S(1)}, u32[]{:S(2)}, u32[]{:S(2)}) collective-permute-start(bf16[8,32,2560]{2,1,0:T(8,128)(2,1)S(1)} %constant_dynamic-update-slice_fusion.10.near_ref), channel_id=1, source_target_pairs={{0,2},{2,0},{4,6},{6,4},{8,10},{10,8},{12,14},{14,12},{16,18},{18,... | collective-permute-start | bytes 3932168 | tf_op jit(solution)/shard_map/ppermute | solution.py:971
  50.8 3.8 %collective-permute-start.15 = (f32[6,256]{1,0:T(8,128)S(1)}, f32[6,256]{1,0:T(8,128)S(1)}, u32[]{:S(2)}, u32[]{:S(2)}) collective-permute-start(f32[6,256]{1,0:T(8,128)S(1)} %pad_maximum_fusion.2), channel_id=1, source_target_pairs={{1,0},{0,1},{3,2},{2,3},{5,4},{4,5},{7,6},{6,7},{9,8},{8,9},{11,10... | collective-permute-start | bytes 18440 | tf_op jit(solution)/shard_map/ppermute | solution.py:944
  51.6 12.1 %collective-permute-start.11 = (bf16[256,256]{1,0:T(8,128)(2,1)S(1)}, bf16[256,256]{1,0:T(8,128)(2,1)S(1)}, u32[]{:S(2)}, u32[]{:S(2)}) collective-permute-start(bf16[256,256]{1,0:T(8,128)(2,1)S(1)} %get-tuple-element.157.own_ref.refs_5_), channel_id=1, source_target_pairs={{1,0},{0,1},{3,2},{2,3},{5,4},{4,5},{7,6},{6,7},{9,8},{8,9},{11,10... | collective-permute-start | bytes 393224 | tf_op jit(solution)/shard_map/ppermute | solution.py:944
  59.6 1.1 copy-start.3
  62.9 9.3 %collective-permute-start.16 = (bf16[256,512]{1,0:T(8,128)(2,1)S(1)}, bf16[256,512]{1,0:T(8,128)(2,1)S(1)}, u32[]{:S(2)}, u32[]{:S(2)}) collective-permute-start(bf16[256,512]{1,0:T(8,128)(2,1)S(1)} %get-tuple-element.168.part_ref), channel_id=1, source_target_pairs={{1,0},{0,1},{3,2},{2,3},{5,4},{4,5},{7,6},{6,7},{9,8},{8,9},{11,10... | collective-permute-start | bytes 786440 | tf_op jit(solution)/shard_map/ppermute | solution.py:944
  65.8 12.1 %collective-permute-start.17 = (bf16[256,512]{1,0:T(8,128)(2,1)S(1)}, bf16[256,512]{1,0:T(8,128)(2,1)S(1)}, u32[]{:S(2)}, u32[]{:S(2)}) collective-permute-start(bf16[256,512]{1,0:T(8,128)(2,1)S(1)} %get-tuple-element.170.part_ref), channel_id=1, source_target_pairs={{1,0},{0,1},{3,2},{2,3},{5,4},{4,5},{7,6},{6,7},{9,8},{8,9},{11,10... | collective-permute-start | bytes 786440 | tf_op jit(solution)/shard_map/ppermute | solution.py:944
  74.6 9.8 %collective-permute-start.18 = (bf16[256,512]{1,0:T(8,128)(2,1)S(1)}, bf16[256,512]{1,0:T(8,128)(2,1)S(1)}, u32[]{:S(2)}, u32[]{:S(2)}) collective-permute-start(bf16[256,512]{1,0:T(8,128)(2,1)S(1)} %get-tuple-element.191.part_ref), channel_id=1, source_target_pairs={{1,0},{0,1},{3,2},{2,3},{5,4},{4,5},{7,6},{6,7},{9,8},{8,9},{11,10... | collective-permute-start | bytes 786440 | tf_op jit(solution)/shard_map/ppermute | solution.py:944
  83.6 5.8 %collective-permute-start.19 = (bf16[512,1024]{1,0:T(8,128)(2,1)S(1)}, bf16[512,1024]{1,0:T(8,128)(2,1)S(1)}, u32[]{:S(2)}, u32[]{:S(2)}) collective-permute-start(bf16[512,1024]{1,0:T(8,128)(2,1)S(1)} %get-tuple-element.200), channel_id=1, source_target_pairs={{0,2},{2,0},{4,6},{6,4},{8,10},{10,8},{12,14},{14,12},{16,18},{18,... | collective-permute-start | bytes 3145736 | tf_op jit(solution)/shard_map/ppermute | solution.py:971
  83.7 10.6 %collective-permute-start.20 = (bf16[256,512]{1,0:T(8,128)(2,1)S(1)}, bf16[256,512]{1,0:T(8,128)(2,1)S(1)}, u32[]{:S(2)}, u32[]{:S(2)}) collective-permute-start(bf16[256,512]{1,0:T(8,128)(2,1)S(1)} %get-tuple-element.204.part_ref), channel_id=1, source_target_pairs={{1,0},{0,1},{3,2},{2,3},{5,4},{4,5},{7,6},{6,7},{9,8},{8,9},{11,10... | collective-permute-start | bytes 786440 | tf_op jit(solution)/shard_map/ppermute | solution.py:944
  89.6 10.5 %collective-permute-start.21 = (bf16[256,1024]{1,0:T(8,128)(2,1)S(1)}, bf16[256,1024]{1,0:T(8,128)(2,1)S(1)}, u32[]{:S(2)}, u32[]{:S(2)}) collective-permute-start(bf16[256,1024]{1,0:T(8,128)(2,1)S(1)} %get-tuple-element.217), channel_id=1, source_target_pairs={{0,4},{2,10},{4,0},{6,14},{8,12},{10,2},{12,8},{14,6},{16,20},{18,... | collective-permute-start | bytes 1572872 | tf_op jit(solution)/shard_map/ppermute | solution.py:971
  102.1 3.5 %collective-permute-start.22 = (bf16[1056,256]{1,0:T(8,128)(2,1)S(1)}, bf16[1056,256]{1,0:T(8,128)(2,1)S(1)}, u32[]{:S(2)}, u32[]{:S(2)}) collective-permute-start(bf16[1056,256]{1,0:T(8,128)(2,1)S(1)} %get-tuple-element.232), channel_id=1, source_target_pairs={{0,2},{2,0},{4,6},{6,4},{8,10},{10,8},{12,14},{14,12},{16,18},{18,... | collective-permute-start | bytes 1622024 | tf_op jit(solution)/shard_map/ppermute | solution.py:971
  104.3 16.6 %collective-permute-start.24 = (bf16[128,1024]{1,0:T(8,128)(2,1)S(1)}, bf16[128,1024]{1,0:T(8,128)(2,1)S(1)}, u32[]{:S(2)}, u32[]{:S(2)}) collective-permute-start(bf16[128,1024]{1,0:T(8,128)(2,1)S(1)} %get-tuple-element.243), channel_id=1, source_target_pairs={{0,8},{2,18},{4,12},{6,22},{8,0},{10,26},{12,4},{14,30},{16,24},{1... | collective-permute-start | bytes 786440 | tf_op jit(solution)/shard_map/ppermute | solution.py:971
  105.0 19.7 %collective-permute-start.26 = (bf16[384,512]{1,0:T(8,128)(2,1)S(1)}, bf16[384,512]{1,0:T(8,128)(2,1)S(1)}, u32[]{:S(2)}, u32[]{:S(2)}) collective-permute-start(bf16[384,512]{1,0:T(8,128)(2,1)S(1)} %get-tuple-element.248), channel_id=1, source_target_pairs={{2,4},{4,2},{6,8},{8,6},{10,12},{12,10},{14,16},{16,14},{18,20},{2... | collective-permute-start | bytes 1179656 | tf_op jit(solution)/shard_map/ppermute | solution.py:979
  105.8 18.9 %collective-permute-start.25 = (bf16[384,512]{1,0:T(8,128)(2,1)S(1)}, bf16[384,512]{1,0:T(8,128)(2,1)S(1)}, u32[]{:S(2)}, u32[]{:S(2)}) collective-permute-start(bf16[384,512]{1,0:T(8,128)(2,1)S(1)} %get-tuple-element.247), channel_id=1, source_target_pairs={{0,2},{2,0},{4,6},{6,4},{8,10},{10,8},{12,14},{14,12},{16,18},{18,... | collective-permute-start | bytes 1179656 | tf_op jit(solution)/shard_map/ppermute | solution.py:978
  109.2 11.6 %collective-permute-start.23 = (bf16[544,256]{1,0:T(8,128)(2,1)S(1)}, bf16[544,256]{1,0:T(8,128)(2,1)S(1)}, u32[]{:S(2)}, u32[]{:S(2)}) collective-permute-start(bf16[544,256]{1,0:T(8,128)(2,1)S(1)} %get-tuple-element.239), channel_id=1, source_target_pairs={{0,4},{2,10},{4,0},{6,14},{8,12},{10,2},{12,8},{14,6},{16,20},{18,... | collective-permute-start | bytes 835592 | tf_op jit(solution)/shard_map/ppermute | solution.py:971
  121.0 6.8 %collective-permute-start.28 = (bf16[288,256]{1,0:T(8,128)(2,1)S(1)}, bf16[288,256]{1,0:T(8,128)(2,1)S(1)}, u32[]{:S(2)}, u32[]{:S(2)}) collective-permute-start(bf16[288,256]{1,0:T(8,128)(2,1)S(1)} %get-tuple-element.252), channel_id=1, source_target_pairs={{0,8},{2,18},{4,12},{6,22},{8,0},{10,26},{12,4},{14,30},{16,24},{1... | collective-permute-start | bytes 442376 | tf_op jit(solution)/shard_map/ppermute | solution.py:971
  124.9 10.7 %collective-permute-start.27 = (bf16[512,256]{1,0:T(8,128)(2,1)S(1)}, bf16[512,256]{1,0:T(8,128)(2,1)S(1)}, u32[]{:S(2)}, u32[]{:S(2)}) collective-permute-start(bf16[512,256]{1,0:T(8,128)(2,1)S(1)} %get-tuple-element.250), channel_id=1, source_target_pairs={{1,0},{0,1},{3,2},{2,3},{5,4},{4,5},{7,6},{6,7},{9,8},{8,9},{11,10... | collective-permute-start | bytes 786440 | tf_op jit(solution)/shard_map/ppermute | solution.py:944
  126.4 6.7 %collective-permute-start.29 = (bf16[64,1024]{1,0:T(8,128)(2,1)S(1)}, bf16[64,1024]{1,0:T(8,128)(2,1)S(1)}, u32[]{:S(2)}, u32[]{:S(2)}) collective-permute-start(bf16[64,1024]{1,0:T(8,128)(2,1)S(1)} %get-tuple-element.256), channel_id=1, source_target_pairs={{0,16},{2,6},{4,20},{6,2},{8,24},{10,14},{12,28},{14,10},{16,0},{1... | collective-permute-start | bytes 393224 | tf_op jit(solution)/shard_map/ppermute | solution.py:971
  127.8 7.1 %collective-permute-start.30 = (bf16[160,256]{1,0:T(8,128)(2,1)S(1)}, bf16[160,256]{1,0:T(8,128)(2,1)S(1)}, u32[]{:S(2)}, u32[]{:S(2)}) collective-permute-start(bf16[160,256]{1,0:T(8,128)(2,1)S(1)} %get-tuple-element.259), channel_id=1, source_target_pairs={{0,16},{2,6},{4,20},{6,2},{8,24},{10,14},{12,28},{14,10},{16,0},{1... | collective-permute-start | bytes 245768 | tf_op jit(solution)/shard_map/ppermute | solution.py:971

commit v4 on v3

--- a/solution.py
+++ b/solution.py
@@ -70,23 +70,22 @@
     return jax.ShapeDtypeStruct(shape, dtype)
 
 
-def segment_of(positions, lengths_ref, token_count):
-    sequences, documents = lengths_ref.shape
+def segment_of(positions, lengths_ref, documents, token_count):
     found = jnp.zeros(positions.shape, jnp.int32)
     end = jnp.int32(0)
-    for sequence in range(sequences):
-        for document in range(documents):
-            end = end + lengths_ref[sequence, document]
-            found = found + (positions >= end).astype(jnp.int32)
+    for document in range(documents):
+        end = end + lengths_ref[document]
+        found = found + (positions >= end).astype(jnp.int32)
     return jnp.where((positions >= 0) & (positions < token_count), found, -1)
 
 
-def dense_kernel(fill, token_count, offset, lengths_ref, base_ref, band_ref, dense_ref):
-    first = base_ref[0] + (pl.program_id(0) + offset) * BLOCK
+def dense_kernel(fill, token_count, offset, lengths_ref, band_ref, dense_ref):
+    documents = lengths_ref.shape[0] - 1
+    first = lengths_ref[documents] + (pl.program_id(0) + offset) * BLOCK
     query = first + lax.broadcasted_iota(jnp.int32, (BLOCK, 1), 0)
     key = first - MAXDOC + lax.broadcasted_iota(jnp.int32, (1, WINDOW), 1)
-    same = segment_of(query, lengths_ref, token_count) == segment_of(
-        key, lengths_ref, token_count
+    same = segment_of(query, lengths_ref, documents, token_count) == segment_of(
+        key, lengths_ref, documents, token_count
     )
     for head in range(band_ref.shape[0]):
         wide = jnp.concatenate(
@@ -96,24 +95,20 @@
         dense_ref[head] = jnp.where(same, turned, fill).astype(BF16)
 
 
-def to_dense(banded, lengths, base, fill, token_count, chunk):
+def to_dense(banded, lengths, fill, token_count, chunk):
     heads, count, _ = banded.shape
     count //= CHUNKS
     offset = chunk * (count // BLOCK)
     return pl.pallas_call(
         functools.partial(dense_kernel, fill, token_count, offset),
         grid=(count // BLOCK,),
-        in_specs=[
-            pl.BlockSpec(memory_space=SMEM),
-            pl.BlockSpec(memory_space=SMEM),
-            heads_block(heads, BAND, offset),
-        ],
+        in_specs=[pl.BlockSpec(memory_space=SMEM), heads_block(heads, BAND, offset)],
         out_specs=heads_block(heads, WINDOW),
         out_shape=struct((heads, count, WINDOW), BF16),
         compiler_params=params(),
-        cost_estimate=lasting(8.0 if fill else 1.0),
+        cost_estimate=lasting(8.0 if fill and chunk == 0 else 1.0),
         name="to_dense",
-    )(lengths, base, banded)
+    )(lengths, banded)
 
 
 def band_kernel(masked, *refs):
@@ -160,7 +155,7 @@
         out_specs=heads_block(heads, BAND),
         out_shape=struct((heads, CHUNKS * count, BAND), BF16),
         compiler_params=params(),
-        cost_estimate=lasting(5.0),
+        cost_estimate=lasting(5.0 if masked else 0.5),
         name="to_band",
     )(*chunks)
 
@@ -862,9 +857,10 @@
 
 def token_grad_kernel(even_ref, *refs):
     query_refs, res_refs = refs[:CHUNKS], refs[CHUNKS : 2 * CHUNKS]
-    key_ref, value_ref, *weight_refs, own_ref, inside_ref, across_ref = refs[2 * CHUNKS :]
-    count = own_ref.shape[0]
-    own = res_refs[0].shape[1]
+    key_ref, value_ref, *weight_refs = refs[2 * CHUNKS : 2 * CHUNKS + 5]
+    own_ref, rim_ref, *out_refs = refs[2 * CHUNKS + 5 :]
+    own_outs, rim_outs = out_refs[: len(out_refs) // 2], out_refs[len(out_refs) // 2 :]
+    count, own = own_ref.shape
     even = even_ref[0] == 1
 
     def piece(start):
@@ -872,71 +868,95 @@
             value_ref[start : start + BLOCK, :], weight_refs[2][...]
         )
 
+    def spread(value, start, stays_ref, leave_refs):
+        stays_ref[start : start + BLOCK, :] = value[:, :own]
+        for place, ref in enumerate(leave_refs, 1):
+            lanes = slice(place * own, (place + 1) * own)
+            ref[start : start + BLOCK, :] = value[:, lanes].astype(BF16)
+
     for start in range(0, HALO, BLOCK):
-        low = piece(PAD + start).astype(BF16)
-        high = piece(MAXDOC + count + start).astype(BF16)
-        inside_ref[start : start + BLOCK, :] = jnp.where(even, high, low)
-        across_ref[start : start + BLOCK, :] = jnp.where(even, low, high)
+        low, high = piece(PAD + start), piece(MAXDOC + count + start)
+        spread(jnp.where(even, high, low), start, rim_ref, rim_outs)
+        spread(jnp.where(even, low, high), HALO + start, rim_ref, rim_outs)
     for start in range(0, count, BLOCK):
         chunk, inside = divmod(start, count // CHUNKS)
         total = piece(MAXDOC + start) + dot_nt(
             query_refs[chunk][inside : inside + BLOCK, :], weight_refs[0][...]
         )
-        own_ref[start : start + BLOCK, :] = total
-        own_ref[start : start + BLOCK, :own] += res_refs[chunk][inside : inside + BLOCK, :]
+        spread(total, start, own_ref, own_outs)
+        own_ref[start : start + BLOCK, :] += res_refs[chunk][inside : inside + BLOCK, :]
 
 
 def token_grads(even, query, res, key, value, weights):
     count = CHUNKS * query[0].shape[0]
-    features = weights[0].shape[0]
+    own = res[0].shape[1]
+    leave = weights[0].shape[0] // own - 1
     operands = (*query, *res, key, value, *weights)
-    shapes = [struct((count, features), F32)] + [struct((HALO, features), BF16)] * 2
-    return pl.pallas_call(
+    shapes = [struct((count, own), F32), struct((2 * HALO, own), F32)]
+    shapes += [struct((count, own), BF16)] * leave + [struct((2 * HALO, own), BF16)] * leave
+    result = pl.pallas_call(
         token_grad_kernel,
         grid=(1,),
         in_specs=[pl.BlockSpec(memory_space=SMEM)] + [whole(x.shape) for x in operands],
         out_specs=[whole(x.shape) for x in shapes],
         out_shape=shapes,
         compiler_params=params(),
-        cost_estimate=lasting(0.6),
+        cost_estimate=lasting(5.0),
         name="token_grads",
     )(even, *operands)
-
-
-def token_sum_kernel(even_ref, own_ref, inside_ref, across_ref, stays_ref, *leave_refs):
+    return result[0], result[1], result[2 : 2 + leave], result[2 + leave :]
+
+
+def rim_sum_kernel(rim_ref, *refs):
+    *arrived_refs, inside_ref, across_ref = refs
+    total = rim_ref[...] + sum(ref[...].astype(F32) for ref in arrived_refs)
+    inside_ref[...] = total[:HALO].astype(BF16)
+    across_ref[...] = total[HALO:].astype(BF16)
+
+
+def rim_sum(rim, arrived):
+    own = rim.shape[1]
+    operands = (rim, *arrived)
+    return pl.pallas_call(
+        rim_sum_kernel,
+        grid=(1,),
+        in_specs=[whole(x.shape) for x in operands],
+        out_specs=[whole((HALO, own))] * 2,
+        out_shape=[struct((HALO, own), BF16)] * 2,
+        compiler_params=params(),
+        cost_estimate=lasting(0.3),
+        name="rim_sum",
+    )(*operands)
+
+
+def token_sum_kernel(even_ref, own_ref, inside_ref, across_ref, *refs):
+    *arrived_refs, out_ref = refs
     even = even_ref[0] == 1
-    width = stays_ref.shape[1]
     inside, across = inside_ref[...].astype(F32), across_ref[...].astype(F32)
     low, high = jnp.where(even, across, inside), jnp.where(even, inside, across)
     rest = own_ref.shape[0] - HALO
     for start in range(0, own_ref.shape[0], BLOCK):
-        piece = own_ref[start : start + BLOCK, :]
+        rows_here = slice(start, start + BLOCK)
+        piece = own_ref[rows_here, :] + sum(ref[rows_here, :].astype(F32) for ref in arrived_refs)
         if start < HALO:
-            piece = piece + low[start : start + BLOCK, :]
+            piece = piece + low[rows_here, :]
         if start >= rest:
             piece = piece + high[start - rest : start - rest + BLOCK, :]
-        stays_ref[start : start + BLOCK, :] = piece[:, :width]
-        for place, ref in enumerate(leave_refs, 1):
-            ref[start : start + BLOCK, :] = piece[:, place * width : (place + 1) * width].astype(
-                BF16
-            )
-
-
-def token_sum(even, own, inside, across, width):
-    count, features = own.shape
-    shapes = [struct((count, width), F32)]
-    shapes += [struct((count, width), BF16)] * (features // width - 1)
+        out_ref[rows_here, :] = piece.astype(BF16)
+
+
+def token_sum(even, own, inside, across, arrived):
+    operands = (own, inside, across, *arrived)
     return pl.pallas_call(
         token_sum_kernel,
         grid=(1,),
-        in_specs=[pl.BlockSpec(memory_space=SMEM)]
-        + [whole(x.shape) for x in (own, inside, across)],
-        out_specs=[whole(x.shape) for x in shapes],
-        out_shape=shapes,
+        in_specs=[pl.BlockSpec(memory_space=SMEM)] + [whole(x.shape) for x in operands],
+        out_specs=whole(own.shape),
+        out_shape=struct(own.shape, BF16),
         compiler_params=params(),
         cost_estimate=lasting(0.3),
         name="token_sum",
-    )(even, own, inside, across)
+    )(even, *operands)
 
 
 def from_next(x, axis, step):
@@ -1067,13 +1087,13 @@
     turned = odd ^ (places >= half)
     met = jnp.where(turned, distances_of(odd_order, places), distances_of(even_order, places))
     blocks = (((met + (places >= half)) ^ row_index) - offset) % row_count
-    base = (row_index * count)[None]
+    lengths = jnp.concatenate([doc_lengths.reshape(-1), (row_index * count)[None]])
 
     even = 1 - row_index % 2
     even = even.astype(jnp.int32)[None]
 
     def dense_of(banded, fill, chunk, *needed):
-        dense = to_dense(after(banded, *needed), doc_lengths, base, fill, token_count, chunk)
+        dense = to_dense(after(banded, *needed), lengths, fill, token_count, chunk)
         return dense
 
     prev_logits = pltpu.with_memory_space_constraint(prev_logits, pltpu.HBM)
@@ -1085,15 +1105,14 @@
     tokens_full, inside, across = join(even, [tokens] + others(after(tokens, out_turned)))
     feed_rows = Gather(jnp.concatenate([out_turned, *out_other, up_weight, down_weight.T], 1))
     qkv_rows.put()
-    norms = jnp.concatenate([norm_gain, norm_shift, out_bias], 0)
     grad_full = jnp.concatenate([out_grad] + others(out_grad), 1)
-    prev_dense = [dense_of(prev_logits, MASKED_SCORE, 0, qkv_rows.held, grad_full)]
     inside, across = with_next(inside, across)
-    qkv_rows.put(prev_dense[0])
-    feed_rows.put(prev_dense[0])
-    prev_dense.append(
-        dense_of(prev_logits, MASKED_SCORE, 1, qkv_rows.held, feed_rows.held, tokens_full)
-    )
+    qkv_rows.put(tokens_full)
+    feed_rows.put(qkv_rows.held)
+    prev_dense = [
+        dense_of(prev_logits, MASKED_SCORE, 0, qkv_rows.held, feed_rows.held, tokens_full)
+    ]
+    prev_dense.append(dense_of(prev_logits, MASKED_SCORE, 1, prev_dense[0], grad_full))
     while qkv_rows.step < qkv_rows.count:
         qkv_rows.put(prev_dense[1], inside, across)
     feed_rows.put(qkv_rows.held)
@@ -1101,15 +1120,16 @@
         slots, even, after(tokens_full, feed_rows.held), inside, across, qkv_rows.held,
         qkv_rows.arrived, qv_bias,
     )
+    norms = jnp.concatenate([norm_gain, norm_shift, out_bias], 0)
+    norms = jnp.concatenate([norms] + others(after(norms, query)), 1)
     scores, probs, attended, attended_other = [], [], [], []
     for chunk in range(CHUNKS):
         score, prob, mix = attend_forward(query, key, value, prev_dense[chunk], chunk)
-        query = after(query, mix)
+        query = after(query, mix, norms)
         scores.append(score)
         probs.append(prob)
         attended.append(mix)
         attended_other.append(jnp.concatenate(others(mix), 1))
-    norms = jnp.concatenate([norms] + others(after(norms, mix)), 1)
     feed_rows.put(mix, attended_other[0])
     while feed_rows.step < feed_rows.count:
         feed_rows.put()
@@ -1170,21 +1190,26 @@
         key_grad, value_grad, branch_low, attended,
     )
     last_sum = Reduction(keep, send, sums, (3, 0), (2, 2, 2, 2, hidden_rows))
-    center, inside, across = token_grads(
+    center, rim, center_parts, rim_parts = token_grads(
         even, query_grad, res_one, after(key_grad, keep), value_grad, projections
     )
+
+    def spread_over(parts):
+        return [from_next(part, "col", -step) for step, part in enumerate(parts, 1)]
+
     last_sum.add(center)
-    inside, across = with_next(after(inside, last_sum.keep), across)
+    rim_parts = spread_over(rim_parts)
+    center_parts = spread_over(after(x, rim) for x in center_parts)
     prev_dense_grad[0] = after(prev_dense_grad[0], last_sum.keep)
     prev_grad = to_band(prev_dense_grad, False)
     last_sum.add(prev_grad)
-    feed_sum.add(last_sum.keep)
-    tokens_grad, *parts = token_sum(even, after(center, feed_sum.keep), inside, across, own)
-    for step, part in enumerate(parts, 1):
-        tokens_grad = tokens_grad + from_next(part, "col", -step).astype(F32)
-    last_sum.add(parts[0])
+    inside, across = rim_sum(after(rim, last_sum.keep), rim_parts)
+    feed_sum.add(inside)
+    inside, across = with_next(inside, across)
+    last_sum.add(feed_sum.keep)
+    tokens_grad = token_sum(even, after(center, last_sum.keep), inside, across, center_parts)
     while feed_sum.result is None:
-        feed_sum.add(last_sum.keep)
+        feed_sum.add(tokens_grad)
     while last_sum.result is None:
         last_sum.add(feed_sum.result[0])
     qkv_grad, out_grad_rows, qv_sum, bias_sum, gain_sum, shift_sum, hidden_sum = last_sum.result
@@ -1192,7 +1217,7 @@
     return (
         output,
         new_logits,
-        tokens_grad.astype(BF16),
+        tokens_grad,
         prev_grad,
         qkv_grad,
         qv_sum,

time: 137 us -> 127 us (0.927)
  waiting for transfers between devices: 21.6 us -> 14.2 us
  starting transfers between devices: 46.6 us -> 43 us
    ppermute x11 -> x12, waiting for transfers between devices: 11.4 us -> 6.11 us  [from_next(): lax.ppermute(x, axis, [((i + step) % count, i) for i in range(count)])]
    ppermute x16, starting transfers between devices: 29.2 us -> 25.4 us  [with_partner(): lax.ppermute(x, 'row', [(i, i ^ orders[i % 2][step]) for i in range(count)])]
    ppermute x16, waiting for transfers between devices: 10.2 us -> 8.13 us  [with_partner(): lax.ppermute(x, 'row', [(i, i ^ orders[i % 2][step]) for i in range(count)])]
    ppermute x11 -> x12, starting transfers between devices: 12.5 us -> 14.1 us  [from_next(): lax.ppermute(x, axis, [((i + step) % count, i) for i in range(count)])]
    ppermute x2, starting transfers between devices: 3.55 us -> 2.16 us  [with_next(): lax.ppermute(inside, 'row', [(i, i ^ 1) for i in range(count)])]
  transfers between devices with their start and end apart: 31 -> 32, of which waited for: 9 -> 6; matrix products, arithmetic and copies ran while one was open for 2% -> 3% of each run, Pallas kernels for 44% -> 48%
where the time goes in v4:
time: 127 us
  Pallas kernels  63.2 us (50%)
  starting transfers between devices  43 us (34%)
  waiting for transfers between devices  14.2 us (11%)
  other arithmetic  3.21 us (3%)
  local copies, waits for them, and re-layouts  2.2 us (2%)
    ppermute x16, starting transfers between devices, with_partner(): lax.ppermute(x, 'row', [(i, i ^ orders[i % 2][step]) for i in range(count)])  25.4 us
    ppermute x12, starting transfers between devices, from_next(): lax.ppermute(x, axis, [((i + step) % count, i) for i in range(count)])  14.1 us
    pallas_call x4, Pallas kernels, to_dense(): pl.pallas_call(functools.partial(dense_kernel, fill, token_count, offset)...  12.4 us
    pallas_call x2, Pallas kernels, to_band(): pl.pallas_call(functools.partial(band_kernel, masked), grid=(CHUNKS * ste...  10 us
    pallas_call x2, Pallas kernels, attend_backward(): pl.pallas_call(functools.partial(backward_kernel, offset, last), grid=(co...  9.17 us
    ppermute x16, waiting for transfers between devices, with_partner(): lax.ppermute(x, 'row', [(i, i ^ orders[i % 2][step]) for i in range(count)])  8.13 us
    pallas_call x2, Pallas kernels, attend_forward(): pl.pallas_call(functools.partial(forward_kernel, offset), grid=(count //...  7.69 us
    ppermute x12, waiting for transfers between devices, from_next(): lax.ppermute(x, axis, [((i + step) % count, i) for i in range(count)])  6.11 us
  transfers between devices with their start and end apart: 32, of which 6 were waited for; matrix products, arithmetic and copies ran while one was open for 3% of the time, Pallas kernels for 48%

profile of v4, /device:TPU:0, one launch (start us, length us, event | category | flops | bytes accessed | tf_op | source)
XLA Modules:
  0.0 127.0 jit_solution(10304181578544234466)
XLA Ops:
  0.6 3.0 %collective-permute-start.1 = (bf16[32,256]{1,0:T(8,128)(2,1)}, bf16[32,256]{1,0:T(8,128)(2,1)S(1)}, u32[]{:S(2)}, u32[]{:S(2)}) collective-permute-start(bf16[32,256]{1,0:T(8,128)(2,1)} %bitcast.17), channel_id=1, source_target_pairs={{1,0},{0,1},{3,2},{2,3},{5,4},{4,5},{7,6},{6,7},{9,8},{8,9},{11,10... | collective-permute-start | bytes 49160 | tf_op jit(solution)/shard_map/ppermute | solution.py:964
  3.7 3.0 %collective-permute-start.2 = (bf16[1,3,32,256]{3,2,1,0:T(8,128)(2,1)}, bf16[1,3,32,256]{3,2,1,0:T(8,128)(2,1)S(1)}, u32[]{:S(2)}, u32[]{:S(2)}) collective-permute-start(bf16[1,3,32,256]{3,2,1,0:T(8,128)(2,1)} %bitcast.15), channel_id=1, source_target_pairs={{0,16},{2,6},{4,20},{6,2},{8,24},{10,14},{12,28},{14,10},{16,0},{1... | collective-permute-start | bytes 147464 | tf_op jit(solution)/shard_map/ppermute | solution.py:991
  6.8 1.5 %collective-permute-start.5 = (bf16[512,256]{1,0:T(8,128)(2,1)}, bf16[512,256]{1,0:T(8,128)(2,1)S(1)}, u32[]{:S(2)}, u32[]{:S(2)}) collective-permute-start(bf16[512,256]{1,0:T(8,128)(2,1)} %param.26), channel_id=1, source_target_pairs={{1,0},{0,1},{3,2},{2,3},{5,4},{4,5},{7,6},{6,7},{9,8},{8,9},{11,10... | collective-permute-start | bytes 786440 | tf_op jit(solution)/shard_map/ppermute | solution.py:964
  8.3 1.0 constant_dynamic-update-slice_fusion.5
  9.3 0.7 pad_add_fusion.lengths_ref
  10.0 0.7 pad_maximum_fusion.2
  10.8 0.9 maximum_bitcast_fusion
  11.7 0.4 collective-permute-start.4
  12.1 0.8 pad_maximum_fusion
  12.9 1.6 %collective-permute-start.3 = (bf16[2,3,32,256]{3,2,1,0:T(8,128)(2,1)S(1)}, bf16[2,3,32,256]{3,2,1,0:T(8,128)(2,1)S(1)}, u32[]{:S(2)}, u32[]{:S(2)}) collective-permute-start(bf16[2,3,32,256]{3,2,1,0:T(8,128)(2,1)S(1)} %pad_maximum_fusion), channel_id=1, source_target_pairs={{0,8},{2,18},{4,12},{6,22},{8,0},{10,26},{12,4},{14,30},{16,24},{1... | collective-permute-start | bytes 294920 | tf_op jit(solution)/shard_map/ppermute | solution.py:991
  14.5 0.9 copy-done
  15.6 2.8 %collective-permute-done.3 = bf16[2,3,32,256]{3,2,1,0:T(8,128)(2,1)S(1)} collective-permute-done((bf16[2,3,32,256]{3,2,1,0:T(8,128)(2,1)S(1)}, bf16[2,3,32,256]{3,2,1,0:T(8,128)(2,1)S(1)}, u32[]{:S(2)}, u32[]{:S(2)}) %collective-permute-start.3) | collective-permute-done | bytes 98336 | tf_op jit(solution)/shard_map/ppermute | solution.py:991
  18.4 1.6 %collective-permute-start.8 = (bf16[4,3,32,256]{3,2,1,0:T(8,128)(2,1)S(1)}, bf16[4,3,32,256]{3,2,1,0:T(8,128)(2,1)S(1)}, u32[]{:S(2)}, u32[]{:S(2)}) collective-permute-start(bf16[4,3,32,256]{3,2,1,0:T(8,128)(2,1)S(1)} %constant_dynamic-update-slice_fusion), channel_id=1, source_target_pairs={{0,4},{2,10},{4,0},{6,14},{8,12},{10,2},{12,8},{14,6},{16,20},{18,... | collective-permute-start | bytes 589832 | tf_op jit(solution)/shard_map/ppermute | solution.py:991
  20.0 1.2 collective-permute-start.9
  21.3 1.5 %collective-permute-start.6 = (bf16[384,512]{1,0:T(8,128)(2,1)S(1)}, bf16[384,512]{1,0:T(8,128)(2,1)S(1)}, u32[]{:S(2)}, u32[]{:S(2)}) collective-permute-start(bf16[384,512]{1,0:T(8,128)(2,1)S(1)} %get-tuple-element.149), channel_id=1, source_target_pairs={{0,2},{2,0},{4,6},{6,4},{8,10},{10,8},{12,14},{14,12},{16,18},{18,... | collective-permute-start | bytes 1179656 | tf_op jit(solution)/shard_map/ppermute | solution.py:998
  22.7 0.7 collective-permute-start.7
  23.4 3.1 %to_dense.4.prev_ref = bf16[4,256,1152]{2,1,0:T(8,128)(2,1)S(1)} custom-call(s32[34]{0:T(128)S(1)} %pad_add_fusion.lengths_ref, bf16[4,512,1024]{2,1,0:T(8,128)(2,1)} %band_ref.1), custom_call_target="tpu_custom_call" | custom-call | flops 8000000000 | tf_op jit(solution)/shard_map/to_dense/pallas_call | solution.py:102
  26.5 3.1 %to_dense.5.prev_ref = bf16[4,256,1152]{2,1,0:T(8,128)(2,1)S(1)} custom-call(s32[34]{0:T(128)S(1)} %pad_add_fusion.lengths_ref, bf16[4,512,1024]{2,1,0:T(8,128)(2,1)} %band_ref.1), custom_call_target="tpu_custom_call" | custom-call | flops 1000000000 | tf_op jit(solution)/shard_map/to_dense/pallas_call | solution.py:102
  29.7 5.5 %collective-permute-start.10 = (bf16[8,3,32,256]{3,2,1,0:T(8,128)(2,1)S(1)}, bf16[8,3,32,256]{3,2,1,0:T(8,128)(2,1)S(1)}, u32[]{:S(2)}, u32[]{:S(2)}) collective-permute-start(bf16[8,3,32,256]{3,2,1,0:T(8,128)(2,1)S(1)} %constant_dynamic-update-slice_fusion.6.near_ref), channel_id=1, source_target_pairs={{0,2},{2,0},{4,6},{6,4},{8,10},{10,8},{12,14},{14,12},{16,18},{18,... | collective-permute-start | bytes 1179656 | tf_op jit(solution)/shard_map/ppermute | solution.py:991
  35.3 2.4 %collective-permute-start.14 = (bf16[4,32,2560]{2,1,0:T(8,128)(2,1)S(1)}, bf16[4,32,2560]{2,1,0:T(8,128)(2,1)S(1)}, u32[]{:S(2)}, u32[]{:S(2)}) collective-permute-start(bf16[4,32,2560]{2,1,0:T(8,128)(2,1)S(1)} %constant_dynamic-update-slice_fusion.8), channel_id=1, source_target_pairs={{0,4},{2,10},{4,0},{6,14},{8,12},{10,2},{12,8},{14,6},{16,20},{18,... | collective-permute-start | bytes 1966088 | tf_op jit(solution)/shard_map/ppermute | solution.py:991
  37.8 1.8 %project.1 = (bf16[512,256]{1,0:T(8,128)(2,1)S(1)}, bf16[1536,256]{1,0:T(8,128)(2,1)S(1)}, bf16[1536,256]{1,0:T(8,128)(2,1)S(1)}, bf16[384,512]{1,0:T(8,128)(2,1...) custom-call(s32[16]{0:T(128)S(1)} %fusion.7.slot_ref, ...), custom_call_target="tpu_custom_call" | custom-call | flops 2000000000 | tf_op jit(solution)/shard_map/project/pallas_call | solution.py:266
  39.6 0.6 collective-permute-start.11
  40.2 3.8 %attend_forward.2 = (bf16[4,256,1152]{2,1,0:T(8,128)(2,1)S(1)}, bf16[4,256,1152]{2,1,0:T(8,128)(2,1)S(1)}, bf16[256,256]{1,0:T(8,128)(2,1)S(1)}) custom-call(bf16[512,256]{1,0:T(8,128)(2,1)S(1)} %get-tuple-element.197.query_ref, bf16[1536,256]{1,0:T(8,128)(2,1)S(1)} %get-tuple-element.155.key_ref, bf16[1536,256]{1,0:T(8,128)(2,1)S(1)} %get-tuple-element.156.value_ref, ...), custom_call_target="tpu_custom_call" | custom-call | flops 3800000000 | tf_op jit(solution)/shard_map/attend_forward/pallas_call | solution.py:308
  44.0 1.6 %collective-permute-start.13 = (bf16[256,256]{1,0:T(8,128)(2,1)S(1)}, bf16[256,256]{1,0:T(8,128)(2,1)S(1)}, u32[]{:S(2)}, u32[]{:S(2)}) collective-permute-start(bf16[256,256]{1,0:T(8,128)(2,1)S(1)} %get-tuple-element.157.own_ref.refs_4_), channel_id=1, source_target_pairs={{1,0},{0,1},{3,2},{2,3},{5,4},{4,5},{7,6},{6,7},{9,8},{8,9},{11,10... | collective-permute-start | bytes 393224 | tf_op jit(solution)/shard_map/ppermute | solution.py:964
  45.6 3.9 %attend_forward.3 = (bf16[4,256,1152]{2,1,0:T(8,128)(2,1)S(1)}, bf16[4,256,1152]{2,1,0:T(8,128)(2,1)S(1)}, bf16[256,256]{1,0:T(8,128)(2,1)S(1)}) custom-call(bf16[512,256]{1,0:T(8,128)(2,1)S(1)} %get-tuple-element.197.query_ref, bf16[1536,256]{1,0:T(8,128)(2,1)S(1)} %get-tuple-element.155.key_ref, bf16[1536,256]{1,0:T(8,128)(2,1)S(1)} %get-tuple-element.156.value_ref, ...), custom_call_target="tpu_custom_call" | custom-call | flops 3800000000 | tf_op jit(solution)/shard_map/attend_forward/pallas_call | solution.py:308
  49.7 1.1 collective-permute-start.12
  50.8 5.0 %to_band.2 = bf16[4,512,1024]{2,1,0:T(8,128)(2,1)} custom-call(bf16[4,256,1152]{2,1,0:T(8,128)(2,1)S(1)} %get-tuple-element.163.refs_0_, bf16[4,256,1152]{2,1,0:T(8,128)(2,1)S(1)} %get-tuple-element.164.refs_1_), custom_call_target="tpu_custom_call" | custom-call | flops 5000000000 | tf_op jit(solution)/shard_map/to_band/pallas_call | solution.py:151
  55.8 1.1 in_order.1
  56.9 2.2 %feed_first.2 = (f32[256,512]{1,0:T(8,128)S(1)}, f32[256,1]{1,0:T(8,128)S(1)}, bf16[256,512]{1,0:T(8,128)(2,1)S(1)}, bf16[256,1024]{1,0:T(8,128)(2,1)S(1)}, bf16...) custom-call(bf16[256,256]{1,0:T(8,128)(2,1)S(1)} %get-tuple-element.157.own_ref.refs_4_, ...), custom_call_target="tpu_custom_call" | custom-call | flops 1000000000 | tf_op jit(solution)/shard_map/feed_first/pallas_call | solution.py:496
  59.1 1.0 collective-permute-start.16
  60.2 2.1 %feed_first.3 = (f32[256,512]{1,0:T(8,128)S(1)}, f32[256,1]{1,0:T(8,128)S(1)}, bf16[256,512]{1,0:T(8,128)(2,1)S(1)}, bf16[256,1024]{1,0:T(8,128)(2,1)S(1)}, bf16...) custom-call(bf16[256,256]{1,0:T(8,128)(2,1)S(1)} %get-tuple-element.160.own_ref.refs_5_, ...), custom_call_target="tpu_custom_call" | custom-call | flops 1000000000 | tf_op jit(solution)/shard_map/feed_first/pallas_call | solution.py:496
  62.3 1.1 collective-permute-start.17
  63.4 3.1 %to_dense.6.logit_ref = bf16[4,256,1152]{2,1,0:T(8,128)(2,1)S(1)} custom-call(s32[34]{0:T(128)S(1)} %pad_add_fusion.lengths_ref, bf16[4,512,1024]{2,1,0:T(8,128)(2,1)} %band_ref.3), custom_call_target="tpu_custom_call" | custom-call | flops 1000000000 | tf_op jit(solution)/shard_map/to_dense/pallas_call | solution.py:102
  66.5 1.8 %collective-permute-done.16.recv_ref = bf16[256,512]{1,0:T(8,128)(2,1)S(1)} collective-permute-done((bf16[256,512]{1,0:T(8,128)(2,1)S(1)}, bf16[256,512]{1,0:T(8,128)(2,1)S(1)}, u32[]{:S(2)}, u32[]{:S(2)}) %collective-permute-start.16) | collective-permute-done | bytes 262176 | tf_op jit(solution)/shard_map/ppermute | solution.py:964
  68.3 2.4 %feed_second.2 = (f32[16,256]{1,0:T(8,128)S(1)}, bf16[512,256]{1,0:T(8,128)(2,1)}, f32[256,512]{1,0:T(8,128)S(1)}, bf16[256,512]{1,0:T(8,128)(2,1)S(1)}, bf16[25...) custom-call(f32[16,256]{1,0:T(8,128)S(1)} %broadcast_in_dim.18.start_ref, ...), custom_call_target="tpu_custom_call" | custom-call | flops 700000000 | tf_op jit(solution)/shard_map/feed_second/pallas_call | solution.py:575
  70.8 1.0 collective-permute-start.18
  71.8 2.2 %collective-permute-done.17.recv_ref = bf16[256,512]{1,0:T(8,128)(2,1)S(1)} collective-permute-done((bf16[256,512]{1,0:T(8,128)(2,1)S(1)}, bf16[256,512]{1,0:T(8,128)(2,1)S(1)}, u32[]{:S(2)}, u32[]{:S(2)}) %collective-permute-start.17) | collective-permute-done | bytes 262176 | tf_op jit(solution)/shard_map/ppermute | solution.py:964
  74.0 2.4 %feed_second.3 = (f32[16,256]{1,0:T(8,128)S(1)}, bf16[512,256]{1,0:T(8,128)(2,1)}, f32[256,512]{1,0:T(8,128)S(1)}, bf16[256,512]{1,0:T(8,128)(2,1)S(1)}, bf16[25...) custom-call(f32[16,256]{1,0:T(8,128)S(1)} %get-tuple-element.177.start_ref, ...), custom_call_target="tpu_custom_call", output_to_operand_aliasing={{1}: (9, {})} | custom-call | flops 700000000 | tf_op jit(solution)/shard_map/feed_second/pallas_call | solution.py:575
  76.4 3.3 %feed_grads.1 = (f32[512,1024]{1,0:T(8,128)S(1)}, bf16[512,1024]{1,0:T(8,128)(2,1)S(1)}) custom-call(s32[16]{0:T(128)S(1)} %and_select_fusion.block_ref, bf16[256,512]{1,0:T(8,128)(2,1)S(1)} %get-tuple-element.183.refs_0_, bf16[256,512]{1,0:T(8,128)(2,1)S(1)} %get-tuple-element.184.refs_1_, bf16[256,512]{1,0:T(8,128)(2,1)S(1)} %get-tuple-element.185.refs_2_, ...), custom_call_target="tpu_custom_call" | custom-call | flops 1000000000 | tf_op jit(solution)/shard_map/feed_grads/pallas_call | solution.py:696
  79.8 1.0 collective-permute-start.20
  80.9 0.7 feed_third.2
  81.6 4.2 %attend_backward.2 = (bf16[4,256,1152]{2,1,0:T(8,128)(2,1)S(1)}, bf16[256,256]{1,0:T(8,128)(2,1)S(1)}, f32[256,1536]{1,0:T(8,128)S(1)}, f32[256,1536]{1,0:T(8,128)S(1)}) custom-call(bf16[256,256]{1,0:T(8,128)(2,1)S(1)} %get-tuple-element.196.grad_ref, bf16[512,256]{1,0:T(8,128)(2,1)S(1)} %get-tuple-element.197.query_ref, ...), custom_call_target="tpu_custom_call" | custom-call | flops 20000000000 | tf_op jit(solution)/shard_map/attend_backward/pallas_call | solution.py:392
  86.1 1.6 %collective-permute-start.21 = (bf16[256,1024]{1,0:T(8,128)(2,1)S(1)}, bf16[256,1024]{1,0:T(8,128)(2,1)S(1)}, u32[]{:S(2)}, u32[]{:S(2)}) collective-permute-start(bf16[256,1024]{1,0:T(8,128)(2,1)S(1)} %get-tuple-element.219), channel_id=1, source_target_pairs={{0,4},{2,10},{4,0},{6,14},{8,12},{10,2},{12,8},{14,6},{16,20},{18,... | collective-permute-start | bytes 1572872 | tf_op jit(solution)/shard_map/ppermute | solution.py:991
  87.7 3.1 %to_dense.7.logit_ref = bf16[4,256,1152]{2,1,0:T(8,128)(2,1)S(1)} custom-call(s32[34]{0:T(128)S(1)} %pad_add_fusion.lengths_ref, bf16[4,512,1024]{2,1,0:T(8,128)(2,1)} %band_ref.3), custom_call_target="tpu_custom_call" | custom-call | flops 1000000000 | tf_op jit(solution)/shard_map/to_dense/pallas_call | solution.py:102
  90.8 0.8 feed_third.3
  91.6 5.0 %attend_backward.3 = (bf16[4,256,1152]{2,1,0:T(8,128)(2,1)S(1)}, bf16[256,256]{1,0:T(8,128)(2,1)S(1)}, bf16[1536,256]{1,0:T(8,128)(2,1)S(1)}, bf16[1536,256]{1,0:T(8,128)(2,1)S(1)}) custom-call(bf16[256,256]{1,0:T(8,128)(2,1)S(1)} %get-tuple-element.209.grad_ref, bf16[512,256]{1,0:T(8,128)(2,1)S(1)} %get-tuple-element.197.query_ref, ...), custom_call_target="tpu_custom_call" | custom-call | flops 3000000000 | tf_op jit(solution)/shard_map/attend_backward/pallas_call | solution.py:392
  96.6 1.9 %project_grads.1 = (f32[1024,256]{1,0:T(8,128)S(1)}, bf16[1056,256]{1,0:T(8,128)(2,1)S(1)}, f32[16,256]{1,0:T(8,128)S(1)}) custom-call(s32[16]{0:T(128)S(1)} %and_select_fusion.block_ref, f32[16,256]{1,0:T(8,128)S(1)} %get-tuple-element.221.start_ref, bf16[256,256]{1,0:T(8,128)(2,1)S(1)} %get-tuple-element.199.refs_0_, ...), custom_call_target="tpu_custom_call" | custom-call | flops 600000000 | tf_op jit(solution)/shard_map/project_grads/pallas_call | solution.py:753
  98.6 2.1 %token_grads.1 = (f32[512,256]{1,0:T(8,128)S(1)}, f32[768,256]{1,0:T(8,128)S(1)}, bf16[512,256]{1,0:T(8,128)(2,1)S(1)}, bf16[768,256]{1,0:T(8,128)(2,1)S(1)}) custom-call(s32[1]{0:T(128)} %bitcast.2.even_ref, bf16[256,256]{1,0:T(8,128)(2,1)S(1)} %get-tuple-element.199.refs_0_, bf16[256,256]{1,0:T(8,128)(2,1)S(1)} %get-tuple-element.213.refs_1_, ...), custom_call_target="tpu_custom_call" | custom-call | flops 5000000000 | tf_op jit(solution)/shard_map/token_grads/pallas_call | solution.py:897
  100.8 1.4 %collective-permute-start.24 = (bf16[768,256]{1,0:T(8,128)(2,1)S(1)}, bf16[768,256]{1,0:T(8,128)(2,1)S(1)}, u32[]{:S(2)}, u32[]{:S(2)}) collective-permute-start(bf16[768,256]{1,0:T(8,128)(2,1)S(1)} %get-tuple-element.246), channel_id=1, source_target_pairs={{1,0},{0,1},{3,2},{2,3},{5,4},{4,5},{7,6},{6,7},{9,8},{8,9},{11,10... | collective-permute-start | bytes 1179656 | tf_op jit(solution)/shard_map/ppermute | solution.py:964
  102.3 0.5 collective-permute-start.23
  102.8 1.5 %collective-permute-start.25 = (bf16[128,1024]{1,0:T(8,128)(2,1)S(1)}, bf16[128,1024]{1,0:T(8,128)(2,1)S(1)}, u32[]{:S(2)}, u32[]{:S(2)}) collective-permute-start(bf16[128,1024]{1,0:T(8,128)(2,1)S(1)} %get-tuple-element.249), channel_id=1, source_target_pairs={{0,8},{2,18},{4,12},{6,22},{8,0},{10,26},{12,4},{14,30},{16,24},{1... | collective-permute-start | bytes 786440 | tf_op jit(solution)/shard_map/ppermute | solution.py:991
  104.3 0.7 collective-permute-start.29
  104.9 5.0 %to_band.3 = bf16[4,512,1024]{2,1,0:T(8,128)(2,1)} custom-call(bf16[4,256,1152]{2,1,0:T(8,128)(2,1)S(1)} %get-tuple-element.238.refs_0_, bf16[4,256,1152]{2,1,0:T(8,128)(2,1)S(1)} %get-tuple-element.239.refs_1_), custom_call_target="tpu_custom_call" | custom-call | flops 500000000 | tf_op jit(solution)/shard_map/to_band/pallas_call | solution.py:151
  110.0 0.7 collective-permute-start.26
  110.7 2.1 %collective-permute-done.24.refs_0_ = bf16[768,256]{1,0:T(8,128)(2,1)S(1)} collective-permute-done((bf16[768,256]{1,0:T(8,128)(2,1)S(1)}, bf16[768,256]{1,0:T(8,128)(2,1)S(1)}, u32[]{:S(2)}, u32[]{:S(2)}) %collective-permute-start.24) | collective-permute-done | bytes 393248 | tf_op jit(solution)/shard_map/ppermute | solution.py:964
  112.8 0.7 collective-permute-start.27
  113.6 0.7 collective-permute-start.28
  114.3 3.8 %collective-permute-start.30 = (bf16[64,1024]{1,0:T(8,128)(2,1)S(1)}, bf16[64,1024]{1,0:T(8,128)(2,1)S(1)}, u32[]{:S(2)}, u32[]{:S(2)}) collective-permute-start(bf16[64,1024]{1,0:T(8,128)(2,1)S(1)} %get-tuple-element.260), channel_id=1, source_target_pairs={{0,16},{2,6},{4,20},{6,2},{8,24},{10,14},{12,28},{14,10},{16,0},{1... | collective-permute-start | bytes 393224 | tf_op jit(solution)/shard_map/ppermute | solution.py:991
  118.2 1.2 collective-permute-start.31
  119.4 0.9 token_sum.1
  120.3 2.9 %collective-permute-done.30.arrived_ref = bf16[64,1024]{1,0:T(8,128)(2,1)S(1)} collective-permute-done((bf16[64,1024]{1,0:T(8,128)(2,1)S(1)}, bf16[64,1024]{1,0:T(8,128)(2,1)S(1)}, u32[]{:S(2)}, u32[]{:S(2)}) %collective-permute-start.30) | collective-permute-done | bytes 131104 | tf_op jit(solution)/shard_map/ppermute | solution.py:991
  123.2 0.7 finish.2
  123.9 2.4 %collective-permute-done.31.arrived_ref = bf16[160,256]{1,0:T(8,128)(2,1)S(1)} collective-permute-done((bf16[160,256]{1,0:T(8,128)(2,1)S(1)}, bf16[160,256]{1,0:T(8,128)(2,1)S(1)}, u32[]{:S(2)}, u32[]{:S(2)}) %collective-permute-start.31) | collective-permute-done | bytes 81952 | tf_op jit(solution)/shard_map/ppermute | solution.py:991
  126.3 0.7 finish.3
  (64 shorter events, 1.4 us)
Async XLA Ops:
  0.6 10.1 %collective-permute-start.1 = (bf16[32,256]{1,0:T(8,128)(2,1)}, bf16[32,256]{1,0:T(8,128)(2,1)S(1)}, u32[]{:S(2)}, u32[]{:S(2)}) collective-permute-start(bf16[32,256]{1,0:T(8,128)(2,1)} %bitcast.17), channel_id=1, source_target_pairs={{1,0},{0,1},{3,2},{2,3},{5,4},{4,5},{7,6},{6,7},{9,8},{8,9},{11,10... | collective-permute-start | bytes 49160 | tf_op jit(solution)/shard_map/ppermute | solution.py:964
  3.6 10.9 %collective-permute-start = (bf16[512,256]{1,0:T(8,128)(2,1)}, bf16[512,256]{1,0:T(8,128)(2,1)S(1)}, u32[]{:S(2)}, u32[]{:S(2)}) collective-permute-start(bf16[512,256]{1,0:T(8,128)(2,1)} %refs_0_.1), channel_id=1, source_target_pairs={{1,0},{0,1},{3,2},{2,3},{5,4},{4,5},{7,6},{6,7},{9,8},{8,9},{11,10... | collective-permute-start | bytes 786440 | tf_op jit(solution)/shard_map/ppermute | solution.py:964
  3.7 8.3 %collective-permute-start.2 = (bf16[1,3,32,256]{3,2,1,0:T(8,128)(2,1)}, bf16[1,3,32,256]{3,2,1,0:T(8,128)(2,1)S(1)}, u32[]{:S(2)}, u32[]{:S(2)}) collective-permute-start(bf16[1,3,32,256]{3,2,1,0:T(8,128)(2,1)} %bitcast.15), channel_id=1, source_target_pairs={{0,16},{2,6},{4,20},{6,2},{8,24},{10,14},{12,28},{14,10},{16,0},{1... | collective-permute-start | bytes 147464 | tf_op jit(solution)/shard_map/ppermute | solution.py:991
  6.8 19.7 %collective-permute-start.5 = (bf16[512,256]{1,0:T(8,128)(2,1)}, bf16[512,256]{1,0:T(8,128)(2,1)S(1)}, u32[]{:S(2)}, u32[]{:S(2)}) collective-permute-start(bf16[512,256]{1,0:T(8,128)(2,1)} %param.26), channel_id=1, source_target_pairs={{1,0},{0,1},{3,2},{2,3},{5,4},{4,5},{7,6},{6,7},{9,8},{8,9},{11,10... | collective-permute-start | bytes 786440 | tf_op jit(solution)/shard_map/ppermute | solution.py:964
  11.7 8.3 %collective-permute-start.4 = (bf16[1,32,2560]{2,1,0:T(8,128)(2,1)S(1)}, bf16[1,32,2560]{2,1,0:T(8,128)(2,1)S(1)}, u32[]{:S(2)}, u32[]{:S(2)}) collective-permute-start(bf16[1,32,2560]{2,1,0:T(8,128)(2,1)S(1)} %maximum_bitcast_fusion), channel_id=1, source_target_pairs={{0,16},{2,6},{4,20},{6,2},{8,24},{10,14},{12,28},{14,10},{16,0},{1... | collective-permute-start | bytes 491528 | tf_op jit(solution)/shard_map/ppermute | solution.py:991
  12.9 5.5 %collective-permute-start.3 = (bf16[2,3,32,256]{3,2,1,0:T(8,128)(2,1)S(1)}, bf16[2,3,32,256]{3,2,1,0:T(8,128)(2,1)S(1)}, u32[]{:S(2)}, u32[]{:S(2)}) collective-permute-start(bf16[2,3,32,256]{3,2,1,0:T(8,128)(2,1)S(1)} %pad_maximum_fusion), channel_id=1, source_target_pairs={{0,8},{2,18},{4,12},{6,22},{8,0},{10,26},{12,4},{14,30},{16,24},{1... | collective-permute-start | bytes 294920 | tf_op jit(solution)/shard_map/ppermute | solution.py:991
  14.5 1.0 copy-start
  18.4 11.3 %collective-permute-start.8 = (bf16[4,3,32,256]{3,2,1,0:T(8,128)(2,1)S(1)}, bf16[4,3,32,256]{3,2,1,0:T(8,128)(2,1)S(1)}, u32[]{:S(2)}, u32[]{:S(2)}) collective-permute-start(bf16[4,3,32,256]{3,2,1,0:T(8,128)(2,1)S(1)} %constant_dynamic-update-slice_fusion), channel_id=1, source_target_pairs={{0,4},{2,10},{4,0},{6,14},{8,12},{10,2},{12,8},{14,6},{16,20},{18,... | collective-permute-start | bytes 589832 | tf_op jit(solution)/shard_map/ppermute | solution.py:991
  20.0 15.3 %collective-permute-start.9 = (bf16[2,32,2560]{2,1,0:T(8,128)(2,1)S(1)}, bf16[2,32,2560]{2,1,0:T(8,128)(2,1)S(1)}, u32[]{:S(2)}, u32[]{:S(2)}) collective-permute-start(bf16[2,32,2560]{2,1,0:T(8,128)(2,1)S(1)} %constant_dynamic-update-slice_fusion.2), channel_id=1, source_target_pairs={{0,8},{2,18},{4,12},{6,22},{8,0},{10,26},{12,4},{14,30},{16,24},{1... | collective-permute-start | bytes 983048 | tf_op jit(solution)/shard_map/ppermute | solution.py:991
  21.3 8.4 %collective-permute-start.6 = (bf16[384,512]{1,0:T(8,128)(2,1)S(1)}, bf16[384,512]{1,0:T(8,128)(2,1)S(1)}, u32[]{:S(2)}, u32[]{:S(2)}) collective-permute-start(bf16[384,512]{1,0:T(8,128)(2,1)S(1)} %get-tuple-element.149), channel_id=1, source_target_pairs={{0,2},{2,0},{4,6},{6,4},{8,10},{10,8},{12,14},{14,12},{16,18},{18,... | collective-permute-start | bytes 1179656 | tf_op jit(solution)/shard_map/ppermute | solution.py:998
  22.7 7.0 %collective-permute-start.7 = (bf16[384,512]{1,0:T(8,128)(2,1)S(1)}, bf16[384,512]{1,0:T(8,128)(2,1)S(1)}, u32[]{:S(2)}, u32[]{:S(2)}) collective-permute-start(bf16[384,512]{1,0:T(8,128)(2,1)S(1)} %get-tuple-element.150), channel_id=1, source_target_pairs={{2,4},{4,2},{6,8},{8,6},{10,12},{12,10},{14,16},{16,14},{18,20},{2... | collective-permute-start | bytes 1179656 | tf_op jit(solution)/shard_map/ppermute | solution.py:999
  26.5 11.3 %copy-start.2 = (f32[2,256]{1,0:T(2,128)S(1)}, f32[2,256]{1,0:T(2,128)}, u32[]{:S(2)}) copy-start(f32[2,256]{1,0:T(2,128)} %bias_ref.1) | copy-start | bytes 6148
  29.7 8.0 %collective-permute-start.10 = (bf16[8,3,32,256]{3,2,1,0:T(8,128)(2,1)S(1)}, bf16[8,3,32,256]{3,2,1,0:T(8,128)(2,1)S(1)}, u32[]{:S(2)}, u32[]{:S(2)}) collective-permute-start(bf16[8,3,32,256]{3,2,1,0:T(8,128)(2,1)S(1)} %constant_dynamic-update-slice_fusion.6.near_ref), channel_id=1, source_target_pairs={{0,2},{2,0},{4,6},{6,4},{8,10},{10,8},{12,14},{14,12},{16,18},{18,... | collective-permute-start | bytes 1179656 | tf_op jit(solution)/shard_map/ppermute | solution.py:991
  35.3 14.2 %collective-permute-start.14 = (bf16[4,32,2560]{2,1,0:T(8,128)(2,1)S(1)}, bf16[4,32,2560]{2,1,0:T(8,128)(2,1)S(1)}, u32[]{:S(2)}, u32[]{:S(2)}) collective-permute-start(bf16[4,32,2560]{2,1,0:T(8,128)(2,1)S(1)} %constant_dynamic-update-slice_fusion.8), channel_id=1, source_target_pairs={{0,4},{2,10},{4,0},{6,14},{8,12},{10,2},{12,8},{14,6},{16,20},{18,... | collective-permute-start | bytes 1966088 | tf_op jit(solution)/shard_map/ppermute | solution.py:991
  39.6 6.0 %collective-permute-start.11 = (f32[6,256]{1,0:T(8,128)S(1)}, f32[6,256]{1,0:T(8,128)S(1)}, u32[]{:S(2)}, u32[]{:S(2)}) collective-permute-start(f32[6,256]{1,0:T(8,128)S(1)} %pad_maximum_fusion.2), channel_id=1, source_target_pairs={{1,0},{0,1},{3,2},{2,3},{5,4},{4,5},{7,6},{6,7},{9,8},{8,9},{11,10... | collective-permute-start | bytes 18440 | tf_op jit(solution)/shard_map/ppermute | solution.py:964
  40.2 5.4 %copy-start.3 = (f32[2,256]{1,0:T(2,128)S(1)}, f32[2,256]{1,0:T(2,128)}, u32[]{:S(2)}) copy-start(f32[2,256]{1,0:T(2,128)} %param.20) | copy-start | bytes 6148
  40.2 5.4 %copy-start.4 = (f32[2,256]{1,0:T(2,128)S(1)}, f32[2,256]{1,0:T(2,128)}, u32[]{:S(2)}) copy-start(f32[2,256]{1,0:T(2,128)} %param.25) | copy-start | bytes 6148
  40.2 5.4 %copy-start.5 = (f32[2,256]{1,0:T(2,128)S(1)}, f32[2,256]{1,0:T(2,128)}, u32[]{:S(2)}) copy-start(f32[2,256]{1,0:T(2,128)} %param.24) | copy-start | bytes 6148
  44.0 5.5 %collective-permute-start.13 = (bf16[256,256]{1,0:T(8,128)(2,1)S(1)}, bf16[256,256]{1,0:T(8,128)(2,1)S(1)}, u32[]{:S(2)}, u32[]{:S(2)}) collective-permute-start(bf16[256,256]{1,0:T(8,128)(2,1)S(1)} %get-tuple-element.157.own_ref.refs_4_), channel_id=1, source_target_pairs={{1,0},{0,1},{3,2},{2,3},{5,4},{4,5},{7,6},{6,7},{9,8},{8,9},{11,10... | collective-permute-start | bytes 393224 | tf_op jit(solution)/shard_map/ppermute | solution.py:964
  49.6 6.2 %collective-permute-start.15 = (bf16[8,32,2560]{2,1,0:T(8,128)(2,1)S(1)}, bf16[8,32,2560]{2,1,0:T(8,128)(2,1)S(1)}, u32[]{:S(2)}, u32[]{:S(2)}) collective-permute-start(bf16[8,32,2560]{2,1,0:T(8,128)(2,1)S(1)} %constant_dynamic-update-slice_fusion.10.near_ref), channel_id=1, source_target_pairs={{0,2},{2,0},{4,6},{6,4},{8,10},{10,8},{12,14},{14,12},{16,18},{18,... | collective-permute-start | bytes 3932168 | tf_op jit(solution)/shard_map/ppermute | solution.py:991
  49.7 10.5 %collective-permute-start.12 = (bf16[256,256]{1,0:T(8,128)(2,1)S(1)}, bf16[256,256]{1,0:T(8,128)(2,1)S(1)}, u32[]{:S(2)}, u32[]{:S(2)}) collective-permute-start(bf16[256,256]{1,0:T(8,128)(2,1)S(1)} %get-tuple-element.160.own_ref.refs_5_), channel_id=1, source_target_pairs={{1,0},{0,1},{3,2},{2,3},{5,4},{4,5},{7,6},{6,7},{9,8},{8,9},{11,10... | collective-permute-start | bytes 393224 | tf_op jit(solution)/shard_map/ppermute | solution.py:964
  55.8 1.1 copy-start.1
  59.1 9.2 %collective-permute-start.16 = (bf16[256,512]{1,0:T(8,128)(2,1)S(1)}, bf16[256,512]{1,0:T(8,128)(2,1)S(1)}, u32[]{:S(2)}, u32[]{:S(2)}) collective-permute-start(bf16[256,512]{1,0:T(8,128)(2,1)S(1)} %get-tuple-element.170.part_ref), channel_id=1, source_target_pairs={{1,0},{0,1},{3,2},{2,3},{5,4},{4,5},{7,6},{6,7},{9,8},{8,9},{11,10... | collective-permute-start | bytes 786440 | tf_op jit(solution)/shard_map/ppermute | solution.py:964
  62.3 11.6 %collective-permute-start.17 = (bf16[256,512]{1,0:T(8,128)(2,1)S(1)}, bf16[256,512]{1,0:T(8,128)(2,1)S(1)}, u32[]{:S(2)}, u32[]{:S(2)}) collective-permute-start(bf16[256,512]{1,0:T(8,128)(2,1)S(1)} %get-tuple-element.172.part_ref), channel_id=1, source_target_pairs={{1,0},{0,1},{3,2},{2,3},{5,4},{4,5},{7,6},{6,7},{9,8},{8,9},{11,10... | collective-permute-start | bytes 786440 | tf_op jit(solution)/shard_map/ppermute | solution.py:964
  70.8 10.1 %collective-permute-start.18 = (bf16[256,512]{1,0:T(8,128)(2,1)S(1)}, bf16[256,512]{1,0:T(8,128)(2,1)S(1)}, u32[]{:S(2)}, u32[]{:S(2)}) collective-permute-start(bf16[256,512]{1,0:T(8,128)(2,1)S(1)} %get-tuple-element.193.part_ref), channel_id=1, source_target_pairs={{1,0},{0,1},{3,2},{2,3},{5,4},{4,5},{7,6},{6,7},{9,8},{8,9},{11,10... | collective-permute-start | bytes 786440 | tf_op jit(solution)/shard_map/ppermute | solution.py:964
  79.7 6.1 %collective-permute-start.19 = (bf16[512,1024]{1,0:T(8,128)(2,1)S(1)}, bf16[512,1024]{1,0:T(8,128)(2,1)S(1)}, u32[]{:S(2)}, u32[]{:S(2)}) collective-permute-start(bf16[512,1024]{1,0:T(8,128)(2,1)S(1)} %get-tuple-element.202), channel_id=1, source_target_pairs={{0,2},{2,0},{4,6},{6,4},{8,10},{10,8},{12,14},{14,12},{16,18},{18,... | collective-permute-start | bytes 3145736 | tf_op jit(solution)/shard_map/ppermute | solution.py:991
  79.8 11.0 %collective-permute-start.20 = (bf16[256,512]{1,0:T(8,128)(2,1)S(1)}, bf16[256,512]{1,0:T(8,128)(2,1)S(1)}, u32[]{:S(2)}, u32[]{:S(2)}) collective-permute-start(bf16[256,512]{1,0:T(8,128)(2,1)S(1)} %get-tuple-element.206.part_ref), channel_id=1, source_target_pairs={{1,0},{0,1},{3,2},{2,3},{5,4},{4,5},{7,6},{6,7},{9,8},{8,9},{11,10... | collective-permute-start | bytes 786440 | tf_op jit(solution)/shard_map/ppermute | solution.py:964
  86.1 10.5 %collective-permute-start.21 = (bf16[256,1024]{1,0:T(8,128)(2,1)S(1)}, bf16[256,1024]{1,0:T(8,128)(2,1)S(1)}, u32[]{:S(2)}, u32[]{:S(2)}) collective-permute-start(bf16[256,1024]{1,0:T(8,128)(2,1)S(1)} %get-tuple-element.219), channel_id=1, source_target_pairs={{0,4},{2,10},{4,0},{6,14},{8,12},{10,2},{12,8},{14,6},{16,20},{18,... | collective-permute-start | bytes 1572872 | tf_op jit(solution)/shard_map/ppermute | solution.py:991
  98.6 3.6 %collective-permute-start.22 = (bf16[1056,256]{1,0:T(8,128)(2,1)S(1)}, bf16[1056,256]{1,0:T(8,128)(2,1)S(1)}, u32[]{:S(2)}, u32[]{:S(2)}) collective-permute-start(bf16[1056,256]{1,0:T(8,128)(2,1)S(1)} %get-tuple-element.234), channel_id=1, source_target_pairs={{0,2},{2,0},{4,6},{6,4},{8,10},{10,8},{12,14},{14,12},{16,18},{18,... | collective-permute-start | bytes 1622024 | tf_op jit(solution)/shard_map/ppermute | solution.py:991
  100.8 12.0 %collective-permute-start.24 = (bf16[768,256]{1,0:T(8,128)(2,1)S(1)}, bf16[768,256]{1,0:T(8,128)(2,1)S(1)}, u32[]{:S(2)}, u32[]{:S(2)}) collective-permute-start(bf16[768,256]{1,0:T(8,128)(2,1)S(1)} %get-tuple-element.246), channel_id=1, source_target_pairs={{1,0},{0,1},{3,2},{2,3},{5,4},{4,5},{7,6},{6,7},{9,8},{8,9},{11,10... | collective-permute-start | bytes 1179656 | tf_op jit(solution)/shard_map/ppermute | solution.py:964
  102.3 7.7 %collective-permute-start.23 = (bf16[544,256]{1,0:T(8,128)(2,1)S(1)}, bf16[544,256]{1,0:T(8,128)(2,1)S(1)}, u32[]{:S(2)}, u32[]{:S(2)}) collective-permute-start(bf16[544,256]{1,0:T(8,128)(2,1)S(1)} %get-tuple-element.241), channel_id=1, source_target_pairs={{0,4},{2,10},{4,0},{6,14},{8,12},{10,2},{12,8},{14,6},{16,20},{18,... | collective-permute-start | bytes 835592 | tf_op jit(solution)/shard_map/ppermute | solution.py:991
  102.8 11.5 %collective-permute-start.25 = (bf16[128,1024]{1,0:T(8,128)(2,1)S(1)}, bf16[128,1024]{1,0:T(8,128)(2,1)S(1)}, u32[]{:S(2)}, u32[]{:S(2)}) collective-permute-start(bf16[128,1024]{1,0:T(8,128)(2,1)S(1)} %get-tuple-element.249), channel_id=1, source_target_pairs={{0,8},{2,18},{4,12},{6,22},{8,0},{10,26},{12,4},{14,30},{16,24},{1... | collective-permute-start | bytes 786440 | tf_op jit(solution)/shard_map/ppermute | solution.py:991
  104.3 15.2 %collective-permute-start.29 = (bf16[512,256]{1,0:T(8,128)(2,1)S(1)}, bf16[512,256]{1,0:T(8,128)(2,1)S(1)}, u32[]{:S(2)}, u32[]{:S(2)}) collective-permute-start(bf16[512,256]{1,0:T(8,128)(2,1)S(1)} %get-tuple-element.258), channel_id=1, source_target_pairs={{1,0},{0,1},{3,2},{2,3},{5,4},{4,5},{7,6},{6,7},{9,8},{8,9},{11,10... | collective-permute-start | bytes 786440 | tf_op jit(solution)/shard_map/ppermute | solution.py:964
  110.0 8.1 %collective-permute-start.26 = (bf16[288,256]{1,0:T(8,128)(2,1)S(1)}, bf16[288,256]{1,0:T(8,128)(2,1)S(1)}, u32[]{:S(2)}, u32[]{:S(2)}) collective-permute-start(bf16[288,256]{1,0:T(8,128)(2,1)S(1)} %get-tuple-element.252), channel_id=1, source_target_pairs={{0,8},{2,18},{4,12},{6,22},{8,0},{10,26},{12,4},{14,30},{16,24},{1... | collective-permute-start | bytes 442376 | tf_op jit(solution)/shard_map/ppermute | solution.py:991
  112.8 6.6 %collective-permute-start.27 = (bf16[384,256]{1,0:T(8,128)(2,1)S(1)}, bf16[384,256]{1,0:T(8,128)(2,1)S(1)}, u32[]{:S(2)}, u32[]{:S(2)}) collective-permute-start(bf16[384,256]{1,0:T(8,128)(2,1)S(1)} %get-tuple-element.247), channel_id=1, source_target_pairs={{0,2},{2,0},{4,6},{6,4},{8,10},{10,8},{12,14},{14,12},{16,18},{18,... | collective-permute-start | bytes 589832 | tf_op jit(solution)/shard_map/ppermute | solution.py:998
  113.6 5.9 %collective-permute-start.28 = (bf16[384,256]{1,0:T(8,128)(2,1)S(1)}, bf16[384,256]{1,0:T(8,128)(2,1)S(1)}, u32[]{:S(2)}, u32[]{:S(2)}) collective-permute-start(bf16[384,256]{1,0:T(8,128)(2,1)S(1)} %get-tuple-element.256), channel_id=1, source_target_pairs={{2,4},{4,2},{6,8},{8,6},{10,12},{12,10},{14,16},{16,14},{18,20},{2... | collective-permute-start | bytes 589832 | tf_op jit(solution)/shard_map/ppermute | solution.py:999
  114.3 8.9 %collective-permute-start.30 = (bf16[64,1024]{1,0:T(8,128)(2,1)S(1)}, bf16[64,1024]{1,0:T(8,128)(2,1)S(1)}, u32[]{:S(2)}, u32[]{:S(2)}) collective-permute-start(bf16[64,1024]{1,0:T(8,128)(2,1)S(1)} %get-tuple-element.260), channel_id=1, source_target_pairs={{0,16},{2,6},{4,20},{6,2},{8,24},{10,14},{12,28},{14,10},{16,0},{1... | collective-permute-start | bytes 393224 | tf_op jit(solution)/shard_map/ppermute | solution.py:991
  118.2 8.1 %collective-permute-start.31 = (bf16[160,256]{1,0:T(8,128)(2,1)S(1)}, bf16[160,256]{1,0:T(8,128)(2,1)S(1)}, u32[]{:S(2)}, u32[]{:S(2)}) collective-permute-start(bf16[160,256]{1,0:T(8,128)(2,1)S(1)} %get-tuple-element.263), channel_id=1, source_target_pairs={{0,16},{2,6},{4,20},{6,2},{8,24},{10,14},{12,28},{14,10},{16,0},{1... | collective-permute-start | bytes 245768 | tf_op jit(solution)/shard_map/ppermute | solution.py:991

commit v5 on v4

--- a/solution.py
+++ b/solution.py
@@ -184,41 +184,13 @@
     return joined
 
 
-def join_kernel(even_ref, *refs):
-    *part_refs, all_ref, inside_ref, across_ref = refs
-    count = all_ref.shape[0]
-    width = part_refs[0].shape[1]
-    even = even_ref[0] == 1
-    for place, ref in enumerate(part_refs):
-        lanes = slice(place * width, (place + 1) * width)
-        all_ref[:, lanes] = ref[...]
-        tail, head = ref[count - HALO :, :], ref[:HALO, :]
-        inside_ref[:, lanes] = jnp.where(even, tail, head)
-        across_ref[:, lanes] = jnp.where(even, head, tail)
-
-
-def join(even, parts):
-    count, width = parts[0].shape
-    features = len(parts) * width
-    shapes = ((count, features), (HALO, features), (HALO, features))
-    return pl.pallas_call(
-        join_kernel,
-        grid=(1,),
-        in_specs=[pl.BlockSpec(memory_space=SMEM)] + [whole(x.shape) for x in parts],
-        out_specs=[whole(shape) for shape in shapes],
-        out_shape=[struct(shape, BF16) for shape in shapes],
-        compiler_params=params(),
-        cost_estimate=lasting(0.5),
-        name="join",
-    )(even, *parts)
-
-
 def project_kernel(
-    slot_ref, even_ref, token_ref, inside_ref, across_ref, near_ref, far_ref, bias_ref,
-    query_ref, key_ref, value_ref, low_ref, high_ref, *weight_refs,
+    parts, slot_ref, even_ref, near_ref, far_ref, bias_ref, *refs
 ):
+    token_refs, inside_refs, across_refs = (refs[k * parts : (k + 1) * parts] for k in range(3))
+    all_ref, query_ref, key_ref, value_ref, low_ref, high_ref, *weight_refs = refs[3 * parts :]
     half, _, depth, _ = near_ref.shape
-    count = token_ref.shape[0]
+    count, width = token_refs[0].shape
 
     def put(place, source_ref, slot):
         for which, ref in enumerate(weight_refs):
@@ -236,11 +208,15 @@
             put(place, far_ref, slot - half)
 
     even = even_ref[0] == 1
-    inside, across = inside_ref[...], across_ref[...]
-    low_rows, high_rows = jnp.where(even, across, inside), jnp.where(even, inside, across)
-    low_ref[...] = low_rows
-    high_ref[...] = high_rows
-    own = token_ref[...]
+    for place, (own_ref, inside_ref, across_ref) in enumerate(
+        zip(token_refs, inside_refs, across_refs)
+    ):
+        lanes = slice(place * width, (place + 1) * width)
+        inside, across = inside_ref[...], across_ref[...]
+        all_ref[:, lanes] = own_ref[...]
+        low_ref[:, lanes] = jnp.where(even, across, inside)
+        high_ref[:, lanes] = jnp.where(even, inside, across)
+    own, low_rows, high_rows = all_ref[...], low_ref[...], high_ref[...]
     query = (dot_nn(own, weight_refs[0][...]) + bias_ref[0:1, :]).astype(BF16)
     empty = jnp.zeros((PAD, query.shape[1]), BF16)
     query_ref[...] = query * jnp.asarray(HEAD_DIM ** (-0.5), BF16)
@@ -256,15 +232,16 @@
         out_ref[MAXDOC + count + HALO :, :] = empty
 
 
-def project(slots, even, tokens, inside, across, near, far, bias):
-    count, features = tokens.shape
+def project(slots, even, near, far, bias, tokens, inside, across):
+    count, part = tokens[0].shape
+    features = len(tokens) * part
     width = near.shape[3]
-    operands = (tokens, inside, across, near, far, bias)
+    operands = (near, far, bias, *tokens, *inside, *across)
     extended = (count + BAND, width)
-    shapes = [(count, width), extended, extended, inside.shape, across.shape]
-    shapes += [(features, width)] * 3
-    return pl.pallas_call(
-        project_kernel,
+    shapes = [(count, features), (count, width), extended, extended]
+    shapes += [(HALO, features)] * 2 + [(features, width)] * 3
+    return pl.pallas_call(
+        functools.partial(project_kernel, len(tokens)),
         grid=(1,),
         in_specs=[pl.BlockSpec(memory_space=SMEM)] * 2 + [whole(x.shape) for x in operands],
         out_specs=[whole(shape) for shape in shapes],
@@ -1087,7 +1064,6 @@
     turned = odd ^ (places >= half)
     met = jnp.where(turned, distances_of(odd_order, places), distances_of(even_order, places))
     blocks = (((met + (places >= half)) ^ row_index) - offset) % row_count
-    lengths = jnp.concatenate([doc_lengths.reshape(-1), (row_index * count)[None]])
 
     even = 1 - row_index % 2
     even = even.astype(jnp.int32)[None]
@@ -1102,56 +1078,68 @@
     out_turned = out_weight.T
     out_other = others(out_turned)
     qkv_rows = Gather(qkv_weight)
-    tokens_full, inside, across = join(even, [tokens] + others(after(tokens, out_turned)))
+    tokens_other = others(after(tokens, out_turned))
     feed_rows = Gather(jnp.concatenate([out_turned, *out_other, up_weight, down_weight.T], 1))
-    qkv_rows.put()
-    grad_full = jnp.concatenate([out_grad] + others(out_grad), 1)
-    inside, across = with_next(inside, across)
-    qkv_rows.put(tokens_full)
+    tail = row_index % 2 * (count - HALO)
+    ready = after(tokens, feed_rows.held)
+    inside, across = with_next(
+        lax.dynamic_slice_in_dim(ready, count - HALO - tail, HALO, 0),
+        lax.dynamic_slice_in_dim(ready, tail, HALO, 0),
+    )
+    qkv_rows.put(feed_rows.held)
+    inside_other, across_other = others(inside), others(across)
     feed_rows.put(qkv_rows.held)
+    qkv_rows.put(feed_rows.held, *tokens_other)
+    lengths = jnp.concatenate(
+        [after(doc_lengths, qkv_rows.held).reshape(-1), (row_index * count)[None]]
+    )
     prev_dense = [
-        dense_of(prev_logits, MASKED_SCORE, 0, qkv_rows.held, feed_rows.held, tokens_full)
+        dense_of(prev_logits, MASKED_SCORE, 0, qkv_rows.held, feed_rows.held, inside, across)
     ]
-    prev_dense.append(dense_of(prev_logits, MASKED_SCORE, 1, prev_dense[0], grad_full))
+    grad_other = others(after(out_grad, *inside_other))
     while qkv_rows.step < qkv_rows.count:
-        qkv_rows.put(prev_dense[1], inside, across)
+        qkv_rows.put(prev_dense[0], *inside_other, *across_other)
     feed_rows.put(qkv_rows.held)
-    query, key, value, low_tokens, high_tokens, *projections = project(
-        slots, even, after(tokens_full, feed_rows.held), inside, across, qkv_rows.held,
-        qkv_rows.arrived, qv_bias,
-    )
-    norms = jnp.concatenate([norm_gain, norm_shift, out_bias], 0)
-    norms = jnp.concatenate([norms] + others(after(norms, query)), 1)
+    tokens_full, query, key, value, low_tokens, high_tokens, *projections = project(
+        slots, even, qkv_rows.held, qkv_rows.arrived, qv_bias, [after(tokens, feed_rows.held), *tokens_other],
+        [inside, *inside_other], [across, *across_other],
+    )
+    grad_full = jnp.concatenate([after(out_grad, query)] + grad_other, 1)
+    norms = jnp.concatenate([after(norm_gain, query), norm_shift, out_bias], 0)
+    norms = jnp.concatenate([norms] + others(norms), 1)
     scores, probs, attended, attended_other = [], [], [], []
     for chunk in range(CHUNKS):
-        score, prob, mix = attend_forward(query, key, value, prev_dense[chunk], chunk)
-        query = after(query, mix, norms)
+        score, prob, mix = attend_forward(
+            after(query, feed_rows.held) if chunk else query, key, value, prev_dense[chunk], chunk
+        )
         scores.append(score)
         probs.append(prob)
         attended.append(mix)
         attended_other.append(jnp.concatenate(others(mix), 1))
-    feed_rows.put(mix, attended_other[0])
-    while feed_rows.step < feed_rows.count:
-        feed_rows.put()
-    new_logits = to_band([after(scores[0], feed_rows.held), *scores[1:]], True)
+        if chunk == 0:
+            prev_dense.append(dense_of(prev_logits, MASKED_SCORE, 1, mix, norms, grad_full))
+            while feed_rows.step < feed_rows.count:
+                feed_rows.put(prev_dense[1], attended_other[0])
     other_out, *weights = in_order(
-        slots, after(feed_rows.held, new_logits), feed_rows.arrived,
+        slots, after(feed_rows.held, mix), feed_rows.arrived,
         (width, (col_count - 1) * width, up_weight.shape[1], up_weight.shape[1]),
     )
     weights[0], other_out = other_out, weights[0]
     ups = up_bias[None]
-    firsts = []
+    firsts, logit_dense = [], []
     for chunk in range(CHUNKS):
         result = feed_first(
             attended[chunk], attended_other[chunk], tokens_full, other_out, weights, norms, ups,
             chunk,
         )
-        ups = after(ups, result[-1])
+        if chunk == 0:
+            logit_dense.append(dense_of(logit_grad, 0.0, 0, result[-1]))
+            ups = after(ups, logit_dense[0])
         firsts.append((*result, exchanged(result[-1])))
     normed, inverse, upper, act, slope, down_part, down_other = zip(*firsts)
 
-    logit_dense = [dense_of(logit_grad, 0.0, 0, down_part[-1])]
-    sums = after(jnp.zeros((SUM_ROWS, own), F32), logit_dense[0])
+    new_logits = to_band([after(scores[0], down_part[-1]), *scores[1:]], True)
+    sums = after(jnp.zeros((SUM_ROWS, own), F32), new_logits)
     output = None
     seconds = []
     for chunk in range(CHUNKS):

time: 127 us -> 122 us (0.961)
  starting transfers between devices: 43 us -> 39.6 us
  other arithmetic: 3.21 us -> 1.03 us
    ppermute x16, starting transfers between devices: 25.4 us -> 21 us  [with_partner(): lax.ppermute(x, 'row', [(i, i ^ orders[i % 2][step]) for i in range(count)])]
    ppermute x12 -> x14, starting transfers between devices: 14.1 us -> 16.6 us  [from_next(): lax.ppermute(x, axis, [((i + step) % count, i) for i in range(count)])]
    concatenate x4 -> x3, other arithmetic: 2.27 us -> 0.1 us  [the longest x1 0.07 us: on_device(): jnp.concatenate([after(doc_lengths, qkv_rows.held).reshape(-1), (row_inde...]
    ppermute x2, starting transfers between devices: 2.16 us -> 0.65 us  [with_next(): lax.ppermute(inside, 'row', [(i, i ^ 1) for i in range(count)])]
    ppermute x12 -> x14, waiting for transfers between devices: 6.11 us -> 5.43 us  [from_next(): lax.ppermute(x, axis, [((i + step) % count, i) for i in range(count)])]
  transfers between devices with their start and end apart: 32 -> 34, of which waited for: 6 -> 7; matrix products, arithmetic and copies ran while one was open for 3% -> 3% of each run, Pallas kernels for 48% -> 50%
where the time goes in v5:
time: 122 us
  Pallas kernels  63.4 us (52%)
  starting transfers between devices  39.6 us (32%)
  waiting for transfers between devices  14.4 us (12%)
  local copies, waits for them, and re-layouts  2.13 us (2%)
    ppermute x16, starting transfers between devices, with_partner(): lax.ppermute(x, 'row', [(i, i ^ orders[i % 2][step]) for i in range(count)])  21 us
    ppermute x14, starting transfers between devices, from_next(): lax.ppermute(x, axis, [((i + step) % count, i) for i in range(count)])  16.6 us
    pallas_call x4, Pallas kernels, to_dense(): pl.pallas_call(functools.partial(dense_kernel, fill, token_count, offset)...  12.4 us
    pallas_call x2, Pallas kernels, to_band(): pl.pallas_call(functools.partial(band_kernel, masked), grid=(CHUNKS * ste...  10 us
    pallas_call x2, Pallas kernels, attend_backward(): pl.pallas_call(functools.partial(backward_kernel, offset, last), grid=(co...  9.2 us
    ppermute x16, waiting for transfers between devices, with_partner(): lax.ppermute(x, 'row', [(i, i ^ orders[i % 2][step]) for i in range(count)])  8.98 us
    pallas_call x2, Pallas kernels, attend_forward(): pl.pallas_call(functools.partial(forward_kernel, offset), grid=(count //...  7.75 us
    ppermute x14, waiting for transfers between devices, from_next(): lax.ppermute(x, axis, [((i + step) % count, i) for i in range(count)])  5.43 us
  transfers between devices with their start and end apart: 34, of which 7 were waited for; matrix products, arithmetic and copies ran while one was open for 3% of the time, Pallas kernels for 50%

profile of v5, /device:TPU:0, one launch (start us, length us, event | category | flops | bytes accessed | tf_op | source)
XLA Modules:
  0.0 121.8 jit_solution(15371309892589326244)
XLA Ops:
  0.7 3.0 %collective-permute-start = (bf16[32,256]{1,0:T(8,128)(2,1)}, bf16[32,256]{1,0:T(8,128)(2,1)S(1)}, u32[]{:S(2)}, u32[]{:S(2)}) collective-permute-start(bf16[32,256]{1,0:T(8,128)(2,1)} %bitcast.17), channel_id=1, source_target_pairs={{1,0},{0,1},{3,2},{2,3},{5,4},{4,5},{7,6},{6,7},{9,8},{8,9},{11,10... | collective-permute-start | bytes 49160 | tf_op jit(solution)/shard_map/ppermute | solution.py:941
  3.7 2.6 %collective-permute-start.1 = (bf16[1,3,32,256]{3,2,1,0:T(8,128)(2,1)}, bf16[1,3,32,256]{3,2,1,0:T(8,128)(2,1)S(1)}, u32[]{:S(2)}, u32[]{:S(2)}) collective-permute-start(bf16[1,3,32,256]{3,2,1,0:T(8,128)(2,1)} %bitcast.15), channel_id=1, source_target_pairs={{0,16},{2,6},{4,20},{6,2},{8,24},{10,14},{12,28},{14,10},{16,0},{1... | collective-permute-start | bytes 147464 | tf_op jit(solution)/shard_map/ppermute | solution.py:968
  6.2 0.5 collective-permute-start.3
  6.8 0.9 maximum_bitcast_fusion
  7.7 1.9 %collective-permute-start.2 = (bf16[1,32,2560]{2,1,0:T(8,128)(2,1)S(1)}, bf16[1,32,2560]{2,1,0:T(8,128)(2,1)S(1)}, u32[]{:S(2)}, u32[]{:S(2)}) collective-permute-start(bf16[1,32,2560]{2,1,0:T(8,128)(2,1)S(1)} %maximum_bitcast_fusion), channel_id=1, source_target_pairs={{0,16},{2,6},{4,20},{6,2},{8,24},{10,14},{12,28},{14,10},{16,0},{1... | collective-permute-start | bytes 491528 | tf_op jit(solution)/shard_map/ppermute | solution.py:968
  9.7 1.0 constant_dynamic-slice_fusion
  10.8 0.7 collective-permute-start.6
  11.5 0.8 constant_dynamic-update-slice_fusion.1
  12.3 4.4 %collective-permute-start.4 = (bf16[2,3,32,256]{3,2,1,0:T(8,128)(2,1)S(1)}, bf16[2,3,32,256]{3,2,1,0:T(8,128)(2,1)S(1)}, u32[]{:S(2)}, u32[]{:S(2)}) collective-permute-start(bf16[2,3,32,256]{3,2,1,0:T(8,128)(2,1)S(1)} %constant_dynamic-update-slice_fusion), channel_id=1, source_target_pairs={{0,8},{2,18},{4,12},{6,22},{8,0},{10,26},{12,4},{14,30},{16,24},{1... | collective-permute-start | bytes 294920 | tf_op jit(solution)/shard_map/ppermute | solution.py:968
  16.8 1.7 %collective-permute-start.7 = (bf16[384,256]{1,0:T(8,128)(2,1)S(1)}, bf16[384,256]{1,0:T(8,128)(2,1)S(1)}, u32[]{:S(2)}, u32[]{:S(2)}) collective-permute-start(bf16[384,256]{1,0:T(8,128)(2,1)S(1)} %collective-permute-done.5.refs_2_), channel_id=1, source_target_pairs={{1,0},{0,1},{3,2},{2,3},{5,4},{4,5},{7,6},{6,7},{9,8},{8,9},{11,10... | collective-permute-start | bytes 589832 | tf_op jit(solution)/shard_map/ppermute | solution.py:941
  18.5 0.4 collective-permute-start.8
  18.9 2.4 %collective-permute-done.4 = bf16[2,3,32,256]{3,2,1,0:T(8,128)(2,1)S(1)} collective-permute-done((bf16[2,3,32,256]{3,2,1,0:T(8,128)(2,1)S(1)}, bf16[2,3,32,256]{3,2,1,0:T(8,128)(2,1)S(1)}, u32[]{:S(2)}, u32[]{:S(2)}) %collective-permute-start.4) | collective-permute-done | bytes 98336 | tf_op jit(solution)/shard_map/ppermute | solution.py:968
  21.3 1.5 %collective-permute-start.9 = (bf16[4,3,32,256]{3,2,1,0:T(8,128)(2,1)S(1)}, bf16[4,3,32,256]{3,2,1,0:T(8,128)(2,1)S(1)}, u32[]{:S(2)}, u32[]{:S(2)}) collective-permute-start(bf16[4,3,32,256]{3,2,1,0:T(8,128)(2,1)S(1)} %constant_dynamic-update-slice_fusion.4), channel_id=1, source_target_pairs={{0,4},{2,10},{4,0},{6,14},{8,12},{10,2},{12,8},{14,6},{16,20},{18,... | collective-permute-start | bytes 589832 | tf_op jit(solution)/shard_map/ppermute | solution.py:968
  22.9 3.1 %to_dense.4.prev_ref = bf16[4,256,1152]{2,1,0:T(8,128)(2,1)S(1)} custom-call(s32[34]{0:T(128)S(1)} %pad_add_fusion.lengths_ref, bf16[4,512,1024]{2,1,0:T(8,128)(2,1)} %band_ref.1), custom_call_target="tpu_custom_call" | custom-call | flops 8000000000 | tf_op jit(solution)/shard_map/to_dense/pallas_call | solution.py:102
  26.1 2.7 %collective-permute-done.8.refs_5_ = bf16[384,256]{1,0:T(8,128)(2,1)S(1)} collective-permute-done((bf16[384,256]{1,0:T(8,128)(2,1)S(1)}, bf16[384,256]{1,0:T(8,128)(2,1)S(1)}, u32[]{:S(2)}, u32[]{:S(2)}) %collective-permute-start.8) | collective-permute-done | bytes 196640 | tf_op jit(solution)/shard_map/ppermute | solution.py:941
  28.7 1.6 %collective-permute-start.13 = (bf16[512,256]{1,0:T(8,128)(2,1)S(1)}, bf16[512,256]{1,0:T(8,128)(2,1)S(1)}, u32[]{:S(2)}, u32[]{:S(2)}) collective-permute-start(bf16[512,256]{1,0:T(8,128)(2,1)S(1)} %copy-done.3), channel_id=1, source_target_pairs={{1,0},{0,1},{3,2},{2,3},{5,4},{4,5},{7,6},{6,7},{9,8},{8,9},{11,10... | collective-permute-start | bytes 786440 | tf_op jit(solution)/shard_map/ppermute | solution.py:941
  30.4 0.2 collective-permute-start.10
  30.6 1.4 %collective-permute-start.15 = (bf16[4,32,2560]{2,1,0:T(8,128)(2,1)S(1)}, bf16[4,32,2560]{2,1,0:T(8,128)(2,1)S(1)}, u32[]{:S(2)}, u32[]{:S(2)}) collective-permute-start(bf16[4,32,2560]{2,1,0:T(8,128)(2,1)S(1)} %constant_dynamic-update-slice_fusion.8), channel_id=1, source_target_pairs={{0,4},{2,10},{4,0},{6,14},{8,12},{10,2},{12,8},{14,6},{16,20},{18,... | collective-permute-start | bytes 1966088 | tf_op jit(solution)/shard_map/ppermute | solution.py:968
  32.0 0.2 collective-permute-done.10.far_ref
  32.2 1.9 %project.1 = (bf16[512,512]{1,0:T(8,128)(2,1)S(1)}, bf16[512,256]{1,0:T(8,128)(2,1)S(1)}, bf16[1536,256]{1,0:T(8,128)(2,1)S(1)}, bf16[1536,256]{1,0:T(8,128)(2,1...) custom-call(s32[16]{0:T(128)S(1)} %fusion.7.slot_ref, ...), custom_call_target="tpu_custom_call" | custom-call | flops 2000000000 | tf_op jit(solution)/shard_map/project/pallas_call | solution.py:243
  34.1 1.6 %collective-permute-start.12 = (f32[6,256]{1,0:T(8,128)S(1)}, f32[6,256]{1,0:T(8,128)S(1)}, u32[]{:S(2)}, u32[]{:S(2)}) collective-permute-start(f32[6,256]{1,0:T(8,128)S(1)} %pad_maximum_fusion.1), channel_id=1, source_target_pairs={{1,0},{0,1},{3,2},{2,3},{5,4},{4,5},{7,6},{6,7},{9,8},{8,9},{11,10... | collective-permute-start | bytes 18440 | tf_op jit(solution)/shard_map/ppermute | solution.py:941
  35.8 3.9 %attend_forward.2 = (bf16[4,256,1152]{2,1,0:T(8,128)(2,1)S(1)}, bf16[4,256,1152]{2,1,0:T(8,128)(2,1)S(1)}, bf16[256,256]{1,0:T(8,128)(2,1)S(1)}) custom-call(bf16[512,256]{1,0:T(8,128)(2,1)S(1)} %get-tuple-element.165.query_ref, bf16[1536,256]{1,0:T(8,128)(2,1)S(1)} %get-tuple-element.156.key_ref, bf16[1536,256]{1,0:T(8,128)(2,1)S(1)} %get-tuple-element.157.value_ref, ...), custom_call_target="tpu_custom_call" | custom-call | flops 3800000000 | tf_op jit(solution)/shard_map/attend_forward/pallas_call | solution.py:285
  39.6 0.5 collective-permute-start.14
  40.2 3.1 %to_dense.5.prev_ref = bf16[4,256,1152]{2,1,0:T(8,128)(2,1)S(1)} custom-call(s32[34]{0:T(128)S(1)} %pad_add_fusion.lengths_ref, bf16[4,512,1024]{2,1,0:T(8,128)(2,1)} %band_ref.1), custom_call_target="tpu_custom_call" | custom-call | flops 1000000000 | tf_op jit(solution)/shard_map/to_dense/pallas_call | solution.py:102
  43.4 1.6 %collective-permute-done.14.other_ref = bf16[256,256]{1,0:T(8,128)(2,1)S(1)} collective-permute-done((bf16[256,256]{1,0:T(8,128)(2,1)S(1)}, bf16[256,256]{1,0:T(8,128)(2,1)S(1)}, u32[]{:S(2)}, u32[]{:S(2)}) %collective-permute-start.14) | collective-permute-done | bytes 131104 | tf_op jit(solution)/shard_map/ppermute | solution.py:941
  45.2 3.9 %attend_forward.3 = (bf16[4,256,1152]{2,1,0:T(8,128)(2,1)S(1)}, bf16[4,256,1152]{2,1,0:T(8,128)(2,1)S(1)}, bf16[256,256]{1,0:T(8,128)(2,1)S(1)}) custom-call(bf16[512,256]{1,0:T(8,128)(2,1)S(1)} %get-tuple-element.165.query_ref, bf16[1536,256]{1,0:T(8,128)(2,1)S(1)} %get-tuple-element.156.key_ref, bf16[1536,256]{1,0:T(8,128)(2,1)S(1)} %get-tuple-element.157.value_ref, ...), custom_call_target="tpu_custom_call" | custom-call | flops 3800000000 | tf_op jit(solution)/shard_map/attend_forward/pallas_call | solution.py:285
  49.1 0.6 collective-permute-start.16
  49.7 1.1 in_order.1
  50.8 2.2 %feed_first.2 = (f32[256,512]{1,0:T(8,128)S(1)}, f32[256,1]{1,0:T(8,128)S(1)}, bf16[256,512]{1,0:T(8,128)(2,1)S(1)}, bf16[256,1024]{1,0:T(8,128)(2,1)S(1)}, bf16...) custom-call(bf16[256,256]{1,0:T(8,128)(2,1)S(1)} %get-tuple-element.159.own_ref.refs_4_, ...), custom_call_target="tpu_custom_call" | custom-call | flops 1000000000 | tf_op jit(solution)/shard_map/feed_first/pallas_call | solution.py:473
  52.9 1.6 %collective-permute-start.18 = (bf16[256,512]{1,0:T(8,128)(2,1)S(1)}, bf16[256,512]{1,0:T(8,128)(2,1)S(1)}, u32[]{:S(2)}, u32[]{:S(2)}) collective-permute-start(bf16[256,512]{1,0:T(8,128)(2,1)S(1)} %get-tuple-element.173.part_ref), channel_id=1, source_target_pairs={{1,0},{0,1},{3,2},{2,3},{5,4},{4,5},{7,6},{6,7},{9,8},{8,9},{11,10... | collective-permute-start | bytes 786440 | tf_op jit(solution)/shard_map/ppermute | solution.py:941
  54.5 3.1 %to_dense.6.logit_ref = bf16[4,256,1152]{2,1,0:T(8,128)(2,1)S(1)} custom-call(s32[34]{0:T(128)S(1)} %pad_add_fusion.lengths_ref, bf16[4,512,1024]{2,1,0:T(8,128)(2,1)} %band_ref.3), custom_call_target="tpu_custom_call" | custom-call | flops 1000000000 | tf_op jit(solution)/shard_map/to_dense/pallas_call | solution.py:102
  57.6 2.2 %feed_first.3 = (f32[256,512]{1,0:T(8,128)S(1)}, f32[256,1]{1,0:T(8,128)S(1)}, bf16[256,512]{1,0:T(8,128)(2,1)S(1)}, bf16[256,1024]{1,0:T(8,128)(2,1)S(1)}, bf16...) custom-call(bf16[256,256]{1,0:T(8,128)(2,1)S(1)} %get-tuple-element.166.own_ref.refs_5_, ...), custom_call_target="tpu_custom_call" | custom-call | flops 1000000000 | tf_op jit(solution)/shard_map/feed_first/pallas_call | solution.py:473
  59.8 0.6 collective-permute-start.19
  60.4 5.0 %to_band.2 = bf16[4,512,1024]{2,1,0:T(8,128)(2,1)} custom-call(bf16[4,256,1152]{2,1,0:T(8,128)(2,1)S(1)} %get-tuple-element.177.refs_0_, bf16[4,256,1152]{2,1,0:T(8,128)(2,1)S(1)} %get-tuple-element.178.refs_1_), custom_call_target="tpu_custom_call" | custom-call | flops 5000000000 | tf_op jit(solution)/shard_map/to_band/pallas_call | solution.py:151
  65.4 2.4 %feed_second.2 = (f32[16,256]{1,0:T(8,128)S(1)}, bf16[512,256]{1,0:T(8,128)(2,1)}, f32[256,512]{1,0:T(8,128)S(1)}, bf16[256,512]{1,0:T(8,128)(2,1)S(1)}, bf16[25...) custom-call(f32[16,256]{1,0:T(8,128)S(1)} %broadcast_in_dim.18.start_ref, ...), custom_call_target="tpu_custom_call" | custom-call | flops 700000000 | tf_op jit(solution)/shard_map/feed_second/pallas_call | solution.py:552
  67.9 1.5 %collective-permute-start.20 = (bf16[256,512]{1,0:T(8,128)(2,1)S(1)}, bf16[256,512]{1,0:T(8,128)(2,1)S(1)}, u32[]{:S(2)}, u32[]{:S(2)}) collective-permute-start(bf16[256,512]{1,0:T(8,128)(2,1)S(1)} %get-tuple-element.198.part_ref), channel_id=1, source_target_pairs={{1,0},{0,1},{3,2},{2,3},{5,4},{4,5},{7,6},{6,7},{9,8},{8,9},{11,10... | collective-permute-start | bytes 786440 | tf_op jit(solution)/shard_map/ppermute | solution.py:941
  69.4 2.5 %feed_second.3 = (f32[16,256]{1,0:T(8,128)S(1)}, bf16[512,256]{1,0:T(8,128)(2,1)}, f32[256,512]{1,0:T(8,128)S(1)}, bf16[256,512]{1,0:T(8,128)(2,1)S(1)}, bf16[25...) custom-call(f32[16,256]{1,0:T(8,128)S(1)} %get-tuple-element.182.start_ref, ...), custom_call_target="tpu_custom_call", output_to_operand_aliasing={{1}: (9, {})} | custom-call | flops 700000000 | tf_op jit(solution)/shard_map/feed_second/pallas_call | solution.py:552
  71.8 3.4 %feed_grads.1 = (f32[512,1024]{1,0:T(8,128)S(1)}, bf16[512,1024]{1,0:T(8,128)(2,1)S(1)}) custom-call(s32[16]{0:T(128)S(1)} %and_select_fusion.block_ref, bf16[256,512]{1,0:T(8,128)(2,1)S(1)} %get-tuple-element.188.refs_0_, bf16[256,512]{1,0:T(8,128)(2,1)S(1)} %get-tuple-element.189.refs_1_, bf16[256,512]{1,0:T(8,128)(2,1)S(1)} %get-tuple-element.190.refs_2_, ...), custom_call_target="tpu_custom_call" | custom-call | flops 1000000000 | tf_op jit(solution)/shard_map/feed_grads/pallas_call | solution.py:673
  75.3 0.6 collective-permute-start.22
  75.9 0.8 feed_third.2
  76.6 4.2 %attend_backward.2 = (bf16[4,256,1152]{2,1,0:T(8,128)(2,1)S(1)}, bf16[256,256]{1,0:T(8,128)(2,1)S(1)}, f32[256,1536]{1,0:T(8,128)S(1)}, f32[256,1536]{1,0:T(8,128)S(1)}) custom-call(bf16[256,256]{1,0:T(8,128)(2,1)S(1)} %get-tuple-element.201.grad_ref, bf16[512,256]{1,0:T(8,128)(2,1)S(1)} %get-tuple-element.165.query_ref, ...), custom_call_target="tpu_custom_call" | custom-call | flops 20000000000 | tf_op jit(solution)/shard_map/attend_backward/pallas_call | solution.py:369
  80.9 0.2 fold.6
  81.1 1.3 %collective-permute-start.23 = (bf16[256,1024]{1,0:T(8,128)(2,1)S(1)}, bf16[256,1024]{1,0:T(8,128)(2,1)S(1)}, u32[]{:S(2)}, u32[]{:S(2)}) collective-permute-start(bf16[256,1024]{1,0:T(8,128)(2,1)S(1)} %get-tuple-element.223), channel_id=1, source_target_pairs={{0,4},{2,10},{4,0},{6,14},{8,12},{10,2},{12,8},{14,6},{16,20},{18,... | collective-permute-start | bytes 1572872 | tf_op jit(solution)/shard_map/ppermute | solution.py:968
  82.4 3.1 %to_dense.7.logit_ref = bf16[4,256,1152]{2,1,0:T(8,128)(2,1)S(1)} custom-call(s32[34]{0:T(128)S(1)} %pad_add_fusion.lengths_ref, bf16[4,512,1024]{2,1,0:T(8,128)(2,1)} %band_ref.3), custom_call_target="tpu_custom_call" | custom-call | flops 1000000000 | tf_op jit(solution)/shard_map/to_dense/pallas_call | solution.py:102
  85.5 0.8 feed_third.3
  86.3 5.0 %attend_backward.3 = (bf16[4,256,1152]{2,1,0:T(8,128)(2,1)S(1)}, bf16[256,256]{1,0:T(8,128)(2,1)S(1)}, bf16[1536,256]{1,0:T(8,128)(2,1)S(1)}, bf16[1536,256]{1,0:T(8,128)(2,1)S(1)}) custom-call(bf16[256,256]{1,0:T(8,128)(2,1)S(1)} %get-tuple-element.213.grad_ref, bf16[512,256]{1,0:T(8,128)(2,1)S(1)} %get-tuple-element.165.query_ref, ...), custom_call_target="tpu_custom_call" | custom-call | flops 3000000000 | tf_op jit(solution)/shard_map/attend_backward/pallas_call | solution.py:369
  91.4 1.9 %project_grads.1 = (f32[1024,256]{1,0:T(8,128)S(1)}, bf16[1056,256]{1,0:T(8,128)(2,1)S(1)}, f32[16,256]{1,0:T(8,128)S(1)}) custom-call(s32[16]{0:T(128)S(1)} %and_select_fusion.block_ref, f32[16,256]{1,0:T(8,128)S(1)} %get-tuple-element.225.start_ref, bf16[256,256]{1,0:T(8,128)(2,1)S(1)} %get-tuple-element.203.refs_0_, ...), custom_call_target="tpu_custom_call" | custom-call | flops 600000000 | tf_op jit(solution)/shard_map/project_grads/pallas_call | solution.py:730
  93.3 0.2 collective-permute-start.24
  93.5 2.1 %token_grads.1 = (f32[512,256]{1,0:T(8,128)S(1)}, f32[768,256]{1,0:T(8,128)S(1)}, bf16[512,256]{1,0:T(8,128)(2,1)S(1)}, bf16[768,256]{1,0:T(8,128)(2,1)S(1)}) custom-call(s32[1]{0:T(128)} %bitcast.even_ref, bf16[256,256]{1,0:T(8,128)(2,1)S(1)} %get-tuple-element.203.refs_0_, bf16[256,256]{1,0:T(8,128)(2,1)S(1)} %get-tuple-element.217.refs_1_, ...), custom_call_target="tpu_custom_call" | custom-call | flops 5000000000 | tf_op jit(solution)/shard_map/token_grads/pallas_call | solution.py:874
  95.6 1.6 %collective-permute-start.26 = (bf16[768,256]{1,0:T(8,128)(2,1)S(1)}, bf16[768,256]{1,0:T(8,128)(2,1)S(1)}, u32[]{:S(2)}, u32[]{:S(2)}) collective-permute-start(bf16[768,256]{1,0:T(8,128)(2,1)S(1)} %get-tuple-element.250), channel_id=1, source_target_pairs={{1,0},{0,1},{3,2},{2,3},{5,4},{4,5},{7,6},{6,7},{9,8},{8,9},{11,10... | collective-permute-start | bytes 1179656 | tf_op jit(solution)/shard_map/ppermute | solution.py:941
  97.4 0.7 collective-permute-start.25
  98.0 1.3 %collective-permute-start.27 = (bf16[128,1024]{1,0:T(8,128)(2,1)S(1)}, bf16[128,1024]{1,0:T(8,128)(2,1)S(1)}, u32[]{:S(2)}, u32[]{:S(2)}) collective-permute-start(bf16[128,1024]{1,0:T(8,128)(2,1)S(1)} %get-tuple-element.253), channel_id=1, source_target_pairs={{0,8},{2,18},{4,12},{6,22},{8,0},{10,26},{12,4},{14,30},{16,24},{1... | collective-permute-start | bytes 786440 | tf_op jit(solution)/shard_map/ppermute | solution.py:968
  99.3 0.7 collective-permute-start.31
  100.0 5.0 %to_band.3 = bf16[4,512,1024]{2,1,0:T(8,128)(2,1)} custom-call(bf16[4,256,1152]{2,1,0:T(8,128)(2,1)S(1)} %get-tuple-element.242.refs_0_, bf16[4,256,1152]{2,1,0:T(8,128)(2,1)S(1)} %get-tuple-element.243.refs_1_), custom_call_target="tpu_custom_call" | custom-call | flops 500000000 | tf_op jit(solution)/shard_map/to_band/pallas_call | solution.py:151
  105.1 1.4 %collective-permute-start.28 = (bf16[288,256]{1,0:T(8,128)(2,1)S(1)}, bf16[288,256]{1,0:T(8,128)(2,1)S(1)}, u32[]{:S(2)}, u32[]{:S(2)}) collective-permute-start(bf16[288,256]{1,0:T(8,128)(2,1)S(1)} %get-tuple-element.256), channel_id=1, source_target_pairs={{0,8},{2,18},{4,12},{6,22},{8,0},{10,26},{12,4},{14,30},{16,24},{1... | collective-permute-start | bytes 442376 | tf_op jit(solution)/shard_map/ppermute | solution.py:968
  106.5 1.1 collective-permute-done.26.refs_0_
  107.7 0.6 collective-permute-start.29
  108.3 0.7 collective-permute-start.30
  109.0 3.9 %collective-permute-start.32 = (bf16[64,1024]{1,0:T(8,128)(2,1)S(1)}, bf16[64,1024]{1,0:T(8,128)(2,1)S(1)}, u32[]{:S(2)}, u32[]{:S(2)}) collective-permute-start(bf16[64,1024]{1,0:T(8,128)(2,1)S(1)} %get-tuple-element.264), channel_id=1, source_target_pairs={{0,16},{2,6},{4,20},{6,2},{8,24},{10,14},{12,28},{14,10},{16,0},{1... | collective-permute-start | bytes 393224 | tf_op jit(solution)/shard_map/ppermute | solution.py:968
  113.1 0.9 token_sum.1
  114.0 6.2 %collective-permute-done.32.arrived_ref = bf16[64,1024]{1,0:T(8,128)(2,1)S(1)} collective-permute-done((bf16[64,1024]{1,0:T(8,128)(2,1)S(1)}, bf16[64,1024]{1,0:T(8,128)(2,1)S(1)}, u32[]{:S(2)}, u32[]{:S(2)}) %collective-permute-start.32) | collective-permute-done | bytes 131104 | tf_op jit(solution)/shard_map/ppermute | solution.py:968
  120.2 0.7 finish.2
  120.9 0.2 collective-permute-done.33.arrived_ref
  121.1 0.7 finish.3
  (73 shorter events, 1.3 us)
Async XLA Ops:
  0.6 22.2 %copy-start.7 = (s32[1,33]{1,0:T(1,128)S(1)}, s32[1,33]{1,0:T(1,128)}, u32[]{:S(2)}) copy-start(s32[1,33]{1,0:T(1,128)} %param.16) | copy-start | bytes 400
  0.7 6.2 %collective-permute-start = (bf16[32,256]{1,0:T(8,128)(2,1)}, bf16[32,256]{1,0:T(8,128)(2,1)S(1)}, u32[]{:S(2)}, u32[]{:S(2)}) collective-permute-start(bf16[32,256]{1,0:T(8,128)(2,1)} %bitcast.17), channel_id=1, source_target_pairs={{1,0},{0,1},{3,2},{2,3},{5,4},{4,5},{7,6},{6,7},{9,8},{8,9},{11,10... | collective-permute-start | bytes 49160 | tf_op jit(solution)/shard_map/ppermute | solution.py:941
  3.7 8.6 %collective-permute-start.1 = (bf16[1,3,32,256]{3,2,1,0:T(8,128)(2,1)}, bf16[1,3,32,256]{3,2,1,0:T(8,128)(2,1)S(1)}, u32[]{:S(2)}, u32[]{:S(2)}) collective-permute-start(bf16[1,3,32,256]{3,2,1,0:T(8,128)(2,1)} %bitcast.15), channel_id=1, source_target_pairs={{0,16},{2,6},{4,20},{6,2},{8,24},{10,14},{12,28},{14,10},{16,0},{1... | collective-permute-start | bytes 147464 | tf_op jit(solution)/shard_map/ppermute | solution.py:968
  6.2 12.6 %collective-permute-start.3 = (bf16[512,256]{1,0:T(8,128)(2,1)}, bf16[512,256]{1,0:T(8,128)(2,1)S(1)}, u32[]{:S(2)}, u32[]{:S(2)}) collective-permute-start(bf16[512,256]{1,0:T(8,128)(2,1)} %refs_0_), channel_id=1, source_target_pairs={{1,0},{0,1},{3,2},{2,3},{5,4},{4,5},{7,6},{6,7},{9,8},{8,9},{11,10... | collective-permute-start | bytes 786440 | tf_op jit(solution)/shard_map/ppermute | solution.py:941
  7.7 8.9 %collective-permute-start.2 = (bf16[1,32,2560]{2,1,0:T(8,128)(2,1)S(1)}, bf16[1,32,2560]{2,1,0:T(8,128)(2,1)S(1)}, u32[]{:S(2)}, u32[]{:S(2)}) collective-permute-start(bf16[1,32,2560]{2,1,0:T(8,128)(2,1)S(1)} %maximum_bitcast_fusion), channel_id=1, source_target_pairs={{0,16},{2,6},{4,20},{6,2},{8,24},{10,14},{12,28},{14,10},{16,0},{1... | collective-permute-start | bytes 491528 | tf_op jit(solution)/shard_map/ppermute | solution.py:968
  10.7 6.1 %collective-permute-start.5 = (bf16[384,256]{1,0:T(8,128)(2,1)S(1)}, bf16[384,256]{1,0:T(8,128)(2,1)S(1)}, u32[]{:S(2)}, u32[]{:S(2)}) collective-permute-start(bf16[384,256]{1,0:T(8,128)(2,1)S(1)} %get-tuple-element.278), channel_id=1, source_target_pairs={{0,2},{2,0},{4,6},{6,4},{8,10},{10,8},{12,14},{14,12},{16,18},{18,... | collective-permute-start | bytes 589832 | tf_op jit(solution)/shard_map/ppermute | solution.py:975
  10.8 7.7 %collective-permute-start.6 = (bf16[384,256]{1,0:T(8,128)(2,1)S(1)}, bf16[384,256]{1,0:T(8,128)(2,1)S(1)}, u32[]{:S(2)}, u32[]{:S(2)}) collective-permute-start(bf16[384,256]{1,0:T(8,128)(2,1)S(1)} %get-tuple-element.277), channel_id=1, source_target_pairs={{2,4},{4,2},{6,8},{8,6},{10,12},{12,10},{14,16},{16,14},{18,20},{2... | collective-permute-start | bytes 589832 | tf_op jit(solution)/shard_map/ppermute | solution.py:976
  12.3 9.0 %collective-permute-start.4 = (bf16[2,3,32,256]{3,2,1,0:T(8,128)(2,1)S(1)}, bf16[2,3,32,256]{3,2,1,0:T(8,128)(2,1)S(1)}, u32[]{:S(2)}, u32[]{:S(2)}) collective-permute-start(bf16[2,3,32,256]{3,2,1,0:T(8,128)(2,1)S(1)} %constant_dynamic-update-slice_fusion), channel_id=1, source_target_pairs={{0,8},{2,18},{4,12},{6,22},{8,0},{10,26},{12,4},{14,30},{16,24},{1... | collective-permute-start | bytes 294920 | tf_op jit(solution)/shard_map/ppermute | solution.py:968
  16.7 13.9 %collective-permute-start.11 = (bf16[2,32,2560]{2,1,0:T(8,128)(2,1)S(1)}, bf16[2,32,2560]{2,1,0:T(8,128)(2,1)S(1)}, u32[]{:S(2)}, u32[]{:S(2)}) collective-permute-start(bf16[2,32,2560]{2,1,0:T(8,128)(2,1)S(1)} %constant_dynamic-update-slice_fusion.2), channel_id=1, source_target_pairs={{0,8},{2,18},{4,12},{6,22},{8,0},{10,26},{12,4},{14,30},{16,24},{1... | collective-permute-start | bytes 983048 | tf_op jit(solution)/shard_map/ppermute | solution.py:968
  16.8 9.3 %collective-permute-start.7 = (bf16[384,256]{1,0:T(8,128)(2,1)S(1)}, bf16[384,256]{1,0:T(8,128)(2,1)S(1)}, u32[]{:S(2)}, u32[]{:S(2)}) collective-permute-start(bf16[384,256]{1,0:T(8,128)(2,1)S(1)} %collective-permute-done.5.refs_2_), channel_id=1, source_target_pairs={{1,0},{0,1},{3,2},{2,3},{5,4},{4,5},{7,6},{6,7},{9,8},{8,9},{11,10... | collective-permute-start | bytes 589832 | tf_op jit(solution)/shard_map/ppermute | solution.py:941
  18.5 10.2 %collective-permute-start.8 = (bf16[384,256]{1,0:T(8,128)(2,1)S(1)}, bf16[384,256]{1,0:T(8,128)(2,1)S(1)}, u32[]{:S(2)}, u32[]{:S(2)}) collective-permute-start(bf16[384,256]{1,0:T(8,128)(2,1)S(1)} %collective-permute-done.6.refs_4_), channel_id=1, source_target_pairs={{1,0},{0,1},{3,2},{2,3},{5,4},{4,5},{7,6},{6,7},{9,8},{8,9},{11,10... | collective-permute-start | bytes 589832 | tf_op jit(solution)/shard_map/ppermute | solution.py:941
  21.3 9.1 %collective-permute-start.9 = (bf16[4,3,32,256]{3,2,1,0:T(8,128)(2,1)S(1)}, bf16[4,3,32,256]{3,2,1,0:T(8,128)(2,1)S(1)}, u32[]{:S(2)}, u32[]{:S(2)}) collective-permute-start(bf16[4,3,32,256]{3,2,1,0:T(8,128)(2,1)S(1)} %constant_dynamic-update-slice_fusion.4), channel_id=1, source_target_pairs={{0,4},{2,10},{4,0},{6,14},{8,12},{10,2},{12,8},{14,6},{16,20},{18,... | collective-permute-start | bytes 589832 | tf_op jit(solution)/shard_map/ppermute | solution.py:968
  22.9 5.8 %copy-start.3 = (bf16[512,256]{1,0:T(8,128)(2,1)S(1)}, bf16[512,256]{1,0:T(8,128)(2,1)}, u32[]{:S(2)}) copy-start(bf16[512,256]{1,0:T(8,128)(2,1)} %param.26) | copy-start | bytes 786436
  22.9 9.3 %copy-start = (bf16[512,256]{1,0:T(8,128)(2,1)S(1)}, bf16[512,256]{1,0:T(8,128)(2,1)}, u32[]{:S(2)}) copy-start(bf16[512,256]{1,0:T(8,128)(2,1)} %refs_0_) | copy-start | bytes 786436
  22.9 9.3 %copy-start.2 = (f32[2,256]{1,0:T(2,128)S(1)}, f32[2,256]{1,0:T(2,128)}, u32[]{:S(2)}) copy-start(f32[2,256]{1,0:T(2,128)} %bias_ref.1) | copy-start | bytes 6148
  28.7 11.5 %collective-permute-start.13 = (bf16[512,256]{1,0:T(8,128)(2,1)S(1)}, bf16[512,256]{1,0:T(8,128)(2,1)S(1)}, u32[]{:S(2)}, u32[]{:S(2)}) collective-permute-start(bf16[512,256]{1,0:T(8,128)(2,1)S(1)} %copy-done.3), channel_id=1, source_target_pairs={{1,0},{0,1},{3,2},{2,3},{5,4},{4,5},{7,6},{6,7},{9,8},{8,9},{11,10... | collective-permute-start | bytes 786440 | tf_op jit(solution)/shard_map/ppermute | solution.py:941
  30.4 1.8 %collective-permute-start.10 = (bf16[8,3,32,256]{3,2,1,0:T(8,128)(2,1)S(1)}, bf16[8,3,32,256]{3,2,1,0:T(8,128)(2,1)S(1)}, u32[]{:S(2)}, u32[]{:S(2)}) collective-permute-start(bf16[8,3,32,256]{3,2,1,0:T(8,128)(2,1)S(1)} %constant_dynamic-update-slice_fusion.6.near_ref), channel_id=1, source_target_pairs={{0,2},{2,0},{4,6},{6,4},{8,10},{10,8},{12,14},{14,12},{16,18},{18,... | collective-permute-start | bytes 1179656 | tf_op jit(solution)/shard_map/ppermute | solution.py:968
  30.6 14.4 %collective-permute-start.15 = (bf16[4,32,2560]{2,1,0:T(8,128)(2,1)S(1)}, bf16[4,32,2560]{2,1,0:T(8,128)(2,1)S(1)}, u32[]{:S(2)}, u32[]{:S(2)}) collective-permute-start(bf16[4,32,2560]{2,1,0:T(8,128)(2,1)S(1)} %constant_dynamic-update-slice_fusion.8), channel_id=1, source_target_pairs={{0,4},{2,10},{4,0},{6,14},{8,12},{10,2},{12,8},{14,6},{16,20},{18,... | collective-permute-start | bytes 1966088 | tf_op jit(solution)/shard_map/ppermute | solution.py:968
  32.2 1.9 %copy-start.4 = (f32[2,256]{1,0:T(2,128)S(1)}, f32[2,256]{1,0:T(2,128)}, u32[]{:S(2)}) copy-start(f32[2,256]{1,0:T(2,128)} %param.20) | copy-start | bytes 6148
  32.2 1.9 %copy-start.5 = (f32[2,256]{1,0:T(2,128)S(1)}, f32[2,256]{1,0:T(2,128)}, u32[]{:S(2)}) copy-start(f32[2,256]{1,0:T(2,128)} %param.25) | copy-start | bytes 6148
  32.2 1.9 %copy-start.6 = (f32[2,256]{1,0:T(2,128)S(1)}, f32[2,256]{1,0:T(2,128)}, u32[]{:S(2)}) copy-start(f32[2,256]{1,0:T(2,128)} %param.24) | copy-start | bytes 6148
  34.1 6.1 %collective-permute-start.12 = (f32[6,256]{1,0:T(8,128)S(1)}, f32[6,256]{1,0:T(8,128)S(1)}, u32[]{:S(2)}, u32[]{:S(2)}) collective-permute-start(f32[6,256]{1,0:T(8,128)S(1)} %pad_maximum_fusion.1), channel_id=1, source_target_pairs={{1,0},{0,1},{3,2},{2,3},{5,4},{4,5},{7,6},{6,7},{9,8},{8,9},{11,10... | collective-permute-start | bytes 18440 | tf_op jit(solution)/shard_map/ppermute | solution.py:941
  39.6 5.3 %collective-permute-start.14 = (bf16[256,256]{1,0:T(8,128)(2,1)S(1)}, bf16[256,256]{1,0:T(8,128)(2,1)S(1)}, u32[]{:S(2)}, u32[]{:S(2)}) collective-permute-start(bf16[256,256]{1,0:T(8,128)(2,1)S(1)} %get-tuple-element.159.own_ref.refs_4_), channel_id=1, source_target_pairs={{1,0},{0,1},{3,2},{2,3},{5,4},{4,5},{7,6},{6,7},{9,8},{8,9},{11,10... | collective-permute-start | bytes 393224 | tf_op jit(solution)/shard_map/ppermute | solution.py:941
  45.1 4.6 %collective-permute-start.17 = (bf16[8,32,2560]{2,1,0:T(8,128)(2,1)S(1)}, bf16[8,32,2560]{2,1,0:T(8,128)(2,1)S(1)}, u32[]{:S(2)}, u32[]{:S(2)}) collective-permute-start(bf16[8,32,2560]{2,1,0:T(8,128)(2,1)S(1)} %constant_dynamic-update-slice_fusion.12.near_ref), channel_id=1, source_target_pairs={{0,2},{2,0},{4,6},{6,4},{8,10},{10,8},{12,14},{14,12},{16,18},{18,... | collective-permute-start | bytes 3932168 | tf_op jit(solution)/shard_map/ppermute | solution.py:968
  49.1 1.7 %copy-start.1 = (f32[1024]{0:T(1024)S(1)}, f32[1024]{0:T(1024)}, u32[]{:S(2)}) copy-start(f32[1024]{0:T(1024)} %param.22) | copy-start | bytes 12292
  49.1 8.5 %collective-permute-start.16 = (bf16[256,256]{1,0:T(8,128)(2,1)S(1)}, bf16[256,256]{1,0:T(8,128)(2,1)S(1)}, u32[]{:S(2)}, u32[]{:S(2)}) collective-permute-start(bf16[256,256]{1,0:T(8,128)(2,1)S(1)} %get-tuple-element.166.own_ref.refs_5_), channel_id=1, source_target_pairs={{1,0},{0,1},{3,2},{2,3},{5,4},{4,5},{7,6},{6,7},{9,8},{8,9},{11,10... | collective-permute-start | bytes 393224 | tf_op jit(solution)/shard_map/ppermute | solution.py:941
  52.9 12.5 %collective-permute-start.18 = (bf16[256,512]{1,0:T(8,128)(2,1)S(1)}, bf16[256,512]{1,0:T(8,128)(2,1)S(1)}, u32[]{:S(2)}, u32[]{:S(2)}) collective-permute-start(bf16[256,512]{1,0:T(8,128)(2,1)S(1)} %get-tuple-element.173.part_ref), channel_id=1, source_target_pairs={{1,0},{0,1},{3,2},{2,3},{5,4},{4,5},{7,6},{6,7},{9,8},{8,9},{11,10... | collective-permute-start | bytes 786440 | tf_op jit(solution)/shard_map/ppermute | solution.py:941
  59.8 9.6 %collective-permute-start.19 = (bf16[256,512]{1,0:T(8,128)(2,1)S(1)}, bf16[256,512]{1,0:T(8,128)(2,1)S(1)}, u32[]{:S(2)}, u32[]{:S(2)}) collective-permute-start(bf16[256,512]{1,0:T(8,128)(2,1)S(1)} %get-tuple-element.176.part_ref), channel_id=1, source_target_pairs={{1,0},{0,1},{3,2},{2,3},{5,4},{4,5},{7,6},{6,7},{9,8},{8,9},{11,10... | collective-permute-start | bytes 786440 | tf_op jit(solution)/shard_map/ppermute | solution.py:941
  67.9 8.0 %collective-permute-start.20 = (bf16[256,512]{1,0:T(8,128)(2,1)S(1)}, bf16[256,512]{1,0:T(8,128)(2,1)S(1)}, u32[]{:S(2)}, u32[]{:S(2)}) collective-permute-start(bf16[256,512]{1,0:T(8,128)(2,1)S(1)} %get-tuple-element.198.part_ref), channel_id=1, source_target_pairs={{1,0},{0,1},{3,2},{2,3},{5,4},{4,5},{7,6},{6,7},{9,8},{8,9},{11,10... | collective-permute-start | bytes 786440 | tf_op jit(solution)/shard_map/ppermute | solution.py:941
  75.2 5.7 %collective-permute-start.21 = (bf16[512,1024]{1,0:T(8,128)(2,1)S(1)}, bf16[512,1024]{1,0:T(8,128)(2,1)S(1)}, u32[]{:S(2)}, u32[]{:S(2)}) collective-permute-start(bf16[512,1024]{1,0:T(8,128)(2,1)S(1)} %get-tuple-element.206), channel_id=1, source_target_pairs={{0,2},{2,0},{4,6},{6,4},{8,10},{10,8},{12,14},{14,12},{16,18},{18,... | collective-permute-start | bytes 3145736 | tf_op jit(solution)/shard_map/ppermute | solution.py:968
  75.3 10.2 %collective-permute-start.22 = (bf16[256,512]{1,0:T(8,128)(2,1)S(1)}, bf16[256,512]{1,0:T(8,128)(2,1)S(1)}, u32[]{:S(2)}, u32[]{:S(2)}) collective-permute-start(bf16[256,512]{1,0:T(8,128)(2,1)S(1)} %get-tuple-element.210.part_ref), channel_id=1, source_target_pairs={{1,0},{0,1},{3,2},{2,3},{5,4},{4,5},{7,6},{6,7},{9,8},{8,9},{11,10... | collective-permute-start | bytes 786440 | tf_op jit(solution)/shard_map/ppermute | solution.py:941
  81.1 10.1 %collective-permute-start.23 = (bf16[256,1024]{1,0:T(8,128)(2,1)S(1)}, bf16[256,1024]{1,0:T(8,128)(2,1)S(1)}, u32[]{:S(2)}, u32[]{:S(2)}) collective-permute-start(bf16[256,1024]{1,0:T(8,128)(2,1)S(1)} %get-tuple-element.223), channel_id=1, source_target_pairs={{0,4},{2,10},{4,0},{6,14},{8,12},{10,2},{12,8},{14,6},{16,20},{18,... | collective-permute-start | bytes 1572872 | tf_op jit(solution)/shard_map/ppermute | solution.py:968
  93.3 4.0 %collective-permute-start.24 = (bf16[1056,256]{1,0:T(8,128)(2,1)S(1)}, bf16[1056,256]{1,0:T(8,128)(2,1)S(1)}, u32[]{:S(2)}, u32[]{:S(2)}) collective-permute-start(bf16[1056,256]{1,0:T(8,128)(2,1)S(1)} %get-tuple-element.238), channel_id=1, source_target_pairs={{0,2},{2,0},{4,6},{6,4},{8,10},{10,8},{12,14},{14,12},{16,18},{18,... | collective-permute-start | bytes 1622024 | tf_op jit(solution)/shard_map/ppermute | solution.py:968
  95.6 12.0 %collective-permute-start.26 = (bf16[768,256]{1,0:T(8,128)(2,1)S(1)}, bf16[768,256]{1,0:T(8,128)(2,1)S(1)}, u32[]{:S(2)}, u32[]{:S(2)}) collective-permute-start(bf16[768,256]{1,0:T(8,128)(2,1)S(1)} %get-tuple-element.250), channel_id=1, source_target_pairs={{1,0},{0,1},{3,2},{2,3},{5,4},{4,5},{7,6},{6,7},{9,8},{8,9},{11,10... | collective-permute-start | bytes 1179656 | tf_op jit(solution)/shard_map/ppermute | solution.py:941
  97.4 7.7 %collective-permute-start.25 = (bf16[544,256]{1,0:T(8,128)(2,1)S(1)}, bf16[544,256]{1,0:T(8,128)(2,1)S(1)}, u32[]{:S(2)}, u32[]{:S(2)}) collective-permute-start(bf16[544,256]{1,0:T(8,128)(2,1)S(1)} %get-tuple-element.245), channel_id=1, source_target_pairs={{0,4},{2,10},{4,0},{6,14},{8,12},{10,2},{12,8},{14,6},{16,20},{18,... | collective-permute-start | bytes 835592 | tf_op jit(solution)/shard_map/ppermute | solution.py:968
  98.0 10.9 %collective-permute-start.27 = (bf16[128,1024]{1,0:T(8,128)(2,1)S(1)}, bf16[128,1024]{1,0:T(8,128)(2,1)S(1)}, u32[]{:S(2)}, u32[]{:S(2)}) collective-permute-start(bf16[128,1024]{1,0:T(8,128)(2,1)S(1)} %get-tuple-element.253), channel_id=1, source_target_pairs={{0,8},{2,18},{4,12},{6,22},{8,0},{10,26},{12,4},{14,30},{16,24},{1... | collective-permute-start | bytes 786440 | tf_op jit(solution)/shard_map/ppermute | solution.py:968
  99.3 13.8 %collective-permute-start.31 = (bf16[512,256]{1,0:T(8,128)(2,1)S(1)}, bf16[512,256]{1,0:T(8,128)(2,1)S(1)}, u32[]{:S(2)}, u32[]{:S(2)}) collective-permute-start(bf16[512,256]{1,0:T(8,128)(2,1)S(1)} %get-tuple-element.262), channel_id=1, source_target_pairs={{1,0},{0,1},{3,2},{2,3},{5,4},{4,5},{7,6},{6,7},{9,8},{8,9},{11,10... | collective-permute-start | bytes 786440 | tf_op jit(solution)/shard_map/ppermute | solution.py:941
  105.1 7.8 %collective-permute-start.28 = (bf16[288,256]{1,0:T(8,128)(2,1)S(1)}, bf16[288,256]{1,0:T(8,128)(2,1)S(1)}, u32[]{:S(2)}, u32[]{:S(2)}) collective-permute-start(bf16[288,256]{1,0:T(8,128)(2,1)S(1)} %get-tuple-element.256), channel_id=1, source_target_pairs={{0,8},{2,18},{4,12},{6,22},{8,0},{10,26},{12,4},{14,30},{16,24},{1... | collective-permute-start | bytes 442376 | tf_op jit(solution)/shard_map/ppermute | solution.py:968
  107.7 5.4 %collective-permute-start.29 = (bf16[384,256]{1,0:T(8,128)(2,1)S(1)}, bf16[384,256]{1,0:T(8,128)(2,1)S(1)}, u32[]{:S(2)}, u32[]{:S(2)}) collective-permute-start(bf16[384,256]{1,0:T(8,128)(2,1)S(1)} %get-tuple-element.251), channel_id=1, source_target_pairs={{0,2},{2,0},{4,6},{6,4},{8,10},{10,8},{12,14},{14,12},{16,18},{18,... | collective-permute-start | bytes 589832 | tf_op jit(solution)/shard_map/ppermute | solution.py:975
  108.3 4.8 %collective-permute-start.30 = (bf16[384,256]{1,0:T(8,128)(2,1)S(1)}, bf16[384,256]{1,0:T(8,128)(2,1)S(1)}, u32[]{:S(2)}, u32[]{:S(2)}) collective-permute-start(bf16[384,256]{1,0:T(8,128)(2,1)S(1)} %get-tuple-element.260), channel_id=1, source_target_pairs={{2,4},{4,2},{6,8},{8,6},{10,12},{12,10},{14,16},{16,14},{18,20},{2... | collective-permute-start | bytes 589832 | tf_op jit(solution)/shard_map/ppermute | solution.py:976
  109.0 11.2 %collective-permute-start.32 = (bf16[64,1024]{1,0:T(8,128)(2,1)S(1)}, bf16[64,1024]{1,0:T(8,128)(2,1)S(1)}, u32[]{:S(2)}, u32[]{:S(2)}) collective-permute-start(bf16[64,1024]{1,0:T(8,128)(2,1)S(1)} %get-tuple-element.264), channel_id=1, source_target_pairs={{0,16},{2,6},{4,20},{6,2},{8,24},{10,14},{12,28},{14,10},{16,0},{1... | collective-permute-start | bytes 393224 | tf_op jit(solution)/shard_map/ppermute | solution.py:968
  113.0 8.1 %collective-permute-start.33 = (bf16[160,256]{1,0:T(8,128)(2,1)S(1)}, bf16[160,256]{1,0:T(8,128)(2,1)S(1)}, u32[]{:S(2)}, u32[]{:S(2)}) collective-permute-start(bf16[160,256]{1,0:T(8,128)(2,1)S(1)} %get-tuple-element.267), channel_id=1, source_target_pairs={{0,16},{2,6},{4,20},{6,2},{8,24},{10,14},{12,28},{14,10},{16,0},{1... | collective-permute-start | bytes 245768 | tf_op jit(solution)/shard_map/ppermute | solution.py:968

commit v6 on v5

--- a/solution.py
+++ b/solution.py
@@ -111,13 +111,13 @@
     )(lengths, banded)
 
 
-def band_kernel(masked, *refs):
-    dense_refs, band_ref = refs[:-1], refs[-1]
+def band_kernel(masked, chunks, *refs):
+    dense_refs, band_ref = refs[:chunks], refs[-1]
     lane = lax.broadcasted_iota(jnp.int32, (BLOCK, BLOCK), 1)
     row = lax.broadcasted_iota(jnp.int32, (BLOCK, BLOCK), 0)
     source = (lane + row) & (BLOCK - 1)
     near = lane + row < BLOCK
-    steps = pl.num_programs(0) // CHUNKS
+    steps = pl.num_programs(0) // chunks
 
     def turn(dense_ref):
         for head in range(band_ref.shape[0]):
@@ -139,7 +139,7 @@
             turn(dense_ref)
 
 
-def to_band(chunks, masked):
+def to_band(chunks, masked, first=0, held=None):
     heads, count, _ = chunks[0].shape
     steps = count // BLOCK
 
@@ -149,15 +149,17 @@
         )
 
     return pl.pallas_call(
-        functools.partial(band_kernel, masked),
-        grid=(CHUNKS * steps,),
-        in_specs=[block_of(chunk) for chunk in range(CHUNKS)],
-        out_specs=heads_block(heads, BAND),
+        functools.partial(band_kernel, masked, len(chunks)),
+        grid=(len(chunks) * steps,),
+        in_specs=[block_of(chunk) for chunk in range(len(chunks))]
+        + ([] if held is None else [pl.BlockSpec(memory_space=pl.ANY)]),
+        out_specs=heads_block(heads, BAND, first * steps),
         out_shape=struct((heads, CHUNKS * count, BAND), BF16),
-        compiler_params=params(),
-        cost_estimate=lasting(5.0 if masked else 0.5),
+        input_output_aliases={} if held is None else {len(chunks): 0},
+        compiler_params=params(),
+        cost_estimate=lasting(5.0 if masked and held is None else 0.3),
         name="to_band",
-    )(*chunks)
+    )(*chunks, *(() if held is None else (held,)))
 
 
 def head_split(block, size):
@@ -1138,7 +1140,7 @@
         firsts.append((*result, exchanged(result[-1])))
     normed, inverse, upper, act, slope, down_part, down_other = zip(*firsts)
 
-    new_logits = to_band([after(scores[0], down_part[-1]), *scores[1:]], True)
+    new_logits = to_band([after(scores[0], down_part[-1])], True)
     sums = after(jnp.zeros((SUM_ROWS, own), F32), new_logits)
     output = None
     seconds = []
@@ -1195,7 +1197,9 @@
     feed_sum.add(inside)
     inside, across = with_next(inside, across)
     last_sum.add(feed_sum.keep)
-    tokens_grad = token_sum(even, after(center, last_sum.keep), inside, across, center_parts)
+    for chunk in range(1, CHUNKS):
+        new_logits = to_band([after(scores[chunk], last_sum.keep)], True, chunk, new_logits)
+    tokens_grad = token_sum(even, after(center, new_logits), inside, across, center_parts)
     while feed_sum.result is None:
         feed_sum.add(tokens_grad)
     while last_sum.result is None:

time: 122 us -> 121 us (level)
  waiting for transfers between devices: 14.4 us -> 12.1 us
    ppermute x16, waiting for transfers between devices: 8.98 us -> 6.01 us  [with_partner(): lax.ppermute(x, 'row', [(i, i ^ orders[i % 2][step]) for i in range(count)])]
    pallas_call x2 -> x3, Pallas kernels: 10 us -> 11 us  [to_band(): pl.pallas_call(functools.partial(band_kernel, masked, len(chunks)), grid=...]
  transfers between devices with their start and end apart: 34 -> 34, of which waited for: 7 -> 8; matrix products, arithmetic and copies ran while one was open for 3% -> 3% of each run, Pallas kernels for 50% -> 51%
where the time goes in v6:
time: 121 us; the launch traced here: 120 us
  Pallas kernels  64.3 us (53%)
  starting transfers between devices  39.7 us (33%)
  waiting for transfers between devices  12.1 us (10%)
  local copies, waits for them, and re-layouts  2.13 us (2%)
    ppermute x16, starting transfers between devices, with_partner(): lax.ppermute(x, 'row', [(i, i ^ orders[i % 2][step]) for i in range(count)])  21.2 us
    ppermute x14, starting transfers between devices, from_next(): lax.ppermute(x, axis, [((i + step) % count, i) for i in range(count)])  16.5 us
    pallas_call x4, Pallas kernels, to_dense(): pl.pallas_call(functools.partial(dense_kernel, fill, token_count, offset)...  12.4 us
    pallas_call x3, Pallas kernels, to_band(): pl.pallas_call(functools.partial(band_kernel, masked, len(chunks)), grid=...  11 us
    pallas_call x2, Pallas kernels, attend_backward(): pl.pallas_call(functools.partial(backward_kernel, offset, last), grid=(co...  9.2 us
    pallas_call x2, Pallas kernels, attend_forward(): pl.pallas_call(functools.partial(forward_kernel, offset), grid=(count //...  7.75 us
    ppermute x14, waiting for transfers between devices, from_next(): lax.ppermute(x, axis, [((i + step) % count, i) for i in range(count)])  6.06 us
    ppermute x16, waiting for transfers between devices, with_partner(): lax.ppermute(x, 'row', [(i, i ^ orders[i % 2][step]) for i in range(count)])  6.01 us
  transfers between devices with their start and end apart: 34, of which 8 were waited for; matrix products, arithmetic and copies ran while one was open for 3% of the time, Pallas kernels for 51%

profile of v6, /device:TPU:0, one launch (start us, length us, event | category | flops | bytes accessed | tf_op | source)
XLA Modules:
  0.0 120.4 jit_solution(3230352954513970337)
XLA Ops:
  0.7 3.0 %collective-permute-start = (bf16[32,256]{1,0:T(8,128)(2,1)}, bf16[32,256]{1,0:T(8,128)(2,1)S(1)}, u32[]{:S(2)}, u32[]{:S(2)}) collective-permute-start(bf16[32,256]{1,0:T(8,128)(2,1)} %bitcast.17), channel_id=1, source_target_pairs={{1,0},{0,1},{3,2},{2,3},{5,4},{4,5},{7,6},{6,7},{9,8},{8,9},{11,10... | collective-permute-start | bytes 49160 | tf_op jit(solution)/shard_map/ppermute | solution.py:943
  3.7 2.6 %collective-permute-start.1 = (bf16[1,3,32,256]{3,2,1,0:T(8,128)(2,1)}, bf16[1,3,32,256]{3,2,1,0:T(8,128)(2,1)S(1)}, u32[]{:S(2)}, u32[]{:S(2)}) collective-permute-start(bf16[1,3,32,256]{3,2,1,0:T(8,128)(2,1)} %bitcast.15), channel_id=1, source_target_pairs={{0,16},{2,6},{4,20},{6,2},{8,24},{10,14},{12,28},{14,10},{16,0},{1... | collective-permute-start | bytes 147464 | tf_op jit(solution)/shard_map/ppermute | solution.py:970
  6.2 0.5 collective-permute-start.3
  6.8 0.9 maximum_bitcast_fusion
  7.7 1.9 %collective-permute-start.2 = (bf16[1,32,2560]{2,1,0:T(8,128)(2,1)S(1)}, bf16[1,32,2560]{2,1,0:T(8,128)(2,1)S(1)}, u32[]{:S(2)}, u32[]{:S(2)}) collective-permute-start(bf16[1,32,2560]{2,1,0:T(8,128)(2,1)S(1)} %maximum_bitcast_fusion), channel_id=1, source_target_pairs={{0,16},{2,6},{4,20},{6,2},{8,24},{10,14},{12,28},{14,10},{16,0},{1... | collective-permute-start | bytes 491528 | tf_op jit(solution)/shard_map/ppermute | solution.py:970
  9.7 1.0 constant_dynamic-slice_fusion
  10.8 0.7 collective-permute-start.6
  11.5 0.8 constant_dynamic-update-slice_fusion.1
  12.3 4.4 %collective-permute-start.4 = (bf16[2,3,32,256]{3,2,1,0:T(8,128)(2,1)S(1)}, bf16[2,3,32,256]{3,2,1,0:T(8,128)(2,1)S(1)}, u32[]{:S(2)}, u32[]{:S(2)}) collective-permute-start(bf16[2,3,32,256]{3,2,1,0:T(8,128)(2,1)S(1)} %constant_dynamic-update-slice_fusion), channel_id=1, source_target_pairs={{0,8},{2,18},{4,12},{6,22},{8,0},{10,26},{12,4},{14,30},{16,24},{1... | collective-permute-start | bytes 294920 | tf_op jit(solution)/shard_map/ppermute | solution.py:970
  16.8 1.7 %collective-permute-start.7 = (bf16[384,256]{1,0:T(8,128)(2,1)S(1)}, bf16[384,256]{1,0:T(8,128)(2,1)S(1)}, u32[]{:S(2)}, u32[]{:S(2)}) collective-permute-start(bf16[384,256]{1,0:T(8,128)(2,1)S(1)} %collective-permute-done.5.refs_2_), channel_id=1, source_target_pairs={{1,0},{0,1},{3,2},{2,3},{5,4},{4,5},{7,6},{6,7},{9,8},{8,9},{11,10... | collective-permute-start | bytes 589832 | tf_op jit(solution)/shard_map/ppermute | solution.py:943
  18.5 0.4 collective-permute-start.8
  18.9 2.4 %collective-permute-done.4 = bf16[2,3,32,256]{3,2,1,0:T(8,128)(2,1)S(1)} collective-permute-done((bf16[2,3,32,256]{3,2,1,0:T(8,128)(2,1)S(1)}, bf16[2,3,32,256]{3,2,1,0:T(8,128)(2,1)S(1)}, u32[]{:S(2)}, u32[]{:S(2)}) %collective-permute-start.4) | collective-permute-done | bytes 98336 | tf_op jit(solution)/shard_map/ppermute | solution.py:970
  21.3 1.5 %collective-permute-start.9 = (bf16[4,3,32,256]{3,2,1,0:T(8,128)(2,1)S(1)}, bf16[4,3,32,256]{3,2,1,0:T(8,128)(2,1)S(1)}, u32[]{:S(2)}, u32[]{:S(2)}) collective-permute-start(bf16[4,3,32,256]{3,2,1,0:T(8,128)(2,1)S(1)} %constant_dynamic-update-slice_fusion.4), channel_id=1, source_target_pairs={{0,4},{2,10},{4,0},{6,14},{8,12},{10,2},{12,8},{14,6},{16,20},{18,... | collective-permute-start | bytes 589832 | tf_op jit(solution)/shard_map/ppermute | solution.py:970
  22.9 3.1 %to_dense.4.prev_ref = bf16[4,256,1152]{2,1,0:T(8,128)(2,1)S(1)} custom-call(s32[34]{0:T(128)S(1)} %pad_add_fusion.lengths_ref, bf16[4,512,1024]{2,1,0:T(8,128)(2,1)} %band_ref.1), custom_call_target="tpu_custom_call" | custom-call | flops 8000000000 | tf_op jit(solution)/shard_map/to_dense/pallas_call | solution.py:102
  26.1 2.7 %collective-permute-done.8.refs_5_ = bf16[384,256]{1,0:T(8,128)(2,1)S(1)} collective-permute-done((bf16[384,256]{1,0:T(8,128)(2,1)S(1)}, bf16[384,256]{1,0:T(8,128)(2,1)S(1)}, u32[]{:S(2)}, u32[]{:S(2)}) %collective-permute-start.8) | collective-permute-done | bytes 196640 | tf_op jit(solution)/shard_map/ppermute | solution.py:943
  28.7 1.6 %collective-permute-start.13 = (bf16[512,256]{1,0:T(8,128)(2,1)S(1)}, bf16[512,256]{1,0:T(8,128)(2,1)S(1)}, u32[]{:S(2)}, u32[]{:S(2)}) collective-permute-start(bf16[512,256]{1,0:T(8,128)(2,1)S(1)} %copy-done.3), channel_id=1, source_target_pairs={{1,0},{0,1},{3,2},{2,3},{5,4},{4,5},{7,6},{6,7},{9,8},{8,9},{11,10... | collective-permute-start | bytes 786440 | tf_op jit(solution)/shard_map/ppermute | solution.py:943
  30.4 0.2 collective-permute-start.10
  30.6 1.4 %collective-permute-start.15 = (bf16[4,32,2560]{2,1,0:T(8,128)(2,1)S(1)}, bf16[4,32,2560]{2,1,0:T(8,128)(2,1)S(1)}, u32[]{:S(2)}, u32[]{:S(2)}) collective-permute-start(bf16[4,32,2560]{2,1,0:T(8,128)(2,1)S(1)} %constant_dynamic-update-slice_fusion.8), channel_id=1, source_target_pairs={{0,4},{2,10},{4,0},{6,14},{8,12},{10,2},{12,8},{14,6},{16,20},{18,... | collective-permute-start | bytes 1966088 | tf_op jit(solution)/shard_map/ppermute | solution.py:970
  32.0 0.2 collective-permute-done.10.far_ref
  32.2 1.9 %project.1 = (bf16[512,512]{1,0:T(8,128)(2,1)S(1)}, bf16[512,256]{1,0:T(8,128)(2,1)S(1)}, bf16[1536,256]{1,0:T(8,128)(2,1)S(1)}, bf16[1536,256]{1,0:T(8,128)(2,1...) custom-call(s32[16]{0:T(128)S(1)} %fusion.7.slot_ref, ...), custom_call_target="tpu_custom_call" | custom-call | flops 2000000000 | tf_op jit(solution)/shard_map/project/pallas_call | solution.py:245
  34.1 1.6 %collective-permute-start.12 = (f32[6,256]{1,0:T(8,128)S(1)}, f32[6,256]{1,0:T(8,128)S(1)}, u32[]{:S(2)}, u32[]{:S(2)}) collective-permute-start(f32[6,256]{1,0:T(8,128)S(1)} %pad_maximum_fusion.1), channel_id=1, source_target_pairs={{1,0},{0,1},{3,2},{2,3},{5,4},{4,5},{7,6},{6,7},{9,8},{8,9},{11,10... | collective-permute-start | bytes 18440 | tf_op jit(solution)/shard_map/ppermute | solution.py:943
  35.8 3.9 %attend_forward.2 = (bf16[4,256,1152]{2,1,0:T(8,128)(2,1)S(1)}, bf16[4,256,1152]{2,1,0:T(8,128)(2,1)S(1)}, bf16[256,256]{1,0:T(8,128)(2,1)S(1)}) custom-call(bf16[512,256]{1,0:T(8,128)(2,1)S(1)} %get-tuple-element.166.query_ref, bf16[1536,256]{1,0:T(8,128)(2,1)S(1)} %get-tuple-element.157.key_ref, bf16[1536,256]{1,0:T(8,128)(2,1)S(1)} %get-tuple-element.158.value_ref, ...), custom_call_target="tpu_custom_call" | custom-call | flops 3800000000 | tf_op jit(solution)/shard_map/attend_forward/pallas_call | solution.py:287
  39.6 0.5 collective-permute-start.14
  40.2 3.1 %to_dense.5.prev_ref = bf16[4,256,1152]{2,1,0:T(8,128)(2,1)S(1)} custom-call(s32[34]{0:T(128)S(1)} %pad_add_fusion.lengths_ref, bf16[4,512,1024]{2,1,0:T(8,128)(2,1)} %band_ref.1), custom_call_target="tpu_custom_call" | custom-call | flops 1000000000 | tf_op jit(solution)/shard_map/to_dense/pallas_call | solution.py:102
  43.4 1.6 %collective-permute-done.14.other_ref = bf16[256,256]{1,0:T(8,128)(2,1)S(1)} collective-permute-done((bf16[256,256]{1,0:T(8,128)(2,1)S(1)}, bf16[256,256]{1,0:T(8,128)(2,1)S(1)}, u32[]{:S(2)}, u32[]{:S(2)}) %collective-permute-start.14) | collective-permute-done | bytes 131104 | tf_op jit(solution)/shard_map/ppermute | solution.py:943
  45.2 3.9 %attend_forward.3 = (bf16[4,256,1152]{2,1,0:T(8,128)(2,1)S(1)}, bf16[4,256,1152]{2,1,0:T(8,128)(2,1)S(1)}, bf16[256,256]{1,0:T(8,128)(2,1)S(1)}) custom-call(bf16[512,256]{1,0:T(8,128)(2,1)S(1)} %get-tuple-element.166.query_ref, bf16[1536,256]{1,0:T(8,128)(2,1)S(1)} %get-tuple-element.157.key_ref, bf16[1536,256]{1,0:T(8,128)(2,1)S(1)} %get-tuple-element.158.value_ref, ...), custom_call_target="tpu_custom_call" | custom-call | flops 3800000000 | tf_op jit(solution)/shard_map/attend_forward/pallas_call | solution.py:287
  49.1 0.6 collective-permute-start.16
  49.7 1.1 in_order.1
  50.8 2.2 %feed_first.2 = (f32[256,512]{1,0:T(8,128)S(1)}, f32[256,1]{1,0:T(8,128)S(1)}, bf16[256,512]{1,0:T(8,128)(2,1)S(1)}, bf16[256,1024]{1,0:T(8,128)(2,1)S(1)}, bf16...) custom-call(bf16[256,256]{1,0:T(8,128)(2,1)S(1)} %get-tuple-element.160.own_ref.refs_4_, ...), custom_call_target="tpu_custom_call" | custom-call | flops 1000000000 | tf_op jit(solution)/shard_map/feed_first/pallas_call | solution.py:475
  52.9 1.6 %collective-permute-start.18 = (bf16[256,512]{1,0:T(8,128)(2,1)S(1)}, bf16[256,512]{1,0:T(8,128)(2,1)S(1)}, u32[]{:S(2)}, u32[]{:S(2)}) collective-permute-start(bf16[256,512]{1,0:T(8,128)(2,1)S(1)} %get-tuple-element.174.part_ref), channel_id=1, source_target_pairs={{1,0},{0,1},{3,2},{2,3},{5,4},{4,5},{7,6},{6,7},{9,8},{8,9},{11,10... | collective-permute-start | bytes 786440 | tf_op jit(solution)/shard_map/ppermute | solution.py:943
  54.5 3.1 %to_dense.6.logit_ref = bf16[4,256,1152]{2,1,0:T(8,128)(2,1)S(1)} custom-call(s32[34]{0:T(128)S(1)} %pad_add_fusion.lengths_ref, bf16[4,512,1024]{2,1,0:T(8,128)(2,1)} %band_ref.3), custom_call_target="tpu_custom_call" | custom-call | flops 1000000000 | tf_op jit(solution)/shard_map/to_dense/pallas_call | solution.py:102
  57.6 2.2 %feed_first.3 = (f32[256,512]{1,0:T(8,128)S(1)}, f32[256,1]{1,0:T(8,128)S(1)}, bf16[256,512]{1,0:T(8,128)(2,1)S(1)}, bf16[256,1024]{1,0:T(8,128)(2,1)S(1)}, bf16...) custom-call(bf16[256,256]{1,0:T(8,128)(2,1)S(1)} %get-tuple-element.167.own_ref.refs_5_, ...), custom_call_target="tpu_custom_call" | custom-call | flops 1000000000 | tf_op jit(solution)/shard_map/feed_first/pallas_call | solution.py:475
  59.8 0.6 collective-permute-start.19
  60.4 3.0 %to_band.3.refs_1_ = bf16[4,512,1024]{2,1,0:T(8,128)(2,1)} custom-call(bf16[4,256,1152]{2,1,0:T(8,128)(2,1)S(1)} %get-tuple-element.178.refs_0_), custom_call_target="tpu_custom_call" | custom-call | flops 5000000000 | tf_op jit(solution)/shard_map/to_band/pallas_call | solution.py:151
  63.3 2.4 %feed_second.2 = (f32[16,256]{1,0:T(8,128)S(1)}, bf16[512,256]{1,0:T(8,128)(2,1)}, f32[256,512]{1,0:T(8,128)S(1)}, bf16[256,512]{1,0:T(8,128)(2,1)S(1)}, bf16[25...) custom-call(f32[16,256]{1,0:T(8,128)S(1)} %broadcast_in_dim.18.start_ref, ...), custom_call_target="tpu_custom_call" | custom-call | flops 700000000 | tf_op jit(solution)/shard_map/feed_second/pallas_call | solution.py:554
  65.8 1.5 %collective-permute-start.20 = (bf16[256,512]{1,0:T(8,128)(2,1)S(1)}, bf16[256,512]{1,0:T(8,128)(2,1)S(1)}, u32[]{:S(2)}, u32[]{:S(2)}) collective-permute-start(bf16[256,512]{1,0:T(8,128)(2,1)S(1)} %get-tuple-element.199.part_ref), channel_id=1, source_target_pairs={{1,0},{0,1},{3,2},{2,3},{5,4},{4,5},{7,6},{6,7},{9,8},{8,9},{11,10... | collective-permute-start | bytes 786440 | tf_op jit(solution)/shard_map/ppermute | solution.py:943
  67.3 0.7 collective-permute-done.19.recv_ref
  68.0 2.4 %feed_second.3 = (f32[16,256]{1,0:T(8,128)S(1)}, bf16[512,256]{1,0:T(8,128)(2,1)}, f32[256,512]{1,0:T(8,128)S(1)}, bf16[256,512]{1,0:T(8,128)(2,1)S(1)}, bf16[25...) custom-call(f32[16,256]{1,0:T(8,128)S(1)} %get-tuple-element.182.start_ref, ...), custom_call_target="tpu_custom_call", output_to_operand_aliasing={{1}: (9, {})} | custom-call | flops 700000000 | tf_op jit(solution)/shard_map/feed_second/pallas_call | solution.py:554
  70.4 3.4 %feed_grads.1 = (f32[512,1024]{1,0:T(8,128)S(1)}, bf16[512,1024]{1,0:T(8,128)(2,1)S(1)}) custom-call(s32[16]{0:T(128)S(1)} %and_select_fusion.block_ref, bf16[256,512]{1,0:T(8,128)(2,1)S(1)} %get-tuple-element.189.refs_0_, bf16[256,512]{1,0:T(8,128)(2,1)S(1)} %get-tuple-element.190.refs_1_, bf16[256,512]{1,0:T(8,128)(2,1)S(1)} %get-tuple-element.191.refs_2_, ...), custom_call_target="tpu_custom_call" | custom-call | flops 1000000000 | tf_op jit(solution)/shard_map/feed_grads/pallas_call | solution.py:675
  73.9 0.6 collective-permute-start.22
  74.5 0.8 feed_third.2
  75.2 4.2 %attend_backward.2 = (bf16[4,256,1152]{2,1,0:T(8,128)(2,1)S(1)}, bf16[256,256]{1,0:T(8,128)(2,1)S(1)}, f32[256,1536]{1,0:T(8,128)S(1)}, f32[256,1536]{1,0:T(8,128)S(1)}) custom-call(bf16[256,256]{1,0:T(8,128)(2,1)S(1)} %get-tuple-element.203.grad_ref, bf16[512,256]{1,0:T(8,128)(2,1)S(1)} %get-tuple-element.166.query_ref, ...), custom_call_target="tpu_custom_call" | custom-call | flops 20000000000 | tf_op jit(solution)/shard_map/attend_backward/pallas_call | solution.py:371
  79.5 0.2 fold.6
  79.7 1.5 %collective-permute-start.23 = (bf16[256,1024]{1,0:T(8,128)(2,1)S(1)}, bf16[256,1024]{1,0:T(8,128)(2,1)S(1)}, u32[]{:S(2)}, u32[]{:S(2)}) collective-permute-start(bf16[256,1024]{1,0:T(8,128)(2,1)S(1)} %get-tuple-element.221), channel_id=1, source_target_pairs={{0,4},{2,10},{4,0},{6,14},{8,12},{10,2},{12,8},{14,6},{16,20},{18,... | collective-permute-start | bytes 1572872 | tf_op jit(solution)/shard_map/ppermute | solution.py:970
  81.2 3.1 %to_dense.7.logit_ref = bf16[4,256,1152]{2,1,0:T(8,128)(2,1)S(1)} custom-call(s32[34]{0:T(128)S(1)} %pad_add_fusion.lengths_ref, bf16[4,512,1024]{2,1,0:T(8,128)(2,1)} %band_ref.3), custom_call_target="tpu_custom_call" | custom-call | flops 1000000000 | tf_op jit(solution)/shard_map/to_dense/pallas_call | solution.py:102
  84.3 0.8 feed_third.3
  85.1 5.0 %attend_backward.3 = (bf16[4,256,1152]{2,1,0:T(8,128)(2,1)S(1)}, bf16[256,256]{1,0:T(8,128)(2,1)S(1)}, bf16[1536,256]{1,0:T(8,128)(2,1)S(1)}, bf16[1536,256]{1,0:T(8,128)(2,1)S(1)}) custom-call(bf16[256,256]{1,0:T(8,128)(2,1)S(1)} %get-tuple-element.215.grad_ref, bf16[512,256]{1,0:T(8,128)(2,1)S(1)} %get-tuple-element.166.query_ref, ...), custom_call_target="tpu_custom_call" | custom-call | flops 3000000000 | tf_op jit(solution)/shard_map/attend_backward/pallas_call | solution.py:371
  90.2 1.9 %project_grads.1 = (f32[1024,256]{1,0:T(8,128)S(1)}, bf16[1056,256]{1,0:T(8,128)(2,1)S(1)}, f32[16,256]{1,0:T(8,128)S(1)}) custom-call(s32[16]{0:T(128)S(1)} %and_select_fusion.block_ref, f32[16,256]{1,0:T(8,128)S(1)} %get-tuple-element.223.start_ref, bf16[256,256]{1,0:T(8,128)(2,1)S(1)} %get-tuple-element.205.refs_0_, ...), custom_call_target="tpu_custom_call" | custom-call | flops 600000000 | tf_op jit(solution)/shard_map/project_grads/pallas_call | solution.py:732
  92.2 2.1 %token_grads.1 = (f32[512,256]{1,0:T(8,128)S(1)}, f32[768,256]{1,0:T(8,128)S(1)}, bf16[512,256]{1,0:T(8,128)(2,1)S(1)}, bf16[768,256]{1,0:T(8,128)(2,1)S(1)}) custom-call(s32[1]{0:T(128)} %bitcast.even_ref, bf16[256,256]{1,0:T(8,128)(2,1)S(1)} %get-tuple-element.205.refs_0_, bf16[256,256]{1,0:T(8,128)(2,1)S(1)} %get-tuple-element.219.refs_1_, ...), custom_call_target="tpu_custom_call" | custom-call | flops 5000000000 | tf_op jit(solution)/shard_map/token_grads/pallas_call | solution.py:876
  94.3 1.6 %collective-permute-start.26 = (bf16[768,256]{1,0:T(8,128)(2,1)S(1)}, bf16[768,256]{1,0:T(8,128)(2,1)S(1)}, u32[]{:S(2)}, u32[]{:S(2)}) collective-permute-start(bf16[768,256]{1,0:T(8,128)(2,1)S(1)} %get-tuple-element.251), channel_id=1, source_target_pairs={{1,0},{0,1},{3,2},{2,3},{5,4},{4,5},{7,6},{6,7},{9,8},{8,9},{11,10... | collective-permute-start | bytes 1179656 | tf_op jit(solution)/shard_map/ppermute | solution.py:943
  96.1 0.6 collective-permute-start.25
  96.6 1.4 %collective-permute-start.27 = (bf16[128,1024]{1,0:T(8,128)(2,1)S(1)}, bf16[128,1024]{1,0:T(8,128)(2,1)S(1)}, u32[]{:S(2)}, u32[]{:S(2)}) collective-permute-start(bf16[128,1024]{1,0:T(8,128)(2,1)S(1)} %get-tuple-element.254), channel_id=1, source_target_pairs={{0,8},{2,18},{4,12},{6,22},{8,0},{10,26},{12,4},{14,30},{16,24},{1... | collective-permute-start | bytes 786440 | tf_op jit(solution)/shard_map/ppermute | solution.py:970
  98.0 0.6 collective-permute-start.31
  98.6 5.0 %to_band.4 = bf16[4,512,1024]{2,1,0:T(8,128)(2,1)} custom-call(bf16[4,256,1152]{2,1,0:T(8,128)(2,1)S(1)} %get-tuple-element.243.refs_0_, bf16[4,256,1152]{2,1,0:T(8,128)(2,1)S(1)} %get-tuple-element.244.refs_1_), custom_call_target="tpu_custom_call" | custom-call | flops 300000000 | tf_op jit(solution)/shard_map/to_band/pallas_call | solution.py:151
  103.7 1.5 %collective-permute-start.28 = (bf16[288,256]{1,0:T(8,128)(2,1)S(1)}, bf16[288,256]{1,0:T(8,128)(2,1)S(1)}, u32[]{:S(2)}, u32[]{:S(2)}) collective-permute-start(bf16[288,256]{1,0:T(8,128)(2,1)S(1)} %get-tuple-element.257), channel_id=1, source_target_pairs={{0,8},{2,18},{4,12},{6,22},{8,0},{10,26},{12,4},{14,30},{16,24},{1... | collective-permute-start | bytes 442376 | tf_op jit(solution)/shard_map/ppermute | solution.py:970
  105.2 1.1 collective-permute-done.26.refs_0_
  106.4 0.6 collective-permute-start.29
  106.9 0.7 collective-permute-start.30
  107.7 3.9 %collective-permute-start.32 = (bf16[64,1024]{1,0:T(8,128)(2,1)S(1)}, bf16[64,1024]{1,0:T(8,128)(2,1)S(1)}, u32[]{:S(2)}, u32[]{:S(2)}) collective-permute-start(bf16[64,1024]{1,0:T(8,128)(2,1)S(1)} %get-tuple-element.266), channel_id=1, source_target_pairs={{0,16},{2,6},{4,20},{6,2},{8,24},{10,14},{12,28},{14,10},{16,0},{1... | collective-permute-start | bytes 393224 | tf_op jit(solution)/shard_map/ppermute | solution.py:970
  111.7 3.0 %to_band.5 = bf16[4,512,1024]{2,1,0:T(8,128)(2,1)} custom-call(bf16[4,256,1152]{2,1,0:T(8,128)(2,1)S(1)} %get-tuple-element.260.refs_0_, bf16[4,512,1024]{2,1,0:T(8,128)(2,1)} %to_band.3.refs_1_), custom_call_target="tpu_custom_call", output_to_operand_aliasing={{}: (1, {})} | custom-call | flops 300000000 | tf_op jit(solution)/shard_map/to_band/pallas_call | solution.py:151
  114.7 0.9 token_sum.1
  115.6 3.2 %collective-permute-done.32.arrived_ref = bf16[64,1024]{1,0:T(8,128)(2,1)S(1)} collective-permute-done((bf16[64,1024]{1,0:T(8,128)(2,1)S(1)}, bf16[64,1024]{1,0:T(8,128)(2,1)S(1)}, u32[]{:S(2)}, u32[]{:S(2)}) %collective-permute-start.32) | collective-permute-done | bytes 131104 | tf_op jit(solution)/shard_map/ppermute | solution.py:970
  118.8 0.7 finish.2
  119.7 0.7 finish.3
  (74 shorter events, 1.5 us)
Async XLA Ops:
  0.6 22.2 %copy-start.7 = (s32[1,33]{1,0:T(1,128)S(1)}, s32[1,33]{1,0:T(1,128)}, u32[]{:S(2)}) copy-start(s32[1,33]{1,0:T(1,128)} %param.16) | copy-start | bytes 400
  0.7 6.2 %collective-permute-start = (bf16[32,256]{1,0:T(8,128)(2,1)}, bf16[32,256]{1,0:T(8,128)(2,1)S(1)}, u32[]{:S(2)}, u32[]{:S(2)}) collective-permute-start(bf16[32,256]{1,0:T(8,128)(2,1)} %bitcast.17), channel_id=1, source_target_pairs={{1,0},{0,1},{3,2},{2,3},{5,4},{4,5},{7,6},{6,7},{9,8},{8,9},{11,10... | collective-permute-start | bytes 49160 | tf_op jit(solution)/shard_map/ppermute | solution.py:943
  3.7 8.6 %collective-permute-start.1 = (bf16[1,3,32,256]{3,2,1,0:T(8,128)(2,1)}, bf16[1,3,32,256]{3,2,1,0:T(8,128)(2,1)S(1)}, u32[]{:S(2)}, u32[]{:S(2)}) collective-permute-start(bf16[1,3,32,256]{3,2,1,0:T(8,128)(2,1)} %bitcast.15), channel_id=1, source_target_pairs={{0,16},{2,6},{4,20},{6,2},{8,24},{10,14},{12,28},{14,10},{16,0},{1... | collective-permute-start | bytes 147464 | tf_op jit(solution)/shard_map/ppermute | solution.py:970
  6.2 12.6 %collective-permute-start.3 = (bf16[512,256]{1,0:T(8,128)(2,1)}, bf16[512,256]{1,0:T(8,128)(2,1)S(1)}, u32[]{:S(2)}, u32[]{:S(2)}) collective-permute-start(bf16[512,256]{1,0:T(8,128)(2,1)} %refs_0_), channel_id=1, source_target_pairs={{1,0},{0,1},{3,2},{2,3},{5,4},{4,5},{7,6},{6,7},{9,8},{8,9},{11,10... | collective-permute-start | bytes 786440 | tf_op jit(solution)/shard_map/ppermute | solution.py:943
  7.7 8.9 %collective-permute-start.2 = (bf16[1,32,2560]{2,1,0:T(8,128)(2,1)S(1)}, bf16[1,32,2560]{2,1,0:T(8,128)(2,1)S(1)}, u32[]{:S(2)}, u32[]{:S(2)}) collective-permute-start(bf16[1,32,2560]{2,1,0:T(8,128)(2,1)S(1)} %maximum_bitcast_fusion), channel_id=1, source_target_pairs={{0,16},{2,6},{4,20},{6,2},{8,24},{10,14},{12,28},{14,10},{16,0},{1... | collective-permute-start | bytes 491528 | tf_op jit(solution)/shard_map/ppermute | solution.py:970
  10.7 6.1 %collective-permute-start.5 = (bf16[384,256]{1,0:T(8,128)(2,1)S(1)}, bf16[384,256]{1,0:T(8,128)(2,1)S(1)}, u32[]{:S(2)}, u32[]{:S(2)}) collective-permute-start(bf16[384,256]{1,0:T(8,128)(2,1)S(1)} %get-tuple-element.280), channel_id=1, source_target_pairs={{0,2},{2,0},{4,6},{6,4},{8,10},{10,8},{12,14},{14,12},{16,18},{18,... | collective-permute-start | bytes 589832 | tf_op jit(solution)/shard_map/ppermute | solution.py:977
  10.8 7.7 %collective-permute-start.6 = (bf16[384,256]{1,0:T(8,128)(2,1)S(1)}, bf16[384,256]{1,0:T(8,128)(2,1)S(1)}, u32[]{:S(2)}, u32[]{:S(2)}) collective-permute-start(bf16[384,256]{1,0:T(8,128)(2,1)S(1)} %get-tuple-element.279), channel_id=1, source_target_pairs={{2,4},{4,2},{6,8},{8,6},{10,12},{12,10},{14,16},{16,14},{18,20},{2... | collective-permute-start | bytes 589832 | tf_op jit(solution)/shard_map/ppermute | solution.py:978
  12.3 9.0 %collective-permute-start.4 = (bf16[2,3,32,256]{3,2,1,0:T(8,128)(2,1)S(1)}, bf16[2,3,32,256]{3,2,1,0:T(8,128)(2,1)S(1)}, u32[]{:S(2)}, u32[]{:S(2)}) collective-permute-start(bf16[2,3,32,256]{3,2,1,0:T(8,128)(2,1)S(1)} %constant_dynamic-update-slice_fusion), channel_id=1, source_target_pairs={{0,8},{2,18},{4,12},{6,22},{8,0},{10,26},{12,4},{14,30},{16,24},{1... | collective-permute-start | bytes 294920 | tf_op jit(solution)/shard_map/ppermute | solution.py:970
  16.7 13.9 %collective-permute-start.11 = (bf16[2,32,2560]{2,1,0:T(8,128)(2,1)S(1)}, bf16[2,32,2560]{2,1,0:T(8,128)(2,1)S(1)}, u32[]{:S(2)}, u32[]{:S(2)}) collective-permute-start(bf16[2,32,2560]{2,1,0:T(8,128)(2,1)S(1)} %constant_dynamic-update-slice_fusion.2), channel_id=1, source_target_pairs={{0,8},{2,18},{4,12},{6,22},{8,0},{10,26},{12,4},{14,30},{16,24},{1... | collective-permute-start | bytes 983048 | tf_op jit(solution)/shard_map/ppermute | solution.py:970
  16.8 9.3 %collective-permute-start.7 = (bf16[384,256]{1,0:T(8,128)(2,1)S(1)}, bf16[384,256]{1,0:T(8,128)(2,1)S(1)}, u32[]{:S(2)}, u32[]{:S(2)}) collective-permute-start(bf16[384,256]{1,0:T(8,128)(2,1)S(1)} %collective-permute-done.5.refs_2_), channel_id=1, source_target_pairs={{1,0},{0,1},{3,2},{2,3},{5,4},{4,5},{7,6},{6,7},{9,8},{8,9},{11,10... | collective-permute-start | bytes 589832 | tf_op jit(solution)/shard_map/ppermute | solution.py:943
  18.5 10.2 %collective-permute-start.8 = (bf16[384,256]{1,0:T(8,128)(2,1)S(1)}, bf16[384,256]{1,0:T(8,128)(2,1)S(1)}, u32[]{:S(2)}, u32[]{:S(2)}) collective-permute-start(bf16[384,256]{1,0:T(8,128)(2,1)S(1)} %collective-permute-done.6.refs_4_), channel_id=1, source_target_pairs={{1,0},{0,1},{3,2},{2,3},{5,4},{4,5},{7,6},{6,7},{9,8},{8,9},{11,10... | collective-permute-start | bytes 589832 | tf_op jit(solution)/shard_map/ppermute | solution.py:943
  21.3 9.1 %collective-permute-start.9 = (bf16[4,3,32,256]{3,2,1,0:T(8,128)(2,1)S(1)}, bf16[4,3,32,256]{3,2,1,0:T(8,128)(2,1)S(1)}, u32[]{:S(2)}, u32[]{:S(2)}) collective-permute-start(bf16[4,3,32,256]{3,2,1,0:T(8,128)(2,1)S(1)} %constant_dynamic-update-slice_fusion.4), channel_id=1, source_target_pairs={{0,4},{2,10},{4,0},{6,14},{8,12},{10,2},{12,8},{14,6},{16,20},{18,... | collective-permute-start | bytes 589832 | tf_op jit(solution)/shard_map/ppermute | solution.py:970
  22.9 5.8 %copy-start.3 = (bf16[512,256]{1,0:T(8,128)(2,1)S(1)}, bf16[512,256]{1,0:T(8,128)(2,1)}, u32[]{:S(2)}) copy-start(bf16[512,256]{1,0:T(8,128)(2,1)} %param.26) | copy-start | bytes 786436
  22.9 9.3 %copy-start = (bf16[512,256]{1,0:T(8,128)(2,1)S(1)}, bf16[512,256]{1,0:T(8,128)(2,1)}, u32[]{:S(2)}) copy-start(bf16[512,256]{1,0:T(8,128)(2,1)} %refs_0_) | copy-start | bytes 786436
  22.9 9.3 %copy-start.2 = (f32[2,256]{1,0:T(2,128)S(1)}, f32[2,256]{1,0:T(2,128)}, u32[]{:S(2)}) copy-start(f32[2,256]{1,0:T(2,128)} %bias_ref.1) | copy-start | bytes 6148
  28.7 11.5 %collective-permute-start.13 = (bf16[512,256]{1,0:T(8,128)(2,1)S(1)}, bf16[512,256]{1,0:T(8,128)(2,1)S(1)}, u32[]{:S(2)}, u32[]{:S(2)}) collective-permute-start(bf16[512,256]{1,0:T(8,128)(2,1)S(1)} %copy-done.3), channel_id=1, source_target_pairs={{1,0},{0,1},{3,2},{2,3},{5,4},{4,5},{7,6},{6,7},{9,8},{8,9},{11,10... | collective-permute-start | bytes 786440 | tf_op jit(solution)/shard_map/ppermute | solution.py:943
  30.4 1.8 %collective-permute-start.10 = (bf16[8,3,32,256]{3,2,1,0:T(8,128)(2,1)S(1)}, bf16[8,3,32,256]{3,2,1,0:T(8,128)(2,1)S(1)}, u32[]{:S(2)}, u32[]{:S(2)}) collective-permute-start(bf16[8,3,32,256]{3,2,1,0:T(8,128)(2,1)S(1)} %constant_dynamic-update-slice_fusion.6.near_ref), channel_id=1, source_target_pairs={{0,2},{2,0},{4,6},{6,4},{8,10},{10,8},{12,14},{14,12},{16,18},{18,... | collective-permute-start | bytes 1179656 | tf_op jit(solution)/shard_map/ppermute | solution.py:970
  30.6 14.4 %collective-permute-start.15 = (bf16[4,32,2560]{2,1,0:T(8,128)(2,1)S(1)}, bf16[4,32,2560]{2,1,0:T(8,128)(2,1)S(1)}, u32[]{:S(2)}, u32[]{:S(2)}) collective-permute-start(bf16[4,32,2560]{2,1,0:T(8,128)(2,1)S(1)} %constant_dynamic-update-slice_fusion.8), channel_id=1, source_target_pairs={{0,4},{2,10},{4,0},{6,14},{8,12},{10,2},{12,8},{14,6},{16,20},{18,... | collective-permute-start | bytes 1966088 | tf_op jit(solution)/shard_map/ppermute | solution.py:970
  32.2 1.9 %copy-start.4 = (f32[2,256]{1,0:T(2,128)S(1)}, f32[2,256]{1,0:T(2,128)}, u32[]{:S(2)}) copy-start(f32[2,256]{1,0:T(2,128)} %param.20) | copy-start | bytes 6148
  32.2 1.9 %copy-start.5 = (f32[2,256]{1,0:T(2,128)S(1)}, f32[2,256]{1,0:T(2,128)}, u32[]{:S(2)}) copy-start(f32[2,256]{1,0:T(2,128)} %param.25) | copy-start | bytes 6148
  32.2 1.9 %copy-start.6 = (f32[2,256]{1,0:T(2,128)S(1)}, f32[2,256]{1,0:T(2,128)}, u32[]{:S(2)}) copy-start(f32[2,256]{1,0:T(2,128)} %param.24) | copy-start | bytes 6148
  34.1 6.1 %collective-permute-start.12 = (f32[6,256]{1,0:T(8,128)S(1)}, f32[6,256]{1,0:T(8,128)S(1)}, u32[]{:S(2)}, u32[]{:S(2)}) collective-permute-start(f32[6,256]{1,0:T(8,128)S(1)} %pad_maximum_fusion.1), channel_id=1, source_target_pairs={{1,0},{0,1},{3,2},{2,3},{5,4},{4,5},{7,6},{6,7},{9,8},{8,9},{11,10... | collective-permute-start | bytes 18440 | tf_op jit(solution)/shard_map/ppermute | solution.py:943
  39.6 5.3 %collective-permute-start.14 = (bf16[256,256]{1,0:T(8,128)(2,1)S(1)}, bf16[256,256]{1,0:T(8,128)(2,1)S(1)}, u32[]{:S(2)}, u32[]{:S(2)}) collective-permute-start(bf16[256,256]{1,0:T(8,128)(2,1)S(1)} %get-tuple-element.160.own_ref.refs_4_), channel_id=1, source_target_pairs={{1,0},{0,1},{3,2},{2,3},{5,4},{4,5},{7,6},{6,7},{9,8},{8,9},{11,10... | collective-permute-start | bytes 393224 | tf_op jit(solution)/shard_map/ppermute | solution.py:943
  45.1 4.6 %collective-permute-start.17 = (bf16[8,32,2560]{2,1,0:T(8,128)(2,1)S(1)}, bf16[8,32,2560]{2,1,0:T(8,128)(2,1)S(1)}, u32[]{:S(2)}, u32[]{:S(2)}) collective-permute-start(bf16[8,32,2560]{2,1,0:T(8,128)(2,1)S(1)} %constant_dynamic-update-slice_fusion.12.near_ref), channel_id=1, source_target_pairs={{0,2},{2,0},{4,6},{6,4},{8,10},{10,8},{12,14},{14,12},{16,18},{18,... | collective-permute-start | bytes 3932168 | tf_op jit(solution)/shard_map/ppermute | solution.py:970
  49.1 1.7 %copy-start.1 = (f32[1024]{0:T(1024)S(1)}, f32[1024]{0:T(1024)}, u32[]{:S(2)}) copy-start(f32[1024]{0:T(1024)} %param.22) | copy-start | bytes 12292
  49.1 8.5 %collective-permute-start.16 = (bf16[256,256]{1,0:T(8,128)(2,1)S(1)}, bf16[256,256]{1,0:T(8,128)(2,1)S(1)}, u32[]{:S(2)}, u32[]{:S(2)}) collective-permute-start(bf16[256,256]{1,0:T(8,128)(2,1)S(1)} %get-tuple-element.167.own_ref.refs_5_), channel_id=1, source_target_pairs={{1,0},{0,1},{3,2},{2,3},{5,4},{4,5},{7,6},{6,7},{9,8},{8,9},{11,10... | collective-permute-start | bytes 393224 | tf_op jit(solution)/shard_map/ppermute | solution.py:943
  52.9 10.4 %collective-permute-start.18 = (bf16[256,512]{1,0:T(8,128)(2,1)S(1)}, bf16[256,512]{1,0:T(8,128)(2,1)S(1)}, u32[]{:S(2)}, u32[]{:S(2)}) collective-permute-start(bf16[256,512]{1,0:T(8,128)(2,1)S(1)} %get-tuple-element.174.part_ref), channel_id=1, source_target_pairs={{1,0},{0,1},{3,2},{2,3},{5,4},{4,5},{7,6},{6,7},{9,8},{8,9},{11,10... | collective-permute-start | bytes 786440 | tf_op jit(solution)/shard_map/ppermute | solution.py:943
  59.8 8.2 %collective-permute-start.19 = (bf16[256,512]{1,0:T(8,128)(2,1)S(1)}, bf16[256,512]{1,0:T(8,128)(2,1)S(1)}, u32[]{:S(2)}, u32[]{:S(2)}) collective-permute-start(bf16[256,512]{1,0:T(8,128)(2,1)S(1)} %get-tuple-element.177.part_ref), channel_id=1, source_target_pairs={{1,0},{0,1},{3,2},{2,3},{5,4},{4,5},{7,6},{6,7},{9,8},{8,9},{11,10... | collective-permute-start | bytes 786440 | tf_op jit(solution)/shard_map/ppermute | solution.py:943
  65.8 8.7 %collective-permute-start.20 = (bf16[256,512]{1,0:T(8,128)(2,1)S(1)}, bf16[256,512]{1,0:T(8,128)(2,1)S(1)}, u32[]{:S(2)}, u32[]{:S(2)}) collective-permute-start(bf16[256,512]{1,0:T(8,128)(2,1)S(1)} %get-tuple-element.199.part_ref), channel_id=1, source_target_pairs={{1,0},{0,1},{3,2},{2,3},{5,4},{4,5},{7,6},{6,7},{9,8},{8,9},{11,10... | collective-permute-start | bytes 786440 | tf_op jit(solution)/shard_map/ppermute | solution.py:943
  73.8 5.7 %collective-permute-start.21 = (bf16[512,1024]{1,0:T(8,128)(2,1)S(1)}, bf16[512,1024]{1,0:T(8,128)(2,1)S(1)}, u32[]{:S(2)}, u32[]{:S(2)}) collective-permute-start(bf16[512,1024]{1,0:T(8,128)(2,1)S(1)} %get-tuple-element.207), channel_id=1, source_target_pairs={{0,2},{2,0},{4,6},{6,4},{8,10},{10,8},{12,14},{14,12},{16,18},{18,... | collective-permute-start | bytes 3145736 | tf_op jit(solution)/shard_map/ppermute | solution.py:970
  73.9 10.4 %collective-permute-start.22 = (bf16[256,512]{1,0:T(8,128)(2,1)S(1)}, bf16[256,512]{1,0:T(8,128)(2,1)S(1)}, u32[]{:S(2)}, u32[]{:S(2)}) collective-permute-start(bf16[256,512]{1,0:T(8,128)(2,1)S(1)} %get-tuple-element.211.part_ref), channel_id=1, source_target_pairs={{1,0},{0,1},{3,2},{2,3},{5,4},{4,5},{7,6},{6,7},{9,8},{8,9},{11,10... | collective-permute-start | bytes 786440 | tf_op jit(solution)/shard_map/ppermute | solution.py:943
  79.7 10.3 %collective-permute-start.23 = (bf16[256,1024]{1,0:T(8,128)(2,1)S(1)}, bf16[256,1024]{1,0:T(8,128)(2,1)S(1)}, u32[]{:S(2)}, u32[]{:S(2)}) collective-permute-start(bf16[256,1024]{1,0:T(8,128)(2,1)S(1)} %get-tuple-element.221), channel_id=1, source_target_pairs={{0,4},{2,10},{4,0},{6,14},{8,12},{10,2},{12,8},{14,6},{16,20},{18,... | collective-permute-start | bytes 1572872 | tf_op jit(solution)/shard_map/ppermute | solution.py:970
  92.1 3.9 %collective-permute-start.24 = (bf16[1056,256]{1,0:T(8,128)(2,1)S(1)}, bf16[1056,256]{1,0:T(8,128)(2,1)S(1)}, u32[]{:S(2)}, u32[]{:S(2)}) collective-permute-start(bf16[1056,256]{1,0:T(8,128)(2,1)S(1)} %get-tuple-element.239), channel_id=1, source_target_pairs={{0,2},{2,0},{4,6},{6,4},{8,10},{10,8},{12,14},{14,12},{16,18},{18,... | collective-permute-start | bytes 1622024 | tf_op jit(solution)/shard_map/ppermute | solution.py:970
  94.3 12.0 %collective-permute-start.26 = (bf16[768,256]{1,0:T(8,128)(2,1)S(1)}, bf16[768,256]{1,0:T(8,128)(2,1)S(1)}, u32[]{:S(2)}, u32[]{:S(2)}) collective-permute-start(bf16[768,256]{1,0:T(8,128)(2,1)S(1)} %get-tuple-element.251), channel_id=1, source_target_pairs={{1,0},{0,1},{3,2},{2,3},{5,4},{4,5},{7,6},{6,7},{9,8},{8,9},{11,10... | collective-permute-start | bytes 1179656 | tf_op jit(solution)/shard_map/ppermute | solution.py:943
  96.1 7.6 %collective-permute-start.25 = (bf16[544,256]{1,0:T(8,128)(2,1)S(1)}, bf16[544,256]{1,0:T(8,128)(2,1)S(1)}, u32[]{:S(2)}, u32[]{:S(2)}) collective-permute-start(bf16[544,256]{1,0:T(8,128)(2,1)S(1)} %get-tuple-element.246), channel_id=1, source_target_pairs={{0,4},{2,10},{4,0},{6,14},{8,12},{10,2},{12,8},{14,6},{16,20},{18,... | collective-permute-start | bytes 835592 | tf_op jit(solution)/shard_map/ppermute | solution.py:970
  96.6 11.0 %collective-permute-start.27 = (bf16[128,1024]{1,0:T(8,128)(2,1)S(1)}, bf16[128,1024]{1,0:T(8,128)(2,1)S(1)}, u32[]{:S(2)}, u32[]{:S(2)}) collective-permute-start(bf16[128,1024]{1,0:T(8,128)(2,1)S(1)} %get-tuple-element.254), channel_id=1, source_target_pairs={{0,8},{2,18},{4,12},{6,22},{8,0},{10,26},{12,4},{14,30},{16,24},{1... | collective-permute-start | bytes 786440 | tf_op jit(solution)/shard_map/ppermute | solution.py:970
  98.0 16.7 %collective-permute-start.31 = (bf16[512,256]{1,0:T(8,128)(2,1)S(1)}, bf16[512,256]{1,0:T(8,128)(2,1)S(1)}, u32[]{:S(2)}, u32[]{:S(2)}) collective-permute-start(bf16[512,256]{1,0:T(8,128)(2,1)S(1)} %get-tuple-element.264), channel_id=1, source_target_pairs={{1,0},{0,1},{3,2},{2,3},{5,4},{4,5},{7,6},{6,7},{9,8},{8,9},{11,10... | collective-permute-start | bytes 786440 | tf_op jit(solution)/shard_map/ppermute | solution.py:943
  103.7 7.9 %collective-permute-start.28 = (bf16[288,256]{1,0:T(8,128)(2,1)S(1)}, bf16[288,256]{1,0:T(8,128)(2,1)S(1)}, u32[]{:S(2)}, u32[]{:S(2)}) collective-permute-start(bf16[288,256]{1,0:T(8,128)(2,1)S(1)} %get-tuple-element.257), channel_id=1, source_target_pairs={{0,8},{2,18},{4,12},{6,22},{8,0},{10,26},{12,4},{14,30},{16,24},{1... | collective-permute-start | bytes 442376 | tf_op jit(solution)/shard_map/ppermute | solution.py:970
  106.4 8.3 %collective-permute-start.29 = (bf16[384,256]{1,0:T(8,128)(2,1)S(1)}, bf16[384,256]{1,0:T(8,128)(2,1)S(1)}, u32[]{:S(2)}, u32[]{:S(2)}) collective-permute-start(bf16[384,256]{1,0:T(8,128)(2,1)S(1)} %get-tuple-element.252), channel_id=1, source_target_pairs={{0,2},{2,0},{4,6},{6,4},{8,10},{10,8},{12,14},{14,12},{16,18},{18,... | collective-permute-start | bytes 589832 | tf_op jit(solution)/shard_map/ppermute | solution.py:977
  106.9 7.8 %collective-permute-start.30 = (bf16[384,256]{1,0:T(8,128)(2,1)S(1)}, bf16[384,256]{1,0:T(8,128)(2,1)S(1)}, u32[]{:S(2)}, u32[]{:S(2)}) collective-permute-start(bf16[384,256]{1,0:T(8,128)(2,1)S(1)} %get-tuple-element.262), channel_id=1, source_target_pairs={{2,4},{4,2},{6,8},{8,6},{10,12},{12,10},{14,16},{16,14},{18,20},{2... | collective-permute-start | bytes 589832 | tf_op jit(solution)/shard_map/ppermute | solution.py:978
  107.7 11.2 %collective-permute-start.32 = (bf16[64,1024]{1,0:T(8,128)(2,1)S(1)}, bf16[64,1024]{1,0:T(8,128)(2,1)S(1)}, u32[]{:S(2)}, u32[]{:S(2)}) collective-permute-start(bf16[64,1024]{1,0:T(8,128)(2,1)S(1)} %get-tuple-element.266), channel_id=1, source_target_pairs={{0,16},{2,6},{4,20},{6,2},{8,24},{10,14},{12,28},{14,10},{16,0},{1... | collective-permute-start | bytes 393224 | tf_op jit(solution)/shard_map/ppermute | solution.py:970
  111.6 8.1 %collective-permute-start.33 = (bf16[160,256]{1,0:T(8,128)(2,1)S(1)}, bf16[160,256]{1,0:T(8,128)(2,1)S(1)}, u32[]{:S(2)}, u32[]{:S(2)}) collective-permute-start(bf16[160,256]{1,0:T(8,128)(2,1)S(1)} %get-tuple-element.269), channel_id=1, source_target_pairs={{0,16},{2,6},{4,20},{6,2},{8,24},{10,14},{12,28},{14,10},{16,0},{1... | collective-permute-start | bytes 245768 | tf_op jit(solution)/shard_map/ppermute | solution.py:970

commit v7 on v6

--- a/solution.py
+++ b/solution.py
@@ -254,30 +254,52 @@
     )(slots, even, *operands)
 
 
+def by_edge(block, last, body):
+    edge = (block == 0) | (block == last)
+
+    @pl.when(edge)
+    def _():
+        body(BLOCK, WINDOW - 2 * BLOCK)
+
+    @pl.when(jnp.logical_not(edge))
+    def _():
+        body(0, WINDOW)
+
+
 def forward_kernel(
     offset, query_ref, key_ref, value_ref, prev_ref, score_ref, prob_ref, attended_ref
 ):
     heads = prev_ref.shape[0]
     size = min(2, heads)
     span = size * HEAD_DIM
-    window = pl.ds(pl.multiple_of((pl.program_id(0) + offset) * BLOCK, BLOCK), WINDOW)
-    for group in range(heads // size):
-        lanes = slice(group * span, (group + 1) * span)
-        query = head_split(query_ref[:, lanes], size)
-        dense = dot_nt(query, key_ref[window, lanes])
-        weights = []
-        for h in range(size):
-            head = group * size + h
-            score = dense[h * BLOCK : (h + 1) * BLOCK] + prev_ref[head].astype(F32)
-            score_ref[head] = score.astype(BF16)
-            peak = jnp.max(score, -1, keepdims=True)
-            grown = jnp.exp(score - peak)
-            total = jnp.sum(grown, -1, keepdims=True)
-            prob = (grown * (1.0 / total)).astype(BF16)
-            prob_ref[head] = prob
-            weights.append(prob)
-        mixed = dot_nn(jnp.concatenate(weights, 0), value_ref[window, lanes])
-        attended_ref[:, lanes] = head_join(mixed, size).astype(BF16)
+    block = pl.program_id(0) + offset
+
+    def body(first, width):
+        window = pl.ds(pl.multiple_of(block * BLOCK + first, BLOCK), width)
+        inside = slice(first, first + width)
+        for group in range(heads // size):
+            lanes = slice(group * span, (group + 1) * span)
+            query = head_split(query_ref[:, lanes], size)
+            dense = dot_nt(query, key_ref[window, lanes])
+            weights = []
+            for h in range(size):
+                head = group * size + h
+                score = dense[h * BLOCK : (h + 1) * BLOCK] + prev_ref[head, :, inside].astype(F32)
+                score_ref[head, :, inside] = score.astype(BF16)
+                if first:
+                    empty = jnp.full((BLOCK, first), MASKED_SCORE, BF16)
+                    score_ref[head, :, :first] = empty
+                    score_ref[head, :, first + width :] = empty
+                peak = jnp.max(score, -1, keepdims=True)
+                grown = jnp.exp(score - peak)
+                total = jnp.sum(grown, -1, keepdims=True)
+                prob = (grown * (1.0 / total)).astype(BF16)
+                prob_ref[head, :, inside] = prob
+                weights.append(prob)
+            mixed = dot_nn(jnp.concatenate(weights, 0), value_ref[window, lanes])
+            attended_ref[:, lanes] = head_join(mixed, size).astype(BF16)
+
+    by_edge(block, key_ref.shape[0] // BLOCK - WINDOW // BLOCK, body)
 
 
 def attend_forward(query, key, value, prev, chunk):
@@ -327,29 +349,40 @@
             key_sum[...] = jnp.zeros_like(key_sum)
             value_sum[...] = jnp.zeros_like(value_sum)
 
-    window = pl.ds(pl.multiple_of((step + offset) * BLOCK, BLOCK), WINDOW)
-    for group in range(heads // size):
-        lanes = slice(group * span, (group + 1) * span)
-        query = head_split(query_ref[:, lanes], size)
-        grad = head_split(grad_ref[:, lanes], size)
-        key = key_ref[window, lanes]
-        prob_grad = dot_nt(grad, value_ref[window, lanes])
-        probs, scores = [], []
-        for h in range(size):
-            head = group * size + h
-            low = prob_ref[head]
-            prob = low.astype(F32)
-            slope = prob_grad[h * BLOCK : (h + 1) * BLOCK]
-            inner = jnp.sum(prob * slope, -1, keepdims=True)
-            score = (prob * (slope - inner) + logit_ref[head].astype(F32)).astype(BF16)
-            prev_ref[head] = score
-            probs.append(low)
-            scores.append(score)
-        stacked = jnp.concatenate(scores, 0)
-        mixed = head_join(dot_nn(stacked, key), size) * HEAD_DIM ** (-0.5)
-        query_grad_ref[:, lanes] = mixed.astype(BF16)
-        key_sum[lanes, window] += dot_tn(query, stacked)
-        value_sum[lanes, window] += dot_tn(grad, jnp.concatenate(probs, 0))
+    block = step + offset
+
+    def body(first, width):
+        window = pl.ds(pl.multiple_of(block * BLOCK + first, BLOCK), width)
+        inside = slice(first, first + width)
+        for group in range(heads // size):
+            lanes = slice(group * span, (group + 1) * span)
+            query = head_split(query_ref[:, lanes], size)
+            grad = head_split(grad_ref[:, lanes], size)
+            key = key_ref[window, lanes]
+            prob_grad = dot_nt(grad, value_ref[window, lanes])
+            probs, scores = [], []
+            for h in range(size):
+                head = group * size + h
+                low = prob_ref[head, :, inside]
+                prob = low.astype(F32)
+                slope = prob_grad[h * BLOCK : (h + 1) * BLOCK]
+                inner = jnp.sum(prob * slope, -1, keepdims=True)
+                score = prob * (slope - inner) + logit_ref[head, :, inside].astype(F32)
+                score = score.astype(BF16)
+                prev_ref[head, :, inside] = score
+                if first:
+                    empty = jnp.zeros((BLOCK, first), BF16)
+                    prev_ref[head, :, :first] = empty
+                    prev_ref[head, :, first + width :] = empty
+                probs.append(low)
+                scores.append(score)
+            stacked = jnp.concatenate(scores, 0)
+            mixed = head_join(dot_nn(stacked, key), size) * HEAD_DIM ** (-0.5)
+            query_grad_ref[:, lanes] = mixed.astype(BF16)
+            key_sum[lanes, window] += dot_tn(query, stacked)
+            value_sum[lanes, window] += dot_tn(grad, jnp.concatenate(probs, 0))
+
+    by_edge(block, key_ref.shape[0] // BLOCK - WINDOW // BLOCK, body)
 
     if last:
 

time: 121 us -> 120 us (level)
  no operation moved by 1% of the time
where the time goes in v7:
time: 120 us
  Pallas kernels  63.5 us (53%)
  starting transfers between devices  39.7 us (33%)
  waiting for transfers between devices  12.1 us (10%)
  local copies, waits for them, and re-layouts  2.13 us (2%)
    ppermute x16, starting transfers between devices, with_partner(): lax.ppermute(x, 'row', [(i, i ^ orders[i % 2][step]) for i in range(count)])  21.1 us
    ppermute x14, starting transfers between devices, from_next(): lax.ppermute(x, axis, [((i + step) % count, i) for i in range(count)])  16.6 us
    pallas_call x4, Pallas kernels, to_dense(): pl.pallas_call(functools.partial(dense_kernel, fill, token_count, offset)...  12.4 us
    pallas_call x3, Pallas kernels, to_band(): pl.pallas_call(functools.partial(band_kernel, masked, len(chunks)), grid=...  11 us
    pallas_call x2, Pallas kernels, attend_backward(): pl.pallas_call(functools.partial(backward_kernel, offset, last), grid=(co...  8.72 us
    pallas_call x2, Pallas kernels, attend_forward(): pl.pallas_call(functools.partial(forward_kernel, offset), grid=(count //...  7.42 us
    ppermute x14, waiting for transfers between devices, from_next(): lax.ppermute(x, axis, [((i + step) % count, i) for i in range(count)])  6.09 us
    ppermute x16, waiting for transfers between devices, with_partner(): lax.ppermute(x, 'row', [(i, i ^ orders[i % 2][step]) for i in range(count)])  6.01 us
  transfers between devices with their start and end apart: 34, of which 8 were waited for; matrix products, arithmetic and copies ran while one was open for 3% of the time, Pallas kernels for 51%

profile of v7, /device:TPU:0, one launch (start us, length us, event | category | flops | bytes accessed | tf_op | source)
XLA Modules:
  0.0 119.6 jit_solution(11630518072329267112)
XLA Ops:
  0.7 3.0 %collective-permute-start = (bf16[32,256]{1,0:T(8,128)(2,1)}, bf16[32,256]{1,0:T(8,128)(2,1)S(1)}, u32[]{:S(2)}, u32[]{:S(2)}) collective-permute-start(bf16[32,256]{1,0:T(8,128)(2,1)} %bitcast.17), channel_id=1, source_target_pairs={{1,0},{0,1},{3,2},{2,3},{5,4},{4,5},{7,6},{6,7},{9,8},{8,9},{11,10... | collective-permute-start | bytes 49160 | tf_op jit(solution)/shard_map/ppermute | solution.py:976
  3.7 2.6 %collective-permute-start.1 = (bf16[1,3,32,256]{3,2,1,0:T(8,128)(2,1)}, bf16[1,3,32,256]{3,2,1,0:T(8,128)(2,1)S(1)}, u32[]{:S(2)}, u32[]{:S(2)}) collective-permute-start(bf16[1,3,32,256]{3,2,1,0:T(8,128)(2,1)} %bitcast.15), channel_id=1, source_target_pairs={{0,16},{2,6},{4,20},{6,2},{8,24},{10,14},{12,28},{14,10},{16,0},{1... | collective-permute-start | bytes 147464 | tf_op jit(solution)/shard_map/ppermute | solution.py:1003
  6.2 0.5 collective-permute-start.3
  6.8 0.9 maximum_bitcast_fusion
  7.7 1.9 %collective-permute-start.2 = (bf16[1,32,2560]{2,1,0:T(8,128)(2,1)S(1)}, bf16[1,32,2560]{2,1,0:T(8,128)(2,1)S(1)}, u32[]{:S(2)}, u32[]{:S(2)}) collective-permute-start(bf16[1,32,2560]{2,1,0:T(8,128)(2,1)S(1)} %maximum_bitcast_fusion), channel_id=1, source_target_pairs={{0,16},{2,6},{4,20},{6,2},{8,24},{10,14},{12,28},{14,10},{16,0},{1... | collective-permute-start | bytes 491528 | tf_op jit(solution)/shard_map/ppermute | solution.py:1003
  9.7 1.0 constant_dynamic-slice_fusion
  10.8 0.7 collective-permute-start.6
  11.5 0.8 constant_dynamic-update-slice_fusion.1
  12.3 4.4 %collective-permute-start.4 = (bf16[2,3,32,256]{3,2,1,0:T(8,128)(2,1)S(1)}, bf16[2,3,32,256]{3,2,1,0:T(8,128)(2,1)S(1)}, u32[]{:S(2)}, u32[]{:S(2)}) collective-permute-start(bf16[2,3,32,256]{3,2,1,0:T(8,128)(2,1)S(1)} %constant_dynamic-update-slice_fusion), channel_id=1, source_target_pairs={{0,8},{2,18},{4,12},{6,22},{8,0},{10,26},{12,4},{14,30},{16,24},{1... | collective-permute-start | bytes 294920 | tf_op jit(solution)/shard_map/ppermute | solution.py:1003
  16.8 1.7 %collective-permute-start.7 = (bf16[384,256]{1,0:T(8,128)(2,1)S(1)}, bf16[384,256]{1,0:T(8,128)(2,1)S(1)}, u32[]{:S(2)}, u32[]{:S(2)}) collective-permute-start(bf16[384,256]{1,0:T(8,128)(2,1)S(1)} %collective-permute-done.5.refs_2_), channel_id=1, source_target_pairs={{1,0},{0,1},{3,2},{2,3},{5,4},{4,5},{7,6},{6,7},{9,8},{8,9},{11,10... | collective-permute-start | bytes 589832 | tf_op jit(solution)/shard_map/ppermute | solution.py:976
  18.5 0.4 collective-permute-start.8
  18.9 2.4 %collective-permute-done.4 = bf16[2,3,32,256]{3,2,1,0:T(8,128)(2,1)S(1)} collective-permute-done((bf16[2,3,32,256]{3,2,1,0:T(8,128)(2,1)S(1)}, bf16[2,3,32,256]{3,2,1,0:T(8,128)(2,1)S(1)}, u32[]{:S(2)}, u32[]{:S(2)}) %collective-permute-start.4) | collective-permute-done | bytes 98336 | tf_op jit(solution)/shard_map/ppermute | solution.py:1003
  21.3 1.5 %collective-permute-start.9 = (bf16[4,3,32,256]{3,2,1,0:T(8,128)(2,1)S(1)}, bf16[4,3,32,256]{3,2,1,0:T(8,128)(2,1)S(1)}, u32[]{:S(2)}, u32[]{:S(2)}) collective-permute-start(bf16[4,3,32,256]{3,2,1,0:T(8,128)(2,1)S(1)} %constant_dynamic-update-slice_fusion.4), channel_id=1, source_target_pairs={{0,4},{2,10},{4,0},{6,14},{8,12},{10,2},{12,8},{14,6},{16,20},{18,... | collective-permute-start | bytes 589832 | tf_op jit(solution)/shard_map/ppermute | solution.py:1003
  22.9 3.1 %to_dense.4.prev_ref = bf16[4,256,1152]{2,1,0:T(8,128)(2,1)S(1)} custom-call(s32[34]{0:T(128)S(1)} %pad_add_fusion.lengths_ref, bf16[4,512,1024]{2,1,0:T(8,128)(2,1)} %band_ref.1), custom_call_target="tpu_custom_call" | custom-call | flops 8000000000 | tf_op jit(solution)/shard_map/to_dense/pallas_call | solution.py:102
  26.1 2.7 %collective-permute-done.8.refs_5_ = bf16[384,256]{1,0:T(8,128)(2,1)S(1)} collective-permute-done((bf16[384,256]{1,0:T(8,128)(2,1)S(1)}, bf16[384,256]{1,0:T(8,128)(2,1)S(1)}, u32[]{:S(2)}, u32[]{:S(2)}) %collective-permute-start.8) | collective-permute-done | bytes 196640 | tf_op jit(solution)/shard_map/ppermute | solution.py:976
  28.7 1.6 %collective-permute-start.13 = (bf16[512,256]{1,0:T(8,128)(2,1)S(1)}, bf16[512,256]{1,0:T(8,128)(2,1)S(1)}, u32[]{:S(2)}, u32[]{:S(2)}) collective-permute-start(bf16[512,256]{1,0:T(8,128)(2,1)S(1)} %copy-done.3), channel_id=1, source_target_pairs={{1,0},{0,1},{3,2},{2,3},{5,4},{4,5},{7,6},{6,7},{9,8},{8,9},{11,10... | collective-permute-start | bytes 786440 | tf_op jit(solution)/shard_map/ppermute | solution.py:976
  30.4 0.2 collective-permute-start.10
  30.6 1.4 %collective-permute-start.15 = (bf16[4,32,2560]{2,1,0:T(8,128)(2,1)S(1)}, bf16[4,32,2560]{2,1,0:T(8,128)(2,1)S(1)}, u32[]{:S(2)}, u32[]{:S(2)}) collective-permute-start(bf16[4,32,2560]{2,1,0:T(8,128)(2,1)S(1)} %constant_dynamic-update-slice_fusion.8), channel_id=1, source_target_pairs={{0,4},{2,10},{4,0},{6,14},{8,12},{10,2},{12,8},{14,6},{16,20},{18,... | collective-permute-start | bytes 1966088 | tf_op jit(solution)/shard_map/ppermute | solution.py:1003
  32.0 0.2 collective-permute-done.10.far_ref
  32.2 1.9 %project.1 = (bf16[512,512]{1,0:T(8,128)(2,1)S(1)}, bf16[512,256]{1,0:T(8,128)(2,1)S(1)}, bf16[1536,256]{1,0:T(8,128)(2,1)S(1)}, bf16[1536,256]{1,0:T(8,128)(2,1...) custom-call(s32[16]{0:T(128)S(1)} %fusion.7.slot_ref, ...), custom_call_target="tpu_custom_call" | custom-call | flops 2000000000 | tf_op jit(solution)/shard_map/project/pallas_call | solution.py:245
  34.1 1.6 %collective-permute-start.12 = (f32[6,256]{1,0:T(8,128)S(1)}, f32[6,256]{1,0:T(8,128)S(1)}, u32[]{:S(2)}, u32[]{:S(2)}) collective-permute-start(f32[6,256]{1,0:T(8,128)S(1)} %pad_maximum_fusion.1), channel_id=1, source_target_pairs={{1,0},{0,1},{3,2},{2,3},{5,4},{4,5},{7,6},{6,7},{9,8},{8,9},{11,10... | collective-permute-start | bytes 18440 | tf_op jit(solution)/shard_map/ppermute | solution.py:976
  35.8 3.7 %attend_forward.2 = (bf16[4,256,1152]{2,1,0:T(8,128)(2,1)S(1)}, bf16[4,256,1152]{2,1,0:T(8,128)(2,1)S(1)}, bf16[256,256]{1,0:T(8,128)(2,1)S(1)}) custom-call(bf16[512,256]{1,0:T(8,128)(2,1)S(1)} %get-tuple-element.166.query_ref, bf16[1536,256]{1,0:T(8,128)(2,1)S(1)} %get-tuple-element.157.key_ref, bf16[1536,256]{1,0:T(8,128)(2,1)S(1)} %get-tuple-element.158.value_ref, ...), custom_call_target="tpu_custom_call" | custom-call | flops 3800000000 | tf_op jit(solution)/shard_map/attend_forward/pallas_call | solution.py:309
  39.5 0.5 collective-permute-start.14
  40.1 3.1 %to_dense.5.prev_ref = bf16[4,256,1152]{2,1,0:T(8,128)(2,1)S(1)} custom-call(s32[34]{0:T(128)S(1)} %pad_add_fusion.lengths_ref, bf16[4,512,1024]{2,1,0:T(8,128)(2,1)} %band_ref.1), custom_call_target="tpu_custom_call" | custom-call | flops 1000000000 | tf_op jit(solution)/shard_map/to_dense/pallas_call | solution.py:102
  43.2 1.6 %collective-permute-done.14.other_ref = bf16[256,256]{1,0:T(8,128)(2,1)S(1)} collective-permute-done((bf16[256,256]{1,0:T(8,128)(2,1)S(1)}, bf16[256,256]{1,0:T(8,128)(2,1)S(1)}, u32[]{:S(2)}, u32[]{:S(2)}) %collective-permute-start.14) | collective-permute-done | bytes 131104 | tf_op jit(solution)/shard_map/ppermute | solution.py:976
  45.0 3.7 %attend_forward.3 = (bf16[4,256,1152]{2,1,0:T(8,128)(2,1)S(1)}, bf16[4,256,1152]{2,1,0:T(8,128)(2,1)S(1)}, bf16[256,256]{1,0:T(8,128)(2,1)S(1)}) custom-call(bf16[512,256]{1,0:T(8,128)(2,1)S(1)} %get-tuple-element.166.query_ref, bf16[1536,256]{1,0:T(8,128)(2,1)S(1)} %get-tuple-element.157.key_ref, bf16[1536,256]{1,0:T(8,128)(2,1)S(1)} %get-tuple-element.158.value_ref, ...), custom_call_target="tpu_custom_call" | custom-call | flops 3800000000 | tf_op jit(solution)/shard_map/attend_forward/pallas_call | solution.py:309
  48.8 0.6 collective-permute-start.16
  49.3 1.1 in_order.1
  50.4 2.2 %feed_first.2 = (f32[256,512]{1,0:T(8,128)S(1)}, f32[256,1]{1,0:T(8,128)S(1)}, bf16[256,512]{1,0:T(8,128)(2,1)S(1)}, bf16[256,1024]{1,0:T(8,128)(2,1)S(1)}, bf16...) custom-call(bf16[256,256]{1,0:T(8,128)(2,1)S(1)} %get-tuple-element.160.own_ref.refs_4_, ...), custom_call_target="tpu_custom_call" | custom-call | flops 1000000000 | tf_op jit(solution)/shard_map/feed_first/pallas_call | solution.py:508
  52.6 1.6 %collective-permute-start.18 = (bf16[256,512]{1,0:T(8,128)(2,1)S(1)}, bf16[256,512]{1,0:T(8,128)(2,1)S(1)}, u32[]{:S(2)}, u32[]{:S(2)}) collective-permute-start(bf16[256,512]{1,0:T(8,128)(2,1)S(1)} %get-tuple-element.174.part_ref), channel_id=1, source_target_pairs={{1,0},{0,1},{3,2},{2,3},{5,4},{4,5},{7,6},{6,7},{9,8},{8,9},{11,10... | collective-permute-start | bytes 786440 | tf_op jit(solution)/shard_map/ppermute | solution.py:976
  54.2 3.1 %to_dense.6.logit_ref = bf16[4,256,1152]{2,1,0:T(8,128)(2,1)S(1)} custom-call(s32[34]{0:T(128)S(1)} %pad_add_fusion.lengths_ref, bf16[4,512,1024]{2,1,0:T(8,128)(2,1)} %band_ref.3), custom_call_target="tpu_custom_call" | custom-call | flops 1000000000 | tf_op jit(solution)/shard_map/to_dense/pallas_call | solution.py:102
  57.3 2.2 %feed_first.3 = (f32[256,512]{1,0:T(8,128)S(1)}, f32[256,1]{1,0:T(8,128)S(1)}, bf16[256,512]{1,0:T(8,128)(2,1)S(1)}, bf16[256,1024]{1,0:T(8,128)(2,1)S(1)}, bf16...) custom-call(bf16[256,256]{1,0:T(8,128)(2,1)S(1)} %get-tuple-element.167.own_ref.refs_5_, ...), custom_call_target="tpu_custom_call" | custom-call | flops 1000000000 | tf_op jit(solution)/shard_map/feed_first/pallas_call | solution.py:508
  59.5 0.6 collective-permute-start.19
  60.1 3.0 %to_band.3.refs_1_ = bf16[4,512,1024]{2,1,0:T(8,128)(2,1)} custom-call(bf16[4,256,1152]{2,1,0:T(8,128)(2,1)S(1)} %get-tuple-element.178.refs_0_), custom_call_target="tpu_custom_call" | custom-call | flops 5000000000 | tf_op jit(solution)/shard_map/to_band/pallas_call | solution.py:151
  63.0 2.4 %feed_second.2 = (f32[16,256]{1,0:T(8,128)S(1)}, bf16[512,256]{1,0:T(8,128)(2,1)}, f32[256,512]{1,0:T(8,128)S(1)}, bf16[256,512]{1,0:T(8,128)(2,1)S(1)}, bf16[25...) custom-call(f32[16,256]{1,0:T(8,128)S(1)} %broadcast_in_dim.18.start_ref, ...), custom_call_target="tpu_custom_call" | custom-call | flops 700000000 | tf_op jit(solution)/shard_map/feed_second/pallas_call | solution.py:587
  65.5 1.5 %collective-permute-start.20 = (bf16[256,512]{1,0:T(8,128)(2,1)S(1)}, bf16[256,512]{1,0:T(8,128)(2,1)S(1)}, u32[]{:S(2)}, u32[]{:S(2)}) collective-permute-start(bf16[256,512]{1,0:T(8,128)(2,1)S(1)} %get-tuple-element.199.part_ref), channel_id=1, source_target_pairs={{1,0},{0,1},{3,2},{2,3},{5,4},{4,5},{7,6},{6,7},{9,8},{8,9},{11,10... | collective-permute-start | bytes 786440 | tf_op jit(solution)/shard_map/ppermute | solution.py:976
  67.0 0.7 collective-permute-done.19.recv_ref
  67.7 2.4 %feed_second.3 = (f32[16,256]{1,0:T(8,128)S(1)}, bf16[512,256]{1,0:T(8,128)(2,1)}, f32[256,512]{1,0:T(8,128)S(1)}, bf16[256,512]{1,0:T(8,128)(2,1)S(1)}, bf16[25...) custom-call(f32[16,256]{1,0:T(8,128)S(1)} %get-tuple-element.182.start_ref, ...), custom_call_target="tpu_custom_call", output_to_operand_aliasing={{1}: (9, {})} | custom-call | flops 700000000 | tf_op jit(solution)/shard_map/feed_second/pallas_call | solution.py:587
  70.1 3.4 %feed_grads.1 = (f32[512,1024]{1,0:T(8,128)S(1)}, bf16[512,1024]{1,0:T(8,128)(2,1)S(1)}) custom-call(s32[16]{0:T(128)S(1)} %and_select_fusion.block_ref, bf16[256,512]{1,0:T(8,128)(2,1)S(1)} %get-tuple-element.189.refs_0_, bf16[256,512]{1,0:T(8,128)(2,1)S(1)} %get-tuple-element.190.refs_1_, bf16[256,512]{1,0:T(8,128)(2,1)S(1)} %get-tuple-element.191.refs_2_, ...), custom_call_target="tpu_custom_call" | custom-call | flops 1000000000 | tf_op jit(solution)/shard_map/feed_grads/pallas_call | solution.py:708
  73.6 0.6 collective-permute-start.22
  74.2 0.8 feed_third.2
  74.9 4.0 %attend_backward.2 = (bf16[4,256,1152]{2,1,0:T(8,128)(2,1)S(1)}, bf16[256,256]{1,0:T(8,128)(2,1)S(1)}, f32[256,1536]{1,0:T(8,128)S(1)}, f32[256,1536]{1,0:T(8,128)S(1)}) custom-call(bf16[256,256]{1,0:T(8,128)(2,1)S(1)} %get-tuple-element.203.grad_ref, bf16[512,256]{1,0:T(8,128)(2,1)S(1)} %get-tuple-element.166.query_ref, ...), custom_call_target="tpu_custom_call" | custom-call | flops 20000000000 | tf_op jit(solution)/shard_map/attend_backward/pallas_call | solution.py:404
  79.0 0.2 fold.6
  79.2 1.5 %collective-permute-start.23 = (bf16[256,1024]{1,0:T(8,128)(2,1)S(1)}, bf16[256,1024]{1,0:T(8,128)(2,1)S(1)}, u32[]{:S(2)}, u32[]{:S(2)}) collective-permute-start(bf16[256,1024]{1,0:T(8,128)(2,1)S(1)} %get-tuple-element.221), channel_id=1, source_target_pairs={{0,4},{2,10},{4,0},{6,14},{8,12},{10,2},{12,8},{14,6},{16,20},{18,... | collective-permute-start | bytes 1572872 | tf_op jit(solution)/shard_map/ppermute | solution.py:1003
  80.7 3.1 %to_dense.7.logit_ref = bf16[4,256,1152]{2,1,0:T(8,128)(2,1)S(1)} custom-call(s32[34]{0:T(128)S(1)} %pad_add_fusion.lengths_ref, bf16[4,512,1024]{2,1,0:T(8,128)(2,1)} %band_ref.3), custom_call_target="tpu_custom_call" | custom-call | flops 1000000000 | tf_op jit(solution)/shard_map/to_dense/pallas_call | solution.py:102
  83.8 0.7 feed_third.3
  84.6 4.7 %attend_backward.3 = (bf16[4,256,1152]{2,1,0:T(8,128)(2,1)S(1)}, bf16[256,256]{1,0:T(8,128)(2,1)S(1)}, bf16[1536,256]{1,0:T(8,128)(2,1)S(1)}, bf16[1536,256]{1,0:T(8,128)(2,1)S(1)}) custom-call(bf16[256,256]{1,0:T(8,128)(2,1)S(1)} %get-tuple-element.215.grad_ref, bf16[512,256]{1,0:T(8,128)(2,1)S(1)} %get-tuple-element.166.query_ref, ...), custom_call_target="tpu_custom_call" | custom-call | flops 3000000000 | tf_op jit(solution)/shard_map/attend_backward/pallas_call | solution.py:404
  89.4 1.9 %project_grads.1 = (f32[1024,256]{1,0:T(8,128)S(1)}, bf16[1056,256]{1,0:T(8,128)(2,1)S(1)}, f32[16,256]{1,0:T(8,128)S(1)}) custom-call(s32[16]{0:T(128)S(1)} %and_select_fusion.block_ref, f32[16,256]{1,0:T(8,128)S(1)} %get-tuple-element.223.start_ref, bf16[256,256]{1,0:T(8,128)(2,1)S(1)} %get-tuple-element.205.refs_0_, ...), custom_call_target="tpu_custom_call" | custom-call | flops 600000000 | tf_op jit(solution)/shard_map/project_grads/pallas_call | solution.py:765
  91.4 2.1 %token_grads.1 = (f32[512,256]{1,0:T(8,128)S(1)}, f32[768,256]{1,0:T(8,128)S(1)}, bf16[512,256]{1,0:T(8,128)(2,1)S(1)}, bf16[768,256]{1,0:T(8,128)(2,1)S(1)}) custom-call(s32[1]{0:T(128)} %bitcast.even_ref, bf16[256,256]{1,0:T(8,128)(2,1)S(1)} %get-tuple-element.205.refs_0_, bf16[256,256]{1,0:T(8,128)(2,1)S(1)} %get-tuple-element.219.refs_1_, ...), custom_call_target="tpu_custom_call" | custom-call | flops 5000000000 | tf_op jit(solution)/shard_map/token_grads/pallas_call | solution.py:909
  93.5 1.6 %collective-permute-start.26 = (bf16[768,256]{1,0:T(8,128)(2,1)S(1)}, bf16[768,256]{1,0:T(8,128)(2,1)S(1)}, u32[]{:S(2)}, u32[]{:S(2)}) collective-permute-start(bf16[768,256]{1,0:T(8,128)(2,1)S(1)} %get-tuple-element.251), channel_id=1, source_target_pairs={{1,0},{0,1},{3,2},{2,3},{5,4},{4,5},{7,6},{6,7},{9,8},{8,9},{11,10... | collective-permute-start | bytes 1179656 | tf_op jit(solution)/shard_map/ppermute | solution.py:976
  95.3 0.7 collective-permute-start.25
  95.9 1.3 %collective-permute-start.27 = (bf16[128,1024]{1,0:T(8,128)(2,1)S(1)}, bf16[128,1024]{1,0:T(8,128)(2,1)S(1)}, u32[]{:S(2)}, u32[]{:S(2)}) collective-permute-start(bf16[128,1024]{1,0:T(8,128)(2,1)S(1)} %get-tuple-element.254), channel_id=1, source_target_pairs={{0,8},{2,18},{4,12},{6,22},{8,0},{10,26},{12,4},{14,30},{16,24},{1... | collective-permute-start | bytes 786440 | tf_op jit(solution)/shard_map/ppermute | solution.py:1003
  97.2 0.7 collective-permute-start.31
  97.9 5.0 %to_band.4 = bf16[4,512,1024]{2,1,0:T(8,128)(2,1)} custom-call(bf16[4,256,1152]{2,1,0:T(8,128)(2,1)S(1)} %get-tuple-element.243.refs_0_, bf16[4,256,1152]{2,1,0:T(8,128)(2,1)S(1)} %get-tuple-element.244.refs_1_), custom_call_target="tpu_custom_call" | custom-call | flops 300000000 | tf_op jit(solution)/shard_map/to_band/pallas_call | solution.py:151
  103.0 1.4 %collective-permute-start.28 = (bf16[288,256]{1,0:T(8,128)(2,1)S(1)}, bf16[288,256]{1,0:T(8,128)(2,1)S(1)}, u32[]{:S(2)}, u32[]{:S(2)}) collective-permute-start(bf16[288,256]{1,0:T(8,128)(2,1)S(1)} %get-tuple-element.257), channel_id=1, source_target_pairs={{0,8},{2,18},{4,12},{6,22},{8,0},{10,26},{12,4},{14,30},{16,24},{1... | collective-permute-start | bytes 442376 | tf_op jit(solution)/shard_map/ppermute | solution.py:1003
  104.4 1.1 collective-permute-done.26.refs_0_
  105.6 0.6 collective-permute-start.29
  106.2 0.7 collective-permute-start.30
  106.9 4.0 %collective-permute-start.32 = (bf16[64,1024]{1,0:T(8,128)(2,1)S(1)}, bf16[64,1024]{1,0:T(8,128)(2,1)S(1)}, u32[]{:S(2)}, u32[]{:S(2)}) collective-permute-start(bf16[64,1024]{1,0:T(8,128)(2,1)S(1)} %get-tuple-element.266), channel_id=1, source_target_pairs={{0,16},{2,6},{4,20},{6,2},{8,24},{10,14},{12,28},{14,10},{16,0},{1... | collective-permute-start | bytes 393224 | tf_op jit(solution)/shard_map/ppermute | solution.py:1003
  111.0 3.0 %to_band.5 = bf16[4,512,1024]{2,1,0:T(8,128)(2,1)} custom-call(bf16[4,256,1152]{2,1,0:T(8,128)(2,1)S(1)} %get-tuple-element.260.refs_0_, bf16[4,512,1024]{2,1,0:T(8,128)(2,1)} %to_band.3.refs_1_), custom_call_target="tpu_custom_call", output_to_operand_aliasing={{}: (1, {})} | custom-call | flops 300000000 | tf_op jit(solution)/shard_map/to_band/pallas_call | solution.py:151
  114.0 0.9 token_sum.1
  114.8 3.2 %collective-permute-done.32.arrived_ref = bf16[64,1024]{1,0:T(8,128)(2,1)S(1)} collective-permute-done((bf16[64,1024]{1,0:T(8,128)(2,1)S(1)}, bf16[64,1024]{1,0:T(8,128)(2,1)S(1)}, u32[]{:S(2)}, u32[]{:S(2)}) %collective-permute-start.32) | collective-permute-done | bytes 131104 | tf_op jit(solution)/shard_map/ppermute | solution.py:1003
  118.1 0.7 finish.2
  118.9 0.7 finish.3
  (74 shorter events, 1.5 us)
Async XLA Ops:
  0.6 22.2 %copy-start.7 = (s32[1,33]{1,0:T(1,128)S(1)}, s32[1,33]{1,0:T(1,128)}, u32[]{:S(2)}) copy-start(s32[1,33]{1,0:T(1,128)} %param.16) | copy-start | bytes 400
  0.7 6.2 %collective-permute-start = (bf16[32,256]{1,0:T(8,128)(2,1)}, bf16[32,256]{1,0:T(8,128)(2,1)S(1)}, u32[]{:S(2)}, u32[]{:S(2)}) collective-permute-start(bf16[32,256]{1,0:T(8,128)(2,1)} %bitcast.17), channel_id=1, source_target_pairs={{1,0},{0,1},{3,2},{2,3},{5,4},{4,5},{7,6},{6,7},{9,8},{8,9},{11,10... | collective-permute-start | bytes 49160 | tf_op jit(solution)/shard_map/ppermute | solution.py:976
  3.7 8.6 %collective-permute-start.1 = (bf16[1,3,32,256]{3,2,1,0:T(8,128)(2,1)}, bf16[1,3,32,256]{3,2,1,0:T(8,128)(2,1)S(1)}, u32[]{:S(2)}, u32[]{:S(2)}) collective-permute-start(bf16[1,3,32,256]{3,2,1,0:T(8,128)(2,1)} %bitcast.15), channel_id=1, source_target_pairs={{0,16},{2,6},{4,20},{6,2},{8,24},{10,14},{12,28},{14,10},{16,0},{1... | collective-permute-start | bytes 147464 | tf_op jit(solution)/shard_map/ppermute | solution.py:1003
  6.2 12.6 %collective-permute-start.3 = (bf16[512,256]{1,0:T(8,128)(2,1)}, bf16[512,256]{1,0:T(8,128)(2,1)S(1)}, u32[]{:S(2)}, u32[]{:S(2)}) collective-permute-start(bf16[512,256]{1,0:T(8,128)(2,1)} %refs_0_), channel_id=1, source_target_pairs={{1,0},{0,1},{3,2},{2,3},{5,4},{4,5},{7,6},{6,7},{9,8},{8,9},{11,10... | collective-permute-start | bytes 786440 | tf_op jit(solution)/shard_map/ppermute | solution.py:976
  7.7 8.9 %collective-permute-start.2 = (bf16[1,32,2560]{2,1,0:T(8,128)(2,1)S(1)}, bf16[1,32,2560]{2,1,0:T(8,128)(2,1)S(1)}, u32[]{:S(2)}, u32[]{:S(2)}) collective-permute-start(bf16[1,32,2560]{2,1,0:T(8,128)(2,1)S(1)} %maximum_bitcast_fusion), channel_id=1, source_target_pairs={{0,16},{2,6},{4,20},{6,2},{8,24},{10,14},{12,28},{14,10},{16,0},{1... | collective-permute-start | bytes 491528 | tf_op jit(solution)/shard_map/ppermute | solution.py:1003
  10.7 6.1 %collective-permute-start.5 = (bf16[384,256]{1,0:T(8,128)(2,1)S(1)}, bf16[384,256]{1,0:T(8,128)(2,1)S(1)}, u32[]{:S(2)}, u32[]{:S(2)}) collective-permute-start(bf16[384,256]{1,0:T(8,128)(2,1)S(1)} %get-tuple-element.280), channel_id=1, source_target_pairs={{0,2},{2,0},{4,6},{6,4},{8,10},{10,8},{12,14},{14,12},{16,18},{18,... | collective-permute-start | bytes 589832 | tf_op jit(solution)/shard_map/ppermute | solution.py:1010
  10.8 7.7 %collective-permute-start.6 = (bf16[384,256]{1,0:T(8,128)(2,1)S(1)}, bf16[384,256]{1,0:T(8,128)(2,1)S(1)}, u32[]{:S(2)}, u32[]{:S(2)}) collective-permute-start(bf16[384,256]{1,0:T(8,128)(2,1)S(1)} %get-tuple-element.279), channel_id=1, source_target_pairs={{2,4},{4,2},{6,8},{8,6},{10,12},{12,10},{14,16},{16,14},{18,20},{2... | collective-permute-start | bytes 589832 | tf_op jit(solution)/shard_map/ppermute | solution.py:1011
  12.3 9.0 %collective-permute-start.4 = (bf16[2,3,32,256]{3,2,1,0:T(8,128)(2,1)S(1)}, bf16[2,3,32,256]{3,2,1,0:T(8,128)(2,1)S(1)}, u32[]{:S(2)}, u32[]{:S(2)}) collective-permute-start(bf16[2,3,32,256]{3,2,1,0:T(8,128)(2,1)S(1)} %constant_dynamic-update-slice_fusion), channel_id=1, source_target_pairs={{0,8},{2,18},{4,12},{6,22},{8,0},{10,26},{12,4},{14,30},{16,24},{1... | collective-permute-start | bytes 294920 | tf_op jit(solution)/shard_map/ppermute | solution.py:1003
  16.7 13.9 %collective-permute-start.11 = (bf16[2,32,2560]{2,1,0:T(8,128)(2,1)S(1)}, bf16[2,32,2560]{2,1,0:T(8,128)(2,1)S(1)}, u32[]{:S(2)}, u32[]{:S(2)}) collective-permute-start(bf16[2,32,2560]{2,1,0:T(8,128)(2,1)S(1)} %constant_dynamic-update-slice_fusion.2), channel_id=1, source_target_pairs={{0,8},{2,18},{4,12},{6,22},{8,0},{10,26},{12,4},{14,30},{16,24},{1... | collective-permute-start | bytes 983048 | tf_op jit(solution)/shard_map/ppermute | solution.py:1003
  16.8 9.3 %collective-permute-start.7 = (bf16[384,256]{1,0:T(8,128)(2,1)S(1)}, bf16[384,256]{1,0:T(8,128)(2,1)S(1)}, u32[]{:S(2)}, u32[]{:S(2)}) collective-permute-start(bf16[384,256]{1,0:T(8,128)(2,1)S(1)} %collective-permute-done.5.refs_2_), channel_id=1, source_target_pairs={{1,0},{0,1},{3,2},{2,3},{5,4},{4,5},{7,6},{6,7},{9,8},{8,9},{11,10... | collective-permute-start | bytes 589832 | tf_op jit(solution)/shard_map/ppermute | solution.py:976
  18.5 10.2 %collective-permute-start.8 = (bf16[384,256]{1,0:T(8,128)(2,1)S(1)}, bf16[384,256]{1,0:T(8,128)(2,1)S(1)}, u32[]{:S(2)}, u32[]{:S(2)}) collective-permute-start(bf16[384,256]{1,0:T(8,128)(2,1)S(1)} %collective-permute-done.6.refs_4_), channel_id=1, source_target_pairs={{1,0},{0,1},{3,2},{2,3},{5,4},{4,5},{7,6},{6,7},{9,8},{8,9},{11,10... | collective-permute-start | bytes 589832 | tf_op jit(solution)/shard_map/ppermute | solution.py:976
  21.3 9.1 %collective-permute-start.9 = (bf16[4,3,32,256]{3,2,1,0:T(8,128)(2,1)S(1)}, bf16[4,3,32,256]{3,2,1,0:T(8,128)(2,1)S(1)}, u32[]{:S(2)}, u32[]{:S(2)}) collective-permute-start(bf16[4,3,32,256]{3,2,1,0:T(8,128)(2,1)S(1)} %constant_dynamic-update-slice_fusion.4), channel_id=1, source_target_pairs={{0,4},{2,10},{4,0},{6,14},{8,12},{10,2},{12,8},{14,6},{16,20},{18,... | collective-permute-start | bytes 589832 | tf_op jit(solution)/shard_map/ppermute | solution.py:1003
  22.9 5.8 %copy-start.3 = (bf16[512,256]{1,0:T(8,128)(2,1)S(1)}, bf16[512,256]{1,0:T(8,128)(2,1)}, u32[]{:S(2)}) copy-start(bf16[512,256]{1,0:T(8,128)(2,1)} %param.26) | copy-start | bytes 786436
  22.9 9.3 %copy-start = (bf16[512,256]{1,0:T(8,128)(2,1)S(1)}, bf16[512,256]{1,0:T(8,128)(2,1)}, u32[]{:S(2)}) copy-start(bf16[512,256]{1,0:T(8,128)(2,1)} %refs_0_) | copy-start | bytes 786436
  22.9 9.3 %copy-start.2 = (f32[2,256]{1,0:T(2,128)S(1)}, f32[2,256]{1,0:T(2,128)}, u32[]{:S(2)}) copy-start(f32[2,256]{1,0:T(2,128)} %bias_ref.1) | copy-start | bytes 6148
  28.7 11.3 %collective-permute-start.13 = (bf16[512,256]{1,0:T(8,128)(2,1)S(1)}, bf16[512,256]{1,0:T(8,128)(2,1)S(1)}, u32[]{:S(2)}, u32[]{:S(2)}) collective-permute-start(bf16[512,256]{1,0:T(8,128)(2,1)S(1)} %copy-done.3), channel_id=1, source_target_pairs={{1,0},{0,1},{3,2},{2,3},{5,4},{4,5},{7,6},{6,7},{9,8},{8,9},{11,10... | collective-permute-start | bytes 786440 | tf_op jit(solution)/shard_map/ppermute | solution.py:976
  30.4 1.8 %collective-permute-start.10 = (bf16[8,3,32,256]{3,2,1,0:T(8,128)(2,1)S(1)}, bf16[8,3,32,256]{3,2,1,0:T(8,128)(2,1)S(1)}, u32[]{:S(2)}, u32[]{:S(2)}) collective-permute-start(bf16[8,3,32,256]{3,2,1,0:T(8,128)(2,1)S(1)} %constant_dynamic-update-slice_fusion.6.near_ref), channel_id=1, source_target_pairs={{0,2},{2,0},{4,6},{6,4},{8,10},{10,8},{12,14},{14,12},{16,18},{18,... | collective-permute-start | bytes 1179656 | tf_op jit(solution)/shard_map/ppermute | solution.py:1003
  30.6 14.2 %collective-permute-start.15 = (bf16[4,32,2560]{2,1,0:T(8,128)(2,1)S(1)}, bf16[4,32,2560]{2,1,0:T(8,128)(2,1)S(1)}, u32[]{:S(2)}, u32[]{:S(2)}) collective-permute-start(bf16[4,32,2560]{2,1,0:T(8,128)(2,1)S(1)} %constant_dynamic-update-slice_fusion.8), channel_id=1, source_target_pairs={{0,4},{2,10},{4,0},{6,14},{8,12},{10,2},{12,8},{14,6},{16,20},{18,... | collective-permute-start | bytes 1966088 | tf_op jit(solution)/shard_map/ppermute | solution.py:1003
  32.2 1.9 %copy-start.4 = (f32[2,256]{1,0:T(2,128)S(1)}, f32[2,256]{1,0:T(2,128)}, u32[]{:S(2)}) copy-start(f32[2,256]{1,0:T(2,128)} %param.20) | copy-start | bytes 6148
  32.2 1.9 %copy-start.5 = (f32[2,256]{1,0:T(2,128)S(1)}, f32[2,256]{1,0:T(2,128)}, u32[]{:S(2)}) copy-start(f32[2,256]{1,0:T(2,128)} %param.25) | copy-start | bytes 6148
  32.2 1.9 %copy-start.6 = (f32[2,256]{1,0:T(2,128)S(1)}, f32[2,256]{1,0:T(2,128)}, u32[]{:S(2)}) copy-start(f32[2,256]{1,0:T(2,128)} %param.24) | copy-start | bytes 6148
  34.1 5.9 %collective-permute-start.12 = (f32[6,256]{1,0:T(8,128)S(1)}, f32[6,256]{1,0:T(8,128)S(1)}, u32[]{:S(2)}, u32[]{:S(2)}) collective-permute-start(f32[6,256]{1,0:T(8,128)S(1)} %pad_maximum_fusion.1), channel_id=1, source_target_pairs={{1,0},{0,1},{3,2},{2,3},{5,4},{4,5},{7,6},{6,7},{9,8},{8,9},{11,10... | collective-permute-start | bytes 18440 | tf_op jit(solution)/shard_map/ppermute | solution.py:976
  39.5 5.3 %collective-permute-start.14 = (bf16[256,256]{1,0:T(8,128)(2,1)S(1)}, bf16[256,256]{1,0:T(8,128)(2,1)S(1)}, u32[]{:S(2)}, u32[]{:S(2)}) collective-permute-start(bf16[256,256]{1,0:T(8,128)(2,1)S(1)} %get-tuple-element.160.own_ref.refs_4_), channel_id=1, source_target_pairs={{1,0},{0,1},{3,2},{2,3},{5,4},{4,5},{7,6},{6,7},{9,8},{8,9},{11,10... | collective-permute-start | bytes 393224 | tf_op jit(solution)/shard_map/ppermute | solution.py:976
  44.9 4.4 %collective-permute-start.17 = (bf16[8,32,2560]{2,1,0:T(8,128)(2,1)S(1)}, bf16[8,32,2560]{2,1,0:T(8,128)(2,1)S(1)}, u32[]{:S(2)}, u32[]{:S(2)}) collective-permute-start(bf16[8,32,2560]{2,1,0:T(8,128)(2,1)S(1)} %constant_dynamic-update-slice_fusion.12.near_ref), channel_id=1, source_target_pairs={{0,2},{2,0},{4,6},{6,4},{8,10},{10,8},{12,14},{14,12},{16,18},{18,... | collective-permute-start | bytes 3932168 | tf_op jit(solution)/shard_map/ppermute | solution.py:1003
  48.7 1.7 %copy-start.1 = (f32[1024]{0:T(1024)S(1)}, f32[1024]{0:T(1024)}, u32[]{:S(2)}) copy-start(f32[1024]{0:T(1024)} %param.22) | copy-start | bytes 12292
  48.8 8.5 %collective-permute-start.16 = (bf16[256,256]{1,0:T(8,128)(2,1)S(1)}, bf16[256,256]{1,0:T(8,128)(2,1)S(1)}, u32[]{:S(2)}, u32[]{:S(2)}) collective-permute-start(bf16[256,256]{1,0:T(8,128)(2,1)S(1)} %get-tuple-element.167.own_ref.refs_5_), channel_id=1, source_target_pairs={{1,0},{0,1},{3,2},{2,3},{5,4},{4,5},{7,6},{6,7},{9,8},{8,9},{11,10... | collective-permute-start | bytes 393224 | tf_op jit(solution)/shard_map/ppermute | solution.py:976
  52.6 10.4 %collective-permute-start.18 = (bf16[256,512]{1,0:T(8,128)(2,1)S(1)}, bf16[256,512]{1,0:T(8,128)(2,1)S(1)}, u32[]{:S(2)}, u32[]{:S(2)}) collective-permute-start(bf16[256,512]{1,0:T(8,128)(2,1)S(1)} %get-tuple-element.174.part_ref), channel_id=1, source_target_pairs={{1,0},{0,1},{3,2},{2,3},{5,4},{4,5},{7,6},{6,7},{9,8},{8,9},{11,10... | collective-permute-start | bytes 786440 | tf_op jit(solution)/shard_map/ppermute | solution.py:976
  59.5 8.2 %collective-permute-start.19 = (bf16[256,512]{1,0:T(8,128)(2,1)S(1)}, bf16[256,512]{1,0:T(8,128)(2,1)S(1)}, u32[]{:S(2)}, u32[]{:S(2)}) collective-permute-start(bf16[256,512]{1,0:T(8,128)(2,1)S(1)} %get-tuple-element.177.part_ref), channel_id=1, source_target_pairs={{1,0},{0,1},{3,2},{2,3},{5,4},{4,5},{7,6},{6,7},{9,8},{8,9},{11,10... | collective-permute-start | bytes 786440 | tf_op jit(solution)/shard_map/ppermute | solution.py:976
  65.5 8.7 %collective-permute-start.20 = (bf16[256,512]{1,0:T(8,128)(2,1)S(1)}, bf16[256,512]{1,0:T(8,128)(2,1)S(1)}, u32[]{:S(2)}, u32[]{:S(2)}) collective-permute-start(bf16[256,512]{1,0:T(8,128)(2,1)S(1)} %get-tuple-element.199.part_ref), channel_id=1, source_target_pairs={{1,0},{0,1},{3,2},{2,3},{5,4},{4,5},{7,6},{6,7},{9,8},{8,9},{11,10... | collective-permute-start | bytes 786440 | tf_op jit(solution)/shard_map/ppermute | solution.py:976
  73.5 5.5 %collective-permute-start.21 = (bf16[512,1024]{1,0:T(8,128)(2,1)S(1)}, bf16[512,1024]{1,0:T(8,128)(2,1)S(1)}, u32[]{:S(2)}, u32[]{:S(2)}) collective-permute-start(bf16[512,1024]{1,0:T(8,128)(2,1)S(1)} %get-tuple-element.207), channel_id=1, source_target_pairs={{0,2},{2,0},{4,6},{6,4},{8,10},{10,8},{12,14},{14,12},{16,18},{18,... | collective-permute-start | bytes 3145736 | tf_op jit(solution)/shard_map/ppermute | solution.py:1003
  73.6 10.2 %collective-permute-start.22 = (bf16[256,512]{1,0:T(8,128)(2,1)S(1)}, bf16[256,512]{1,0:T(8,128)(2,1)S(1)}, u32[]{:S(2)}, u32[]{:S(2)}) collective-permute-start(bf16[256,512]{1,0:T(8,128)(2,1)S(1)} %get-tuple-element.211.part_ref), channel_id=1, source_target_pairs={{1,0},{0,1},{3,2},{2,3},{5,4},{4,5},{7,6},{6,7},{9,8},{8,9},{11,10... | collective-permute-start | bytes 786440 | tf_op jit(solution)/shard_map/ppermute | solution.py:976
  79.2 10.1 %collective-permute-start.23 = (bf16[256,1024]{1,0:T(8,128)(2,1)S(1)}, bf16[256,1024]{1,0:T(8,128)(2,1)S(1)}, u32[]{:S(2)}, u32[]{:S(2)}) collective-permute-start(bf16[256,1024]{1,0:T(8,128)(2,1)S(1)} %get-tuple-element.221), channel_id=1, source_target_pairs={{0,4},{2,10},{4,0},{6,14},{8,12},{10,2},{12,8},{14,6},{16,20},{18,... | collective-permute-start | bytes 1572872 | tf_op jit(solution)/shard_map/ppermute | solution.py:1003
  91.3 3.9 %collective-permute-start.24 = (bf16[1056,256]{1,0:T(8,128)(2,1)S(1)}, bf16[1056,256]{1,0:T(8,128)(2,1)S(1)}, u32[]{:S(2)}, u32[]{:S(2)}) collective-permute-start(bf16[1056,256]{1,0:T(8,128)(2,1)S(1)} %get-tuple-element.239), channel_id=1, source_target_pairs={{0,2},{2,0},{4,6},{6,4},{8,10},{10,8},{12,14},{14,12},{16,18},{18,... | collective-permute-start | bytes 1622024 | tf_op jit(solution)/shard_map/ppermute | solution.py:1003
  93.5 12.0 %collective-permute-start.26 = (bf16[768,256]{1,0:T(8,128)(2,1)S(1)}, bf16[768,256]{1,0:T(8,128)(2,1)S(1)}, u32[]{:S(2)}, u32[]{:S(2)}) collective-permute-start(bf16[768,256]{1,0:T(8,128)(2,1)S(1)} %get-tuple-element.251), channel_id=1, source_target_pairs={{1,0},{0,1},{3,2},{2,3},{5,4},{4,5},{7,6},{6,7},{9,8},{8,9},{11,10... | collective-permute-start | bytes 1179656 | tf_op jit(solution)/shard_map/ppermute | solution.py:976
  95.3 7.7 %collective-permute-start.25 = (bf16[544,256]{1,0:T(8,128)(2,1)S(1)}, bf16[544,256]{1,0:T(8,128)(2,1)S(1)}, u32[]{:S(2)}, u32[]{:S(2)}) collective-permute-start(bf16[544,256]{1,0:T(8,128)(2,1)S(1)} %get-tuple-element.246), channel_id=1, source_target_pairs={{0,4},{2,10},{4,0},{6,14},{8,12},{10,2},{12,8},{14,6},{16,20},{18,... | collective-permute-start | bytes 835592 | tf_op jit(solution)/shard_map/ppermute | solution.py:1003
  95.9 10.9 %collective-permute-start.27 = (bf16[128,1024]{1,0:T(8,128)(2,1)S(1)}, bf16[128,1024]{1,0:T(8,128)(2,1)S(1)}, u32[]{:S(2)}, u32[]{:S(2)}) collective-permute-start(bf16[128,1024]{1,0:T(8,128)(2,1)S(1)} %get-tuple-element.254), channel_id=1, source_target_pairs={{0,8},{2,18},{4,12},{6,22},{8,0},{10,26},{12,4},{14,30},{16,24},{1... | collective-permute-start | bytes 786440 | tf_op jit(solution)/shard_map/ppermute | solution.py:1003
  97.2 16.7 %collective-permute-start.31 = (bf16[512,256]{1,0:T(8,128)(2,1)S(1)}, bf16[512,256]{1,0:T(8,128)(2,1)S(1)}, u32[]{:S(2)}, u32[]{:S(2)}) collective-permute-start(bf16[512,256]{1,0:T(8,128)(2,1)S(1)} %get-tuple-element.264), channel_id=1, source_target_pairs={{1,0},{0,1},{3,2},{2,3},{5,4},{4,5},{7,6},{6,7},{9,8},{8,9},{11,10... | collective-permute-start | bytes 786440 | tf_op jit(solution)/shard_map/ppermute | solution.py:976
  103.0 7.8 %collective-permute-start.28 = (bf16[288,256]{1,0:T(8,128)(2,1)S(1)}, bf16[288,256]{1,0:T(8,128)(2,1)S(1)}, u32[]{:S(2)}, u32[]{:S(2)}) collective-permute-start(bf16[288,256]{1,0:T(8,128)(2,1)S(1)} %get-tuple-element.257), channel_id=1, source_target_pairs={{0,8},{2,18},{4,12},{6,22},{8,0},{10,26},{12,4},{14,30},{16,24},{1... | collective-permute-start | bytes 442376 | tf_op jit(solution)/shard_map/ppermute | solution.py:1003
  105.6 8.4 %collective-permute-start.29 = (bf16[384,256]{1,0:T(8,128)(2,1)S(1)}, bf16[384,256]{1,0:T(8,128)(2,1)S(1)}, u32[]{:S(2)}, u32[]{:S(2)}) collective-permute-start(bf16[384,256]{1,0:T(8,128)(2,1)S(1)} %get-tuple-element.252), channel_id=1, source_target_pairs={{0,2},{2,0},{4,6},{6,4},{8,10},{10,8},{12,14},{14,12},{16,18},{18,... | collective-permute-start | bytes 589832 | tf_op jit(solution)/shard_map/ppermute | solution.py:1010
  106.2 7.8 %collective-permute-start.30 = (bf16[384,256]{1,0:T(8,128)(2,1)S(1)}, bf16[384,256]{1,0:T(8,128)(2,1)S(1)}, u32[]{:S(2)}, u32[]{:S(2)}) collective-permute-start(bf16[384,256]{1,0:T(8,128)(2,1)S(1)} %get-tuple-element.262), channel_id=1, source_target_pairs={{2,4},{4,2},{6,8},{8,6},{10,12},{12,10},{14,16},{16,14},{18,20},{2... | collective-permute-start | bytes 589832 | tf_op jit(solution)/shard_map/ppermute | solution.py:1011
  106.9 11.2 %collective-permute-start.32 = (bf16[64,1024]{1,0:T(8,128)(2,1)S(1)}, bf16[64,1024]{1,0:T(8,128)(2,1)S(1)}, u32[]{:S(2)}, u32[]{:S(2)}) collective-permute-start(bf16[64,1024]{1,0:T(8,128)(2,1)S(1)} %get-tuple-element.266), channel_id=1, source_target_pairs={{0,16},{2,6},{4,20},{6,2},{8,24},{10,14},{12,28},{14,10},{16,0},{1... | collective-permute-start | bytes 393224 | tf_op jit(solution)/shard_map/ppermute | solution.py:1003
  110.9 8.1 %collective-permute-start.33 = (bf16[160,256]{1,0:T(8,128)(2,1)S(1)}, bf16[160,256]{1,0:T(8,128)(2,1)S(1)}, u32[]{:S(2)}, u32[]{:S(2)}) collective-permute-start(bf16[160,256]{1,0:T(8,128)(2,1)S(1)} %get-tuple-element.269), channel_id=1, source_target_pairs={{0,16},{2,6},{4,20},{6,2},{8,24},{10,14},{12,28},{14,10},{16,0},{1... | collective-permute-start | bytes 245768 | tf_op jit(solution)/shard_map/ppermute | solution.py:1003

commit v8 on v7

--- a/solution.py
+++ b/solution.py
@@ -1108,7 +1108,6 @@
         return dense
 
     prev_logits = pltpu.with_memory_space_constraint(prev_logits, pltpu.HBM)
-    logit_grad = pltpu.with_memory_space_constraint(logit_grad, pltpu.HBM)
 
     out_turned = out_weight.T
     out_other = others(out_turned)

time: 120 us -> 119 us (level)
    pallas_call x4, Pallas kernels: 12.4 us -> 11.2 us  [to_dense(): pl.pallas_call(functools.partial(dense_kernel, fill, token_count, offset)...]
  transfers between devices with their start and end apart: 34 -> 34, of which waited for: 8 -> 8; matrix products, arithmetic and copies ran while one was open for 3% -> 3% of each run, Pallas kernels for 51% -> 50%
where the time goes in v8:
time: 119 us
  Pallas kernels  62.4 us (52%)
  starting transfers between devices  40 us (34%)
  waiting for transfers between devices  12.3 us (10%)
  local copies, waits for them, and re-layouts  2.14 us (2%)
    ppermute x16, starting transfers between devices, with_partner(): lax.ppermute(x, 'row', [(i, i ^ orders[i % 2][step]) for i in range(count)])  21.7 us
    ppermute x14, starting transfers between devices, from_next(): lax.ppermute(x, axis, [((i + step) % count, i) for i in range(count)])  16.8 us
    pallas_call x4, Pallas kernels, to_dense(): pl.pallas_call(functools.partial(dense_kernel, fill, token_count, offset)...  11.2 us
    pallas_call x3, Pallas kernels, to_band(): pl.pallas_call(functools.partial(band_kernel, masked, len(chunks)), grid=...  11 us
    pallas_call x2, Pallas kernels, attend_backward(): pl.pallas_call(functools.partial(backward_kernel, offset, last), grid=(co...  8.72 us
    pallas_call x2, Pallas kernels, attend_forward(): pl.pallas_call(functools.partial(forward_kernel, offset), grid=(count //...  7.43 us
    ppermute x14, waiting for transfers between devices, from_next(): lax.ppermute(x, axis, [((i + step) % count, i) for i in range(count)])  6.25 us
    ppermute x16, waiting for transfers between devices, with_partner(): lax.ppermute(x, 'row', [(i, i ^ orders[i % 2][step]) for i in range(count)])  6.01 us
  transfers between devices with their start and end apart: 34, of which 8 were waited for; matrix products, arithmetic and copies ran while one was open for 3% of the time, Pallas kernels for 50%

profile of v8, /device:TPU:0, one launch (start us, length us, event | category | flops | bytes accessed | tf_op | source)
XLA Modules:
  0.0 119.1 jit_solution(8784192434491390198)
XLA Ops:
  0.7 3.0 %collective-permute-start = (bf16[32,256]{1,0:T(8,128)(2,1)}, bf16[32,256]{1,0:T(8,128)(2,1)S(1)}, u32[]{:S(2)}, u32[]{:S(2)}) collective-permute-start(bf16[32,256]{1,0:T(8,128)(2,1)} %bitcast.17), channel_id=1, source_target_pairs={{1,0},{0,1},{3,2},{2,3},{5,4},{4,5},{7,6},{6,7},{9,8},{8,9},{11,10... | collective-permute-start | bytes 49160 | tf_op jit(solution)/shard_map/ppermute | solution.py:976
  3.7 2.6 %collective-permute-start.1 = (bf16[1,3,32,256]{3,2,1,0:T(8,128)(2,1)}, bf16[1,3,32,256]{3,2,1,0:T(8,128)(2,1)S(1)}, u32[]{:S(2)}, u32[]{:S(2)}) collective-permute-start(bf16[1,3,32,256]{3,2,1,0:T(8,128)(2,1)} %bitcast.15), channel_id=1, source_target_pairs={{0,16},{2,6},{4,20},{6,2},{8,24},{10,14},{12,28},{14,10},{16,0},{1... | collective-permute-start | bytes 147464 | tf_op jit(solution)/shard_map/ppermute | solution.py:1003
  6.2 0.5 collective-permute-start.3
  6.8 0.9 maximum_bitcast_fusion
  7.7 1.9 %collective-permute-start.2 = (bf16[1,32,2560]{2,1,0:T(8,128)(2,1)S(1)}, bf16[1,32,2560]{2,1,0:T(8,128)(2,1)S(1)}, u32[]{:S(2)}, u32[]{:S(2)}) collective-permute-start(bf16[1,32,2560]{2,1,0:T(8,128)(2,1)S(1)} %maximum_bitcast_fusion), channel_id=1, source_target_pairs={{0,16},{2,6},{4,20},{6,2},{8,24},{10,14},{12,28},{14,10},{16,0},{1... | collective-permute-start | bytes 491528 | tf_op jit(solution)/shard_map/ppermute | solution.py:1003
  9.7 1.0 constant_dynamic-slice_fusion
  10.8 0.7 collective-permute-start.6
  11.5 0.8 constant_dynamic-update-slice_fusion.1
  12.3 4.4 %collective-permute-start.4 = (bf16[2,3,32,256]{3,2,1,0:T(8,128)(2,1)S(1)}, bf16[2,3,32,256]{3,2,1,0:T(8,128)(2,1)S(1)}, u32[]{:S(2)}, u32[]{:S(2)}) collective-permute-start(bf16[2,3,32,256]{3,2,1,0:T(8,128)(2,1)S(1)} %constant_dynamic-update-slice_fusion), channel_id=1, source_target_pairs={{0,8},{2,18},{4,12},{6,22},{8,0},{10,26},{12,4},{14,30},{16,24},{1... | collective-permute-start | bytes 294920 | tf_op jit(solution)/shard_map/ppermute | solution.py:1003
  16.8 1.7 %collective-permute-start.7 = (bf16[384,256]{1,0:T(8,128)(2,1)S(1)}, bf16[384,256]{1,0:T(8,128)(2,1)S(1)}, u32[]{:S(2)}, u32[]{:S(2)}) collective-permute-start(bf16[384,256]{1,0:T(8,128)(2,1)S(1)} %collective-permute-done.5.refs_2_), channel_id=1, source_target_pairs={{1,0},{0,1},{3,2},{2,3},{5,4},{4,5},{7,6},{6,7},{9,8},{8,9},{11,10... | collective-permute-start | bytes 589832 | tf_op jit(solution)/shard_map/ppermute | solution.py:976
  18.5 0.4 collective-permute-start.8
  18.9 2.4 %collective-permute-done.4 = bf16[2,3,32,256]{3,2,1,0:T(8,128)(2,1)S(1)} collective-permute-done((bf16[2,3,32,256]{3,2,1,0:T(8,128)(2,1)S(1)}, bf16[2,3,32,256]{3,2,1,0:T(8,128)(2,1)S(1)}, u32[]{:S(2)}, u32[]{:S(2)}) %collective-permute-start.4) | collective-permute-done | bytes 98336 | tf_op jit(solution)/shard_map/ppermute | solution.py:1003
  21.3 1.5 %collective-permute-start.9 = (bf16[4,3,32,256]{3,2,1,0:T(8,128)(2,1)S(1)}, bf16[4,3,32,256]{3,2,1,0:T(8,128)(2,1)S(1)}, u32[]{:S(2)}, u32[]{:S(2)}) collective-permute-start(bf16[4,3,32,256]{3,2,1,0:T(8,128)(2,1)S(1)} %constant_dynamic-update-slice_fusion.4), channel_id=1, source_target_pairs={{0,4},{2,10},{4,0},{6,14},{8,12},{10,2},{12,8},{14,6},{16,20},{18,... | collective-permute-start | bytes 589832 | tf_op jit(solution)/shard_map/ppermute | solution.py:1003
  22.9 3.1 %to_dense.4.prev_ref = bf16[4,256,1152]{2,1,0:T(8,128)(2,1)S(1)} custom-call(s32[34]{0:T(128)S(1)} %pad_add_fusion.lengths_ref, bf16[4,512,1024]{2,1,0:T(8,128)(2,1)} %band_ref.1), custom_call_target="tpu_custom_call" | custom-call | flops 8000000000 | tf_op jit(solution)/shard_map/to_dense/pallas_call | solution.py:102
  26.1 2.7 %collective-permute-done.8.refs_5_ = bf16[384,256]{1,0:T(8,128)(2,1)S(1)} collective-permute-done((bf16[384,256]{1,0:T(8,128)(2,1)S(1)}, bf16[384,256]{1,0:T(8,128)(2,1)S(1)}, u32[]{:S(2)}, u32[]{:S(2)}) %collective-permute-start.8) | collective-permute-done | bytes 196640 | tf_op jit(solution)/shard_map/ppermute | solution.py:976
  28.7 1.6 %collective-permute-start.13 = (bf16[512,256]{1,0:T(8,128)(2,1)S(1)}, bf16[512,256]{1,0:T(8,128)(2,1)S(1)}, u32[]{:S(2)}, u32[]{:S(2)}) collective-permute-start(bf16[512,256]{1,0:T(8,128)(2,1)S(1)} %copy-done.4), channel_id=1, source_target_pairs={{1,0},{0,1},{3,2},{2,3},{5,4},{4,5},{7,6},{6,7},{9,8},{8,9},{11,10... | collective-permute-start | bytes 786440 | tf_op jit(solution)/shard_map/ppermute | solution.py:976
  30.4 0.2 collective-permute-start.10
  30.6 1.4 %collective-permute-start.15 = (bf16[4,32,2560]{2,1,0:T(8,128)(2,1)S(1)}, bf16[4,32,2560]{2,1,0:T(8,128)(2,1)S(1)}, u32[]{:S(2)}, u32[]{:S(2)}) collective-permute-start(bf16[4,32,2560]{2,1,0:T(8,128)(2,1)S(1)} %constant_dynamic-update-slice_fusion.8), channel_id=1, source_target_pairs={{0,4},{2,10},{4,0},{6,14},{8,12},{10,2},{12,8},{14,6},{16,20},{18,... | collective-permute-start | bytes 1966088 | tf_op jit(solution)/shard_map/ppermute | solution.py:1003
  32.0 0.2 collective-permute-done.10.far_ref
  32.2 1.9 %project.1 = (bf16[512,512]{1,0:T(8,128)(2,1)S(1)}, bf16[512,256]{1,0:T(8,128)(2,1)S(1)}, bf16[1536,256]{1,0:T(8,128)(2,1)S(1)}, bf16[1536,256]{1,0:T(8,128)(2,1...) custom-call(s32[16]{0:T(128)S(1)} %fusion.7.slot_ref, ...), custom_call_target="tpu_custom_call" | custom-call | flops 2000000000 | tf_op jit(solution)/shard_map/project/pallas_call | solution.py:245
  34.1 1.6 %collective-permute-start.12 = (f32[6,256]{1,0:T(8,128)S(1)}, f32[6,256]{1,0:T(8,128)S(1)}, u32[]{:S(2)}, u32[]{:S(2)}) collective-permute-start(f32[6,256]{1,0:T(8,128)S(1)} %pad_maximum_fusion.1), channel_id=1, source_target_pairs={{1,0},{0,1},{3,2},{2,3},{5,4},{4,5},{7,6},{6,7},{9,8},{8,9},{11,10... | collective-permute-start | bytes 18440 | tf_op jit(solution)/shard_map/ppermute | solution.py:976
  35.8 3.7 %attend_forward.2 = (bf16[4,256,1152]{2,1,0:T(8,128)(2,1)S(1)}, bf16[4,256,1152]{2,1,0:T(8,128)(2,1)S(1)}, bf16[256,256]{1,0:T(8,128)(2,1)S(1)}) custom-call(bf16[512,256]{1,0:T(8,128)(2,1)S(1)} %get-tuple-element.166.query_ref, bf16[1536,256]{1,0:T(8,128)(2,1)S(1)} %get-tuple-element.157.key_ref, bf16[1536,256]{1,0:T(8,128)(2,1)S(1)} %get-tuple-element.158.value_ref, ...), custom_call_target="tpu_custom_call" | custom-call | flops 3800000000 | tf_op jit(solution)/shard_map/attend_forward/pallas_call | solution.py:309
  39.5 0.5 collective-permute-start.14
  40.1 3.1 %to_dense.5.prev_ref = bf16[4,256,1152]{2,1,0:T(8,128)(2,1)S(1)} custom-call(s32[34]{0:T(128)S(1)} %pad_add_fusion.lengths_ref, bf16[4,512,1024]{2,1,0:T(8,128)(2,1)} %band_ref.1), custom_call_target="tpu_custom_call" | custom-call | flops 1000000000 | tf_op jit(solution)/shard_map/to_dense/pallas_call | solution.py:102
  43.2 1.6 %collective-permute-done.14.other_ref = bf16[256,256]{1,0:T(8,128)(2,1)S(1)} collective-permute-done((bf16[256,256]{1,0:T(8,128)(2,1)S(1)}, bf16[256,256]{1,0:T(8,128)(2,1)S(1)}, u32[]{:S(2)}, u32[]{:S(2)}) %collective-permute-start.14) | collective-permute-done | bytes 131104 | tf_op jit(solution)/shard_map/ppermute | solution.py:976
  45.0 3.7 %attend_forward.3 = (bf16[4,256,1152]{2,1,0:T(8,128)(2,1)S(1)}, bf16[4,256,1152]{2,1,0:T(8,128)(2,1)S(1)}, bf16[256,256]{1,0:T(8,128)(2,1)S(1)}) custom-call(bf16[512,256]{1,0:T(8,128)(2,1)S(1)} %get-tuple-element.166.query_ref, bf16[1536,256]{1,0:T(8,128)(2,1)S(1)} %get-tuple-element.157.key_ref, bf16[1536,256]{1,0:T(8,128)(2,1)S(1)} %get-tuple-element.158.value_ref, ...), custom_call_target="tpu_custom_call" | custom-call | flops 3800000000 | tf_op jit(solution)/shard_map/attend_forward/pallas_call | solution.py:309
  48.8 0.6 collective-permute-start.16
  49.3 1.1 in_order.1
  50.4 2.2 %feed_first.2 = (f32[256,512]{1,0:T(8,128)S(1)}, f32[256,1]{1,0:T(8,128)S(1)}, bf16[256,512]{1,0:T(8,128)(2,1)S(1)}, bf16[256,1024]{1,0:T(8,128)(2,1)S(1)}, bf16...) custom-call(bf16[256,256]{1,0:T(8,128)(2,1)S(1)} %get-tuple-element.160.own_ref.refs_4_, ...), custom_call_target="tpu_custom_call" | custom-call | flops 1000000000 | tf_op jit(solution)/shard_map/feed_first/pallas_call | solution.py:508
  52.7 1.6 %collective-permute-start.18 = (bf16[256,512]{1,0:T(8,128)(2,1)S(1)}, bf16[256,512]{1,0:T(8,128)(2,1)S(1)}, u32[]{:S(2)}, u32[]{:S(2)}) collective-permute-start(bf16[256,512]{1,0:T(8,128)(2,1)S(1)} %get-tuple-element.174.part_ref), channel_id=1, source_target_pairs={{1,0},{0,1},{3,2},{2,3},{5,4},{4,5},{7,6},{6,7},{9,8},{8,9},{11,10... | collective-permute-start | bytes 786440 | tf_op jit(solution)/shard_map/ppermute | solution.py:976
  54.2 2.5 %to_dense.6.logit_ref = bf16[4,256,1152]{2,1,0:T(8,128)(2,1)S(1)} custom-call(s32[34]{0:T(128)S(1)} %pad_add_fusion.lengths_ref, bf16[4,512,1024]{2,1,0:T(8,128)(2,1)S(1)} %copy-done), custom_call_target="tpu_custom_call" | custom-call | flops 1000000000 | tf_op jit(solution)/shard_map/to_dense/pallas_call | solution.py:102
  56.7 2.2 %feed_first.3 = (f32[256,512]{1,0:T(8,128)S(1)}, f32[256,1]{1,0:T(8,128)S(1)}, bf16[256,512]{1,0:T(8,128)(2,1)S(1)}, bf16[256,1024]{1,0:T(8,128)(2,1)S(1)}, bf16...) custom-call(bf16[256,256]{1,0:T(8,128)(2,1)S(1)} %get-tuple-element.167.own_ref.refs_5_, ...), custom_call_target="tpu_custom_call" | custom-call | flops 1000000000 | tf_op jit(solution)/shard_map/feed_first/pallas_call | solution.py:508
  58.9 0.6 collective-permute-start.19
  59.5 3.0 %to_band.3.refs_1_ = bf16[4,512,1024]{2,1,0:T(8,128)(2,1)} custom-call(bf16[4,256,1152]{2,1,0:T(8,128)(2,1)S(1)} %get-tuple-element.178.refs_0_), custom_call_target="tpu_custom_call" | custom-call | flops 5000000000 | tf_op jit(solution)/shard_map/to_band/pallas_call | solution.py:151
  62.5 2.5 %feed_second.2 = (f32[16,256]{1,0:T(8,128)S(1)}, bf16[512,256]{1,0:T(8,128)(2,1)}, f32[256,512]{1,0:T(8,128)S(1)}, bf16[256,512]{1,0:T(8,128)(2,1)S(1)}, bf16[25...) custom-call(f32[16,256]{1,0:T(8,128)S(1)} %broadcast_in_dim.18.start_ref, ...), custom_call_target="tpu_custom_call" | custom-call | flops 700000000 | tf_op jit(solution)/shard_map/feed_second/pallas_call | solution.py:587
  65.0 1.5 %collective-permute-start.20 = (bf16[256,512]{1,0:T(8,128)(2,1)S(1)}, bf16[256,512]{1,0:T(8,128)(2,1)S(1)}, u32[]{:S(2)}, u32[]{:S(2)}) collective-permute-start(bf16[256,512]{1,0:T(8,128)(2,1)S(1)} %get-tuple-element.199.part_ref), channel_id=1, source_target_pairs={{1,0},{0,1},{3,2},{2,3},{5,4},{4,5},{7,6},{6,7},{9,8},{8,9},{11,10... | collective-permute-start | bytes 786440 | tf_op jit(solution)/shard_map/ppermute | solution.py:976
  66.5 0.6 collective-permute-done.19.recv_ref
  67.1 2.5 %feed_second.3 = (f32[16,256]{1,0:T(8,128)S(1)}, bf16[512,256]{1,0:T(8,128)(2,1)}, f32[256,512]{1,0:T(8,128)S(1)}, bf16[256,512]{1,0:T(8,128)(2,1)S(1)}, bf16[25...) custom-call(f32[16,256]{1,0:T(8,128)S(1)} %get-tuple-element.182.start_ref, ...), custom_call_target="tpu_custom_call", output_to_operand_aliasing={{1}: (9, {})} | custom-call | flops 700000000 | tf_op jit(solution)/shard_map/feed_second/pallas_call | solution.py:587
  69.6 3.3 %feed_grads.1 = (f32[512,1024]{1,0:T(8,128)S(1)}, bf16[512,1024]{1,0:T(8,128)(2,1)S(1)}) custom-call(s32[16]{0:T(128)S(1)} %and_select_fusion.block_ref, bf16[256,512]{1,0:T(8,128)(2,1)S(1)} %get-tuple-element.189.refs_0_, bf16[256,512]{1,0:T(8,128)(2,1)S(1)} %get-tuple-element.190.refs_1_, bf16[256,512]{1,0:T(8,128)(2,1)S(1)} %get-tuple-element.191.refs_2_, ...), custom_call_target="tpu_custom_call" | custom-call | flops 1000000000 | tf_op jit(solution)/shard_map/feed_grads/pallas_call | solution.py:708
  73.0 1.2 %collective-permute-start.22 = (bf16[256,512]{1,0:T(8,128)(2,1)S(1)}, bf16[256,512]{1,0:T(8,128)(2,1)S(1)}, u32[]{:S(2)}, u32[]{:S(2)}) collective-permute-start(bf16[256,512]{1,0:T(8,128)(2,1)S(1)} %get-tuple-element.211.part_ref), channel_id=1, source_target_pairs={{1,0},{0,1},{3,2},{2,3},{5,4},{4,5},{7,6},{6,7},{9,8},{8,9},{11,10... | collective-permute-start | bytes 786440 | tf_op jit(solution)/shard_map/ppermute | solution.py:976
  74.2 0.7 feed_third.2
  75.0 4.0 %attend_backward.2 = (bf16[4,256,1152]{2,1,0:T(8,128)(2,1)S(1)}, bf16[256,256]{1,0:T(8,128)(2,1)S(1)}, f32[256,1536]{1,0:T(8,128)S(1)}, f32[256,1536]{1,0:T(8,128)S(1)}) custom-call(bf16[256,256]{1,0:T(8,128)(2,1)S(1)} %get-tuple-element.203.grad_ref, bf16[512,256]{1,0:T(8,128)(2,1)S(1)} %get-tuple-element.166.query_ref, ...), custom_call_target="tpu_custom_call" | custom-call | flops 20000000000 | tf_op jit(solution)/shard_map/attend_backward/pallas_call | solution.py:404
  79.0 0.2 fold.6
  79.2 1.5 %collective-permute-start.23 = (bf16[256,1024]{1,0:T(8,128)(2,1)S(1)}, bf16[256,1024]{1,0:T(8,128)(2,1)S(1)}, u32[]{:S(2)}, u32[]{:S(2)}) collective-permute-start(bf16[256,1024]{1,0:T(8,128)(2,1)S(1)} %get-tuple-element.221), channel_id=1, source_target_pairs={{0,4},{2,10},{4,0},{6,14},{8,12},{10,2},{12,8},{14,6},{16,20},{18,... | collective-permute-start | bytes 1572872 | tf_op jit(solution)/shard_map/ppermute | solution.py:1003
  80.7 2.5 %to_dense.7.logit_ref = bf16[4,256,1152]{2,1,0:T(8,128)(2,1)S(1)} custom-call(s32[34]{0:T(128)S(1)} %pad_add_fusion.lengths_ref, bf16[4,512,1024]{2,1,0:T(8,128)(2,1)S(1)} %copy-done), custom_call_target="tpu_custom_call" | custom-call | flops 1000000000 | tf_op jit(solution)/shard_map/to_dense/pallas_call | solution.py:102
  83.2 0.8 feed_third.3
  84.0 4.7 %attend_backward.3 = (bf16[4,256,1152]{2,1,0:T(8,128)(2,1)S(1)}, bf16[256,256]{1,0:T(8,128)(2,1)S(1)}, bf16[1536,256]{1,0:T(8,128)(2,1)S(1)}, bf16[1536,256]{1,0:T(8,128)(2,1)S(1)}) custom-call(bf16[256,256]{1,0:T(8,128)(2,1)S(1)} %get-tuple-element.215.grad_ref, bf16[512,256]{1,0:T(8,128)(2,1)S(1)} %get-tuple-element.166.query_ref, ...), custom_call_target="tpu_custom_call" | custom-call | flops 3000000000 | tf_op jit(solution)/shard_map/attend_backward/pallas_call | solution.py:404
  88.8 1.9 %project_grads.1 = (f32[1024,256]{1,0:T(8,128)S(1)}, bf16[1056,256]{1,0:T(8,128)(2,1)S(1)}, f32[16,256]{1,0:T(8,128)S(1)}) custom-call(s32[16]{0:T(128)S(1)} %and_select_fusion.block_ref, f32[16,256]{1,0:T(8,128)S(1)} %get-tuple-element.223.start_ref, bf16[256,256]{1,0:T(8,128)(2,1)S(1)} %get-tuple-element.205.refs_0_, ...), custom_call_target="tpu_custom_call" | custom-call | flops 600000000 | tf_op jit(solution)/shard_map/project_grads/pallas_call | solution.py:765
  90.8 2.1 %token_grads.1 = (f32[512,256]{1,0:T(8,128)S(1)}, f32[768,256]{1,0:T(8,128)S(1)}, bf16[512,256]{1,0:T(8,128)(2,1)S(1)}, bf16[768,256]{1,0:T(8,128)(2,1)S(1)}) custom-call(s32[1]{0:T(128)} %bitcast.even_ref, bf16[256,256]{1,0:T(8,128)(2,1)S(1)} %get-tuple-element.205.refs_0_, bf16[256,256]{1,0:T(8,128)(2,1)S(1)} %get-tuple-element.219.refs_1_, ...), custom_call_target="tpu_custom_call" | custom-call | flops 5000000000 | tf_op jit(solution)/shard_map/token_grads/pallas_call | solution.py:909
  93.0 1.0 collective-permute-start.26
  94.1 1.3 %collective-permute-start.25 = (bf16[544,256]{1,0:T(8,128)(2,1)S(1)}, bf16[544,256]{1,0:T(8,128)(2,1)S(1)}, u32[]{:S(2)}, u32[]{:S(2)}) collective-permute-start(bf16[544,256]{1,0:T(8,128)(2,1)S(1)} %get-tuple-element.246), channel_id=1, source_target_pairs={{0,4},{2,10},{4,0},{6,14},{8,12},{10,2},{12,8},{14,6},{16,20},{18,... | collective-permute-start | bytes 835592 | tf_op jit(solution)/shard_map/ppermute | solution.py:1003
  95.4 1.1 collective-permute-start.27
  96.4 1.0 collective-permute-start.31
  97.4 5.0 %to_band.4 = bf16[4,512,1024]{2,1,0:T(8,128)(2,1)} custom-call(bf16[4,256,1152]{2,1,0:T(8,128)(2,1)S(1)} %get-tuple-element.243.refs_0_, bf16[4,256,1152]{2,1,0:T(8,128)(2,1)S(1)} %get-tuple-element.244.refs_1_), custom_call_target="tpu_custom_call" | custom-call | flops 300000000 | tf_op jit(solution)/shard_map/to_band/pallas_call | solution.py:151
  102.5 1.2 collective-permute-start.28
  103.6 1.3 %collective-permute-done.26.refs_0_ = bf16[768,256]{1,0:T(8,128)(2,1)S(1)} collective-permute-done((bf16[768,256]{1,0:T(8,128)(2,1)S(1)}, bf16[768,256]{1,0:T(8,128)(2,1)S(1)}, u32[]{:S(2)}, u32[]{:S(2)}) %collective-permute-start.26) | collective-permute-done | bytes 393248 | tf_op jit(solution)/shard_map/ppermute | solution.py:976
  105.1 0.7 collective-permute-start.30
  105.8 4.4 %collective-permute-start.32 = (bf16[64,1024]{1,0:T(8,128)(2,1)S(1)}, bf16[64,1024]{1,0:T(8,128)(2,1)S(1)}, u32[]{:S(2)}, u32[]{:S(2)}) collective-permute-start(bf16[64,1024]{1,0:T(8,128)(2,1)S(1)} %get-tuple-element.266), channel_id=1, source_target_pairs={{0,16},{2,6},{4,20},{6,2},{8,24},{10,14},{12,28},{14,10},{16,0},{1... | collective-permute-start | bytes 393224 | tf_op jit(solution)/shard_map/ppermute | solution.py:1003
  110.4 3.0 %to_band.5 = bf16[4,512,1024]{2,1,0:T(8,128)(2,1)} custom-call(bf16[4,256,1152]{2,1,0:T(8,128)(2,1)S(1)} %get-tuple-element.260.refs_0_, bf16[4,512,1024]{2,1,0:T(8,128)(2,1)} %to_band.3.refs_1_), custom_call_target="tpu_custom_call", output_to_operand_aliasing={{}: (1, {})} | custom-call | flops 300000000 | tf_op jit(solution)/shard_map/to_band/pallas_call | solution.py:151
  113.4 0.9 token_sum.1
  114.2 3.3 %collective-permute-done.32.arrived_ref = bf16[64,1024]{1,0:T(8,128)(2,1)S(1)} collective-permute-done((bf16[64,1024]{1,0:T(8,128)(2,1)S(1)}, bf16[64,1024]{1,0:T(8,128)(2,1)S(1)}, u32[]{:S(2)}, u32[]{:S(2)}) %collective-permute-start.32) | collective-permute-done | bytes 131104 | tf_op jit(solution)/shard_map/ppermute | solution.py:1003
  117.5 0.7 finish.2
  118.2 0.2 collective-permute-done.33.arrived_ref
  118.4 0.7 finish.3
  (76 shorter events, 1.5 us)
Async XLA Ops:
  0.6 22.2 %copy-start.8 = (s32[1,33]{1,0:T(1,128)S(1)}, s32[1,33]{1,0:T(1,128)}, u32[]{:S(2)}) copy-start(s32[1,33]{1,0:T(1,128)} %param.16) | copy-start | bytes 400
  0.7 6.2 %collective-permute-start = (bf16[32,256]{1,0:T(8,128)(2,1)}, bf16[32,256]{1,0:T(8,128)(2,1)S(1)}, u32[]{:S(2)}, u32[]{:S(2)}) collective-permute-start(bf16[32,256]{1,0:T(8,128)(2,1)} %bitcast.17), channel_id=1, source_target_pairs={{1,0},{0,1},{3,2},{2,3},{5,4},{4,5},{7,6},{6,7},{9,8},{8,9},{11,10... | collective-permute-start | bytes 49160 | tf_op jit(solution)/shard_map/ppermute | solution.py:976
  3.7 8.6 %collective-permute-start.1 = (bf16[1,3,32,256]{3,2,1,0:T(8,128)(2,1)}, bf16[1,3,32,256]{3,2,1,0:T(8,128)(2,1)S(1)}, u32[]{:S(2)}, u32[]{:S(2)}) collective-permute-start(bf16[1,3,32,256]{3,2,1,0:T(8,128)(2,1)} %bitcast.15), channel_id=1, source_target_pairs={{0,16},{2,6},{4,20},{6,2},{8,24},{10,14},{12,28},{14,10},{16,0},{1... | collective-permute-start | bytes 147464 | tf_op jit(solution)/shard_map/ppermute | solution.py:1003
  6.2 12.6 %collective-permute-start.3 = (bf16[512,256]{1,0:T(8,128)(2,1)}, bf16[512,256]{1,0:T(8,128)(2,1)S(1)}, u32[]{:S(2)}, u32[]{:S(2)}) collective-permute-start(bf16[512,256]{1,0:T(8,128)(2,1)} %refs_0_), channel_id=1, source_target_pairs={{1,0},{0,1},{3,2},{2,3},{5,4},{4,5},{7,6},{6,7},{9,8},{8,9},{11,10... | collective-permute-start | bytes 786440 | tf_op jit(solution)/shard_map/ppermute | solution.py:976
  7.7 8.9 %collective-permute-start.2 = (bf16[1,32,2560]{2,1,0:T(8,128)(2,1)S(1)}, bf16[1,32,2560]{2,1,0:T(8,128)(2,1)S(1)}, u32[]{:S(2)}, u32[]{:S(2)}) collective-permute-start(bf16[1,32,2560]{2,1,0:T(8,128)(2,1)S(1)} %maximum_bitcast_fusion), channel_id=1, source_target_pairs={{0,16},{2,6},{4,20},{6,2},{8,24},{10,14},{12,28},{14,10},{16,0},{1... | collective-permute-start | bytes 491528 | tf_op jit(solution)/shard_map/ppermute | solution.py:1003
  10.7 6.1 %collective-permute-start.5 = (bf16[384,256]{1,0:T(8,128)(2,1)S(1)}, bf16[384,256]{1,0:T(8,128)(2,1)S(1)}, u32[]{:S(2)}, u32[]{:S(2)}) collective-permute-start(bf16[384,256]{1,0:T(8,128)(2,1)S(1)} %get-tuple-element.280), channel_id=1, source_target_pairs={{0,2},{2,0},{4,6},{6,4},{8,10},{10,8},{12,14},{14,12},{16,18},{18,... | collective-permute-start | bytes 589832 | tf_op jit(solution)/shard_map/ppermute | solution.py:1010
  10.8 7.7 %collective-permute-start.6 = (bf16[384,256]{1,0:T(8,128)(2,1)S(1)}, bf16[384,256]{1,0:T(8,128)(2,1)S(1)}, u32[]{:S(2)}, u32[]{:S(2)}) collective-permute-start(bf16[384,256]{1,0:T(8,128)(2,1)S(1)} %get-tuple-element.279), channel_id=1, source_target_pairs={{2,4},{4,2},{6,8},{8,6},{10,12},{12,10},{14,16},{16,14},{18,20},{2... | collective-permute-start | bytes 589832 | tf_op jit(solution)/shard_map/ppermute | solution.py:1011
  12.3 9.0 %collective-permute-start.4 = (bf16[2,3,32,256]{3,2,1,0:T(8,128)(2,1)S(1)}, bf16[2,3,32,256]{3,2,1,0:T(8,128)(2,1)S(1)}, u32[]{:S(2)}, u32[]{:S(2)}) collective-permute-start(bf16[2,3,32,256]{3,2,1,0:T(8,128)(2,1)S(1)} %constant_dynamic-update-slice_fusion), channel_id=1, source_target_pairs={{0,8},{2,18},{4,12},{6,22},{8,0},{10,26},{12,4},{14,30},{16,24},{1... | collective-permute-start | bytes 294920 | tf_op jit(solution)/shard_map/ppermute | solution.py:1003
  16.7 13.9 %collective-permute-start.11 = (bf16[2,32,2560]{2,1,0:T(8,128)(2,1)S(1)}, bf16[2,32,2560]{2,1,0:T(8,128)(2,1)S(1)}, u32[]{:S(2)}, u32[]{:S(2)}) collective-permute-start(bf16[2,32,2560]{2,1,0:T(8,128)(2,1)S(1)} %constant_dynamic-update-slice_fusion.2), channel_id=1, source_target_pairs={{0,8},{2,18},{4,12},{6,22},{8,0},{10,26},{12,4},{14,30},{16,24},{1... | collective-permute-start | bytes 983048 | tf_op jit(solution)/shard_map/ppermute | solution.py:1003
  16.8 9.3 %collective-permute-start.7 = (bf16[384,256]{1,0:T(8,128)(2,1)S(1)}, bf16[384,256]{1,0:T(8,128)(2,1)S(1)}, u32[]{:S(2)}, u32[]{:S(2)}) collective-permute-start(bf16[384,256]{1,0:T(8,128)(2,1)S(1)} %collective-permute-done.5.refs_2_), channel_id=1, source_target_pairs={{1,0},{0,1},{3,2},{2,3},{5,4},{4,5},{7,6},{6,7},{9,8},{8,9},{11,10... | collective-permute-start | bytes 589832 | tf_op jit(solution)/shard_map/ppermute | solution.py:976
  18.5 10.2 %collective-permute-start.8 = (bf16[384,256]{1,0:T(8,128)(2,1)S(1)}, bf16[384,256]{1,0:T(8,128)(2,1)S(1)}, u32[]{:S(2)}, u32[]{:S(2)}) collective-permute-start(bf16[384,256]{1,0:T(8,128)(2,1)S(1)} %collective-permute-done.6.refs_4_), channel_id=1, source_target_pairs={{1,0},{0,1},{3,2},{2,3},{5,4},{4,5},{7,6},{6,7},{9,8},{8,9},{11,10... | collective-permute-start | bytes 589832 | tf_op jit(solution)/shard_map/ppermute | solution.py:976
  21.3 9.1 %collective-permute-start.9 = (bf16[4,3,32,256]{3,2,1,0:T(8,128)(2,1)S(1)}, bf16[4,3,32,256]{3,2,1,0:T(8,128)(2,1)S(1)}, u32[]{:S(2)}, u32[]{:S(2)}) collective-permute-start(bf16[4,3,32,256]{3,2,1,0:T(8,128)(2,1)S(1)} %constant_dynamic-update-slice_fusion.4), channel_id=1, source_target_pairs={{0,4},{2,10},{4,0},{6,14},{8,12},{10,2},{12,8},{14,6},{16,20},{18,... | collective-permute-start | bytes 589832 | tf_op jit(solution)/shard_map/ppermute | solution.py:1003
  22.9 5.8 %copy-start.4 = (bf16[512,256]{1,0:T(8,128)(2,1)S(1)}, bf16[512,256]{1,0:T(8,128)(2,1)}, u32[]{:S(2)}) copy-start(bf16[512,256]{1,0:T(8,128)(2,1)} %param.26) | copy-start | bytes 786436
  22.9 9.3 %copy-start.1 = (bf16[512,256]{1,0:T(8,128)(2,1)S(1)}, bf16[512,256]{1,0:T(8,128)(2,1)}, u32[]{:S(2)}) copy-start(bf16[512,256]{1,0:T(8,128)(2,1)} %refs_0_) | copy-start | bytes 786436
  22.9 9.3 %copy-start.3 = (f32[2,256]{1,0:T(2,128)S(1)}, f32[2,256]{1,0:T(2,128)}, u32[]{:S(2)}) copy-start(f32[2,256]{1,0:T(2,128)} %bias_ref.1) | copy-start | bytes 6148
  28.7 11.3 %collective-permute-start.13 = (bf16[512,256]{1,0:T(8,128)(2,1)S(1)}, bf16[512,256]{1,0:T(8,128)(2,1)S(1)}, u32[]{:S(2)}, u32[]{:S(2)}) collective-permute-start(bf16[512,256]{1,0:T(8,128)(2,1)S(1)} %copy-done.4), channel_id=1, source_target_pairs={{1,0},{0,1},{3,2},{2,3},{5,4},{4,5},{7,6},{6,7},{9,8},{8,9},{11,10... | collective-permute-start | bytes 786440 | tf_op jit(solution)/shard_map/ppermute | solution.py:976
  30.4 1.8 %collective-permute-start.10 = (bf16[8,3,32,256]{3,2,1,0:T(8,128)(2,1)S(1)}, bf16[8,3,32,256]{3,2,1,0:T(8,128)(2,1)S(1)}, u32[]{:S(2)}, u32[]{:S(2)}) collective-permute-start(bf16[8,3,32,256]{3,2,1,0:T(8,128)(2,1)S(1)} %constant_dynamic-update-slice_fusion.6.near_ref), channel_id=1, source_target_pairs={{0,2},{2,0},{4,6},{6,4},{8,10},{10,8},{12,14},{14,12},{16,18},{18,... | collective-permute-start | bytes 1179656 | tf_op jit(solution)/shard_map/ppermute | solution.py:1003
  30.6 14.2 %collective-permute-start.15 = (bf16[4,32,2560]{2,1,0:T(8,128)(2,1)S(1)}, bf16[4,32,2560]{2,1,0:T(8,128)(2,1)S(1)}, u32[]{:S(2)}, u32[]{:S(2)}) collective-permute-start(bf16[4,32,2560]{2,1,0:T(8,128)(2,1)S(1)} %constant_dynamic-update-slice_fusion.8), channel_id=1, source_target_pairs={{0,4},{2,10},{4,0},{6,14},{8,12},{10,2},{12,8},{14,6},{16,20},{18,... | collective-permute-start | bytes 1966088 | tf_op jit(solution)/shard_map/ppermute | solution.py:1003
  32.2 1.9 %copy-start.5 = (f32[2,256]{1,0:T(2,128)S(1)}, f32[2,256]{1,0:T(2,128)}, u32[]{:S(2)}) copy-start(f32[2,256]{1,0:T(2,128)} %param.20) | copy-start | bytes 6148
  32.2 1.9 %copy-start.6 = (f32[2,256]{1,0:T(2,128)S(1)}, f32[2,256]{1,0:T(2,128)}, u32[]{:S(2)}) copy-start(f32[2,256]{1,0:T(2,128)} %param.25) | copy-start | bytes 6148
  32.2 1.9 %copy-start.7 = (f32[2,256]{1,0:T(2,128)S(1)}, f32[2,256]{1,0:T(2,128)}, u32[]{:S(2)}) copy-start(f32[2,256]{1,0:T(2,128)} %param.24) | copy-start | bytes 6148
  34.1 5.9 %collective-permute-start.12 = (f32[6,256]{1,0:T(8,128)S(1)}, f32[6,256]{1,0:T(8,128)S(1)}, u32[]{:S(2)}, u32[]{:S(2)}) collective-permute-start(f32[6,256]{1,0:T(8,128)S(1)} %pad_maximum_fusion.1), channel_id=1, source_target_pairs={{1,0},{0,1},{3,2},{2,3},{5,4},{4,5},{7,6},{6,7},{9,8},{8,9},{11,10... | collective-permute-start | bytes 18440 | tf_op jit(solution)/shard_map/ppermute | solution.py:976
  39.5 5.3 %collective-permute-start.14 = (bf16[256,256]{1,0:T(8,128)(2,1)S(1)}, bf16[256,256]{1,0:T(8,128)(2,1)S(1)}, u32[]{:S(2)}, u32[]{:S(2)}) collective-permute-start(bf16[256,256]{1,0:T(8,128)(2,1)S(1)} %get-tuple-element.160.own_ref.refs_4_), channel_id=1, source_target_pairs={{1,0},{0,1},{3,2},{2,3},{5,4},{4,5},{7,6},{6,7},{9,8},{8,9},{11,10... | collective-permute-start | bytes 393224 | tf_op jit(solution)/shard_map/ppermute | solution.py:976
  44.9 4.4 %collective-permute-start.17 = (bf16[8,32,2560]{2,1,0:T(8,128)(2,1)S(1)}, bf16[8,32,2560]{2,1,0:T(8,128)(2,1)S(1)}, u32[]{:S(2)}, u32[]{:S(2)}) collective-permute-start(bf16[8,32,2560]{2,1,0:T(8,128)(2,1)S(1)} %constant_dynamic-update-slice_fusion.12.near_ref), channel_id=1, source_target_pairs={{0,2},{2,0},{4,6},{6,4},{8,10},{10,8},{12,14},{14,12},{16,18},{18,... | collective-permute-start | bytes 3932168 | tf_op jit(solution)/shard_map/ppermute | solution.py:1003
  48.7 1.7 %copy-start.2 = (f32[1024]{0:T(1024)S(1)}, f32[1024]{0:T(1024)}, u32[]{:S(2)}) copy-start(f32[1024]{0:T(1024)} %param.22) | copy-start | bytes 12292
  48.8 7.9 %collective-permute-start.16 = (bf16[256,256]{1,0:T(8,128)(2,1)S(1)}, bf16[256,256]{1,0:T(8,128)(2,1)S(1)}, u32[]{:S(2)}, u32[]{:S(2)}) collective-permute-start(bf16[256,256]{1,0:T(8,128)(2,1)S(1)} %get-tuple-element.167.own_ref.refs_5_), channel_id=1, source_target_pairs={{1,0},{0,1},{3,2},{2,3},{5,4},{4,5},{7,6},{6,7},{9,8},{8,9},{11,10... | collective-permute-start | bytes 393224 | tf_op jit(solution)/shard_map/ppermute | solution.py:976
  49.3 4.9 %copy-start = (bf16[4,512,1024]{2,1,0:T(8,128)(2,1)S(1)}, bf16[4,512,1024]{2,1,0:T(8,128)(2,1)}, u32[]{:S(2)}) copy-start(bf16[4,512,1024]{2,1,0:T(8,128)(2,1)} %band_ref.3) | copy-start | bytes 12582916
  52.7 9.8 %collective-permute-start.18 = (bf16[256,512]{1,0:T(8,128)(2,1)S(1)}, bf16[256,512]{1,0:T(8,128)(2,1)S(1)}, u32[]{:S(2)}, u32[]{:S(2)}) collective-permute-start(bf16[256,512]{1,0:T(8,128)(2,1)S(1)} %get-tuple-element.174.part_ref), channel_id=1, source_target_pairs={{1,0},{0,1},{3,2},{2,3},{5,4},{4,5},{7,6},{6,7},{9,8},{8,9},{11,10... | collective-permute-start | bytes 786440 | tf_op jit(solution)/shard_map/ppermute | solution.py:976
  58.9 8.2 %collective-permute-start.19 = (bf16[256,512]{1,0:T(8,128)(2,1)S(1)}, bf16[256,512]{1,0:T(8,128)(2,1)S(1)}, u32[]{:S(2)}, u32[]{:S(2)}) collective-permute-start(bf16[256,512]{1,0:T(8,128)(2,1)S(1)} %get-tuple-element.177.part_ref), channel_id=1, source_target_pairs={{1,0},{0,1},{3,2},{2,3},{5,4},{4,5},{7,6},{6,7},{9,8},{8,9},{11,10... | collective-permute-start | bytes 786440 | tf_op jit(solution)/shard_map/ppermute | solution.py:976
  65.0 9.3 %collective-permute-start.20 = (bf16[256,512]{1,0:T(8,128)(2,1)S(1)}, bf16[256,512]{1,0:T(8,128)(2,1)S(1)}, u32[]{:S(2)}, u32[]{:S(2)}) collective-permute-start(bf16[256,512]{1,0:T(8,128)(2,1)S(1)} %get-tuple-element.199.part_ref), channel_id=1, source_target_pairs={{1,0},{0,1},{3,2},{2,3},{5,4},{4,5},{7,6},{6,7},{9,8},{8,9},{11,10... | collective-permute-start | bytes 786440 | tf_op jit(solution)/shard_map/ppermute | solution.py:976
  72.9 6.1 %collective-permute-start.21 = (bf16[512,1024]{1,0:T(8,128)(2,1)S(1)}, bf16[512,1024]{1,0:T(8,128)(2,1)S(1)}, u32[]{:S(2)}, u32[]{:S(2)}) collective-permute-start(bf16[512,1024]{1,0:T(8,128)(2,1)S(1)} %get-tuple-element.207), channel_id=1, source_target_pairs={{0,2},{2,0},{4,6},{6,4},{8,10},{10,8},{12,14},{14,12},{16,18},{18,... | collective-permute-start | bytes 3145736 | tf_op jit(solution)/shard_map/ppermute | solution.py:1003
  73.0 10.2 %collective-permute-start.22 = (bf16[256,512]{1,0:T(8,128)(2,1)S(1)}, bf16[256,512]{1,0:T(8,128)(2,1)S(1)}, u32[]{:S(2)}, u32[]{:S(2)}) collective-permute-start(bf16[256,512]{1,0:T(8,128)(2,1)S(1)} %get-tuple-element.211.part_ref), channel_id=1, source_target_pairs={{1,0},{0,1},{3,2},{2,3},{5,4},{4,5},{7,6},{6,7},{9,8},{8,9},{11,10... | collective-permute-start | bytes 786440 | tf_op jit(solution)/shard_map/ppermute | solution.py:976
  79.2 9.5 %collective-permute-start.23 = (bf16[256,1024]{1,0:T(8,128)(2,1)S(1)}, bf16[256,1024]{1,0:T(8,128)(2,1)S(1)}, u32[]{:S(2)}, u32[]{:S(2)}) collective-permute-start(bf16[256,1024]{1,0:T(8,128)(2,1)S(1)} %get-tuple-element.221), channel_id=1, source_target_pairs={{0,4},{2,10},{4,0},{6,14},{8,12},{10,2},{12,8},{14,6},{16,20},{18,... | collective-permute-start | bytes 1572872 | tf_op jit(solution)/shard_map/ppermute | solution.py:1003
  90.7 3.2 %collective-permute-start.24 = (bf16[1056,256]{1,0:T(8,128)(2,1)S(1)}, bf16[1056,256]{1,0:T(8,128)(2,1)S(1)}, u32[]{:S(2)}, u32[]{:S(2)}) collective-permute-start(bf16[1056,256]{1,0:T(8,128)(2,1)S(1)} %get-tuple-element.239), channel_id=1, source_target_pairs={{0,2},{2,0},{4,6},{6,4},{8,10},{10,8},{12,14},{14,12},{16,18},{18,... | collective-permute-start | bytes 1622024 | tf_op jit(solution)/shard_map/ppermute | solution.py:1003
  93.0 12.0 %collective-permute-start.26 = (bf16[768,256]{1,0:T(8,128)(2,1)S(1)}, bf16[768,256]{1,0:T(8,128)(2,1)S(1)}, u32[]{:S(2)}, u32[]{:S(2)}) collective-permute-start(bf16[768,256]{1,0:T(8,128)(2,1)S(1)} %get-tuple-element.251), channel_id=1, source_target_pairs={{1,0},{0,1},{3,2},{2,3},{5,4},{4,5},{7,6},{6,7},{9,8},{8,9},{11,10... | collective-permute-start | bytes 1179656 | tf_op jit(solution)/shard_map/ppermute | solution.py:976
  94.1 8.3 %collective-permute-start.25 = (bf16[544,256]{1,0:T(8,128)(2,1)S(1)}, bf16[544,256]{1,0:T(8,128)(2,1)S(1)}, u32[]{:S(2)}, u32[]{:S(2)}) collective-permute-start(bf16[544,256]{1,0:T(8,128)(2,1)S(1)} %get-tuple-element.246), channel_id=1, source_target_pairs={{0,4},{2,10},{4,0},{6,14},{8,12},{10,2},{12,8},{14,6},{16,20},{18,... | collective-permute-start | bytes 835592 | tf_op jit(solution)/shard_map/ppermute | solution.py:1003
  95.4 10.4 %collective-permute-start.27 = (bf16[128,1024]{1,0:T(8,128)(2,1)S(1)}, bf16[128,1024]{1,0:T(8,128)(2,1)S(1)}, u32[]{:S(2)}, u32[]{:S(2)}) collective-permute-start(bf16[128,1024]{1,0:T(8,128)(2,1)S(1)} %get-tuple-element.254), channel_id=1, source_target_pairs={{0,8},{2,18},{4,12},{6,22},{8,0},{10,26},{12,4},{14,30},{16,24},{1... | collective-permute-start | bytes 786440 | tf_op jit(solution)/shard_map/ppermute | solution.py:1003
  96.4 17.0 %collective-permute-start.31 = (bf16[512,256]{1,0:T(8,128)(2,1)S(1)}, bf16[512,256]{1,0:T(8,128)(2,1)S(1)}, u32[]{:S(2)}, u32[]{:S(2)}) collective-permute-start(bf16[512,256]{1,0:T(8,128)(2,1)S(1)} %get-tuple-element.264), channel_id=1, source_target_pairs={{1,0},{0,1},{3,2},{2,3},{5,4},{4,5},{7,6},{6,7},{9,8},{8,9},{11,10... | collective-permute-start | bytes 786440 | tf_op jit(solution)/shard_map/ppermute | solution.py:976
  102.5 7.8 %collective-permute-start.28 = (bf16[288,256]{1,0:T(8,128)(2,1)S(1)}, bf16[288,256]{1,0:T(8,128)(2,1)S(1)}, u32[]{:S(2)}, u32[]{:S(2)}) collective-permute-start(bf16[288,256]{1,0:T(8,128)(2,1)S(1)} %get-tuple-element.257), channel_id=1, source_target_pairs={{0,8},{2,18},{4,12},{6,22},{8,0},{10,26},{12,4},{14,30},{16,24},{1... | collective-permute-start | bytes 442376 | tf_op jit(solution)/shard_map/ppermute | solution.py:1003
  105.0 8.4 %collective-permute-start.29 = (bf16[384,256]{1,0:T(8,128)(2,1)S(1)}, bf16[384,256]{1,0:T(8,128)(2,1)S(1)}, u32[]{:S(2)}, u32[]{:S(2)}) collective-permute-start(bf16[384,256]{1,0:T(8,128)(2,1)S(1)} %get-tuple-element.252), channel_id=1, source_target_pairs={{0,2},{2,0},{4,6},{6,4},{8,10},{10,8},{12,14},{14,12},{16,18},{18,... | collective-permute-start | bytes 589832 | tf_op jit(solution)/shard_map/ppermute | solution.py:1010
  105.1 8.3 %collective-permute-start.30 = (bf16[384,256]{1,0:T(8,128)(2,1)S(1)}, bf16[384,256]{1,0:T(8,128)(2,1)S(1)}, u32[]{:S(2)}, u32[]{:S(2)}) collective-permute-start(bf16[384,256]{1,0:T(8,128)(2,1)S(1)} %get-tuple-element.262), channel_id=1, source_target_pairs={{2,4},{4,2},{6,8},{8,6},{10,12},{12,10},{14,16},{16,14},{18,20},{2... | collective-permute-start | bytes 589832 | tf_op jit(solution)/shard_map/ppermute | solution.py:1011
  105.8 11.7 %collective-permute-start.32 = (bf16[64,1024]{1,0:T(8,128)(2,1)S(1)}, bf16[64,1024]{1,0:T(8,128)(2,1)S(1)}, u32[]{:S(2)}, u32[]{:S(2)}) collective-permute-start(bf16[64,1024]{1,0:T(8,128)(2,1)S(1)} %get-tuple-element.266), channel_id=1, source_target_pairs={{0,16},{2,6},{4,20},{6,2},{8,24},{10,14},{12,28},{14,10},{16,0},{1... | collective-permute-start | bytes 393224 | tf_op jit(solution)/shard_map/ppermute | solution.py:1003
  110.3 8.1 %collective-permute-start.33 = (bf16[160,256]{1,0:T(8,128)(2,1)S(1)}, bf16[160,256]{1,0:T(8,128)(2,1)S(1)}, u32[]{:S(2)}, u32[]{:S(2)}) collective-permute-start(bf16[160,256]{1,0:T(8,128)(2,1)S(1)} %get-tuple-element.269), channel_id=1, source_target_pairs={{0,16},{2,6},{4,20},{6,2},{8,24},{10,14},{12,28},{14,10},{16,0},{1... | collective-permute-start | bytes 245768 | tf_op jit(solution)/shard_map/ppermute | solution.py:1003

commit v9 on v8

--- a/solution.py
+++ b/solution.py
@@ -1107,7 +1107,6 @@
         dense = to_dense(after(banded, *needed), lengths, fill, token_count, chunk)
         return dense
 
-    prev_logits = pltpu.with_memory_space_constraint(prev_logits, pltpu.HBM)
 
     out_turned = out_weight.T
     out_other = others(out_turned)

time: 119 us -> 121 us (1.017)
  local copies, waits for them, and re-layouts: 2.14 us -> 4.33 us
  starting transfers between devices: 40 us -> 41.6 us
  Pallas kernels: 62.4 us -> 61.1 us
    unnamed x25 -> x29, local copies, waits for them, and re-layouts: 0.96 us -> 3.16 us
    ppermute x16, starting transfers between devices: 21.7 us -> 23.2 us  [with_partner(): lax.ppermute(x, 'row', [(i, i ^ orders[i % 2][step]) for i in range(count)])]
    pallas_call x4, Pallas kernels: 11.2 us -> 9.91 us  [to_dense(): pl.pallas_call(functools.partial(dense_kernel, fill, token_count, offset)...]
  transfers between devices with their start and end apart: 34 -> 34, of which waited for: 8 -> 7; matrix products, arithmetic and copies ran while one was open for 3% -> 3% of each run, Pallas kernels for 50% -> 49%
where the time goes in v9:
time: 121 us; the launch traced here: 120 us
  Pallas kernels  61.1 us (50%)
  starting transfers between devices  41.6 us (34%)
  waiting for transfers between devices  11.1 us (9%)
  local copies, waits for them, and re-layouts  4.33 us (4%)
    ppermute x16, starting transfers between devices, with_partner(): lax.ppermute(x, 'row', [(i, i ^ orders[i % 2][step]) for i in range(count)])  23.2 us
    ppermute x14, starting transfers between devices, from_next(): lax.ppermute(x, axis, [((i + step) % count, i) for i in range(count)])  16.9 us
    pallas_call x3, Pallas kernels, to_band(): pl.pallas_call(functools.partial(band_kernel, masked, len(chunks)), grid=...  11 us
    pallas_call x4, Pallas kernels, to_dense(): pl.pallas_call(functools.partial(dense_kernel, fill, token_count, offset)...  9.91 us
    pallas_call x2, Pallas kernels, attend_backward(): pl.pallas_call(functools.partial(backward_kernel, offset, last), grid=(co...  8.72 us
    pallas_call x2, Pallas kernels, attend_forward(): pl.pallas_call(functools.partial(forward_kernel, offset), grid=(count //...  7.42 us
    ppermute x16, waiting for transfers between devices, with_partner(): lax.ppermute(x, 'row', [(i, i ^ orders[i % 2][step]) for i in range(count)])  5.85 us
    ppermute x14, waiting for transfers between devices, from_next(): lax.ppermute(x, axis, [((i + step) % count, i) for i in range(count)])  5.24 us
  transfers between devices with their start and end apart: 34, of which 7 were waited for; matrix products, arithmetic and copies ran while one was open for 3% of the time, Pallas kernels for 49%

profile of v9, /device:TPU:0, one launch (start us, length us, event | category | flops | bytes accessed | tf_op | source)
XLA Modules:
  0.0 120.4 jit_solution(13434129877358938906)
XLA Ops:
  0.7 3.0 %collective-permute-start = (bf16[32,256]{1,0:T(8,128)(2,1)}, bf16[32,256]{1,0:T(8,128)(2,1)S(1)}, u32[]{:S(2)}, u32[]{:S(2)}) collective-permute-start(bf16[32,256]{1,0:T(8,128)(2,1)} %bitcast.17), channel_id=1, source_target_pairs={{1,0},{0,1},{3,2},{2,3},{5,4},{4,5},{7,6},{6,7},{9,8},{8,9},{11,10... | collective-permute-start | bytes 49160 | tf_op jit(solution)/shard_map/ppermute | solution.py:976
  3.7 2.6 %collective-permute-start.1 = (bf16[1,3,32,256]{3,2,1,0:T(8,128)(2,1)}, bf16[1,3,32,256]{3,2,1,0:T(8,128)(2,1)S(1)}, u32[]{:S(2)}, u32[]{:S(2)}) collective-permute-start(bf16[1,3,32,256]{3,2,1,0:T(8,128)(2,1)} %bitcast.15), channel_id=1, source_target_pairs={{0,16},{2,6},{4,20},{6,2},{8,24},{10,14},{12,28},{14,10},{16,0},{1... | collective-permute-start | bytes 147464 | tf_op jit(solution)/shard_map/ppermute | solution.py:1003
  6.2 0.5 collective-permute-start.3
  6.8 0.9 maximum_bitcast_fusion
  7.7 1.9 %collective-permute-start.2 = (bf16[1,32,2560]{2,1,0:T(8,128)(2,1)S(1)}, bf16[1,32,2560]{2,1,0:T(8,128)(2,1)S(1)}, u32[]{:S(2)}, u32[]{:S(2)}) collective-permute-start(bf16[1,32,2560]{2,1,0:T(8,128)(2,1)S(1)} %maximum_bitcast_fusion), channel_id=1, source_target_pairs={{0,16},{2,6},{4,20},{6,2},{8,24},{10,14},{12,28},{14,10},{16,0},{1... | collective-permute-start | bytes 491528 | tf_op jit(solution)/shard_map/ppermute | solution.py:1003
  9.7 1.0 constant_dynamic-slice_fusion
  10.8 0.7 collective-permute-start.6
  11.5 0.8 constant_dynamic-update-slice_fusion.1
  12.3 4.4 %collective-permute-start.4 = (bf16[2,3,32,256]{3,2,1,0:T(8,128)(2,1)S(1)}, bf16[2,3,32,256]{3,2,1,0:T(8,128)(2,1)S(1)}, u32[]{:S(2)}, u32[]{:S(2)}) collective-permute-start(bf16[2,3,32,256]{3,2,1,0:T(8,128)(2,1)S(1)} %constant_dynamic-update-slice_fusion), channel_id=1, source_target_pairs={{0,8},{2,18},{4,12},{6,22},{8,0},{10,26},{12,4},{14,30},{16,24},{1... | collective-permute-start | bytes 294920 | tf_op jit(solution)/shard_map/ppermute | solution.py:1003
  16.8 1.7 %collective-permute-start.7 = (bf16[384,256]{1,0:T(8,128)(2,1)S(1)}, bf16[384,256]{1,0:T(8,128)(2,1)S(1)}, u32[]{:S(2)}, u32[]{:S(2)}) collective-permute-start(bf16[384,256]{1,0:T(8,128)(2,1)S(1)} %collective-permute-done.5.refs_2_), channel_id=1, source_target_pairs={{1,0},{0,1},{3,2},{2,3},{5,4},{4,5},{7,6},{6,7},{9,8},{8,9},{11,10... | collective-permute-start | bytes 589832 | tf_op jit(solution)/shard_map/ppermute | solution.py:976
  18.5 0.4 collective-permute-start.8
  18.9 2.4 %collective-permute-done.4 = bf16[2,3,32,256]{3,2,1,0:T(8,128)(2,1)S(1)} collective-permute-done((bf16[2,3,32,256]{3,2,1,0:T(8,128)(2,1)S(1)}, bf16[2,3,32,256]{3,2,1,0:T(8,128)(2,1)S(1)}, u32[]{:S(2)}, u32[]{:S(2)}) %collective-permute-start.4) | collective-permute-done | bytes 98336 | tf_op jit(solution)/shard_map/ppermute | solution.py:1003
  21.3 1.5 %collective-permute-start.9 = (bf16[4,3,32,256]{3,2,1,0:T(8,128)(2,1)S(1)}, bf16[4,3,32,256]{3,2,1,0:T(8,128)(2,1)S(1)}, u32[]{:S(2)}, u32[]{:S(2)}) collective-permute-start(bf16[4,3,32,256]{3,2,1,0:T(8,128)(2,1)S(1)} %constant_dynamic-update-slice_fusion.4), channel_id=1, source_target_pairs={{0,4},{2,10},{4,0},{6,14},{8,12},{10,2},{12,8},{14,6},{16,20},{18,... | collective-permute-start | bytes 589832 | tf_op jit(solution)/shard_map/ppermute | solution.py:1003
  22.9 2.2 %copy-done.1 = bf16[4,512,1024]{2,1,0:T(8,128)(2,1)S(1)} copy-done((bf16[4,512,1024]{2,1,0:T(8,128)(2,1)S(1)}, bf16[4,512,1024]{2,1,0:T(8,128)(2,1)}, u32[]{:S(2)}) %copy-start.1) | copy-done | bytes 4194328
  25.1 2.5 %to_dense.4.prev_ref = bf16[4,256,1152]{2,1,0:T(8,128)(2,1)S(1)} custom-call(s32[34]{0:T(128)S(1)} %pad_add_fusion.lengths_ref, bf16[4,512,1024]{2,1,0:T(8,128)(2,1)S(1)} %copy-done.1), custom_call_target="tpu_custom_call" | custom-call | flops 8000000000 | tf_op jit(solution)/shard_map/to_dense/pallas_call | solution.py:102
  27.6 1.1 collective-permute-done.8.refs_5_
  28.7 1.6 %collective-permute-start.13 = (bf16[512,256]{1,0:T(8,128)(2,1)S(1)}, bf16[512,256]{1,0:T(8,128)(2,1)S(1)}, u32[]{:S(2)}, u32[]{:S(2)}) collective-permute-start(bf16[512,256]{1,0:T(8,128)(2,1)S(1)} %copy-done.6), channel_id=1, source_target_pairs={{1,0},{0,1},{3,2},{2,3},{5,4},{4,5},{7,6},{6,7},{9,8},{8,9},{11,10... | collective-permute-start | bytes 786440 | tf_op jit(solution)/shard_map/ppermute | solution.py:976
  30.4 0.2 collective-permute-start.10
  30.6 2.9 %collective-permute-start.15 = (bf16[4,32,2560]{2,1,0:T(8,128)(2,1)S(1)}, bf16[4,32,2560]{2,1,0:T(8,128)(2,1)S(1)}, u32[]{:S(2)}, u32[]{:S(2)}) collective-permute-start(bf16[4,32,2560]{2,1,0:T(8,128)(2,1)S(1)} %constant_dynamic-update-slice_fusion.8), channel_id=1, source_target_pairs={{0,4},{2,10},{4,0},{6,14},{8,12},{10,2},{12,8},{14,6},{16,20},{18,... | collective-permute-start | bytes 1966088 | tf_op jit(solution)/shard_map/ppermute | solution.py:1003
  33.6 1.9 %project.1 = (bf16[512,512]{1,0:T(8,128)(2,1)S(1)}, bf16[512,256]{1,0:T(8,128)(2,1)S(1)}, bf16[1536,256]{1,0:T(8,128)(2,1)S(1)}, bf16[1536,256]{1,0:T(8,128)(2,1...) custom-call(s32[16]{0:T(128)S(1)} %fusion.7.slot_ref, ...), custom_call_target="tpu_custom_call" | custom-call | flops 2000000000 | tf_op jit(solution)/shard_map/project/pallas_call | solution.py:245
  35.5 1.8 %collective-permute-start.12 = (f32[6,256]{1,0:T(8,128)S(1)}, f32[6,256]{1,0:T(8,128)S(1)}, u32[]{:S(2)}, u32[]{:S(2)}) collective-permute-start(f32[6,256]{1,0:T(8,128)S(1)} %pad_maximum_fusion.1), channel_id=1, source_target_pairs={{1,0},{0,1},{3,2},{2,3},{5,4},{4,5},{7,6},{6,7},{9,8},{8,9},{11,10... | collective-permute-start | bytes 18440 | tf_op jit(solution)/shard_map/ppermute | solution.py:976
  37.3 3.7 %attend_forward.2 = (bf16[4,256,1152]{2,1,0:T(8,128)(2,1)S(1)}, bf16[4,256,1152]{2,1,0:T(8,128)(2,1)S(1)}, bf16[256,256]{1,0:T(8,128)(2,1)S(1)}) custom-call(bf16[512,256]{1,0:T(8,128)(2,1)S(1)} %get-tuple-element.166.query_ref, bf16[1536,256]{1,0:T(8,128)(2,1)S(1)} %get-tuple-element.157.key_ref, bf16[1536,256]{1,0:T(8,128)(2,1)S(1)} %get-tuple-element.158.value_ref, ...), custom_call_target="tpu_custom_call" | custom-call | flops 3800000000 | tf_op jit(solution)/shard_map/attend_forward/pallas_call | solution.py:309
  41.0 0.4 collective-permute-start.14
  41.5 2.5 %to_dense.5.prev_ref = bf16[4,256,1152]{2,1,0:T(8,128)(2,1)S(1)} custom-call(s32[34]{0:T(128)S(1)} %pad_add_fusion.lengths_ref, bf16[4,512,1024]{2,1,0:T(8,128)(2,1)S(1)} %copy-done.2), custom_call_target="tpu_custom_call" | custom-call | flops 1000000000 | tf_op jit(solution)/shard_map/to_dense/pallas_call | solution.py:102
  44.0 2.1 %collective-permute-done.14.other_ref = bf16[256,256]{1,0:T(8,128)(2,1)S(1)} collective-permute-done((bf16[256,256]{1,0:T(8,128)(2,1)S(1)}, bf16[256,256]{1,0:T(8,128)(2,1)S(1)}, u32[]{:S(2)}, u32[]{:S(2)}) %collective-permute-start.14) | collective-permute-done | bytes 131104 | tf_op jit(solution)/shard_map/ppermute | solution.py:976
  46.2 3.7 %attend_forward.3 = (bf16[4,256,1152]{2,1,0:T(8,128)(2,1)S(1)}, bf16[4,256,1152]{2,1,0:T(8,128)(2,1)S(1)}, bf16[256,256]{1,0:T(8,128)(2,1)S(1)}) custom-call(bf16[512,256]{1,0:T(8,128)(2,1)S(1)} %get-tuple-element.166.query_ref, bf16[1536,256]{1,0:T(8,128)(2,1)S(1)} %get-tuple-element.157.key_ref, bf16[1536,256]{1,0:T(8,128)(2,1)S(1)} %get-tuple-element.158.value_ref, ...), custom_call_target="tpu_custom_call" | custom-call | flops 3800000000 | tf_op jit(solution)/shard_map/attend_forward/pallas_call | solution.py:309
  50.0 0.4 collective-permute-start.16
  50.3 1.1 in_order.1
  51.4 2.2 %feed_first.2 = (f32[256,512]{1,0:T(8,128)S(1)}, f32[256,1]{1,0:T(8,128)S(1)}, bf16[256,512]{1,0:T(8,128)(2,1)S(1)}, bf16[256,1024]{1,0:T(8,128)(2,1)S(1)}, bf16...) custom-call(bf16[256,256]{1,0:T(8,128)(2,1)S(1)} %get-tuple-element.160.own_ref.refs_4_, ...), custom_call_target="tpu_custom_call" | custom-call | flops 1000000000 | tf_op jit(solution)/shard_map/feed_first/pallas_call | solution.py:508
  53.6 1.8 %collective-permute-start.18 = (bf16[256,512]{1,0:T(8,128)(2,1)S(1)}, bf16[256,512]{1,0:T(8,128)(2,1)S(1)}, u32[]{:S(2)}, u32[]{:S(2)}) collective-permute-start(bf16[256,512]{1,0:T(8,128)(2,1)S(1)} %get-tuple-element.174.part_ref), channel_id=1, source_target_pairs={{1,0},{0,1},{3,2},{2,3},{5,4},{4,5},{7,6},{6,7},{9,8},{8,9},{11,10... | collective-permute-start | bytes 786440 | tf_op jit(solution)/shard_map/ppermute | solution.py:976
  55.4 2.5 %to_dense.6.logit_ref = bf16[4,256,1152]{2,1,0:T(8,128)(2,1)S(1)} custom-call(s32[34]{0:T(128)S(1)} %pad_add_fusion.lengths_ref, bf16[4,512,1024]{2,1,0:T(8,128)(2,1)S(1)} %copy-done), custom_call_target="tpu_custom_call" | custom-call | flops 1000000000 | tf_op jit(solution)/shard_map/to_dense/pallas_call | solution.py:102
  57.9 2.2 %feed_first.3 = (f32[256,512]{1,0:T(8,128)S(1)}, f32[256,1]{1,0:T(8,128)S(1)}, bf16[256,512]{1,0:T(8,128)(2,1)S(1)}, bf16[256,1024]{1,0:T(8,128)(2,1)S(1)}, bf16...) custom-call(bf16[256,256]{1,0:T(8,128)(2,1)S(1)} %get-tuple-element.167.own_ref.refs_5_, ...), custom_call_target="tpu_custom_call" | custom-call | flops 1000000000 | tf_op jit(solution)/shard_map/feed_first/pallas_call | solution.py:508
  60.1 0.4 collective-permute-start.19
  60.5 3.0 %to_band.3.refs_1_ = bf16[4,512,1024]{2,1,0:T(8,128)(2,1)} custom-call(bf16[4,256,1152]{2,1,0:T(8,128)(2,1)S(1)} %get-tuple-element.178.refs_0_), custom_call_target="tpu_custom_call" | custom-call | flops 5000000000 | tf_op jit(solution)/shard_map/to_band/pallas_call | solution.py:151
  63.5 2.5 %feed_second.2 = (f32[16,256]{1,0:T(8,128)S(1)}, bf16[512,256]{1,0:T(8,128)(2,1)}, f32[256,512]{1,0:T(8,128)S(1)}, bf16[256,512]{1,0:T(8,128)(2,1)S(1)}, bf16[25...) custom-call(f32[16,256]{1,0:T(8,128)S(1)} %broadcast_in_dim.18.start_ref, ...), custom_call_target="tpu_custom_call" | custom-call | flops 700000000 | tf_op jit(solution)/shard_map/feed_second/pallas_call | solution.py:587
  65.9 1.7 %collective-permute-start.20 = (bf16[256,512]{1,0:T(8,128)(2,1)S(1)}, bf16[256,512]{1,0:T(8,128)(2,1)S(1)}, u32[]{:S(2)}, u32[]{:S(2)}) collective-permute-start(bf16[256,512]{1,0:T(8,128)(2,1)S(1)} %get-tuple-element.199.part_ref), channel_id=1, source_target_pairs={{1,0},{0,1},{3,2},{2,3},{5,4},{4,5},{7,6},{6,7},{9,8},{8,9},{11,10... | collective-permute-start | bytes 786440 | tf_op jit(solution)/shard_map/ppermute | solution.py:976
  67.7 0.7 collective-permute-done.19.recv_ref
  68.4 2.5 %feed_second.3 = (f32[16,256]{1,0:T(8,128)S(1)}, bf16[512,256]{1,0:T(8,128)(2,1)}, f32[256,512]{1,0:T(8,128)S(1)}, bf16[256,512]{1,0:T(8,128)(2,1)S(1)}, bf16[25...) custom-call(f32[16,256]{1,0:T(8,128)S(1)} %get-tuple-element.182.start_ref, ...), custom_call_target="tpu_custom_call", output_to_operand_aliasing={{1}: (9, {})} | custom-call | flops 700000000 | tf_op jit(solution)/shard_map/feed_second/pallas_call | solution.py:587
  70.9 3.3 %feed_grads.1 = (f32[512,1024]{1,0:T(8,128)S(1)}, bf16[512,1024]{1,0:T(8,128)(2,1)S(1)}) custom-call(s32[16]{0:T(128)S(1)} %and_select_fusion.block_ref, bf16[256,512]{1,0:T(8,128)(2,1)S(1)} %get-tuple-element.189.refs_0_, bf16[256,512]{1,0:T(8,128)(2,1)S(1)} %get-tuple-element.190.refs_1_, bf16[256,512]{1,0:T(8,128)(2,1)S(1)} %get-tuple-element.191.refs_2_, ...), custom_call_target="tpu_custom_call" | custom-call | flops 1000000000 | tf_op jit(solution)/shard_map/feed_grads/pallas_call | solution.py:708
  74.3 1.1 collective-permute-start.22
  75.4 0.7 feed_third.2
  76.2 4.0 %attend_backward.2 = (bf16[4,256,1152]{2,1,0:T(8,128)(2,1)S(1)}, bf16[256,256]{1,0:T(8,128)(2,1)S(1)}, f32[256,1536]{1,0:T(8,128)S(1)}, f32[256,1536]{1,0:T(8,128)S(1)}) custom-call(bf16[256,256]{1,0:T(8,128)(2,1)S(1)} %get-tuple-element.203.grad_ref, bf16[512,256]{1,0:T(8,128)(2,1)S(1)} %get-tuple-element.166.query_ref, ...), custom_call_target="tpu_custom_call" | custom-call | flops 20000000000 | tf_op jit(solution)/shard_map/attend_backward/pallas_call | solution.py:404
  80.2 0.2 fold.6
  80.5 1.8 %collective-permute-start.23 = (bf16[256,1024]{1,0:T(8,128)(2,1)S(1)}, bf16[256,1024]{1,0:T(8,128)(2,1)S(1)}, u32[]{:S(2)}, u32[]{:S(2)}) collective-permute-start(bf16[256,1024]{1,0:T(8,128)(2,1)S(1)} %get-tuple-element.221), channel_id=1, source_target_pairs={{0,4},{2,10},{4,0},{6,14},{8,12},{10,2},{12,8},{14,6},{16,20},{18,... | collective-permute-start | bytes 1572872 | tf_op jit(solution)/shard_map/ppermute | solution.py:1003
  82.2 2.5 %to_dense.7.logit_ref = bf16[4,256,1152]{2,1,0:T(8,128)(2,1)S(1)} custom-call(s32[34]{0:T(128)S(1)} %pad_add_fusion.lengths_ref, bf16[4,512,1024]{2,1,0:T(8,128)(2,1)S(1)} %copy-done), custom_call_target="tpu_custom_call" | custom-call | flops 1000000000 | tf_op jit(solution)/shard_map/to_dense/pallas_call | solution.py:102
  84.7 0.8 feed_third.3
  85.5 4.7 %attend_backward.3 = (bf16[4,256,1152]{2,1,0:T(8,128)(2,1)S(1)}, bf16[256,256]{1,0:T(8,128)(2,1)S(1)}, bf16[1536,256]{1,0:T(8,128)(2,1)S(1)}, bf16[1536,256]{1,0:T(8,128)(2,1)S(1)}) custom-call(bf16[256,256]{1,0:T(8,128)(2,1)S(1)} %get-tuple-element.215.grad_ref, bf16[512,256]{1,0:T(8,128)(2,1)S(1)} %get-tuple-element.166.query_ref, ...), custom_call_target="tpu_custom_call" | custom-call | flops 3000000000 | tf_op jit(solution)/shard_map/attend_backward/pallas_call | solution.py:404
  90.3 1.9 %project_grads.1 = (f32[1024,256]{1,0:T(8,128)S(1)}, bf16[1056,256]{1,0:T(8,128)(2,1)S(1)}, f32[16,256]{1,0:T(8,128)S(1)}) custom-call(s32[16]{0:T(128)S(1)} %and_select_fusion.block_ref, f32[16,256]{1,0:T(8,128)S(1)} %get-tuple-element.223.start_ref, bf16[256,256]{1,0:T(8,128)(2,1)S(1)} %get-tuple-element.205.refs_0_, ...), custom_call_target="tpu_custom_call" | custom-call | flops 600000000 | tf_op jit(solution)/shard_map/project_grads/pallas_call | solution.py:765
  92.3 2.1 %token_grads.1 = (f32[512,256]{1,0:T(8,128)S(1)}, f32[768,256]{1,0:T(8,128)S(1)}, bf16[512,256]{1,0:T(8,128)(2,1)S(1)}, bf16[768,256]{1,0:T(8,128)(2,1)S(1)}) custom-call(s32[1]{0:T(128)} %bitcast.even_ref, bf16[256,256]{1,0:T(8,128)(2,1)S(1)} %get-tuple-element.205.refs_0_, bf16[256,256]{1,0:T(8,128)(2,1)S(1)} %get-tuple-element.219.refs_1_, ...), custom_call_target="tpu_custom_call" | custom-call | flops 5000000000 | tf_op jit(solution)/shard_map/token_grads/pallas_call | solution.py:909
  94.5 1.0 collective-permute-start.26
  95.6 1.3 %collective-permute-start.25 = (bf16[544,256]{1,0:T(8,128)(2,1)S(1)}, bf16[544,256]{1,0:T(8,128)(2,1)S(1)}, u32[]{:S(2)}, u32[]{:S(2)}) collective-permute-start(bf16[544,256]{1,0:T(8,128)(2,1)S(1)} %get-tuple-element.246), channel_id=1, source_target_pairs={{0,4},{2,10},{4,0},{6,14},{8,12},{10,2},{12,8},{14,6},{16,20},{18,... | collective-permute-start | bytes 835592 | tf_op jit(solution)/shard_map/ppermute | solution.py:1003
  96.9 0.7 collective-permute-start.27
  97.6 1.1 collective-permute-start.31
  98.7 5.0 %to_band.4 = bf16[4,512,1024]{2,1,0:T(8,128)(2,1)} custom-call(bf16[4,256,1152]{2,1,0:T(8,128)(2,1)S(1)} %get-tuple-element.243.refs_0_, bf16[4,256,1152]{2,1,0:T(8,128)(2,1)S(1)} %get-tuple-element.244.refs_1_), custom_call_target="tpu_custom_call" | custom-call | flops 300000000 | tf_op jit(solution)/shard_map/to_band/pallas_call | solution.py:151
  103.7 1.4 %collective-permute-start.28 = (bf16[288,256]{1,0:T(8,128)(2,1)S(1)}, bf16[288,256]{1,0:T(8,128)(2,1)S(1)}, u32[]{:S(2)}, u32[]{:S(2)}) collective-permute-start(bf16[288,256]{1,0:T(8,128)(2,1)S(1)} %get-tuple-element.257), channel_id=1, source_target_pairs={{0,8},{2,18},{4,12},{6,22},{8,0},{10,26},{12,4},{14,30},{16,24},{1... | collective-permute-start | bytes 442376 | tf_op jit(solution)/shard_map/ppermute | solution.py:1003
  105.1 1.3 %collective-permute-done.26.refs_0_ = bf16[768,256]{1,0:T(8,128)(2,1)S(1)} collective-permute-done((bf16[768,256]{1,0:T(8,128)(2,1)S(1)}, bf16[768,256]{1,0:T(8,128)(2,1)S(1)}, u32[]{:S(2)}, u32[]{:S(2)}) %collective-permute-start.26) | collective-permute-done | bytes 393248 | tf_op jit(solution)/shard_map/ppermute | solution.py:976
  106.6 0.7 collective-permute-start.30
  107.3 4.2 %collective-permute-start.32 = (bf16[64,1024]{1,0:T(8,128)(2,1)S(1)}, bf16[64,1024]{1,0:T(8,128)(2,1)S(1)}, u32[]{:S(2)}, u32[]{:S(2)}) collective-permute-start(bf16[64,1024]{1,0:T(8,128)(2,1)S(1)} %get-tuple-element.266), channel_id=1, source_target_pairs={{0,16},{2,6},{4,20},{6,2},{8,24},{10,14},{12,28},{14,10},{16,0},{1... | collective-permute-start | bytes 393224 | tf_op jit(solution)/shard_map/ppermute | solution.py:1003
  111.7 3.0 %to_band.5 = bf16[4,512,1024]{2,1,0:T(8,128)(2,1)} custom-call(bf16[4,256,1152]{2,1,0:T(8,128)(2,1)S(1)} %get-tuple-element.260.refs_0_, bf16[4,512,1024]{2,1,0:T(8,128)(2,1)} %to_band.3.refs_1_), custom_call_target="tpu_custom_call", output_to_operand_aliasing={{}: (1, {})} | custom-call | flops 300000000 | tf_op jit(solution)/shard_map/to_band/pallas_call | solution.py:151
  114.7 0.9 token_sum.1
  115.6 1.0 collective-permute-done.32.arrived_ref
  116.5 0.7 finish.2
  117.3 2.4 %collective-permute-done.33.arrived_ref = bf16[160,256]{1,0:T(8,128)(2,1)S(1)} collective-permute-done((bf16[160,256]{1,0:T(8,128)(2,1)S(1)}, bf16[160,256]{1,0:T(8,128)(2,1)S(1)}, u32[]{:S(2)}, u32[]{:S(2)}) %collective-permute-start.33) | collective-permute-done | bytes 81952 | tf_op jit(solution)/shard_map/ppermute | solution.py:1003
  119.7 0.7 finish.3
  (80 shorter events, 1.5 us)
Async XLA Ops:
  0.6 22.2 %copy-start.10 = (s32[1,33]{1,0:T(1,128)S(1)}, s32[1,33]{1,0:T(1,128)}, u32[]{:S(2)}) copy-start(s32[1,33]{1,0:T(1,128)} %param.16) | copy-start | bytes 400
  0.7 6.2 %collective-permute-start = (bf16[32,256]{1,0:T(8,128)(2,1)}, bf16[32,256]{1,0:T(8,128)(2,1)S(1)}, u32[]{:S(2)}, u32[]{:S(2)}) collective-permute-start(bf16[32,256]{1,0:T(8,128)(2,1)} %bitcast.17), channel_id=1, source_target_pairs={{1,0},{0,1},{3,2},{2,3},{5,4},{4,5},{7,6},{6,7},{9,8},{8,9},{11,10... | collective-permute-start | bytes 49160 | tf_op jit(solution)/shard_map/ppermute | solution.py:976
  3.7 8.6 %collective-permute-start.1 = (bf16[1,3,32,256]{3,2,1,0:T(8,128)(2,1)}, bf16[1,3,32,256]{3,2,1,0:T(8,128)(2,1)S(1)}, u32[]{:S(2)}, u32[]{:S(2)}) collective-permute-start(bf16[1,3,32,256]{3,2,1,0:T(8,128)(2,1)} %bitcast.15), channel_id=1, source_target_pairs={{0,16},{2,6},{4,20},{6,2},{8,24},{10,14},{12,28},{14,10},{16,0},{1... | collective-permute-start | bytes 147464 | tf_op jit(solution)/shard_map/ppermute | solution.py:1003
  6.2 12.6 %collective-permute-start.3 = (bf16[512,256]{1,0:T(8,128)(2,1)}, bf16[512,256]{1,0:T(8,128)(2,1)S(1)}, u32[]{:S(2)}, u32[]{:S(2)}) collective-permute-start(bf16[512,256]{1,0:T(8,128)(2,1)} %refs_0_), channel_id=1, source_target_pairs={{1,0},{0,1},{3,2},{2,3},{5,4},{4,5},{7,6},{6,7},{9,8},{8,9},{11,10... | collective-permute-start | bytes 786440 | tf_op jit(solution)/shard_map/ppermute | solution.py:976
  7.7 8.9 %collective-permute-start.2 = (bf16[1,32,2560]{2,1,0:T(8,128)(2,1)S(1)}, bf16[1,32,2560]{2,1,0:T(8,128)(2,1)S(1)}, u32[]{:S(2)}, u32[]{:S(2)}) collective-permute-start(bf16[1,32,2560]{2,1,0:T(8,128)(2,1)S(1)} %maximum_bitcast_fusion), channel_id=1, source_target_pairs={{0,16},{2,6},{4,20},{6,2},{8,24},{10,14},{12,28},{14,10},{16,0},{1... | collective-permute-start | bytes 491528 | tf_op jit(solution)/shard_map/ppermute | solution.py:1003
  10.7 6.1 %collective-permute-start.5 = (bf16[384,256]{1,0:T(8,128)(2,1)S(1)}, bf16[384,256]{1,0:T(8,128)(2,1)S(1)}, u32[]{:S(2)}, u32[]{:S(2)}) collective-permute-start(bf16[384,256]{1,0:T(8,128)(2,1)S(1)} %get-tuple-element.280), channel_id=1, source_target_pairs={{0,2},{2,0},{4,6},{6,4},{8,10},{10,8},{12,14},{14,12},{16,18},{18,... | collective-permute-start | bytes 589832 | tf_op jit(solution)/shard_map/ppermute | solution.py:1010
  10.8 7.7 %collective-permute-start.6 = (bf16[384,256]{1,0:T(8,128)(2,1)S(1)}, bf16[384,256]{1,0:T(8,128)(2,1)S(1)}, u32[]{:S(2)}, u32[]{:S(2)}) collective-permute-start(bf16[384,256]{1,0:T(8,128)(2,1)S(1)} %get-tuple-element.279), channel_id=1, source_target_pairs={{2,4},{4,2},{6,8},{8,6},{10,12},{12,10},{14,16},{16,14},{18,20},{2... | collective-permute-start | bytes 589832 | tf_op jit(solution)/shard_map/ppermute | solution.py:1011
  12.3 9.0 %collective-permute-start.4 = (bf16[2,3,32,256]{3,2,1,0:T(8,128)(2,1)S(1)}, bf16[2,3,32,256]{3,2,1,0:T(8,128)(2,1)S(1)}, u32[]{:S(2)}, u32[]{:S(2)}) collective-permute-start(bf16[2,3,32,256]{3,2,1,0:T(8,128)(2,1)S(1)} %constant_dynamic-update-slice_fusion), channel_id=1, source_target_pairs={{0,8},{2,18},{4,12},{6,22},{8,0},{10,26},{12,4},{14,30},{16,24},{1... | collective-permute-start | bytes 294920 | tf_op jit(solution)/shard_map/ppermute | solution.py:1003
  16.7 13.9 %collective-permute-start.11 = (bf16[2,32,2560]{2,1,0:T(8,128)(2,1)S(1)}, bf16[2,32,2560]{2,1,0:T(8,128)(2,1)S(1)}, u32[]{:S(2)}, u32[]{:S(2)}) collective-permute-start(bf16[2,32,2560]{2,1,0:T(8,128)(2,1)S(1)} %constant_dynamic-update-slice_fusion.2), channel_id=1, source_target_pairs={{0,8},{2,18},{4,12},{6,22},{8,0},{10,26},{12,4},{14,30},{16,24},{1... | collective-permute-start | bytes 983048 | tf_op jit(solution)/shard_map/ppermute | solution.py:1003
  16.8 10.8 %collective-permute-start.7 = (bf16[384,256]{1,0:T(8,128)(2,1)S(1)}, bf16[384,256]{1,0:T(8,128)(2,1)S(1)}, u32[]{:S(2)}, u32[]{:S(2)}) collective-permute-start(bf16[384,256]{1,0:T(8,128)(2,1)S(1)} %collective-permute-done.5.refs_2_), channel_id=1, source_target_pairs={{1,0},{0,1},{3,2},{2,3},{5,4},{4,5},{7,6},{6,7},{9,8},{8,9},{11,10... | collective-permute-start | bytes 589832 | tf_op jit(solution)/shard_map/ppermute | solution.py:976
  18.5 10.2 %collective-permute-start.8 = (bf16[384,256]{1,0:T(8,128)(2,1)S(1)}, bf16[384,256]{1,0:T(8,128)(2,1)S(1)}, u32[]{:S(2)}, u32[]{:S(2)}) collective-permute-start(bf16[384,256]{1,0:T(8,128)(2,1)S(1)} %collective-permute-done.6.refs_4_), channel_id=1, source_target_pairs={{1,0},{0,1},{3,2},{2,3},{5,4},{4,5},{7,6},{6,7},{9,8},{8,9},{11,10... | collective-permute-start | bytes 589832 | tf_op jit(solution)/shard_map/ppermute | solution.py:976
  21.3 9.1 %collective-permute-start.9 = (bf16[4,3,32,256]{3,2,1,0:T(8,128)(2,1)S(1)}, bf16[4,3,32,256]{3,2,1,0:T(8,128)(2,1)S(1)}, u32[]{:S(2)}, u32[]{:S(2)}) collective-permute-start(bf16[4,3,32,256]{3,2,1,0:T(8,128)(2,1)S(1)} %constant_dynamic-update-slice_fusion.4), channel_id=1, source_target_pairs={{0,4},{2,10},{4,0},{6,14},{8,12},{10,2},{12,8},{14,6},{16,20},{18,... | collective-permute-start | bytes 589832 | tf_op jit(solution)/shard_map/ppermute | solution.py:1003
  22.9 2.2 %copy-start.1 = (bf16[4,512,1024]{2,1,0:T(8,128)(2,1)S(1)}, bf16[4,512,1024]{2,1,0:T(8,128)(2,1)}, u32[]{:S(2)}) copy-start(bf16[4,512,1024]{2,1,0:T(8,128)(2,1)} %band_ref.1) | copy-start | bytes 12582916
  25.1 3.6 %copy-start.6 = (bf16[512,256]{1,0:T(8,128)(2,1)S(1)}, bf16[512,256]{1,0:T(8,128)(2,1)}, u32[]{:S(2)}) copy-start(bf16[512,256]{1,0:T(8,128)(2,1)} %param.26) | copy-start | bytes 786436
  25.1 8.5 %copy-start.3 = (bf16[512,256]{1,0:T(8,128)(2,1)S(1)}, bf16[512,256]{1,0:T(8,128)(2,1)}, u32[]{:S(2)}) copy-start(bf16[512,256]{1,0:T(8,128)(2,1)} %refs_0_) | copy-start | bytes 786436
  25.1 8.5 %copy-start.5 = (f32[2,256]{1,0:T(2,128)S(1)}, f32[2,256]{1,0:T(2,128)}, u32[]{:S(2)}) copy-start(f32[2,256]{1,0:T(2,128)} %bias_ref.1) | copy-start | bytes 6148
  28.7 12.7 %collective-permute-start.13 = (bf16[512,256]{1,0:T(8,128)(2,1)S(1)}, bf16[512,256]{1,0:T(8,128)(2,1)S(1)}, u32[]{:S(2)}, u32[]{:S(2)}) collective-permute-start(bf16[512,256]{1,0:T(8,128)(2,1)S(1)} %copy-done.6), channel_id=1, source_target_pairs={{1,0},{0,1},{3,2},{2,3},{5,4},{4,5},{7,6},{6,7},{9,8},{8,9},{11,10... | collective-permute-start | bytes 786440 | tf_op jit(solution)/shard_map/ppermute | solution.py:976
  30.4 3.1 %collective-permute-start.10 = (bf16[8,3,32,256]{3,2,1,0:T(8,128)(2,1)S(1)}, bf16[8,3,32,256]{3,2,1,0:T(8,128)(2,1)S(1)}, u32[]{:S(2)}, u32[]{:S(2)}) collective-permute-start(bf16[8,3,32,256]{3,2,1,0:T(8,128)(2,1)S(1)} %constant_dynamic-update-slice_fusion.6.near_ref), channel_id=1, source_target_pairs={{0,2},{2,0},{4,6},{6,4},{8,10},{10,8},{12,14},{14,12},{16,18},{18,... | collective-permute-start | bytes 1179656 | tf_op jit(solution)/shard_map/ppermute | solution.py:1003
  30.6 15.4 %collective-permute-start.15 = (bf16[4,32,2560]{2,1,0:T(8,128)(2,1)S(1)}, bf16[4,32,2560]{2,1,0:T(8,128)(2,1)S(1)}, u32[]{:S(2)}, u32[]{:S(2)}) collective-permute-start(bf16[4,32,2560]{2,1,0:T(8,128)(2,1)S(1)} %constant_dynamic-update-slice_fusion.8), channel_id=1, source_target_pairs={{0,4},{2,10},{4,0},{6,14},{8,12},{10,2},{12,8},{14,6},{16,20},{18,... | collective-permute-start | bytes 1966088 | tf_op jit(solution)/shard_map/ppermute | solution.py:1003
  33.5 1.9 %copy-start.7 = (f32[2,256]{1,0:T(2,128)S(1)}, f32[2,256]{1,0:T(2,128)}, u32[]{:S(2)}) copy-start(f32[2,256]{1,0:T(2,128)} %param.20) | copy-start | bytes 6148
  33.6 1.9 %copy-start.8 = (f32[2,256]{1,0:T(2,128)S(1)}, f32[2,256]{1,0:T(2,128)}, u32[]{:S(2)}) copy-start(f32[2,256]{1,0:T(2,128)} %param.25) | copy-start | bytes 6148
  33.6 1.9 %copy-start.9 = (f32[2,256]{1,0:T(2,128)S(1)}, f32[2,256]{1,0:T(2,128)}, u32[]{:S(2)}) copy-start(f32[2,256]{1,0:T(2,128)} %param.24) | copy-start | bytes 6148
  35.5 5.9 %collective-permute-start.12 = (f32[6,256]{1,0:T(8,128)S(1)}, f32[6,256]{1,0:T(8,128)S(1)}, u32[]{:S(2)}, u32[]{:S(2)}) collective-permute-start(f32[6,256]{1,0:T(8,128)S(1)} %pad_maximum_fusion.1), channel_id=1, source_target_pairs={{1,0},{0,1},{3,2},{2,3},{5,4},{4,5},{7,6},{6,7},{9,8},{8,9},{11,10... | collective-permute-start | bytes 18440 | tf_op jit(solution)/shard_map/ppermute | solution.py:976
  37.3 4.2 %copy-start.2 = (bf16[4,512,1024]{2,1,0:T(8,128)(2,1)S(1)}, bf16[4,512,1024]{2,1,0:T(8,128)(2,1)}, u32[]{:S(2)}) copy-start(bf16[4,512,1024]{2,1,0:T(8,128)(2,1)} %band_ref.1) | copy-start | bytes 12582916
  41.0 5.0 %collective-permute-start.14 = (bf16[256,256]{1,0:T(8,128)(2,1)S(1)}, bf16[256,256]{1,0:T(8,128)(2,1)S(1)}, u32[]{:S(2)}, u32[]{:S(2)}) collective-permute-start(bf16[256,256]{1,0:T(8,128)(2,1)S(1)} %get-tuple-element.160.own_ref.refs_4_), channel_id=1, source_target_pairs={{1,0},{0,1},{3,2},{2,3},{5,4},{4,5},{7,6},{6,7},{9,8},{8,9},{11,10... | collective-permute-start | bytes 393224 | tf_op jit(solution)/shard_map/ppermute | solution.py:976
  46.1 4.2 %collective-permute-start.17 = (bf16[8,32,2560]{2,1,0:T(8,128)(2,1)S(1)}, bf16[8,32,2560]{2,1,0:T(8,128)(2,1)S(1)}, u32[]{:S(2)}, u32[]{:S(2)}) collective-permute-start(bf16[8,32,2560]{2,1,0:T(8,128)(2,1)S(1)} %constant_dynamic-update-slice_fusion.12.near_ref), channel_id=1, source_target_pairs={{0,2},{2,0},{4,6},{6,4},{8,10},{10,8},{12,14},{14,12},{16,18},{18,... | collective-permute-start | bytes 3932168 | tf_op jit(solution)/shard_map/ppermute | solution.py:1003
  49.9 1.5 %copy-start.4 = (f32[1024]{0:T(1024)S(1)}, f32[1024]{0:T(1024)}, u32[]{:S(2)}) copy-start(f32[1024]{0:T(1024)} %param.22) | copy-start | bytes 12292
  50.0 8.0 %collective-permute-start.16 = (bf16[256,256]{1,0:T(8,128)(2,1)S(1)}, bf16[256,256]{1,0:T(8,128)(2,1)S(1)}, u32[]{:S(2)}, u32[]{:S(2)}) collective-permute-start(bf16[256,256]{1,0:T(8,128)(2,1)S(1)} %get-tuple-element.167.own_ref.refs_5_), channel_id=1, source_target_pairs={{1,0},{0,1},{3,2},{2,3},{5,4},{4,5},{7,6},{6,7},{9,8},{8,9},{11,10... | collective-permute-start | bytes 393224 | tf_op jit(solution)/shard_map/ppermute | solution.py:976
  50.3 5.1 %copy-start = (bf16[4,512,1024]{2,1,0:T(8,128)(2,1)S(1)}, bf16[4,512,1024]{2,1,0:T(8,128)(2,1)}, u32[]{:S(2)}) copy-start(bf16[4,512,1024]{2,1,0:T(8,128)(2,1)} %band_ref.3) | copy-start | bytes 12582916
  53.6 9.8 %collective-permute-start.18 = (bf16[256,512]{1,0:T(8,128)(2,1)S(1)}, bf16[256,512]{1,0:T(8,128)(2,1)S(1)}, u32[]{:S(2)}, u32[]{:S(2)}) collective-permute-start(bf16[256,512]{1,0:T(8,128)(2,1)S(1)} %get-tuple-element.174.part_ref), channel_id=1, source_target_pairs={{1,0},{0,1},{3,2},{2,3},{5,4},{4,5},{7,6},{6,7},{9,8},{8,9},{11,10... | collective-permute-start | bytes 786440 | tf_op jit(solution)/shard_map/ppermute | solution.py:976
  60.1 8.3 %collective-permute-start.19 = (bf16[256,512]{1,0:T(8,128)(2,1)S(1)}, bf16[256,512]{1,0:T(8,128)(2,1)S(1)}, u32[]{:S(2)}, u32[]{:S(2)}) collective-permute-start(bf16[256,512]{1,0:T(8,128)(2,1)S(1)} %get-tuple-element.177.part_ref), channel_id=1, source_target_pairs={{1,0},{0,1},{3,2},{2,3},{5,4},{4,5},{7,6},{6,7},{9,8},{8,9},{11,10... | collective-permute-start | bytes 786440 | tf_op jit(solution)/shard_map/ppermute | solution.py:976
  65.9 9.5 %collective-permute-start.20 = (bf16[256,512]{1,0:T(8,128)(2,1)S(1)}, bf16[256,512]{1,0:T(8,128)(2,1)S(1)}, u32[]{:S(2)}, u32[]{:S(2)}) collective-permute-start(bf16[256,512]{1,0:T(8,128)(2,1)S(1)} %get-tuple-element.199.part_ref), channel_id=1, source_target_pairs={{1,0},{0,1},{3,2},{2,3},{5,4},{4,5},{7,6},{6,7},{9,8},{8,9},{11,10... | collective-permute-start | bytes 786440 | tf_op jit(solution)/shard_map/ppermute | solution.py:976
  74.2 6.0 %collective-permute-start.21 = (bf16[512,1024]{1,0:T(8,128)(2,1)S(1)}, bf16[512,1024]{1,0:T(8,128)(2,1)S(1)}, u32[]{:S(2)}, u32[]{:S(2)}) collective-permute-start(bf16[512,1024]{1,0:T(8,128)(2,1)S(1)} %get-tuple-element.207), channel_id=1, source_target_pairs={{0,2},{2,0},{4,6},{6,4},{8,10},{10,8},{12,14},{14,12},{16,18},{18,... | collective-permute-start | bytes 3145736 | tf_op jit(solution)/shard_map/ppermute | solution.py:1003
  74.3 10.4 %collective-permute-start.22 = (bf16[256,512]{1,0:T(8,128)(2,1)S(1)}, bf16[256,512]{1,0:T(8,128)(2,1)S(1)}, u32[]{:S(2)}, u32[]{:S(2)}) collective-permute-start(bf16[256,512]{1,0:T(8,128)(2,1)S(1)} %get-tuple-element.211.part_ref), channel_id=1, source_target_pairs={{1,0},{0,1},{3,2},{2,3},{5,4},{4,5},{7,6},{6,7},{9,8},{8,9},{11,10... | collective-permute-start | bytes 786440 | tf_op jit(solution)/shard_map/ppermute | solution.py:976
  80.5 9.8 %collective-permute-start.23 = (bf16[256,1024]{1,0:T(8,128)(2,1)S(1)}, bf16[256,1024]{1,0:T(8,128)(2,1)S(1)}, u32[]{:S(2)}, u32[]{:S(2)}) collective-permute-start(bf16[256,1024]{1,0:T(8,128)(2,1)S(1)} %get-tuple-element.221), channel_id=1, source_target_pairs={{0,4},{2,10},{4,0},{6,14},{8,12},{10,2},{12,8},{14,6},{16,20},{18,... | collective-permute-start | bytes 1572872 | tf_op jit(solution)/shard_map/ppermute | solution.py:1003
  92.2 3.2 %collective-permute-start.24 = (bf16[1056,256]{1,0:T(8,128)(2,1)S(1)}, bf16[1056,256]{1,0:T(8,128)(2,1)S(1)}, u32[]{:S(2)}, u32[]{:S(2)}) collective-permute-start(bf16[1056,256]{1,0:T(8,128)(2,1)S(1)} %get-tuple-element.239), channel_id=1, source_target_pairs={{0,2},{2,0},{4,6},{6,4},{8,10},{10,8},{12,14},{14,12},{16,18},{18,... | collective-permute-start | bytes 1622024 | tf_op jit(solution)/shard_map/ppermute | solution.py:1003
  94.5 12.0 %collective-permute-start.26 = (bf16[768,256]{1,0:T(8,128)(2,1)S(1)}, bf16[768,256]{1,0:T(8,128)(2,1)S(1)}, u32[]{:S(2)}, u32[]{:S(2)}) collective-permute-start(bf16[768,256]{1,0:T(8,128)(2,1)S(1)} %get-tuple-element.251), channel_id=1, source_target_pairs={{1,0},{0,1},{3,2},{2,3},{5,4},{4,5},{7,6},{6,7},{9,8},{8,9},{11,10... | collective-permute-start | bytes 1179656 | tf_op jit(solution)/shard_map/ppermute | solution.py:976
  95.6 8.1 %collective-permute-start.25 = (bf16[544,256]{1,0:T(8,128)(2,1)S(1)}, bf16[544,256]{1,0:T(8,128)(2,1)S(1)}, u32[]{:S(2)}, u32[]{:S(2)}) collective-permute-start(bf16[544,256]{1,0:T(8,128)(2,1)S(1)} %get-tuple-element.246), channel_id=1, source_target_pairs={{0,4},{2,10},{4,0},{6,14},{8,12},{10,2},{12,8},{14,6},{16,20},{18,... | collective-permute-start | bytes 835592 | tf_op jit(solution)/shard_map/ppermute | solution.py:1003
  96.9 10.4 %collective-permute-start.27 = (bf16[128,1024]{1,0:T(8,128)(2,1)S(1)}, bf16[128,1024]{1,0:T(8,128)(2,1)S(1)}, u32[]{:S(2)}, u32[]{:S(2)}) collective-permute-start(bf16[128,1024]{1,0:T(8,128)(2,1)S(1)} %get-tuple-element.254), channel_id=1, source_target_pairs={{0,8},{2,18},{4,12},{6,22},{8,0},{10,26},{12,4},{14,30},{16,24},{1... | collective-permute-start | bytes 786440 | tf_op jit(solution)/shard_map/ppermute | solution.py:1003
  97.6 17.1 %collective-permute-start.31 = (bf16[512,256]{1,0:T(8,128)(2,1)S(1)}, bf16[512,256]{1,0:T(8,128)(2,1)S(1)}, u32[]{:S(2)}, u32[]{:S(2)}) collective-permute-start(bf16[512,256]{1,0:T(8,128)(2,1)S(1)} %get-tuple-element.264), channel_id=1, source_target_pairs={{1,0},{0,1},{3,2},{2,3},{5,4},{4,5},{7,6},{6,7},{9,8},{8,9},{11,10... | collective-permute-start | bytes 786440 | tf_op jit(solution)/shard_map/ppermute | solution.py:976
  103.7 7.9 %collective-permute-start.28 = (bf16[288,256]{1,0:T(8,128)(2,1)S(1)}, bf16[288,256]{1,0:T(8,128)(2,1)S(1)}, u32[]{:S(2)}, u32[]{:S(2)}) collective-permute-start(bf16[288,256]{1,0:T(8,128)(2,1)S(1)} %get-tuple-element.257), channel_id=1, source_target_pairs={{0,8},{2,18},{4,12},{6,22},{8,0},{10,26},{12,4},{14,30},{16,24},{1... | collective-permute-start | bytes 442376 | tf_op jit(solution)/shard_map/ppermute | solution.py:1003
  106.5 8.2 %collective-permute-start.29 = (bf16[384,256]{1,0:T(8,128)(2,1)S(1)}, bf16[384,256]{1,0:T(8,128)(2,1)S(1)}, u32[]{:S(2)}, u32[]{:S(2)}) collective-permute-start(bf16[384,256]{1,0:T(8,128)(2,1)S(1)} %get-tuple-element.252), channel_id=1, source_target_pairs={{0,2},{2,0},{4,6},{6,4},{8,10},{10,8},{12,14},{14,12},{16,18},{18,... | collective-permute-start | bytes 589832 | tf_op jit(solution)/shard_map/ppermute | solution.py:1010
  106.6 8.1 %collective-permute-start.30 = (bf16[384,256]{1,0:T(8,128)(2,1)S(1)}, bf16[384,256]{1,0:T(8,128)(2,1)S(1)}, u32[]{:S(2)}, u32[]{:S(2)}) collective-permute-start(bf16[384,256]{1,0:T(8,128)(2,1)S(1)} %get-tuple-element.262), channel_id=1, source_target_pairs={{2,4},{4,2},{6,8},{8,6},{10,12},{12,10},{14,16},{16,14},{18,20},{2... | collective-permute-start | bytes 589832 | tf_op jit(solution)/shard_map/ppermute | solution.py:1011
  107.3 9.2 %collective-permute-start.32 = (bf16[64,1024]{1,0:T(8,128)(2,1)S(1)}, bf16[64,1024]{1,0:T(8,128)(2,1)S(1)}, u32[]{:S(2)}, u32[]{:S(2)}) collective-permute-start(bf16[64,1024]{1,0:T(8,128)(2,1)S(1)} %get-tuple-element.266), channel_id=1, source_target_pairs={{0,16},{2,6},{4,20},{6,2},{8,24},{10,14},{12,28},{14,10},{16,0},{1... | collective-permute-start | bytes 393224 | tf_op jit(solution)/shard_map/ppermute | solution.py:1003
  111.6 8.1 %collective-permute-start.33 = (bf16[160,256]{1,0:T(8,128)(2,1)S(1)}, bf16[160,256]{1,0:T(8,128)(2,1)S(1)}, u32[]{:S(2)}, u32[]{:S(2)}) collective-permute-start(bf16[160,256]{1,0:T(8,128)(2,1)S(1)} %get-tuple-element.269), channel_id=1, source_target_pairs={{0,16},{2,6},{4,20},{6,2},{8,24},{10,14},{12,28},{14,10},{16,0},{1... | collective-permute-start | bytes 245768 | tf_op jit(solution)/shard_map/ppermute | solution.py:1003
